TPU v7x, 256 devices: a whole 4x4x8 slice. The times are simulated.
256 devices in a mesh: group: 16 (over z, core), inner: 16 (over y, x).
Axes of the slice: x: 4, y: 4, z: 8, core: 2. Of those that a mesh axis runs over, the one named last changes fastest.
Arguments:
- leaf_blocks: float32 [65536, 256], P(('group', 'inner')), may hold values from -3 to 3, as said below
- bases: float32 [65536, 512], P(('group', 'inner')), may hold values from -2 to 2
- targets: float32 [65536, 128], P(('group', 'inner')), may hold values from -30 to 30
- coupling: float32 [8, 64], replicated, may hold values from 0.01 to 1
Outputs:
- solution: float32 [65536, 128], P(('group', 'inner'))
Inputs may be any that keep to these rules, and one draw needn't show every extreme that they name: Each leaf block of leaf_blocks is symmetric with all eigenvalues at least 0.4.
All inputs are finite; a program needn't handle non-finite values.
Results may differ from a plain program's by a relative error of at most 0.00014.
Values sent between devices are 32-bit elements; how exact they have to be, the bound alone decides.
No kernel may reach another device: no remote copies, remote signals or barrier semaphores. Data moves between devices by JAX's collectives and lax.ppermute only.
A program may use at most 64 MiB of HBM per device.

v0:
```python
import jax
import jax.numpy as jnp
from jax import lax
from jax.sharding import PartitionSpec as P


def from_partner(value, axis, distance):
    mask = 2**distance
    pairs = [(source, source ^ mask) for source in range(lax.axis_size(axis))]
    return lax.ppermute(value, axis, pairs)


def chol_solve(factor, rhs_cols):
    forward = lax.linalg.triangular_solve(factor, rhs_cols, left_side=True, lower=True)
    return lax.linalg.triangular_solve(
        factor, forward, left_side=True, lower=True, transpose_a=True
    )


def coefficients(gram_part, weights, projected):
    capacity = gram_part + jnp.diag(1.0 / weights)
    capacity = 0.5 * (capacity + capacity.T)
    return chol_solve(jnp.linalg.cholesky(capacity), projected)


def contract(first_arg, second_arg):
    return lax.dot_general(
        first_arg, second_arg, (((0,), (0,)), ((), ())), precision=lax.Precision.HIGHEST
    )


def matmul(first_arg, second_arg):
    return jnp.dot(first_arg, second_arg, precision=lax.Precision.HIGHEST)


def pair_step(partial_value, which_bit, inner_bits):
    if which_bit < inner_bits:
        return partial_value + from_partner(partial_value, "inner", which_bit)
    return partial_value + from_partner(partial_value, "group", which_bit - inner_bits)


def node_total(partial_value, node_span, inner_bits):
    for which_bit in range(node_span):
        partial_value = pair_step(partial_value, which_bit, inner_bits)
    return partial_value


def per_device(leaf_blocks, bases, targets, coupling):
    low_rank = coupling.shape[1]
    levels = coupling.shape[0]
    inner_bits = lax.axis_size("inner").bit_length() - 1
    factor = jnp.linalg.cholesky(leaf_blocks)
    solved = chol_solve(factor, jnp.concatenate([bases, targets], axis=1))
    for current in range(levels):
        level_basis = bases[:, current * low_rank : (current + 1) * low_rank]
        node_sum = node_total(contract(level_basis, solved), current + 1, inner_bits)
        solve_coef = coefficients(node_sum[:, :low_rank], coupling[current], node_sum[:, low_rank:])
        solved = solved[:, low_rank:] - matmul(solved[:, :low_rank], solve_coef)
    return solved


def solution(mesh):
    in_specs = (
        P(("group", "inner"), None),
        P(("group", "inner"), None),
        P(("group", "inner"), None),
        P(),
    )
    out_specs = P(("group", "inner"), None)
    return jax.shard_map(
        per_device, mesh=mesh, in_specs=in_specs, out_specs=out_specs, check_vma=False
    )
```

profile of v0, /device:TPU:2, one launch (start us, length us, event | category | flops | bytes accessed | tf_op | source)
XLA Modules:
  0.0 401.9 jit_solution(13628189534034849824)
XLA Ops:
  1.2 11.7 %cholesky.64 = f32[128,128]{1,0:T(8,128)S(1)} custom-call(f32[128,128]{1,0:T(8,128)S(1)} %cholesky.338), custom_call_target="Cholesky" | custom-call | tf_op jit(solution)/shard_map/jit(cholesky)/cholesky | solution.py:52
  13.0 9.8 %custom-call.58 = f32[1,128,128]{1,2,0:T(8,128)S(1)} custom-call(f32[1,128,128]{2,1,0:T(8,128)S(1)} %get-tuple-element.27), custom_call_target="InvertDiagBlocksLowerTriangular" | custom-call | tf_op jit(solution)/shard_map/jit(cholesky)/cholesky | solution.py:52
  23.3 11.7 %cholesky.132 = f32[128,128]{1,0:T(8,128)S(1)} custom-call(f32[128,128]{1,0:T(8,128)S(1)} %convolution_subtract_fusion.10), custom_call_target="Cholesky" | custom-call | tf_op jit(solution)/shard_map/jit(cholesky)/cholesky | solution.py:52
  37.2 4.3 %while.1 = (s32[]{:T(128)}, f32[256,256]{1,0:T(8,128)S(1)}, s32[2,2]{1,0:T(2,128)S(1)}, f32[2,128,128]{2,1,0:T(8,128)S(1)}, s32[]{:T(128)}) while((s32[]{:T(128)}, f32[256,256]{1,0:T(8,128)S(1)}, s32[2,2]{1,0:T(2,128)S(1)}, f32[2,128,128]{2,1,0:T(8,128)S(1)}, s32[]{:T(128)}) %tuple.31), condition=%wide.while_cond, body=%wide.while_body.sunk | while | flops 2 | bytes 131181 | solution.py:15
  41.4 19.7 %custom-call.59 = f32[2,128,128]{1,2,0:T(8,128)S(1)} custom-call(f32[2,128,128]{2,1,0:T(8,128)S(1)} %get-tuple-element.13), custom_call_target="InvertDiagBlocksLowerTriangular" | custom-call | tf_op jit(solution)/shard_map/triangular_solve | solution.py:15
  68.3 7.2 %collective-permute-done = f32[64,640]{0,1:T(8,128)S(1)} collective-permute-done((f32[64,640]{0,1:T(8,128)S(1)}, f32[64,640]{0,1:T(8,128)S(1)}, u32[]{:S(2)}, u32[]{:S(2)}) %collective-permute-start) | collective-permute-done | bytes 163872 | tf_op jit(solution)/shard_map/ppermute | solution.py:10
  75.7 5.8 %cholesky.252 = f32[64,64]{1,0:T(8,128)S(1)} custom-call(f32[64,64]{1,0:T(8,128)S(1)} %fusion.91), custom_call_target="Cholesky" | custom-call | tf_op jit(solution)/shard_map/jit(cholesky)/cholesky | solution.py:23
  82.9 4.9 %custom-call.60 = f32[1,64,64]{1,2,0:T(8,128)S(1)} custom-call(f32[1,64,64]{2,1,0:T(8,128)S(1)} %fusion.43), custom_call_target="InvertDiagBlocksLowerTriangular" | custom-call | tf_op jit(solution)/shard_map/triangular_solve | solution.py:15
  90.9 7.4 %collective-permute-done.1 = f32[64,576]{0,1:T(8,128)S(1)} collective-permute-done((f32[64,576]{0,1:T(8,128)S(1)}, f32[64,576]{0,1:T(8,128)S(1)}, u32[]{:S(2)}, u32[]{:S(2)}) %collective-permute-start.1) | collective-permute-done | bytes 147488 | tf_op jit(solution)/shard_map/ppermute | solution.py:10
  98.3 2.8 collective-permute-start.2
  101.1 6.0 %collective-permute-done.2 = f32[64,576]{0,1:T(8,128)S(1)} collective-permute-done((f32[64,576]{0,1:T(8,128)S(1)}, f32[64,576]{0,1:T(8,128)S(1)}, u32[]{:S(2)}, u32[]{:S(2)}) %collective-permute-start.2) | collective-permute-done | bytes 147488 | tf_op jit(solution)/shard_map/ppermute | solution.py:10
  107.4 5.8 %cholesky.263 = f32[64,64]{1,0:T(8,128)S(1)} custom-call(f32[64,64]{1,0:T(8,128)S(1)} %fusion.86), custom_call_target="Cholesky" | custom-call | tf_op jit(solution)/shard_map/jit(cholesky)/cholesky | solution.py:23
  114.6 4.9 %custom-call.61 = f32[1,64,64]{1,2,0:T(8,128)S(1)} custom-call(f32[1,64,64]{2,1,0:T(8,128)S(1)} %fusion.44), custom_call_target="InvertDiagBlocksLowerTriangular" | custom-call | tf_op jit(solution)/shard_map/triangular_solve | solution.py:15
  122.6 5.6 %collective-permute-done.3 = f32[64,512]{0,1:T(8,128)S(1)} collective-permute-done((f32[64,512]{0,1:T(8,128)S(1)}, f32[64,512]{0,1:T(8,128)S(1)}, u32[]{:S(2)}, u32[]{:S(2)}) %collective-permute-start.3) | collective-permute-done | bytes 131104 | tf_op jit(solution)/shard_map/ppermute | solution.py:10
  128.3 4.5 %collective-permute-start.4 = (f32[64,512]{0,1:T(8,128)S(1)}, f32[64,512]{0,1:T(8,128)S(1)}, u32[]{:S(2)}, u32[]{:S(2)}) collective-permute-start(f32[64,512]{0,1:T(8,128)S(1)} %add.227), channel_id=1, source_target_pairs={{0,2},{1,3},{2,0},{3,1},{4,6},{5,7},{6,4},{7,5},{8,10},{9,11},{10,... | collective-permute-start | bytes 393224 | tf_op jit(solution)/shard_map/ppermute | solution.py:10
  132.7 4.4 %collective-permute-done.4 = f32[64,512]{0,1:T(8,128)S(1)} collective-permute-done((f32[64,512]{0,1:T(8,128)S(1)}, f32[64,512]{0,1:T(8,128)S(1)}, u32[]{:S(2)}, u32[]{:S(2)}) %collective-permute-start.4) | collective-permute-done | bytes 131104 | tf_op jit(solution)/shard_map/ppermute | solution.py:10
  138.8 4.8 %collective-permute-done.5 = f32[64,512]{0,1:T(8,128)S(1)} collective-permute-done((f32[64,512]{0,1:T(8,128)S(1)}, f32[64,512]{0,1:T(8,128)S(1)}, u32[]{:S(2)}, u32[]{:S(2)}) %collective-permute-start.5) | collective-permute-done | bytes 131104 | tf_op jit(solution)/shard_map/ppermute | solution.py:10
  143.8 5.8 %cholesky.274 = f32[64,64]{1,0:T(8,128)S(1)} custom-call(f32[64,64]{1,0:T(8,128)S(1)} %fusion.81), custom_call_target="Cholesky" | custom-call | tf_op jit(solution)/shard_map/jit(cholesky)/cholesky | solution.py:23
  151.0 4.9 %custom-call.62 = f32[1,64,64]{1,2,0:T(8,128)S(1)} custom-call(f32[1,64,64]{2,1,0:T(8,128)S(1)} %fusion.45), custom_call_target="InvertDiagBlocksLowerTriangular" | custom-call | tf_op jit(solution)/shard_map/triangular_solve | solution.py:15
  159.2 6.9 %collective-permute-done.6 = f32[64,448]{0,1:T(8,128)S(1)} collective-permute-done((f32[64,448]{0,1:T(8,128)S(1)}, f32[64,448]{0,1:T(8,128)S(1)}, u32[]{:S(2)}, u32[]{:S(2)}) %collective-permute-start.6) | collective-permute-done | bytes 114720 | tf_op jit(solution)/shard_map/ppermute | solution.py:10
  168.0 5.7 %collective-permute-done.7 = f32[64,448]{0,1:T(8,128)S(1)} collective-permute-done((f32[64,448]{0,1:T(8,128)S(1)}, f32[64,448]{0,1:T(8,128)S(1)}, u32[]{:S(2)}, u32[]{:S(2)}) %collective-permute-start.7) | collective-permute-done | bytes 114720 | tf_op jit(solution)/shard_map/ppermute | solution.py:10
  175.4 4.4 %collective-permute-done.8 = f32[64,448]{0,1:T(8,128)S(1)} collective-permute-done((f32[64,448]{0,1:T(8,128)S(1)}, f32[64,448]{0,1:T(8,128)S(1)}, u32[]{:S(2)}, u32[]{:S(2)}) %collective-permute-start.8) | collective-permute-done | bytes 114720 | tf_op jit(solution)/shard_map/ppermute | solution.py:10
  179.9 3.5 collective-permute-start.9
  183.3 4.3 %collective-permute-done.9 = f32[64,448]{0,1:T(8,128)S(1)} collective-permute-done((f32[64,448]{0,1:T(8,128)S(1)}, f32[64,448]{0,1:T(8,128)S(1)}, u32[]{:S(2)}, u32[]{:S(2)}) %collective-permute-start.9) | collective-permute-done | bytes 114720 | tf_op jit(solution)/shard_map/ppermute | solution.py:10
  187.9 5.8 %cholesky.285 = f32[64,64]{1,0:T(8,128)S(1)} custom-call(f32[64,64]{1,0:T(8,128)S(1)} %fusion.76), custom_call_target="Cholesky" | custom-call | tf_op jit(solution)/shard_map/jit(cholesky)/cholesky | solution.py:23
  195.1 4.9 %custom-call.63 = f32[1,64,64]{1,2,0:T(8,128)S(1)} custom-call(f32[1,64,64]{2,1,0:T(8,128)S(1)} %fusion.46), custom_call_target="InvertDiagBlocksLowerTriangular" | custom-call | tf_op jit(solution)/shard_map/triangular_solve | solution.py:15
  202.6 5.1 %collective-permute-done.10 = f32[64,384]{0,1:T(8,128)S(1)} collective-permute-done((f32[64,384]{0,1:T(8,128)S(1)}, f32[64,384]{0,1:T(8,128)S(1)}, u32[]{:S(2)}, u32[]{:S(2)}) %collective-permute-start.10) | collective-permute-done | bytes 98336 | tf_op jit(solution)/shard_map/ppermute | solution.py:10
  207.7 2.4 collective-permute-start.11
  210.1 4.9 %collective-permute-done.11 = f32[64,384]{0,1:T(8,128)S(1)} collective-permute-done((f32[64,384]{0,1:T(8,128)S(1)}, f32[64,384]{0,1:T(8,128)S(1)}, u32[]{:S(2)}, u32[]{:S(2)}) %collective-permute-start.11) | collective-permute-done | bytes 98336 | tf_op jit(solution)/shard_map/ppermute | solution.py:10
  216.6 4.1 %collective-permute-done.12 = f32[64,384]{0,1:T(8,128)S(1)} collective-permute-done((f32[64,384]{0,1:T(8,128)S(1)}, f32[64,384]{0,1:T(8,128)S(1)}, u32[]{:S(2)}, u32[]{:S(2)}) %collective-permute-start.12) | collective-permute-done | bytes 98336 | tf_op jit(solution)/shard_map/ppermute | solution.py:10
  220.7 3.3 collective-permute-start.13
  224.0 4.0 collective-permute-done.13
  229.8 5.8 %cholesky.296 = f32[64,64]{1,0:T(8,128)S(1)} custom-call(f32[64,64]{1,0:T(8,128)S(1)} %fusion.71), custom_call_target="Cholesky" | custom-call | tf_op jit(solution)/shard_map/jit(cholesky)/cholesky | solution.py:23
  237.0 4.9 %custom-call.64 = f32[1,64,64]{1,2,0:T(8,128)S(1)} custom-call(f32[1,64,64]{2,1,0:T(8,128)S(1)} %fusion.47), custom_call_target="InvertDiagBlocksLowerTriangular" | custom-call | tf_op jit(solution)/shard_map/triangular_solve | solution.py:15
  244.4 5.6 %collective-permute-done.15 = f32[64,320]{0,1:T(8,128)S(1)} collective-permute-done((f32[64,320]{0,1:T(8,128)S(1)}, f32[64,320]{0,1:T(8,128)S(1)}, u32[]{:S(2)}, u32[]{:S(2)}) %collective-permute-start.15) | collective-permute-done | bytes 81952 | tf_op jit(solution)/shard_map/ppermute | solution.py:10
  250.1 2.4 collective-permute-start.16
  252.5 4.6 %collective-permute-done.16 = f32[64,320]{0,1:T(8,128)S(1)} collective-permute-done((f32[64,320]{0,1:T(8,128)S(1)}, f32[64,320]{0,1:T(8,128)S(1)}, u32[]{:S(2)}, u32[]{:S(2)}) %collective-permute-start.16) | collective-permute-done | bytes 81952 | tf_op jit(solution)/shard_map/ppermute | solution.py:10
  258.8 3.7 collective-permute-done.17
  262.5 3.3 collective-permute-start.18
  265.8 3.6 collective-permute-done.18
  273.2 4.5 %collective-permute-done.20 = f32[64,320]{0,1:T(8,128)S(1)} collective-permute-done((f32[64,320]{0,1:T(8,128)S(1)}, f32[64,320]{0,1:T(8,128)S(1)}, u32[]{:S(2)}, u32[]{:S(2)}) %collective-permute-start.20) | collective-permute-done | bytes 81952 | tf_op jit(solution)/shard_map/ppermute | solution.py:10
  277.9 5.8 %cholesky.307 = f32[64,64]{1,0:T(8,128)S(1)} custom-call(f32[64,64]{1,0:T(8,128)S(1)} %fusion.66), custom_call_target="Cholesky" | custom-call | tf_op jit(solution)/shard_map/jit(cholesky)/cholesky | solution.py:23
  285.1 4.9 %custom-call.65 = f32[1,64,64]{1,2,0:T(8,128)S(1)} custom-call(f32[1,64,64]{2,1,0:T(8,128)S(1)} %fusion.48), custom_call_target="InvertDiagBlocksLowerTriangular" | custom-call | tf_op jit(solution)/shard_map/triangular_solve | solution.py:15
  292.2 4.4 %collective-permute-done.21 = f32[64,256]{0,1:T(8,128)S(1)} collective-permute-done((f32[64,256]{0,1:T(8,128)S(1)}, f32[64,256]{0,1:T(8,128)S(1)}, u32[]{:S(2)}, u32[]{:S(2)}) %collective-permute-start.21) | collective-permute-done | bytes 65568 | tf_op jit(solution)/shard_map/ppermute | solution.py:10
  296.6 2.5 collective-permute-start.22
  299.1 4.0 %collective-permute-done.22 = f32[64,256]{0,1:T(8,128)S(1)} collective-permute-done((f32[64,256]{0,1:T(8,128)S(1)}, f32[64,256]{0,1:T(8,128)S(1)}, u32[]{:S(2)}, u32[]{:S(2)}) %collective-permute-start.22) | collective-permute-done | bytes 65568 | tf_op jit(solution)/shard_map/ppermute | solution.py:10
  304.8 3.4 collective-permute-done.23
  308.2 4.3 %collective-permute-start.24 = (f32[64,256]{0,1:T(8,128)S(1)}, f32[64,256]{0,1:T(8,128)S(1)}, u32[]{:S(2)}, u32[]{:S(2)}) collective-permute-start(f32[64,256]{0,1:T(8,128)S(1)} %add.255), channel_id=1, source_target_pairs={{0,8},{1,9},{2,10},{3,11},{4,12},{5,13},{6,14},{7,15},{8,0},{9,1},... | collective-permute-start | bytes 196616 | tf_op jit(solution)/shard_map/ppermute | solution.py:10
  312.5 2.9 collective-permute-done.24
  319.0 3.8 collective-permute-done.26
  322.8 3.6 collective-permute-start.27
  326.4 6.0 %collective-permute-done.27 = f32[64,256]{0,1:T(8,128)S(1)} collective-permute-done((f32[64,256]{0,1:T(8,128)S(1)}, f32[64,256]{0,1:T(8,128)S(1)}, u32[]{:S(2)}, u32[]{:S(2)}) %collective-permute-start.27) | collective-permute-done | bytes 65568 | tf_op jit(solution)/shard_map/ppermute | solution.py:10
  332.7 5.9 %cholesky.318 = f32[64,64]{1,0:T(8,128)S(1)} custom-call(f32[64,64]{1,0:T(8,128)S(1)} %copy.44), custom_call_target="Cholesky" | custom-call | tf_op jit(solution)/shard_map/jit(cholesky)/cholesky | solution.py:23
  339.9 4.9 %custom-call.66 = f32[1,64,64]{1,2,0:T(8,128)S(1)} custom-call(f32[1,64,64]{2,1,0:T(8,128)S(1)} %fusion.49), custom_call_target="InvertDiagBlocksLowerTriangular" | custom-call | tf_op jit(solution)/shard_map/triangular_solve | solution.py:15
  346.7 3.8 collective-permute-done.28
  351.8 4.5 %collective-permute-done.29 = f32[64,192]{1,0:T(8,128)S(1)} collective-permute-done((f32[64,192]{1,0:T(8,128)S(1)}, f32[64,192]{1,0:T(8,128)S(1)}, u32[]{:S(2)}, u32[]{:S(2)}) %collective-permute-start.29) | collective-permute-done | bytes 49184 | tf_op jit(solution)/shard_map/ppermute | solution.py:10
  357.0 4.2 %collective-permute-done.30 = f32[64,192]{1,0:T(8,128)S(1)} collective-permute-done((f32[64,192]{1,0:T(8,128)S(1)}, f32[64,192]{1,0:T(8,128)S(1)}, u32[]{:S(2)}, u32[]{:S(2)}) %collective-permute-start.30) | collective-permute-done | bytes 49184 | tf_op jit(solution)/shard_map/ppermute | solution.py:10
  361.2 3.5 collective-permute-start.31
  369.0 3.7 collective-permute-done.33
  374.9 3.8 collective-permute-done.34
  378.7 5.3 %collective-permute-start.35 = (f32[64,192]{1,0:T(8,128)S(1)}, f32[64,192]{1,0:T(8,128)S(1)}, u32[]{:S(2)}, u32[]{:S(2)}) collective-permute-start(f32[64,192]{1,0:T(8,128)S(1)} %add.268), channel_id=1, source_target_pairs={{0,128},{16,144},{32,160},{48,176},{64,192},{80,208},{96,224},{112... | collective-permute-start | bytes 147464 | tf_op jit(solution)/shard_map/ppermute | solution.py:10
  384.2 3.5 collective-permute-done.35
  388.0 5.9 %cholesky.329 = f32[64,64]{1,0:T(8,128)S(1)} custom-call(f32[64,64]{1,0:T(8,128)S(1)} %copy.49), custom_call_target="Cholesky" | custom-call | tf_op jit(solution)/shard_map/jit(cholesky)/cholesky | solution.py:23
  395.2 4.9 %custom-call.67 = f32[1,64,64]{1,2,0:T(8,128)S(1)} custom-call(f32[1,64,64]{2,1,0:T(8,128)S(1)} %fusion.50), custom_call_target="InvertDiagBlocksLowerTriangular" | custom-call | tf_op jit(solution)/shard_map/triangular_solve | solution.py:15
  (201 shorter events, 73.9 us)
Async XLA Ops:
  0.0 1.2 copy-start.1
  37.0 24.1 %copy-start = (f32[256,512]{1,0:T(8,128)S(1)}, f32[256,512]{1,0:T(8,128)}, u32[]{:S(2)}) copy-start(f32[256,512]{1,0:T(8,128)} %param.6) | copy-start | bytes 1572868
  61.1 0.9 copy-start.2
  64.7 3.5 copy-start.3
  66.0 9.5 %collective-permute-start = (f32[64,640]{0,1:T(8,128)S(1)}, f32[64,640]{0,1:T(8,128)S(1)}, u32[]{:S(2)}, u32[]{:S(2)}) collective-permute-start(f32[64,640]{0,1:T(8,128)S(1)} %convolution_bitcast_fusion), channel_id=1, source_target_pairs={{0,1},{1,0},{2,3},{3,2},{4,5},{5,4},{6,7},{7,6},{8,9},{9,8},{10,11... | collective-permute-start | bytes 491528 | tf_op jit(solution)/shard_map/ppermute | solution.py:10
  90.5 7.8 %collective-permute-start.1 = (f32[64,576]{0,1:T(8,128)S(1)}, f32[64,576]{0,1:T(8,128)S(1)}, u32[]{:S(2)}, u32[]{:S(2)}) collective-permute-start(f32[64,576]{0,1:T(8,128)S(1)} %convolution_bitcast_fusion.1), channel_id=1, source_target_pairs={{0,1},{1,0},{2,3},{3,2},{4,5},{5,4},{6,7},{7,6},{8,9},{9,8},{10,11... | collective-permute-start | bytes 442376 | tf_op jit(solution)/shard_map/ppermute | solution.py:10
  98.3 8.8 %collective-permute-start.2 = (f32[64,576]{0,1:T(8,128)S(1)}, f32[64,576]{0,1:T(8,128)S(1)}, u32[]{:S(2)}, u32[]{:S(2)}) collective-permute-start(f32[64,576]{0,1:T(8,128)S(1)} %add.223), channel_id=1, source_target_pairs={{0,2},{1,3},{2,0},{3,1},{4,6},{5,7},{6,4},{7,5},{8,10},{9,11},{10,... | collective-permute-start | bytes 442376 | tf_op jit(solution)/shard_map/ppermute | solution.py:10
  121.8 6.5 %collective-permute-start.3 = (f32[64,512]{0,1:T(8,128)S(1)}, f32[64,512]{0,1:T(8,128)S(1)}, u32[]{:S(2)}, u32[]{:S(2)}) collective-permute-start(f32[64,512]{0,1:T(8,128)S(1)} %convolution_bitcast_fusion.2), channel_id=1, source_target_pairs={{0,1},{1,0},{2,3},{3,2},{4,5},{5,4},{6,7},{7,6},{8,9},{9,8},{10,11... | collective-permute-start | bytes 393224 | tf_op jit(solution)/shard_map/ppermute | solution.py:10
  128.3 8.8 %collective-permute-start.4 = (f32[64,512]{0,1:T(8,128)S(1)}, f32[64,512]{0,1:T(8,128)S(1)}, u32[]{:S(2)}, u32[]{:S(2)}) collective-permute-start(f32[64,512]{0,1:T(8,128)S(1)} %add.227), channel_id=1, source_target_pairs={{0,2},{1,3},{2,0},{3,1},{4,6},{5,7},{6,4},{7,5},{8,10},{9,11},{10,... | collective-permute-start | bytes 393224 | tf_op jit(solution)/shard_map/ppermute | solution.py:10
  137.1 6.5 %collective-permute-start.5 = (f32[64,512]{0,1:T(8,128)S(1)}, f32[64,512]{0,1:T(8,128)S(1)}, u32[]{:S(2)}, u32[]{:S(2)}) collective-permute-start(f32[64,512]{0,1:T(8,128)S(1)} %add.228), channel_id=1, source_target_pairs={{0,4},{1,5},{2,6},{3,7},{4,0},{5,1},{6,2},{7,3},{8,12},{9,13},{10,... | collective-permute-start | bytes 393224 | tf_op jit(solution)/shard_map/ppermute | solution.py:10
  158.3 7.8 %collective-permute-start.6 = (f32[64,448]{0,1:T(8,128)S(1)}, f32[64,448]{0,1:T(8,128)S(1)}, u32[]{:S(2)}, u32[]{:S(2)}) collective-permute-start(f32[64,448]{0,1:T(8,128)S(1)} %convolution_bitcast_fusion.3), channel_id=1, source_target_pairs={{0,1},{1,0},{2,3},{3,2},{4,5},{5,4},{6,7},{7,6},{8,9},{9,8},{10,11... | collective-permute-start | bytes 344072 | tf_op jit(solution)/shard_map/ppermute | solution.py:10
  166.1 7.6 %collective-permute-start.7 = (f32[64,448]{0,1:T(8,128)S(1)}, f32[64,448]{0,1:T(8,128)S(1)}, u32[]{:S(2)}, u32[]{:S(2)}) collective-permute-start(f32[64,448]{0,1:T(8,128)S(1)} %add.232), channel_id=1, source_target_pairs={{0,2},{1,3},{2,0},{3,1},{4,6},{5,7},{6,4},{7,5},{8,10},{9,11},{10,... | collective-permute-start | bytes 344072 | tf_op jit(solution)/shard_map/ppermute | solution.py:10
  173.7 6.1 %collective-permute-start.8 = (f32[64,448]{0,1:T(8,128)S(1)}, f32[64,448]{0,1:T(8,128)S(1)}, u32[]{:S(2)}, u32[]{:S(2)}) collective-permute-start(f32[64,448]{0,1:T(8,128)S(1)} %add.233), channel_id=1, source_target_pairs={{0,4},{1,5},{2,6},{3,7},{4,0},{5,1},{6,2},{7,3},{8,12},{9,13},{10,... | collective-permute-start | bytes 344072 | tf_op jit(solution)/shard_map/ppermute | solution.py:10
  179.9 7.8 %collective-permute-start.9 = (f32[64,448]{0,1:T(8,128)S(1)}, f32[64,448]{0,1:T(8,128)S(1)}, u32[]{:S(2)}, u32[]{:S(2)}) collective-permute-start(f32[64,448]{0,1:T(8,128)S(1)} %add.234), channel_id=1, source_target_pairs={{0,8},{1,9},{2,10},{3,11},{4,12},{5,13},{6,14},{7,15},{8,0},{9,1},... | collective-permute-start | bytes 344072 | tf_op jit(solution)/shard_map/ppermute | solution.py:10
  201.9 5.8 %collective-permute-start.10 = (f32[64,384]{0,1:T(8,128)S(1)}, f32[64,384]{0,1:T(8,128)S(1)}, u32[]{:S(2)}, u32[]{:S(2)}) collective-permute-start(f32[64,384]{0,1:T(8,128)S(1)} %convolution_bitcast_fusion.4), channel_id=1, source_target_pairs={{0,1},{1,0},{2,3},{3,2},{4,5},{5,4},{6,7},{7,6},{8,9},{9,8},{10,11... | collective-permute-start | bytes 294920 | tf_op jit(solution)/shard_map/ppermute | solution.py:10
  207.7 7.3 %collective-permute-start.11 = (f32[64,384]{0,1:T(8,128)S(1)}, f32[64,384]{0,1:T(8,128)S(1)}, u32[]{:S(2)}, u32[]{:S(2)}) collective-permute-start(f32[64,384]{0,1:T(8,128)S(1)} %add.238), channel_id=1, source_target_pairs={{0,2},{1,3},{2,0},{3,1},{4,6},{5,7},{6,4},{7,5},{8,10},{9,11},{10,... | collective-permute-start | bytes 294920 | tf_op jit(solution)/shard_map/ppermute | solution.py:10
  215.0 5.8 %collective-permute-start.12 = (f32[64,384]{0,1:T(8,128)S(1)}, f32[64,384]{0,1:T(8,128)S(1)}, u32[]{:S(2)}, u32[]{:S(2)}) collective-permute-start(f32[64,384]{0,1:T(8,128)S(1)} %add.239), channel_id=1, source_target_pairs={{0,4},{1,5},{2,6},{3,7},{4,0},{5,1},{6,2},{7,3},{8,12},{9,13},{10,... | collective-permute-start | bytes 294920 | tf_op jit(solution)/shard_map/ppermute | solution.py:10
  220.7 7.3 %collective-permute-start.13 = (f32[64,384]{0,1:T(8,128)S(1)}, f32[64,384]{0,1:T(8,128)S(1)}, u32[]{:S(2)}, u32[]{:S(2)}) collective-permute-start(f32[64,384]{0,1:T(8,128)S(1)} %add.240), channel_id=1, source_target_pairs={{0,8},{1,9},{2,10},{3,11},{4,12},{5,13},{6,14},{7,15},{8,0},{9,1},... | collective-permute-start | bytes 294920 | tf_op jit(solution)/shard_map/ppermute | solution.py:10
  228.0 1.5 collective-permute-start.14
  243.8 6.3 %collective-permute-start.15 = (f32[64,320]{0,1:T(8,128)S(1)}, f32[64,320]{0,1:T(8,128)S(1)}, u32[]{:S(2)}, u32[]{:S(2)}) collective-permute-start(f32[64,320]{0,1:T(8,128)S(1)} %convolution_bitcast_fusion.5), channel_id=1, source_target_pairs={{0,1},{1,0},{2,3},{3,2},{4,5},{5,4},{6,7},{7,6},{8,9},{9,8},{10,11... | collective-permute-start | bytes 245768 | tf_op jit(solution)/shard_map/ppermute | solution.py:10
  250.1 7.0 %collective-permute-start.16 = (f32[64,320]{0,1:T(8,128)S(1)}, f32[64,320]{0,1:T(8,128)S(1)}, u32[]{:S(2)}, u32[]{:S(2)}) collective-permute-start(f32[64,320]{0,1:T(8,128)S(1)} %add.245), channel_id=1, source_target_pairs={{0,2},{1,3},{2,0},{3,1},{4,6},{5,7},{6,4},{7,5},{8,10},{9,11},{10,... | collective-permute-start | bytes 245768 | tf_op jit(solution)/shard_map/ppermute | solution.py:10
  257.1 5.4 %collective-permute-start.17 = (f32[64,320]{0,1:T(8,128)S(1)}, f32[64,320]{0,1:T(8,128)S(1)}, u32[]{:S(2)}, u32[]{:S(2)}) collective-permute-start(f32[64,320]{0,1:T(8,128)S(1)} %add.246), channel_id=1, source_target_pairs={{0,4},{1,5},{2,6},{3,7},{4,0},{5,1},{6,2},{7,3},{8,12},{9,13},{10,... | collective-permute-start | bytes 245768 | tf_op jit(solution)/shard_map/ppermute | solution.py:10
  262.5 6.9 %collective-permute-start.18 = (f32[64,320]{0,1:T(8,128)S(1)}, f32[64,320]{0,1:T(8,128)S(1)}, u32[]{:S(2)}, u32[]{:S(2)}) collective-permute-start(f32[64,320]{0,1:T(8,128)S(1)} %add.247), channel_id=1, source_target_pairs={{0,8},{1,9},{2,10},{3,11},{4,12},{5,13},{6,14},{7,15},{8,0},{9,1},... | collective-permute-start | bytes 245768 | tf_op jit(solution)/shard_map/ppermute | solution.py:10
  269.5 1.7 collective-permute-start.19
  271.2 6.5 %collective-permute-start.20 = (f32[64,320]{0,1:T(8,128)S(1)}, f32[64,320]{0,1:T(8,128)S(1)}, u32[]{:S(2)}, u32[]{:S(2)}) collective-permute-start(f32[64,320]{0,1:T(8,128)S(1)} %add.249), channel_id=1, source_target_pairs={{0,32},{16,48},{32,0},{48,16},{64,96},{80,112},{96,64},{112,80},{1... | collective-permute-start | bytes 245768 | tf_op jit(solution)/shard_map/ppermute | solution.py:10
  291.5 5.1 %collective-permute-start.21 = (f32[64,256]{0,1:T(8,128)S(1)}, f32[64,256]{0,1:T(8,128)S(1)}, u32[]{:S(2)}, u32[]{:S(2)}) collective-permute-start(f32[64,256]{0,1:T(8,128)S(1)} %convolution_bitcast_fusion.6), channel_id=1, source_target_pairs={{0,1},{1,0},{2,3},{3,2},{4,5},{5,4},{6,7},{7,6},{8,9},{9,8},{10,11... | collective-permute-start | bytes 196616 | tf_op jit(solution)/shard_map/ppermute | solution.py:10
  296.6 6.6 %collective-permute-start.22 = (f32[64,256]{0,1:T(8,128)S(1)}, f32[64,256]{0,1:T(8,128)S(1)}, u32[]{:S(2)}, u32[]{:S(2)}) collective-permute-start(f32[64,256]{0,1:T(8,128)S(1)} %add.253), channel_id=1, source_target_pairs={{0,2},{1,3},{2,0},{3,1},{4,6},{5,7},{6,4},{7,5},{8,10},{9,11},{10,... | collective-permute-start | bytes 196616 | tf_op jit(solution)/shard_map/ppermute | solution.py:10
  303.2 5.1 %collective-permute-start.23 = (f32[64,256]{0,1:T(8,128)S(1)}, f32[64,256]{0,1:T(8,128)S(1)}, u32[]{:S(2)}, u32[]{:S(2)}) collective-permute-start(f32[64,256]{0,1:T(8,128)S(1)} %add.254), channel_id=1, source_target_pairs={{0,4},{1,5},{2,6},{3,7},{4,0},{5,1},{6,2},{7,3},{8,12},{9,13},{10,... | collective-permute-start | bytes 196616 | tf_op jit(solution)/shard_map/ppermute | solution.py:10
  308.2 7.3 %collective-permute-start.24 = (f32[64,256]{0,1:T(8,128)S(1)}, f32[64,256]{0,1:T(8,128)S(1)}, u32[]{:S(2)}, u32[]{:S(2)}) collective-permute-start(f32[64,256]{0,1:T(8,128)S(1)} %add.255), channel_id=1, source_target_pairs={{0,8},{1,9},{2,10},{3,11},{4,12},{5,13},{6,14},{7,15},{8,0},{9,1},... | collective-permute-start | bytes 196616 | tf_op jit(solution)/shard_map/ppermute | solution.py:10
  315.5 1.4 collective-permute-start.25
  317.0 5.8 %collective-permute-start.26 = (f32[64,256]{0,1:T(8,128)S(1)}, f32[64,256]{0,1:T(8,128)S(1)}, u32[]{:S(2)}, u32[]{:S(2)}) collective-permute-start(f32[64,256]{0,1:T(8,128)S(1)} %add.257), channel_id=1, source_target_pairs={{0,32},{16,48},{32,0},{48,16},{64,96},{80,112},{96,64},{112,80},{1... | collective-permute-start | bytes 196616 | tf_op jit(solution)/shard_map/ppermute | solution.py:10
  322.8 9.6 %collective-permute-start.27 = (f32[64,256]{0,1:T(8,128)S(1)}, f32[64,256]{0,1:T(8,128)S(1)}, u32[]{:S(2)}, u32[]{:S(2)}) collective-permute-start(f32[64,256]{0,1:T(8,128)S(1)} %add.258), channel_id=1, source_target_pairs={{0,64},{16,80},{32,96},{48,112},{64,0},{80,16},{96,32},{112,48},{1... | collective-permute-start | bytes 196616 | tf_op jit(solution)/shard_map/ppermute | solution.py:10
  346.2 4.4 %collective-permute-start.28 = (f32[64,192]{1,0:T(8,128)S(1)}, f32[64,192]{1,0:T(8,128)S(1)}, u32[]{:S(2)}, u32[]{:S(2)}) collective-permute-start(f32[64,192]{1,0:T(8,128)S(1)} %convolution_bitcast_fusion.7), channel_id=1, source_target_pairs={{0,1},{1,0},{2,3},{3,2},{4,5},{5,4},{6,7},{7,6},{8,9},{9,8},{10,11... | collective-permute-start | bytes 147464 | tf_op jit(solution)/shard_map/ppermute | solution.py:10
  350.5 5.9 %collective-permute-start.29 = (f32[64,192]{1,0:T(8,128)S(1)}, f32[64,192]{1,0:T(8,128)S(1)}, u32[]{:S(2)}, u32[]{:S(2)}) collective-permute-start(f32[64,192]{1,0:T(8,128)S(1)} %add.262), channel_id=1, source_target_pairs={{0,2},{1,3},{2,0},{3,1},{4,6},{5,7},{6,4},{7,5},{8,10},{9,11},{10,... | collective-permute-start | bytes 147464 | tf_op jit(solution)/shard_map/ppermute | solution.py:10
  356.4 4.8 %collective-permute-start.30 = (f32[64,192]{1,0:T(8,128)S(1)}, f32[64,192]{1,0:T(8,128)S(1)}, u32[]{:S(2)}, u32[]{:S(2)}) collective-permute-start(f32[64,192]{1,0:T(8,128)S(1)} %add.263), channel_id=1, source_target_pairs={{0,4},{1,5},{2,6},{3,7},{4,0},{5,1},{6,2},{7,3},{8,12},{9,13},{10,... | collective-permute-start | bytes 147464 | tf_op jit(solution)/shard_map/ppermute | solution.py:10
  361.2 5.9 %collective-permute-start.31 = (f32[64,192]{1,0:T(8,128)S(1)}, f32[64,192]{1,0:T(8,128)S(1)}, u32[]{:S(2)}, u32[]{:S(2)}) collective-permute-start(f32[64,192]{1,0:T(8,128)S(1)} %add.264), channel_id=1, source_target_pairs={{0,8},{1,9},{2,10},{3,11},{4,12},{5,13},{6,14},{7,15},{8,0},{9,1},... | collective-permute-start | bytes 147464 | tf_op jit(solution)/shard_map/ppermute | solution.py:10
  367.0 1.3 collective-permute-start.32
  368.4 4.4 %collective-permute-start.33 = (f32[64,192]{1,0:T(8,128)S(1)}, f32[64,192]{1,0:T(8,128)S(1)}, u32[]{:S(2)}, u32[]{:S(2)}) collective-permute-start(f32[64,192]{1,0:T(8,128)S(1)} %add.266), channel_id=1, source_target_pairs={{0,32},{16,48},{32,0},{48,16},{64,96},{80,112},{96,64},{112,80},{1... | collective-permute-start | bytes 147464 | tf_op jit(solution)/shard_map/ppermute | solution.py:10
  372.7 6.0 %collective-permute-start.34 = (f32[64,192]{1,0:T(8,128)S(1)}, f32[64,192]{1,0:T(8,128)S(1)}, u32[]{:S(2)}, u32[]{:S(2)}) collective-permute-start(f32[64,192]{1,0:T(8,128)S(1)} %add.267), channel_id=1, source_target_pairs={{0,64},{16,80},{32,96},{48,112},{64,0},{80,16},{96,32},{112,48},{1... | collective-permute-start | bytes 147464 | tf_op jit(solution)/shard_map/ppermute | solution.py:10
  378.7 9.0 %collective-permute-start.35 = (f32[64,192]{1,0:T(8,128)S(1)}, f32[64,192]{1,0:T(8,128)S(1)}, u32[]{:S(2)}, u32[]{:S(2)}) collective-permute-start(f32[64,192]{1,0:T(8,128)S(1)} %add.268), channel_id=1, source_target_pairs={{0,128},{16,144},{32,160},{48,176},{64,192},{80,208},{96,224},{112... | collective-permute-start | bytes 147464 | tf_op jit(solution)/shard_map/ppermute | solution.py:10
where the time goes:
time: 410 us; the launch traced here: 402 us
  waiting for transfers between devices  153 us (37%)
  other arithmetic  151 us (37%)
  starting transfers between devices  67.9 us (17%)
  matrix products  19.4 us (5%)
  local copies, waits for them, and re-layouts  7.61 us (2%)
    ppermute x36, waiting for transfers between devices, from_partner(): return lax.ppermute(value, axis, pairs)  153 us
    ppermute x36, starting transfers between devices, from_partner(): return lax.ppermute(value, axis, pairs)  67.9 us
    another operation x19, other arithmetic, chol_solve(): lax.linalg.triangular_solve(factor, forward, left_side=True, lower=True,...  64.1 us
    another operation x24, other arithmetic, coefficients(): return chol_solve(jnp.linalg.cholesky(capacity), projected)  52.2 us
    another operation x6, other arithmetic, per_device(): factor = jnp.linalg.cholesky(leaf_blocks)  34 us
  transfers between devices with their start and end apart: 36, of which 36 were waited for; matrix products, arithmetic and copies ran while one was open for 0% of the time, Pallas kernels for 0%

commit v1 on v0

v1 whole, which is shorter than its diff:
```python
import jax
import jax.numpy as jnp
from jax import lax
from jax.experimental import pallas as pl
from jax.experimental.pallas import tpu as pltpu
from jax.sharding import PartitionSpec as P

M = 256
R = 64
LEVELS = 8
NRHS = 128
WIDTH = LEVELS * R + NRHS
F32 = jnp.float32
HI = lax.Precision.HIGHEST


def start_of(level):
    return 128 * ((level - 1) // 2)


def width_of(level):
    return WIDTH - start_of(level)


def offsets(first):
    out, at = {}, 0
    for level in range(first, LEVELS + 1):
        out[level] = at
        at += width_of(level)
    return out, at


def mm(a, b):
    return lax.dot_general(a, b, (((1,), (0,)), ((), ())), precision=HI, preferred_element_type=F32)


def mm_t(a, b):
    return lax.dot_general(a, b, (((0,), (0,)), ((), ())), precision=HI, preferred_element_type=F32)


def chol_inverse(sym):
    row_ids = lax.broadcasted_iota(jnp.int32, (8, 128), 0)
    lane_ids = lax.broadcasted_iota(jnp.int32, (8, 128), 1)
    tiles = []
    for t in range(8):
        eye = jnp.where(lane_ids == row_ids + (R + 8 * t), 1.0, 0.0)[:, R:]
        tiles.append(jnp.concatenate([sym[8 * t : 8 * t + 8, :], eye], axis=1))
    for i in range(R):
        ti, s = i // 8, i % 8
        head = tiles[ti]
        col = jnp.broadcast_to(head[:, i : i + 1], (8, 128))
        scale = lax.rsqrt(jnp.broadcast_to(col[s : s + 1, :], (8, 128)))
        row = jnp.broadcast_to(head[s : s + 1, :], (8, 128)) * scale
        below = jnp.where(row_ids > s, col, 0.0) * scale
        tiles[ti] = jnp.where(row_ids == s, row, head - below * row)
        for t in range(ti + 1, 8):
            col_t = jnp.broadcast_to(tiles[t][:, i : i + 1], (8, 128))
            tiles[t] = tiles[t] - (col_t * scale) * row
    return jnp.concatenate([tile[:, R:] for tile in tiles], axis=0)


def leaf_kernel(d_ref, b_ref, t_ref, y_ref, z_ref, m_ref, aug):
    aug[:, :M] = d_ref[...]
    aug[:, M : M + LEVELS * R] = b_ref[...]
    aug[:, M + LEVELS * R :] = t_ref[...]
    for j in range(4):
        r0 = R * j
        a0 = 128 * (r0 // 128)
        minv = chol_inverse(aug[r0 : r0 + R, r0 : r0 + R])
        m_ref[r0 : r0 + R, :] = minv
        panel = mm(minv, aug[r0 : r0 + R, a0:])
        z_ref[r0 : r0 + R, :] = jnp.zeros((R, M), F32)
        z_ref[r0 : r0 + R, a0:] = panel[:, : M - a0]
        y_ref[r0 : r0 + R, :] = panel[:, M - a0 :]
        for i in range(j + 1, 4):
            c0 = R * i
            s0 = 128 * (c0 // 128)
            aug[c0 : c0 + R, s0:] -= mm_t(panel[:, c0 - a0 : c0 - a0 + R], panel[:, s0 - a0 :])


def back_kernel(y_ref, z_ref, m_ref, w_ref):
    for j in range(3, -1, -1):
        r0 = R * j
        rhs = y_ref[r0 : r0 + R, :]
        if j < 3:
            rhs = rhs - mm(z_ref[r0 : r0 + R, r0 + R :], w_ref[r0 + R :, :])
        w_ref[r0 : r0 + R, :] = mm_t(m_ref[r0 : r0 + R, :], rhs)


def gram_into(y, out_ref, base=None):
    offs, _ = offsets(1)
    for pair in range(4):
        st = 128 * pair
        g = mm_t(y[:, st : st + 128], y[:, st:])
        for h in range(2):
            level = 2 * pair + 1 + h
            o = offs[level]
            piece = g[R * h : R * h + R, :]
            if base is not None:
                piece = piece + base[:, o : o + width_of(level)]
            out_ref[:, o : o + width_of(level)] = piece


def gram_kernel(y_ref, g_ref):
    gram_into(y_ref[...], g_ref)


def reduce_level(k, coupling_ref, rows, p_ref, m_ref):
    o = R * ((k - 1) % 2)
    cap = rows[:, o : o + R]
    ids0 = lax.broadcasted_iota(jnp.int32, (R, R), 0)
    ids1 = lax.broadcasted_iota(jnp.int32, (R, R), 1)
    weights = 1.0 / coupling_ref[k - 1 : k, :]
    cap = cap + jnp.where(ids0 == ids1, jnp.broadcast_to(weights, (R, R)), 0.0)
    cap = 0.5 * (cap + cap.T)
    minv = chol_inverse(cap)
    m_ref[...] = minv
    p = mm(minv, rows)
    p_ref[...] = p
    return p


def next_level(k, p, trailing, n_ref):
    offs, _ = offsets(k + 1)
    sk = start_of(k)
    for pair in range(k // 2, 4):
        st = 128 * pair
        g = mm_t(p[:, st - sk : st - sk + 128], p[:, st - sk :])
        for h in range(2):
            level = 2 * pair + 1 + h
            if level > k:
                o = offs[level]
                n_ref[:, o : o + width_of(level)] = trailing(level) - g[R * h : R * h + R, :]


def first_level_kernel(c_ref, g_ref, y_ref, p_ref, m_ref, n_ref, sums):
    gram_into(y_ref[...], sums, g_ref)
    offs, _ = offsets(1)
    p = reduce_level(1, c_ref, sums[:, : width_of(1)], p_ref, m_ref)
    next_level(1, p, lambda level: sums[:, offs[level] : offs[level] + width_of(level)], n_ref)


def level_kernel(k, c_ref, own_ref, got_ref, p_ref, m_ref, n_ref):
    offs, _ = offsets(k)

    def part(level):
        o = offs[level]
        return own_ref[:, o : o + width_of(level)] + got_ref[:, o : o + width_of(level)]

    p = reduce_level(k, c_ref, part(k), p_ref, m_ref)
    next_level(k, p, part, n_ref)


def apply_level(k, w, p, minv):
    o = R * ((k - 1) % 2)
    cut = (start_of(k + 1) if k < LEVELS else LEVELS * R) - start_of(k)
    coef = mm_t(minv, p[:, cut:])
    return w[:, cut:] - mm(w[:, o : o + R], coef)


def apply_kernel(k, w_ref, p_ref, m_ref, o_ref):
    o_ref[...] = apply_level(k, w_ref[...], p_ref[...], m_ref[...])


def last_kernel(k, c_ref, own_ref, got_ref, w_ref, o_ref, p_ref, m_ref):
    rows = own_ref[...] + got_ref[...]
    p = reduce_level(k, c_ref, rows, p_ref, m_ref)
    o_ref[...] = apply_level(k, w_ref[...], p, m_ref[...])


def call(kernel, outs, *args, scratch=(), flops=10_000_000, name=None):
    vm = pl.BlockSpec(memory_space=pltpu.VMEM)
    shapes = [jax.ShapeDtypeStruct(s, F32) for s in outs]
    return pl.pallas_call(
        kernel,
        out_shape=shapes,
        in_specs=[vm] * len(args),
        out_specs=[vm] * len(shapes),
        scratch_shapes=[pltpu.VMEM(s, F32) for s in scratch],
        cost_estimate=pl.CostEstimate(flops=flops, bytes_accessed=1_000_000, transcendentals=0),
        name=name,
    )(*args)


def exchange(value, level, inner_bits):
    if level <= inner_bits:
        axis, masks = "inner", {1: 1, 2: 2, 3: 4, 4: 8}
        mask = masks[level]
    else:
        axis, masks = "group", {5: 1, 6: 2, 7: 4, 8: 14}
        mask = masks[level]
    return lax.ppermute(value, axis, [(s, s ^ mask) for s in range(lax.axis_size(axis))])


def per_device(leaf_blocks, bases, targets, coupling):
    inner_bits = lax.axis_size("inner").bit_length() - 1
    y, z, m = call(
        leaf_kernel, [(M, WIDTH), (M, M), (M, R)], leaf_blocks, bases, targets,
        scratch=[(M, M + WIDTH)], name="leaf",
    )
    got = exchange(y, 1, inner_bits)
    (own,) = call(gram_kernel, [(R, offsets(1)[1])], y, name="gram")
    (w,) = call(back_kernel, [(M, WIDTH)], y, z, m, name="back")
    for k in range(1, LEVELS):
        outs = [(R, width_of(k)), (R, R), (R, offsets(k + 1)[1])]
        if k == 1:
            p, minv, nxt = call(
                first_level_kernel, outs, coupling, own, got, scratch=[(R, offsets(1)[1])], name="level1"
            )
        else:
            kernel = lambda *refs, k=k: level_kernel(k, *refs)
            p, minv, nxt = call(kernel, outs, coupling, own, got, name="level%d" % k)
        own = nxt
        got = exchange(own, k + 1, inner_bits)
        kernel = lambda *refs, k=k: apply_kernel(k, *refs)
        (w,) = call(kernel, [(M, width_of(k + 1))], w, p, minv, name="apply%d" % k)
    kernel = lambda *refs: last_kernel(LEVELS, *refs)
    return call(
        kernel, [(M, NRHS)], coupling, own, got, w,
        scratch=[(R, width_of(LEVELS)), (R, R)], name="last",
    )[0]


def solution(mesh):
    in_specs = (
        P(("group", "inner"), None),
        P(("group", "inner"), None),
        P(("group", "inner"), None),
        P(),
    )
    out_specs = P(("group", "inner"), None)
    return jax.shard_map(
        per_device, mesh=mesh, in_specs=in_specs, out_specs=out_specs, check_vma=False
    )
```

time: 410 us -> 244 us (0.60); the launches traced: 402 us -> 243 us
  Pallas kernels: 0 us -> 155 us
  other arithmetic: 151 us -> 0 us
  waiting for transfers between devices: 153 us -> 62.4 us
  starting transfers between devices: 67.9 us -> 19.7 us
  matrix products: 19.4 us -> 0 us
    pallas_call x0 -> x18, Pallas kernels: none -> 155 us  [call(): pl.pallas_call(kernel, out_shape=shapes, in_specs=[vm] * len(args), out_s...]
    another operation x49 -> x0, other arithmetic: 150 us -> none  [the longest x19 64.1 us: chol_solve(): lax.linalg.triangular_solve(factor, forward, left_side=True, lower=True,...]
    ppermute x36 -> x8, waiting for transfers between devices: 153 us -> 62.4 us  [exchange(): lax.ppermute(value, axis, [(s, s ^ mask) for s in range(lax.axis_size(axi...]
    ppermute x36 -> x8, starting transfers between devices: 67.9 us -> 19.7 us  [exchange(): lax.ppermute(value, axis, [(s, s ^ mask) for s in range(lax.axis_size(axi...]
    dot_general x16 -> x0, matrix products: 11.4 us -> none  [the longest x8 7.11 us: contract(): lax.dot_general(first_arg, second_arg, (((0,), (0,)), ((), ())), precisio...]
    another operation x24 -> x0, matrix products: 8.02 us -> none  [the longest x11 4.45 us: chol_solve(): lax.linalg.triangular_solve(factor, rhs_cols, left_side=True, lower=True)]
    another operation x9 -> x0, local copies, waits for them, and re-layouts: 4.12 us -> none
  transfers between devices with their start and end apart: 36 -> 8, of which waited for: 36 -> 7; matrix products, arithmetic and copies ran while one was open for 0% -> 0% of each run, Pallas kernels for 0% -> 11%
where the time goes in v1:
time: 244 us; the launch traced here: 243 us
  Pallas kernels  155 us (64%)
  waiting for transfers between devices  62.4 us (26%)
  starting transfers between devices  19.7 us (8%)
  local copies, waits for them, and re-layouts  5.99 us (2%)
    pallas_call x18, Pallas kernels, call(): pl.pallas_call(kernel, out_shape=shapes, in_specs=[vm] * len(args), out_s...  155 us
    ppermute x8, waiting for transfers between devices, exchange(): lax.ppermute(value, axis, [(s, s ^ mask) for s in range(lax.axis_size(axi...  62.4 us
    ppermute x8, starting transfers between devices, exchange(): lax.ppermute(value, axis, [(s, s ^ mask) for s in range(lax.axis_size(axi...  19.7 us
    unnamed x16, local copies, waits for them, and re-layouts  5.99 us
  transfers between devices with their start and end apart: 8, of which 7 were waited for; matrix products, arithmetic and copies ran while one was open for 0% of the time, Pallas kernels for 11%

profile of v1, /device:TPU:2, one launch (start us, length us, event | category | flops | bytes accessed | tf_op | source)
XLA Modules:
  0.0 242.7 jit_solution(11922132750083056222)
XLA Ops:
  0.0 37.8 %leaf.1 = (f32[256,640]{1,0:T(8,128)}, f32[256,256]{1,0:T(8,128)}, f32[256,64]{1,0:T(8,128)}) custom-call(f32[256,256]{1,0:T(8,128)} %d_ref.1, f32[256,512]{1,0:T(8,128)} %b_ref.1, f32[256,128]{1,0:T(8,128)} %t_ref.1), custom_call_target="tpu_custom_call" | custom-call | flops 10000000 | bytes 1000000 | tf_op jit(solution)/shard_map/leaf/pallas_call | solution.py:174
  37.8 2.3 collective-permute-start
  40.1 3.1 %gram.1.g_ref = f32[64,3584]{1,0:T(8,128)} custom-call(f32[256,640]{1,0:T(8,128)} %get-tuple-element.29.y_ref), custom_call_target="tpu_custom_call" | custom-call | flops 10000000 | bytes 1000000 | tf_op jit(solution)/shard_map/gram/pallas_call | solution.py:174
  43.2 11.3 %collective-permute-done.y_ref = f32[256,640]{1,0:T(8,128)S(1)} collective-permute-done((f32[256,640]{1,0:T(8,128)}, f32[256,640]{1,0:T(8,128)S(1)}, u32[]{:S(2)}, u32[]{:S(2)}) %collective-permute-start) | collective-permute-done | bytes 655392 | tf_op jit(solution)/shard_map/ppermute | solution.py:192
  54.5 0.0 copy-start.1
  54.5 0.8 copy-done.1
  55.3 12.4 %level1.1 = (f32[64,640]{1,0:T(8,128)}, f32[64,64]{1,0:T(8,128)}, f32[64,2944]{1,0:T(8,128)}) custom-call(f32[8,64]{1,0:T(8,128)} %refs_0_.13, f32[64,3584]{1,0:T(8,128)} %gram.1.g_ref, f32[256,640]{1,0:T(8,128)} %copy-done.1), custom_call_target="tpu_custom_call" | custom-call | flops 10000000 | bytes 1000000 | tf_op jit(solution)/shard_map/level1/pallas_call | solution.py:174
  67.7 2.1 collective-permute-start.1
  69.9 17.1 %collective-permute-done.1.refs_2_ = f32[64,2944]{1,0:T(8,128)S(1)} collective-permute-done((f32[64,2944]{1,0:T(8,128)}, f32[64,2944]{1,0:T(8,128)S(1)}, u32[]{:S(2)}, u32[]{:S(2)}) %collective-permute-start.1) | collective-permute-done | bytes 753696 | tf_op jit(solution)/shard_map/ppermute | solution.py:192
  86.9 0.0 copy-start
  86.9 0.9 copy-done
  87.8 11.9 %level2.1 = (f32[64,640]{1,0:T(8,128)}, f32[64,64]{1,0:T(8,128)}, f32[64,2304]{1,0:T(8,128)}) custom-call(f32[8,64]{1,0:T(8,128)} %refs_0_.13, f32[64,2944]{1,0:T(8,128)} %get-tuple-element.30.refs_1_, f32[64,2944]{1,0:T(8,128)} %copy-done), custom_call_target="tpu_custom_call" | custom-call | flops 10000000 | bytes 1000000 | tf_op jit(solution)/shard_map/level2/pallas_call | solution.py:174
  99.7 1.8 collective-permute-start.2
  101.5 11.8 %collective-permute-done.2.refs_2_ = f32[64,2304]{1,0:T(8,128)S(1)} collective-permute-done((f32[64,2304]{1,0:T(8,128)}, f32[64,2304]{1,0:T(8,128)S(1)}, u32[]{:S(2)}, u32[]{:S(2)}) %collective-permute-start.2) | collective-permute-done | bytes 589856 | tf_op jit(solution)/shard_map/ppermute | solution.py:192
  113.3 0.0 copy-start.2
  113.3 0.8 copy-done.2
  114.2 11.4 %level3.1 = (f32[64,512]{1,0:T(8,128)}, f32[64,64]{1,0:T(8,128)}, f32[64,1792]{1,0:T(8,128)}) custom-call(f32[8,64]{1,0:T(8,128)} %refs_0_.13, f32[64,2304]{1,0:T(8,128)} %get-tuple-element.31.refs_1_, f32[64,2304]{1,0:T(8,128)} %copy-done.2), custom_call_target="tpu_custom_call" | custom-call | flops 10000000 | bytes 1000000 | tf_op jit(solution)/shard_map/level3/pallas_call | solution.py:174
  125.6 3.4 %collective-permute-start.3 = (f32[64,1792]{1,0:T(8,128)}, f32[64,1792]{1,0:T(8,128)S(1)}, u32[]{:S(2)}, u32[]{:S(2)}) collective-permute-start(f32[64,1792]{1,0:T(8,128)} %get-tuple-element.32.refs_1_), channel_id=1, source_target_pairs={{0,8},{1,9},{2,10},{3,11},{4,12},{5,13},{6,14},{7,15},{8,0},{9,1},... | collective-permute-start | bytes 1376264 | tf_op jit(solution)/shard_map/ppermute | solution.py:192
  128.9 8.1 %collective-permute-done.3.refs_2_ = f32[64,1792]{1,0:T(8,128)S(1)} collective-permute-done((f32[64,1792]{1,0:T(8,128)}, f32[64,1792]{1,0:T(8,128)S(1)}, u32[]{:S(2)}, u32[]{:S(2)}) %collective-permute-start.3) | collective-permute-done | bytes 458784 | tf_op jit(solution)/shard_map/ppermute | solution.py:192
  137.1 0.0 copy-start.3
  137.1 0.8 copy-done.3
  137.8 11.4 %level4.1 = (f32[64,512]{1,0:T(8,128)}, f32[64,64]{1,0:T(8,128)}, f32[64,1280]{1,0:T(8,128)}) custom-call(f32[8,64]{1,0:T(8,128)} %refs_0_.13, f32[64,1792]{1,0:T(8,128)} %get-tuple-element.32.refs_1_, f32[64,1792]{1,0:T(8,128)} %copy-done.3), custom_call_target="tpu_custom_call" | custom-call | flops 10000000 | bytes 1000000 | tf_op jit(solution)/shard_map/level4/pallas_call | solution.py:174
  149.2 0.0 collective-permute-start.4
  149.2 1.8 collective-permute-done.4.refs_2_
  151.1 0.0 copy-start.4
  151.1 0.7 copy-done.4
  151.8 10.9 %level5.1 = (f32[64,384]{1,0:T(8,128)}, f32[64,64]{1,0:T(8,128)}, f32[64,896]{1,0:T(8,128)}) custom-call(f32[8,64]{1,0:T(8,128)} %refs_0_.13, f32[64,1280]{1,0:T(8,128)} %get-tuple-element.33.refs_1_, f32[64,1280]{1,0:T(8,128)} %copy-done.4), custom_call_target="tpu_custom_call" | custom-call | flops 10000000 | bytes 1000000 | tf_op jit(solution)/shard_map/level5/pallas_call | solution.py:174
  162.7 1.9 collective-permute-start.5
  164.6 6.1 %collective-permute-done.5.refs_2_ = f32[64,896]{1,0:T(8,128)S(1)} collective-permute-done((f32[64,896]{1,0:T(8,128)}, f32[64,896]{1,0:T(8,128)S(1)}, u32[]{:S(2)}, u32[]{:S(2)}) %collective-permute-start.5) | collective-permute-done | bytes 229408 | tf_op jit(solution)/shard_map/ppermute | solution.py:192
  170.8 0.0 copy-start.5
  170.8 0.7 copy-done.5
  171.4 11.1 %level6.1 = (f32[64,384]{1,0:T(8,128)}, f32[64,64]{1,0:T(8,128)}, f32[64,512]{1,0:T(8,128)}) custom-call(f32[8,64]{1,0:T(8,128)} %refs_0_.13, f32[64,896]{1,0:T(8,128)} %get-tuple-element.34.refs_1_, f32[64,896]{1,0:T(8,128)} %copy-done.5), custom_call_target="tpu_custom_call" | custom-call | flops 10000000 | bytes 1000000 | tf_op jit(solution)/shard_map/level6/pallas_call | solution.py:174
  182.5 3.3 %collective-permute-start.6 = (f32[64,512]{1,0:T(8,128)}, f32[64,512]{1,0:T(8,128)S(1)}, u32[]{:S(2)}, u32[]{:S(2)}) collective-permute-start(f32[64,512]{1,0:T(8,128)} %get-tuple-element.35.refs_1_), channel_id=1, source_target_pairs={{0,64},{16,80},{32,96},{48,112},{64,0},{80,16},{96,32},{112,48},{1... | collective-permute-start | bytes 393224 | tf_op jit(solution)/shard_map/ppermute | solution.py:192
  185.8 6.1 %collective-permute-done.6.refs_2_ = f32[64,512]{1,0:T(8,128)S(1)} collective-permute-done((f32[64,512]{1,0:T(8,128)}, f32[64,512]{1,0:T(8,128)S(1)}, u32[]{:S(2)}, u32[]{:S(2)}) %collective-permute-start.6) | collective-permute-done | bytes 131104 | tf_op jit(solution)/shard_map/ppermute | solution.py:192
  192.0 0.0 copy-start.6
  192.0 0.6 copy-done.6
  192.6 10.6 %level7.1 = (f32[64,256]{1,0:T(8,128)}, f32[64,64]{1,0:T(8,128)}, f32[64,256]{1,0:T(8,128)}) custom-call(f32[8,64]{1,0:T(8,128)} %refs_0_.13, f32[64,512]{1,0:T(8,128)} %get-tuple-element.35.refs_1_, f32[64,512]{1,0:T(8,128)} %copy-done.6), custom_call_target="tpu_custom_call" | custom-call | flops 10000000 | bytes 1000000 | tf_op jit(solution)/shard_map/level7/pallas_call | solution.py:174
  203.2 4.9 %collective-permute-start.7 = (f32[64,256]{1,0:T(8,128)}, f32[64,256]{1,0:T(8,128)S(1)}, u32[]{:S(2)}, u32[]{:S(2)}) collective-permute-start(f32[64,256]{1,0:T(8,128)} %get-tuple-element.36.refs_1_), channel_id=1, source_target_pairs={{0,224},{16,240},{32,192},{48,208},{64,160},{80,176},{96,128},{112... | collective-permute-start | bytes 196616 | tf_op jit(solution)/shard_map/ppermute | solution.py:192
  208.1 4.0 %back.1.refs_0_ = f32[256,640]{1,0:T(8,128)} custom-call(f32[256,640]{1,0:T(8,128)} %get-tuple-element.29.y_ref, f32[256,256]{1,0:T(8,128)} %get-tuple-element.37.z_ref, f32[256,64]{1,0:T(8,128)} %get-tuple-element.38.m_ref), custom_call_target="tpu_custom_call" | custom-call | flops 10000000 | bytes 1000000 | tf_op jit(solution)/shard_map/back/pallas_call | solution.py:174
  212.2 3.1 %apply1.1.refs_0_ = f32[256,640]{1,0:T(8,128)} custom-call(f32[256,640]{1,0:T(8,128)} %back.1.refs_0_, f32[64,640]{1,0:T(8,128)} %get-tuple-element.39.refs_1_, f32[64,64]{1,0:T(8,128)} %get-tuple-element.40.refs_2_), custom_call_target="tpu_custom_call" | custom-call | flops 10000000 | bytes 1000000 | tf_op jit(solution)/shard_map/apply1/pallas_call | solution.py:174
  215.2 2.8 %apply2.1.refs_0_ = f32[256,512]{1,0:T(8,128)} custom-call(f32[256,640]{1,0:T(8,128)} %apply1.1.refs_0_, f32[64,640]{1,0:T(8,128)} %get-tuple-element.41.refs_1_, f32[64,64]{1,0:T(8,128)} %get-tuple-element.42.refs_2_), custom_call_target="tpu_custom_call" | custom-call | flops 10000000 | bytes 1000000 | tf_op jit(solution)/shard_map/apply2/pallas_call | solution.py:174
  218.1 2.8 %apply3.1.refs_0_ = f32[256,512]{1,0:T(8,128)} custom-call(f32[256,512]{1,0:T(8,128)} %apply2.1.refs_0_, f32[64,512]{1,0:T(8,128)} %get-tuple-element.43.refs_1_, f32[64,64]{1,0:T(8,128)} %get-tuple-element.44.refs_2_), custom_call_target="tpu_custom_call" | custom-call | flops 10000000 | bytes 1000000 | tf_op jit(solution)/shard_map/apply3/pallas_call | solution.py:174
  220.9 2.7 %apply4.1.refs_0_ = f32[256,384]{1,0:T(8,128)} custom-call(f32[256,512]{1,0:T(8,128)} %apply3.1.refs_0_, f32[64,512]{1,0:T(8,128)} %get-tuple-element.45.refs_1_, f32[64,64]{1,0:T(8,128)} %get-tuple-element.46.refs_2_), custom_call_target="tpu_custom_call" | custom-call | flops 10000000 | bytes 1000000 | tf_op jit(solution)/shard_map/apply4/pallas_call | solution.py:174
  223.5 2.6 %apply5.1.refs_0_ = f32[256,384]{1,0:T(8,128)} custom-call(f32[256,384]{1,0:T(8,128)} %apply4.1.refs_0_, f32[64,384]{1,0:T(8,128)} %get-tuple-element.47.refs_1_, f32[64,64]{1,0:T(8,128)} %get-tuple-element.48.refs_2_), custom_call_target="tpu_custom_call" | custom-call | flops 10000000 | bytes 1000000 | tf_op jit(solution)/shard_map/apply5/pallas_call | solution.py:174
  226.1 2.4 %apply6.1.refs_0_ = f32[256,256]{1,0:T(8,128)} custom-call(f32[256,384]{1,0:T(8,128)} %apply5.1.refs_0_, f32[64,384]{1,0:T(8,128)} %get-tuple-element.49.refs_1_, f32[64,64]{1,0:T(8,128)} %get-tuple-element.50.refs_2_), custom_call_target="tpu_custom_call" | custom-call | flops 10000000 | bytes 1000000 | tf_op jit(solution)/shard_map/apply6/pallas_call | solution.py:174
  228.5 2.4 apply7.1.refs_3_
  230.9 0.0 collective-permute-done.7.refs_2_
  230.9 0.0 copy-start.7
  230.9 0.6 copy-done.7
  231.5 11.2 %last.1 = f32[256,128]{1,0:T(8,128)} custom-call(f32[8,64]{1,0:T(8,128)} %refs_0_.13, f32[64,256]{1,0:T(8,128)} %get-tuple-element.36.refs_1_, f32[64,256]{1,0:T(8,128)} %copy-done.7, f32[256,256]{1,0:T(8,128)} %apply7.1.refs_3_), custom_call_target="tpu_custom_call" | custom-call | flops 10000000 | bytes 1000000 | tf_op jit(solution)/shard_map/last/pallas_call | solution.py:174
Async XLA Ops:
  37.8 16.7 %collective-permute-start = (f32[256,640]{1,0:T(8,128)}, f32[256,640]{1,0:T(8,128)S(1)}, u32[]{:S(2)}, u32[]{:S(2)}) collective-permute-start(f32[256,640]{1,0:T(8,128)} %get-tuple-element.29.y_ref), channel_id=1, source_target_pairs={{0,1},{1,0},{2,3},{3,2},{4,5},{5,4},{6,7},{7,6},{8,9},{9,8},{10,11... | collective-permute-start | bytes 1966088 | tf_op jit(solution)/shard_map/ppermute | solution.py:192
  54.5 0.8 copy-start.1
  67.7 19.2 %collective-permute-start.1 = (f32[64,2944]{1,0:T(8,128)}, f32[64,2944]{1,0:T(8,128)S(1)}, u32[]{:S(2)}, u32[]{:S(2)}) collective-permute-start(f32[64,2944]{1,0:T(8,128)} %get-tuple-element.30.refs_1_), channel_id=1, source_target_pairs={{0,2},{1,3},{2,0},{3,1},{4,6},{5,7},{6,4},{7,5},{8,10},{9,11},{10,... | collective-permute-start | bytes 2261000 | tf_op jit(solution)/shard_map/ppermute | solution.py:192
  86.9 0.9 copy-start
  99.7 13.6 %collective-permute-start.2 = (f32[64,2304]{1,0:T(8,128)}, f32[64,2304]{1,0:T(8,128)S(1)}, u32[]{:S(2)}, u32[]{:S(2)}) collective-permute-start(f32[64,2304]{1,0:T(8,128)} %get-tuple-element.31.refs_1_), channel_id=1, source_target_pairs={{0,4},{1,5},{2,6},{3,7},{4,0},{5,1},{6,2},{7,3},{8,12},{9,13},{10,... | collective-permute-start | bytes 1769480 | tf_op jit(solution)/shard_map/ppermute | solution.py:192
  113.3 0.8 copy-start.2
  125.6 11.5 %collective-permute-start.3 = (f32[64,1792]{1,0:T(8,128)}, f32[64,1792]{1,0:T(8,128)S(1)}, u32[]{:S(2)}, u32[]{:S(2)}) collective-permute-start(f32[64,1792]{1,0:T(8,128)} %get-tuple-element.32.refs_1_), channel_id=1, source_target_pairs={{0,8},{1,9},{2,10},{3,11},{4,12},{5,13},{6,14},{7,15},{8,0},{9,1},... | collective-permute-start | bytes 1376264 | tf_op jit(solution)/shard_map/ppermute | solution.py:192
  137.1 0.8 copy-start.3
  149.2 1.8 collective-permute-start.4
  151.1 0.7 copy-start.4
  162.7 8.0 %collective-permute-start.5 = (f32[64,896]{1,0:T(8,128)}, f32[64,896]{1,0:T(8,128)S(1)}, u32[]{:S(2)}, u32[]{:S(2)}) collective-permute-start(f32[64,896]{1,0:T(8,128)} %get-tuple-element.34.refs_1_), channel_id=1, source_target_pairs={{0,32},{16,48},{32,0},{48,16},{64,96},{80,112},{96,64},{112,80},{1... | collective-permute-start | bytes 688136 | tf_op jit(solution)/shard_map/ppermute | solution.py:192
  170.8 0.7 copy-start.5
  182.5 9.4 %collective-permute-start.6 = (f32[64,512]{1,0:T(8,128)}, f32[64,512]{1,0:T(8,128)S(1)}, u32[]{:S(2)}, u32[]{:S(2)}) collective-permute-start(f32[64,512]{1,0:T(8,128)} %get-tuple-element.35.refs_1_), channel_id=1, source_target_pairs={{0,64},{16,80},{32,96},{48,112},{64,0},{80,16},{96,32},{112,48},{1... | collective-permute-start | bytes 393224 | tf_op jit(solution)/shard_map/ppermute | solution.py:192
  192.0 0.6 copy-start.6
  203.2 27.7 %collective-permute-start.7 = (f32[64,256]{1,0:T(8,128)}, f32[64,256]{1,0:T(8,128)S(1)}, u32[]{:S(2)}, u32[]{:S(2)}) collective-permute-start(f32[64,256]{1,0:T(8,128)} %get-tuple-element.36.refs_1_), channel_id=1, source_target_pairs={{0,224},{16,240},{32,192},{48,208},{64,160},{80,176},{96,128},{112... | collective-permute-start | bytes 196616 | tf_op jit(solution)/shard_map/ppermute | solution.py:192
  230.9 0.6 copy-start.7

commit v2 on v1

v2 whole, which is shorter than its diff:
```python
import jax
import jax.numpy as jnp
from jax import lax
from jax.experimental import pallas as pl
from jax.experimental.pallas import tpu as pltpu
from jax.sharding import PartitionSpec as P

M = 256
R = 64
LEVELS = 8
NRHS = 128
WIDTH = LEVELS * R + NRHS
NB = 16
F32 = jnp.float32
HI = lax.Precision.HIGHEST


def start_of(level):
    return 128 * ((level - 1) // 2)


def width_of(level):
    return WIDTH - start_of(level)


def offsets(first):
    out, at = {}, 0
    for level in range(first, LEVELS + 1):
        out[level] = at
        at += width_of(level)
    return out, at


def mm(a, b):
    return lax.dot_general(a, b, (((1,), (0,)), ((), ())), precision=HI, preferred_element_type=F32)


def mm_t(a, b):
    return lax.dot_general(a, b, (((0,), (0,)), ((), ())), precision=HI, preferred_element_type=F32)


def chol_inverse(block, at):
    sub = lax.broadcasted_iota(jnp.int32, (8, 128), 0)
    lane = lax.broadcasted_iota(jnp.int32, (8, 128), 1)
    mine = (lane >= at) & (lane < at + R)
    groups = R // 8
    tiles, pivots = [], [None] * groups
    for g in range(groups):
        eye = jnp.where(lane == sub + (8 * g + R - at), 1.0, 0.0)
        tiles.append(jnp.where(mine, block[8 * g : 8 * g + 8, :], eye))

    def spread(tile, s):
        return jnp.broadcast_to(tile[s : s + 1, :], (8, 128))

    for first in range(0, R, NB):
        cols = {}
        for r in range(first, first + NB):
            for g in range(r // 8, groups):
                cols[r, g] = jnp.broadcast_to(tiles[g][:, at + r : at + r + 1], (8, 128))
        for i in range(first, first + NB):
            gi, s = i // 8, i % 8
            pivot = spread(cols[i, gi], s)
            inv = 1.0 / pivot
            pivots[gi] = pivot if s == 0 else jnp.where(sub >= s, pivot, pivots[gi])
            row = spread(tiles[gi], s)
            below = {g: cols[i, g] for g in range(gi, groups)}
            below[gi] = jnp.where(sub > s, below[gi], 0.0)
            for r in range(i + 1, first + NB):
                mult = spread(cols[i, r // 8], r % 8) * inv
                for g in range(r // 8, groups):
                    cols[r, g] = cols[r, g] - below[g] * mult
            scaled = row * inv
            for g in range(gi, groups):
                if g > gi or s < 7:
                    tiles[g] = tiles[g] - below[g] * scaled
    out = [jnp.where(mine, 0.0, tiles[g] * lax.rsqrt(pivots[g])) for g in range(groups)]
    return jnp.concatenate(out, axis=0)


def leaf_kernel(d_ref, b_ref, t_ref, y_ref, z_ref, m_ref, aug):
    aug[:, :M] = d_ref[...]
    aug[:, M : M + LEVELS * R] = b_ref[...]
    aug[:, M + LEVELS * R :] = t_ref[...]
    for j in range(4):
        r0 = R * j
        a0 = 128 * (r0 // 128)
        minv = chol_inverse(aug[r0 : r0 + R, a0 : a0 + 128], r0 - a0)
        m_ref[r0 : r0 + R, :] = minv
        rows = aug[r0 : r0 + R, a0:]
        panel = mm(minv, jnp.concatenate([rows, rows], axis=0))
        z_ref[r0 : r0 + R, :] = jnp.zeros((R, M), F32)
        z_ref[r0 : r0 + R, a0:] = panel[:, : M - a0]
        y_ref[r0 : r0 + R, :] = panel[:, M - a0 :]
        for i in range(j + 1, 4):
            c0 = R * i
            s0 = 128 * (c0 // 128)
            aug[c0 : c0 + R, s0:] -= mm_t(panel[:, c0 - a0 : c0 - a0 + R], panel[:, s0 - a0 :])


def back_kernel(y_ref, z_ref, m_ref, w_ref):
    for j in range(3, -1, -1):
        r0 = R * j
        o = R - r0 % 128
        rhs = y_ref[r0 : r0 + R, :]
        if j < 3:
            rhs = rhs - mm(z_ref[r0 : r0 + R, r0 + R :], w_ref[r0 + R :, :])
        w_ref[r0 : r0 + R, :] = mm_t(m_ref[r0 : r0 + R, :], rhs)[o : o + R, :]


def gram_pair(y, pair):
    st = 128 * pair
    return mm_t(y[:, st : st + 128], y[:, st:])


def gram_kernel(y_ref, g_ref):
    y = y_ref[...]
    offs, _ = offsets(1)
    for pair in range(4):
        g = gram_pair(y, pair)
        for h in range(2):
            level = 2 * pair + 1 + h
            g_ref[:, offs[level] : offs[level] + width_of(level)] = g[R * h : R * h + R, :]


def reduce_level(k, coupling_ref, rows, p_ref, m_ref):
    o = R * ((k - 1) % 2)
    ids0 = lax.broadcasted_iota(jnp.int32, (R, 128), 0)
    ids1 = lax.broadcasted_iota(jnp.int32, (R, 128), 1)
    weights = 1.0 / coupling_ref[k - 1 : k, :]
    weights = jnp.concatenate([weights, weights], axis=1)
    cap = rows[:, :128] + jnp.where(ids0 + o == ids1, jnp.broadcast_to(weights, (R, 128)), 0.0)
    minv = chol_inverse(cap, o)
    m_ref[...] = minv
    p = mm(minv, jnp.concatenate([rows, rows], axis=0))
    p_ref[...] = p
    return p


def next_level(k, p, trailing, n_ref):
    offs, _ = offsets(k + 1)
    sk = start_of(k)
    for pair in range(k // 2, 4):
        st = 128 * pair
        g = mm_t(p[:, st - sk : st - sk + 128], p[:, st - sk :])
        for h in range(2):
            level = 2 * pair + 1 + h
            if level > k:
                o = offs[level]
                n_ref[:, o : o + width_of(level)] = trailing(level) - g[R * h : R * h + R, :]


def first_level_kernel(c_ref, g_ref, got_ref, dep_ref, p_ref, m_ref, n_ref):
    y = got_ref[...]
    offs, _ = offsets(1)
    grams = {0: gram_pair(y, 0)}

    def part(level):
        pair, h = (level - 1) // 2, (level - 1) % 2
        if pair not in grams:
            grams[pair] = gram_pair(y, pair)
        o = offs[level]
        return g_ref[:, o : o + width_of(level)] + grams[pair][R * h : R * h + R, :]

    p = reduce_level(1, c_ref, part(1), p_ref, m_ref)
    next_level(1, p, part, n_ref)


def level_kernel(k, c_ref, own_ref, got_ref, dep_ref, p_ref, m_ref, n_ref):
    offs, _ = offsets(k)

    def part(level):
        o = offs[level]
        return own_ref[:, o : o + width_of(level)] + got_ref[:, o : o + width_of(level)]

    p = reduce_level(k, c_ref, part(k), p_ref, m_ref)
    next_level(k, p, part, n_ref)


def apply_level(k, w, p, minv):
    o = R * ((k - 1) % 2)
    cut = (start_of(k + 1) if k < LEVELS else LEVELS * R) - start_of(k)
    coef = mm_t(minv, p[:, cut:])[R - o : 2 * R - o, :]
    return w[:, cut:] - mm(w[:, o : o + R], coef)


def apply_kernel(k, w_ref, p_ref, m_ref, o_ref):
    o_ref[...] = apply_level(k, w_ref[...], p_ref[...], m_ref[...])


def last_kernel(k, c_ref, own_ref, got_ref, w_ref, o_ref, p_ref, m_ref):
    p = reduce_level(k, c_ref, own_ref[...] + got_ref[...], p_ref, m_ref)
    o_ref[...] = apply_level(k, w_ref[...], p, m_ref[...])


def call(kernel, outs, *args, hbm=(), scratch=(), flops=10_000_000, name=None):
    vm = pl.BlockSpec(memory_space=pltpu.VMEM)
    hb = pl.BlockSpec(memory_space=pl.ANY)
    shapes = [jax.ShapeDtypeStruct(s, F32) for s in outs]
    return pl.pallas_call(
        kernel,
        out_shape=shapes,
        in_specs=[hb if i in hbm else vm for i in range(len(args))],
        out_specs=[vm] * len(shapes),
        scratch_shapes=[pltpu.VMEM(s, F32) for s in scratch],
        compiler_params=pltpu.CompilerParams(vmem_limit_bytes=16 << 20),
        cost_estimate=pl.CostEstimate(flops=flops, bytes_accessed=1_000_000, transcendentals=0),
        name=name,
    )(*args)


def exchange(value, level, inner_bits):
    axis = "inner" if level <= inner_bits else "group"
    mask = {1: 1, 2: 2, 3: 4, 4: 8, 5: 1, 6: 2, 7: 4, 8: 14}[level]
    return lax.ppermute(value, axis, [(s, s ^ mask) for s in range(lax.axis_size(axis))])


def per_device(leaf_blocks, bases, targets, coupling):
    inner_bits = lax.axis_size("inner").bit_length() - 1
    y, z, m = call(
        leaf_kernel, [(M, WIDTH), (M, M), (M, 128)], leaf_blocks, bases, targets,
        scratch=[(M, M + WIDTH)], name="leaf",
    )
    got = exchange(y, 1, inner_bits)
    (own,) = call(gram_kernel, [(R, offsets(1)[1])], y, name="gram")
    (w,) = call(back_kernel, [(M, WIDTH)], y, z, m, name="back")
    for k in range(1, LEVELS):
        outs = [(R, width_of(k)), (R, 128), (R, offsets(k + 1)[1])]
        kernel = first_level_kernel if k == 1 else (lambda *refs, k=k: level_kernel(k, *refs))
        p, minv, own = call(kernel, outs, coupling, own, got, w, hbm=(3,), name="level%d" % k)
        got = exchange(own, k + 1, inner_bits)
        kernel = lambda *refs, k=k: apply_kernel(k, *refs)
        (w,) = call(kernel, [(M, width_of(k + 1))], w, p, minv, name="apply%d" % k)
    kernel = lambda *refs: last_kernel(LEVELS, *refs)
    return call(
        kernel, [(M, NRHS)], coupling, own, got, w,
        scratch=[(R, width_of(LEVELS)), (R, 128)], name="last",
    )[0]


def solution(mesh):
    in_specs = (
        P(("group", "inner"), None),
        P(("group", "inner"), None),
        P(("group", "inner"), None),
        P(),
    )
    out_specs = P(("group", "inner"), None)
    return jax.shard_map(
        per_device, mesh=mesh, in_specs=in_specs, out_specs=out_specs, check_vma=False
    )
```

time: 244 us -> 121 us (0.50)
  Pallas kernels: 155 us -> 38.6 us
  waiting for transfers between devices: 62.4 us -> 57 us
  local copies, waits for them, and re-layouts: 5.99 us -> 2.9 us
    pallas_call x18, Pallas kernels: 155 us -> 38.6 us  [call(): pl.pallas_call(kernel, out_shape=shapes, in_specs=[hb if i in hbm else vm...]
    ppermute x8, waiting for transfers between devices: 62.4 us -> 57 us  [exchange(): lax.ppermute(value, axis, [(s, s ^ mask) for s in range(lax.axis_size(axi...]
    unnamed x16 -> x8, local copies, waits for them, and re-layouts: 5.99 us -> 2.9 us
  transfers between devices with their start and end apart: 8 -> 8, of which waited for: 7 -> 8; matrix products, arithmetic and copies ran while one was open for 0% -> 0% of each run, Pallas kernels for 11% -> 8%
where the time goes in v2:
time: 121 us; the launch traced here: 120 us
  waiting for transfers between devices  57 us (47%)
  Pallas kernels  38.6 us (32%)
  starting transfers between devices  21 us (17%)
  local copies, waits for them, and re-layouts  2.9 us (2%)
    ppermute x8, waiting for transfers between devices, exchange(): lax.ppermute(value, axis, [(s, s ^ mask) for s in range(lax.axis_size(axi...  57 us
    pallas_call x18, Pallas kernels, call(): pl.pallas_call(kernel, out_shape=shapes, in_specs=[hb if i in hbm else vm...  38.6 us
    ppermute x8, starting transfers between devices, exchange(): lax.ppermute(value, axis, [(s, s ^ mask) for s in range(lax.axis_size(axi...  21 us
    unnamed x8, local copies, waits for them, and re-layouts  2.9 us
  transfers between devices with their start and end apart: 8, of which 8 were waited for; matrix products, arithmetic and copies ran while one was open for 0% of the time, Pallas kernels for 8%

profile of v2, /device:TPU:2, one launch (start us, length us, event | category | flops | bytes accessed | tf_op | source)
XLA Modules:
  0.0 119.7 jit_solution(2714934885552969737)
XLA Ops:
  0.0 0.0 copy-start
  0.0 1.0 copy-done
  1.0 0.0 copy-start.2
  1.0 0.9 copy-done.2
  2.0 0.0 copy-start.3
  2.0 0.9 copy-done.3
  2.9 8.2 %leaf.1 = (f32[256,640]{1,0:T(8,128)S(1)}, f32[256,256]{1,0:T(8,128)S(1)}, f32[256,128]{1,0:T(8,128)S(1)}) custom-call(f32[256,256]{1,0:T(8,128)S(1)} %copy-done.2, f32[256,512]{1,0:T(8,128)S(1)} %copy-done, f32[256,128]{1,0:T(8,128)S(1)} %copy-done.3), custom_call_target="tpu_custom_call" | custom-call | flops 10000000 | bytes 1000000 | tf_op jit(solution)/shard_map/leaf/pallas_call | solution.py:199
  11.1 2.5 %collective-permute-start = (f32[256,640]{1,0:T(8,128)S(1)}, f32[256,640]{1,0:T(8,128)S(1)}, u32[]{:S(2)}, u32[]{:S(2)}) collective-permute-start(f32[256,640]{1,0:T(8,128)S(1)} %get-tuple-element.29.y_ref), channel_id=1, source_target_pairs={{0,1},{1,0},{2,3},{3,2},{4,5},{5,4},{6,7},{7,6},{8,9},{9,8},{10,11... | collective-permute-start | bytes 1966088 | tf_op jit(solution)/shard_map/ppermute | solution.py:214
  13.6 1.1 gram.1.g_ref
  14.7 0.0 copy-start.1
  14.7 2.3 %back.1.dep_ref.refs_0_ = f32[256,640]{1,0:T(8,128)S(1)} custom-call(f32[256,640]{1,0:T(8,128)S(1)} %get-tuple-element.29.y_ref, f32[256,256]{1,0:T(8,128)S(1)} %get-tuple-element.30.z_ref, f32[256,128]{1,0:T(8,128)S(1)} %get-tuple-element.31.m_ref), custom_call_target="tpu_custom_call" | custom-call | flops 10000000 | bytes 1000000 | tf_op jit(solution)/shard_map/back/pallas_call | solution.py:199
  17.0 10.9 %collective-permute-done.got_ref = f32[256,640]{1,0:T(8,128)S(1)} collective-permute-done((f32[256,640]{1,0:T(8,128)S(1)}, f32[256,640]{1,0:T(8,128)S(1)}, u32[]{:S(2)}, u32[]{:S(2)}) %collective-permute-start) | collective-permute-done | bytes 655392 | tf_op jit(solution)/shard_map/ppermute | solution.py:214
  27.8 0.0 copy-done.1
  27.8 3.7 %level1.1 = (f32[64,640]{1,0:T(8,128)S(1)}, f32[64,128]{1,0:T(8,128)S(1)}, f32[64,2944]{1,0:T(8,128)S(1)}) custom-call(f32[8,64]{1,0:T(8,128)S(1)} %copy-done.1, f32[64,3584]{1,0:T(8,128)S(1)} %gram.1.g_ref, f32[256,640]{1,0:T(8,128)S(1)} %collective-permute-done.got_ref, f32[256,640]{1,0:T(8,128)S(1)} %back.1.dep_ref.refs_0_), custom_call_target="tpu_custom_call" | custom-call | flops 10000000 | bytes 1000000 | tf_op jit(solution)/shard_map/level1/pallas_call | solution.py:199
  31.5 2.2 %collective-permute-start.1 = (f32[64,2944]{1,0:T(8,128)S(1)}, f32[64,2944]{1,0:T(8,128)S(1)}, u32[]{:S(2)}, u32[]{:S(2)}) collective-permute-start(f32[64,2944]{1,0:T(8,128)S(1)} %get-tuple-element.32.refs_1_), channel_id=1, source_target_pairs={{0,2},{1,3},{2,0},{3,1},{4,6},{5,7},{6,4},{7,5},{8,10},{9,11},{10,... | collective-permute-start | bytes 2261000 | tf_op jit(solution)/shard_map/ppermute | solution.py:214
  33.7 1.1 apply1.1.refs_3_.refs_0_
  34.9 15.8 %collective-permute-done.1.refs_2_ = f32[64,2944]{1,0:T(8,128)S(1)} collective-permute-done((f32[64,2944]{1,0:T(8,128)S(1)}, f32[64,2944]{1,0:T(8,128)S(1)}, u32[]{:S(2)}, u32[]{:S(2)}) %collective-permute-start.1) | collective-permute-done | bytes 753696 | tf_op jit(solution)/shard_map/ppermute | solution.py:214
  50.6 2.6 %level2.1 = (f32[64,640]{1,0:T(8,128)S(1)}, f32[64,128]{1,0:T(8,128)S(1)}, f32[64,2304]{1,0:T(8,128)S(1)}) custom-call(f32[8,64]{1,0:T(8,128)S(1)} %copy-done.1, f32[64,2944]{1,0:T(8,128)S(1)} %get-tuple-element.32.refs_1_, f32[64,2944]{1,0:T(8,128)S(1)} %collective-permute-done.1.refs_2_, f32[256,640]{1,0:T(8,128)S(1)} %apply1.1.refs_3_.refs_0_), custom_call_target="tpu_custom_call" | custom-call | flops 10000000 | bytes 1000000 | tf_op jit(solution)/shard_map/level2/pallas_call | solution.py:199
  53.2 2.1 %collective-permute-start.2 = (f32[64,2304]{1,0:T(8,128)S(1)}, f32[64,2304]{1,0:T(8,128)S(1)}, u32[]{:S(2)}, u32[]{:S(2)}) collective-permute-start(f32[64,2304]{1,0:T(8,128)S(1)} %get-tuple-element.35.refs_1_), channel_id=1, source_target_pairs={{0,4},{1,5},{2,6},{3,7},{4,0},{5,1},{6,2},{7,3},{8,12},{9,13},{10,... | collective-permute-start | bytes 1769480 | tf_op jit(solution)/shard_map/ppermute | solution.py:214
  55.3 1.0 apply2.1.refs_3_.refs_0_
  56.3 10.7 %collective-permute-done.2.refs_2_ = f32[64,2304]{1,0:T(8,128)S(1)} collective-permute-done((f32[64,2304]{1,0:T(8,128)S(1)}, f32[64,2304]{1,0:T(8,128)S(1)}, u32[]{:S(2)}, u32[]{:S(2)}) %collective-permute-start.2) | collective-permute-done | bytes 589856 | tf_op jit(solution)/shard_map/ppermute | solution.py:214
  66.9 2.5 %level3.1 = (f32[64,512]{1,0:T(8,128)S(1)}, f32[64,128]{1,0:T(8,128)S(1)}, f32[64,1792]{1,0:T(8,128)S(1)}) custom-call(f32[8,64]{1,0:T(8,128)S(1)} %copy-done.1, f32[64,2304]{1,0:T(8,128)S(1)} %get-tuple-element.35.refs_1_, f32[64,2304]{1,0:T(8,128)S(1)} %collective-permute-done.2.refs_2_, f32[256,512]{1,0:T(8,128)S(1)} %apply2.1.refs_3_.refs_0_), custom_call_target="tpu_custom_call" | custom-call | flops 10000000 | bytes 1000000 | tf_op jit(solution)/shard_map/level3/pallas_call | solution.py:199
  69.4 3.5 %collective-permute-start.3 = (f32[64,1792]{1,0:T(8,128)S(1)}, f32[64,1792]{1,0:T(8,128)S(1)}, u32[]{:S(2)}, u32[]{:S(2)}) collective-permute-start(f32[64,1792]{1,0:T(8,128)S(1)} %get-tuple-element.38.refs_1_), channel_id=1, source_target_pairs={{0,8},{1,9},{2,10},{3,11},{4,12},{5,13},{6,14},{7,15},{8,0},{9,1},... | collective-permute-start | bytes 1376264 | tf_op jit(solution)/shard_map/ppermute | solution.py:214
  72.9 1.0 apply3.1.refs_3_.refs_0_
  73.9 7.0 %collective-permute-done.3.refs_2_ = f32[64,1792]{1,0:T(8,128)S(1)} collective-permute-done((f32[64,1792]{1,0:T(8,128)S(1)}, f32[64,1792]{1,0:T(8,128)S(1)}, u32[]{:S(2)}, u32[]{:S(2)}) %collective-permute-start.3) | collective-permute-done | bytes 458784 | tf_op jit(solution)/shard_map/ppermute | solution.py:214
  80.9 2.3 %level4.1 = (f32[64,512]{1,0:T(8,128)S(1)}, f32[64,128]{1,0:T(8,128)S(1)}, f32[64,1280]{1,0:T(8,128)S(1)}) custom-call(f32[8,64]{1,0:T(8,128)S(1)} %copy-done.1, f32[64,1792]{1,0:T(8,128)S(1)} %get-tuple-element.38.refs_1_, f32[64,1792]{1,0:T(8,128)S(1)} %collective-permute-done.3.refs_2_, f32[256,512]{1,0:T(8,128)S(1)} %apply3.1.refs_3_.refs_0_), custom_call_target="tpu_custom_call" | custom-call | flops 10000000 | bytes 1000000 | tf_op jit(solution)/shard_map/level4/pallas_call | solution.py:199
  83.2 0.1 collective-permute-start.4
  83.3 0.9 apply4.1.refs_3_.refs_0_
  84.2 0.7 collective-permute-done.4.refs_2_
  84.9 2.3 %level5.1 = (f32[64,384]{1,0:T(8,128)S(1)}, f32[64,128]{1,0:T(8,128)S(1)}, f32[64,896]{1,0:T(8,128)S(1)}) custom-call(f32[8,64]{1,0:T(8,128)S(1)} %copy-done.1, f32[64,1280]{1,0:T(8,128)S(1)} %get-tuple-element.41.refs_1_, f32[64,1280]{1,0:T(8,128)S(1)} %collective-permute-done.4.refs_2_, f32[256,384]{1,0:T(8,128)S(1)} %apply4.1.refs_3_.refs_0_), custom_call_target="tpu_custom_call" | custom-call | flops 10000000 | bytes 1000000 | tf_op jit(solution)/shard_map/level5/pallas_call | solution.py:199
  87.2 2.0 %collective-permute-start.5 = (f32[64,896]{1,0:T(8,128)S(1)}, f32[64,896]{1,0:T(8,128)S(1)}, u32[]{:S(2)}, u32[]{:S(2)}) collective-permute-start(f32[64,896]{1,0:T(8,128)S(1)} %get-tuple-element.44.refs_1_), channel_id=1, source_target_pairs={{0,32},{16,48},{32,0},{48,16},{64,96},{80,112},{96,64},{112,80},{1... | collective-permute-start | bytes 688136 | tf_op jit(solution)/shard_map/ppermute | solution.py:214
  89.2 0.9 apply5.1.refs_3_.refs_0_
  90.1 5.0 %collective-permute-done.5.refs_2_ = f32[64,896]{1,0:T(8,128)S(1)} collective-permute-done((f32[64,896]{1,0:T(8,128)S(1)}, f32[64,896]{1,0:T(8,128)S(1)}, u32[]{:S(2)}, u32[]{:S(2)}) %collective-permute-start.5) | collective-permute-done | bytes 229408 | tf_op jit(solution)/shard_map/ppermute | solution.py:214
  95.1 2.2 %level6.1 = (f32[64,384]{1,0:T(8,128)S(1)}, f32[64,128]{1,0:T(8,128)S(1)}, f32[64,512]{1,0:T(8,128)S(1)}) custom-call(f32[8,64]{1,0:T(8,128)S(1)} %copy-done.1, f32[64,896]{1,0:T(8,128)S(1)} %get-tuple-element.44.refs_1_, f32[64,896]{1,0:T(8,128)S(1)} %collective-permute-done.5.refs_2_, f32[256,384]{1,0:T(8,128)S(1)} %apply5.1.refs_3_.refs_0_), custom_call_target="tpu_custom_call" | custom-call | flops 10000000 | bytes 1000000 | tf_op jit(solution)/shard_map/level6/pallas_call | solution.py:199
  97.3 3.7 %collective-permute-start.6 = (f32[64,512]{1,0:T(8,128)S(1)}, f32[64,512]{1,0:T(8,128)S(1)}, u32[]{:S(2)}, u32[]{:S(2)}) collective-permute-start(f32[64,512]{1,0:T(8,128)S(1)} %get-tuple-element.47.refs_1_), channel_id=1, source_target_pairs={{0,64},{16,80},{32,96},{48,112},{64,0},{80,16},{96,32},{112,48},{1... | collective-permute-start | bytes 393224 | tf_op jit(solution)/shard_map/ppermute | solution.py:214
  100.9 0.8 apply6.1.refs_3_.refs_0_
  101.7 5.1 %collective-permute-done.6.refs_2_ = f32[64,512]{1,0:T(8,128)S(1)} collective-permute-done((f32[64,512]{1,0:T(8,128)S(1)}, f32[64,512]{1,0:T(8,128)S(1)}, u32[]{:S(2)}, u32[]{:S(2)}) %collective-permute-start.6) | collective-permute-done | bytes 131104 | tf_op jit(solution)/shard_map/ppermute | solution.py:214
  106.8 2.1 %level7.1 = (f32[64,256]{1,0:T(8,128)S(1)}, f32[64,128]{1,0:T(8,128)S(1)}, f32[64,256]{1,0:T(8,128)S(1)}) custom-call(f32[8,64]{1,0:T(8,128)S(1)} %copy-done.1, f32[64,512]{1,0:T(8,128)S(1)} %get-tuple-element.47.refs_1_, f32[64,512]{1,0:T(8,128)S(1)} %collective-permute-done.6.refs_2_, f32[256,256]{1,0:T(8,128)S(1)} %apply6.1.refs_3_.refs_0_), custom_call_target="tpu_custom_call" | custom-call | flops 10000000 | bytes 1000000 | tf_op jit(solution)/shard_map/level7/pallas_call | solution.py:199
  109.0 5.0 %collective-permute-start.7 = (f32[64,256]{1,0:T(8,128)S(1)}, f32[64,256]{1,0:T(8,128)S(1)}, u32[]{:S(2)}, u32[]{:S(2)}) collective-permute-start(f32[64,256]{1,0:T(8,128)S(1)} %get-tuple-element.50.refs_1_), channel_id=1, source_target_pairs={{0,224},{16,240},{32,192},{48,208},{64,160},{80,176},{96,128},{112... | collective-permute-start | bytes 196616 | tf_op jit(solution)/shard_map/ppermute | solution.py:214
  114.0 0.8 apply7.1.refs_3_
  114.8 1.9 %collective-permute-done.7.refs_2_ = f32[64,256]{1,0:T(8,128)S(1)} collective-permute-done((f32[64,256]{1,0:T(8,128)S(1)}, f32[64,256]{1,0:T(8,128)S(1)}, u32[]{:S(2)}, u32[]{:S(2)}) %collective-permute-start.7) | collective-permute-done | bytes 65568 | tf_op jit(solution)/shard_map/ppermute | solution.py:214
  116.7 3.0 %last.1 = f32[256,128]{1,0:T(8,128)} custom-call(f32[8,64]{1,0:T(8,128)S(1)} %copy-done.1, f32[64,256]{1,0:T(8,128)S(1)} %get-tuple-element.50.refs_1_, f32[64,256]{1,0:T(8,128)S(1)} %collective-permute-done.7.refs_2_, f32[256,256]{1,0:T(8,128)S(1)} %apply7.1.refs_3_), custom_call_target="tpu_custom_call" | custom-call | flops 10000000 | bytes 1000000 | tf_op jit(solution)/shard_map/last/pallas_call | solution.py:199
Async XLA Ops:
  0.0 1.0 copy-start
  1.0 0.9 copy-start.2
  2.0 0.9 copy-start.3
  11.1 16.7 %collective-permute-start = (f32[256,640]{1,0:T(8,128)S(1)}, f32[256,640]{1,0:T(8,128)S(1)}, u32[]{:S(2)}, u32[]{:S(2)}) collective-permute-start(f32[256,640]{1,0:T(8,128)S(1)} %get-tuple-element.29.y_ref), channel_id=1, source_target_pairs={{0,1},{1,0},{2,3},{3,2},{4,5},{5,4},{6,7},{7,6},{8,9},{9,8},{10,11... | collective-permute-start | bytes 1966088 | tf_op jit(solution)/shard_map/ppermute | solution.py:214
  14.7 13.2 %copy-start.1 = (f32[8,64]{1,0:T(8,128)S(1)}, f32[8,64]{1,0:T(8,128)}, u32[]{:S(2)}) copy-start(f32[8,64]{1,0:T(8,128)} %refs_0_.13) | copy-start | bytes 6148
  31.5 19.1 %collective-permute-start.1 = (f32[64,2944]{1,0:T(8,128)S(1)}, f32[64,2944]{1,0:T(8,128)S(1)}, u32[]{:S(2)}, u32[]{:S(2)}) collective-permute-start(f32[64,2944]{1,0:T(8,128)S(1)} %get-tuple-element.32.refs_1_), channel_id=1, source_target_pairs={{0,2},{1,3},{2,0},{3,1},{4,6},{5,7},{6,4},{7,5},{8,10},{9,11},{10,... | collective-permute-start | bytes 2261000 | tf_op jit(solution)/shard_map/ppermute | solution.py:214
  53.2 13.7 %collective-permute-start.2 = (f32[64,2304]{1,0:T(8,128)S(1)}, f32[64,2304]{1,0:T(8,128)S(1)}, u32[]{:S(2)}, u32[]{:S(2)}) collective-permute-start(f32[64,2304]{1,0:T(8,128)S(1)} %get-tuple-element.35.refs_1_), channel_id=1, source_target_pairs={{0,4},{1,5},{2,6},{3,7},{4,0},{5,1},{6,2},{7,3},{8,12},{9,13},{10,... | collective-permute-start | bytes 1769480 | tf_op jit(solution)/shard_map/ppermute | solution.py:214
  69.4 11.4 %collective-permute-start.3 = (f32[64,1792]{1,0:T(8,128)S(1)}, f32[64,1792]{1,0:T(8,128)S(1)}, u32[]{:S(2)}, u32[]{:S(2)}) collective-permute-start(f32[64,1792]{1,0:T(8,128)S(1)} %get-tuple-element.38.refs_1_), channel_id=1, source_target_pairs={{0,8},{1,9},{2,10},{3,11},{4,12},{5,13},{6,14},{7,15},{8,0},{9,1},... | collective-permute-start | bytes 1376264 | tf_op jit(solution)/shard_map/ppermute | solution.py:214
  83.2 1.7 %collective-permute-start.4 = (f32[64,1280]{1,0:T(8,128)S(1)}, f32[64,1280]{1,0:T(8,128)S(1)}, u32[]{:S(2)}, u32[]{:S(2)}) collective-permute-start(f32[64,1280]{1,0:T(8,128)S(1)} %get-tuple-element.41.refs_1_), channel_id=1, source_target_pairs={{0,16},{16,0},{32,48},{48,32},{64,80},{80,64},{96,112},{112,96},{1... | collective-permute-start | bytes 983048 | tf_op jit(solution)/shard_map/ppermute | solution.py:214
  87.2 7.9 %collective-permute-start.5 = (f32[64,896]{1,0:T(8,128)S(1)}, f32[64,896]{1,0:T(8,128)S(1)}, u32[]{:S(2)}, u32[]{:S(2)}) collective-permute-start(f32[64,896]{1,0:T(8,128)S(1)} %get-tuple-element.44.refs_1_), channel_id=1, source_target_pairs={{0,32},{16,48},{32,0},{48,16},{64,96},{80,112},{96,64},{112,80},{1... | collective-permute-start | bytes 688136 | tf_op jit(solution)/shard_map/ppermute | solution.py:214
  97.3 9.6 %collective-permute-start.6 = (f32[64,512]{1,0:T(8,128)S(1)}, f32[64,512]{1,0:T(8,128)S(1)}, u32[]{:S(2)}, u32[]{:S(2)}) collective-permute-start(f32[64,512]{1,0:T(8,128)S(1)} %get-tuple-element.47.refs_1_), channel_id=1, source_target_pairs={{0,64},{16,80},{32,96},{48,112},{64,0},{80,16},{96,32},{112,48},{1... | collective-permute-start | bytes 393224 | tf_op jit(solution)/shard_map/ppermute | solution.py:214
  109.0 7.7 %collective-permute-start.7 = (f32[64,256]{1,0:T(8,128)S(1)}, f32[64,256]{1,0:T(8,128)S(1)}, u32[]{:S(2)}, u32[]{:S(2)}) collective-permute-start(f32[64,256]{1,0:T(8,128)S(1)} %get-tuple-element.50.refs_1_), channel_id=1, source_target_pairs={{0,224},{16,240},{32,192},{48,208},{64,160},{80,176},{96,128},{112... | collective-permute-start | bytes 196616 | tf_op jit(solution)/shard_map/ppermute | solution.py:214

commit v3 on v2

--- a/solution.py
+++ b/solution.py
@@ -11,6 +11,7 @@
 NRHS = 128
 WIDTH = LEVELS * R + NRHS
 NB = 16
+SPLIT = 4
 F32 = jnp.float32
 HI = lax.Precision.HIGHEST
 
@@ -77,34 +78,55 @@
     return jnp.concatenate(out, axis=0)
 
 
-def leaf_kernel(d_ref, b_ref, t_ref, y_ref, z_ref, m_ref, aug):
-    aug[:, :M] = d_ref[...]
-    aug[:, M : M + LEVELS * R] = b_ref[...]
-    aug[:, M + LEVELS * R :] = t_ref[...]
-    for j in range(4):
+def sweep(aug, count, y_ref, z_ref, m_ref, late=()):
+    rows = aug.shape[0]
+    cols = aug.shape[1] - WIDTH
+    for j in range(count):
         r0 = R * j
         a0 = 128 * (r0 // 128)
         minv = chol_inverse(aug[r0 : r0 + R, a0 : a0 + 128], r0 - a0)
         m_ref[r0 : r0 + R, :] = minv
-        rows = aug[r0 : r0 + R, a0:]
-        panel = mm(minv, jnp.concatenate([rows, rows], axis=0))
-        z_ref[r0 : r0 + R, :] = jnp.zeros((R, M), F32)
-        z_ref[r0 : r0 + R, a0:] = panel[:, : M - a0]
-        y_ref[r0 : r0 + R, :] = panel[:, M - a0 :]
-        for i in range(j + 1, 4):
+        if j == 0:
+            for copy in late:
+                copy.wait()
+        block = aug[r0 : r0 + R, a0:]
+        panel = mm(minv, jnp.concatenate([block, block], axis=0))
+        z_ref[r0 : r0 + R, :] = panel[:, : cols - a0]
+        y_ref[r0 : r0 + R, :] = panel[:, cols - a0 :]
+        for i in range(j + 1, rows // R):
             c0 = R * i
             s0 = 128 * (c0 // 128)
             aug[c0 : c0 + R, s0:] -= mm_t(panel[:, c0 - a0 : c0 - a0 + R], panel[:, s0 - a0 :])
 
 
-def back_kernel(y_ref, z_ref, m_ref, w_ref):
+def leaf_kernel(d_any, b_any, t_any, y_ref, z_ref, m_ref, rest_ref, aug, sem):
+    at = M + LEVELS * R
+    copies = [
+        pltpu.make_async_copy(d_any, aug.at[:, :M], sem.at[0]),
+        pltpu.make_async_copy(b_any, aug.at[:, M:at], sem.at[1]),
+        pltpu.make_async_copy(t_any, aug.at[:, at:], sem.at[2]),
+    ]
+    for copy in copies:
+        copy.start()
+    copies[0].wait()
+    sweep(aug, 2, y_ref, z_ref, m_ref, copies[1:])
+    rest_ref[...] = aug[M // 2 :, M // 2 :]
+
+
+def leaf2_kernel(rest_ref, y_ref, z_ref, m_ref, aug):
+    aug[...] = rest_ref[...]
+    sweep(aug, 2, y_ref, z_ref, m_ref)
+
+
+def back_kernel(ya_ref, za_ref, ma_ref, yb_ref, zb_ref, mb_ref, w_ref):
     for j in range(3, -1, -1):
-        r0 = R * j
-        o = R - r0 % 128
-        rhs = y_ref[r0 : r0 + R, :]
+        y_ref, z_ref, m_ref = (ya_ref, za_ref, ma_ref) if j < 2 else (yb_ref, zb_ref, mb_ref)
+        q0 = R * (j % 2)
+        rhs = y_ref[q0 : q0 + R, :]
         if j < 3:
-            rhs = rhs - mm(z_ref[r0 : r0 + R, r0 + R :], w_ref[r0 + R :, :])
-        w_ref[r0 : r0 + R, :] = mm_t(m_ref[r0 : r0 + R, :], rhs)[o : o + R, :]
+            z = z_ref[q0 : q0 + R, q0 + R :]
+            rhs = rhs - mm(z, w_ref[R * (j + 1) :, :])
+        w_ref[R * j : R * j + R, :] = mm_t(m_ref[q0 : q0 + R, :], rhs)[R - q0 : 2 * R - q0, :]
 
 
 def gram_pair(y, pair):
@@ -112,14 +134,16 @@
     return mm_t(y[:, st : st + 128], y[:, st:])
 
 
-def gram_kernel(y_ref, g_ref):
-    y = y_ref[...]
+def gram_pairs(ya, yb):
+    return [gram_pair(ya, pair) + gram_pair(yb, pair) for pair in range(4)]
+
+
+def gram_kernel(ya_ref, yb_ref, g_ref):
     offs, _ = offsets(1)
-    for pair in range(4):
-        g = gram_pair(y, pair)
-        for h in range(2):
-            level = 2 * pair + 1 + h
-            g_ref[:, offs[level] : offs[level] + width_of(level)] = g[R * h : R * h + R, :]
+    grams = gram_pairs(ya_ref[...], yb_ref[...])
+    for level in range(1, LEVELS + 1):
+        pair, h = (level - 1) // 2, (level - 1) % 2
+        g_ref[:, offs[level] : offs[level] + width_of(level)] = grams[pair][R * h : R * h + R, :]
 
 
 def reduce_level(k, coupling_ref, rows, p_ref, m_ref):
@@ -149,15 +173,12 @@
                 n_ref[:, o : o + width_of(level)] = trailing(level) - g[R * h : R * h + R, :]
 
 
-def first_level_kernel(c_ref, g_ref, got_ref, dep_ref, p_ref, m_ref, n_ref):
-    y = got_ref[...]
+def first_level_kernel(c_ref, g_ref, ya_ref, yb_ref, dep_ref, p_ref, m_ref, n_ref):
     offs, _ = offsets(1)
-    grams = {0: gram_pair(y, 0)}
+    grams = gram_pairs(ya_ref[...], yb_ref[...])
 
     def part(level):
         pair, h = (level - 1) // 2, (level - 1) % 2
-        if pair not in grams:
-            grams[pair] = gram_pair(y, pair)
         o = offs[level]
         return g_ref[:, o : o + width_of(level)] + grams[pair][R * h : R * h + R, :]
 
@@ -176,65 +197,146 @@
     next_level(k, p, part, n_ref)
 
 
-def apply_level(k, w, p, minv):
+def coefficient(k, p_ref, m_ref):
     o = R * ((k - 1) % 2)
     cut = (start_of(k + 1) if k < LEVELS else LEVELS * R) - start_of(k)
-    coef = mm_t(minv, p[:, cut:])[R - o : 2 * R - o, :]
-    return w[:, cut:] - mm(w[:, o : o + R], coef)
-
-
-def apply_kernel(k, w_ref, p_ref, m_ref, o_ref):
-    o_ref[...] = apply_level(k, w_ref[...], p_ref[...], m_ref[...])
-
-
-def last_kernel(k, c_ref, own_ref, got_ref, w_ref, o_ref, p_ref, m_ref):
-    p = reduce_level(k, c_ref, own_ref[...] + got_ref[...], p_ref, m_ref)
-    o_ref[...] = apply_level(k, w_ref[...], p, m_ref[...])
-
-
-def call(kernel, outs, *args, hbm=(), scratch=(), flops=10_000_000, name=None):
+    return mm_t(m_ref[...], p_ref[:, cut:])[R - o : 2 * R - o, :], o, cut
+
+
+def stack_kernel(k, *refs):
+    *old, p_ref, m_ref, o_ref = refs
+    coef, o, cut = coefficient(k, p_ref, m_ref)
+    rows = 0
+    if old:
+        prev = old[0]
+        rows = prev.shape[0]
+        o_ref[:rows, :] = prev[:, cut:] - mm(prev[:, o : o + R], coef)
+    o_ref[rows:, :] = coef
+
+
+def is_active():
+    x = lax.rem(lax.axis_index("inner"), 4)
+    core = lax.rem(lax.axis_index("group"), 2)
+    middle = (x == 1) | (x == 2)
+    return middle == (core == 0)
+
+
+def fold_kernel(w_ref, own_ref, got_ref, o_ref):
+    coef = jnp.where(is_active(), own_ref[...], got_ref[...])
+    at = start_of(SPLIT + 1)
+    o_ref[...] = w_ref[:, at:] - mm(w_ref[:, :at], coef)
+
+
+def last_kernel(k, c_ref, own_ref, got_ref, old_ref, dep_ref, z_ref, p_ref, m_ref):
+    reduce_level(k, c_ref, own_ref[...] + got_ref[...], p_ref, m_ref)
+    stack_kernel(k, old_ref, p_ref, m_ref, z_ref)
+
+
+def finish_kernel(w_ref, own_ref, got_ref, o_ref):
+    z = jnp.where(is_active(), own_ref[...], got_ref[...])
+    at = w_ref.shape[1] - NRHS
+    o_ref[...] = w_ref[:, at:] - mm(w_ref[:, :at], z)
+
+
+def call(kernel, outs, *args, hbm=(), scratch=(), sems=0, flops=10_000_000, name=None):
     vm = pl.BlockSpec(memory_space=pltpu.VMEM)
     hb = pl.BlockSpec(memory_space=pl.ANY)
     shapes = [jax.ShapeDtypeStruct(s, F32) for s in outs]
+    extra = [pltpu.SemaphoreType.DMA((sems,))] if sems else []
     return pl.pallas_call(
         kernel,
         out_shape=shapes,
         in_specs=[hb if i in hbm else vm for i in range(len(args))],
         out_specs=[vm] * len(shapes),
-        scratch_shapes=[pltpu.VMEM(s, F32) for s in scratch],
+        scratch_shapes=[pltpu.VMEM(s, F32) for s in scratch] + extra,
         compiler_params=pltpu.CompilerParams(vmem_limit_bytes=16 << 20),
         cost_estimate=pl.CostEstimate(flops=flops, bytes_accessed=1_000_000, transcendentals=0),
         name=name,
     )(*args)
 
 
-def exchange(value, level, inner_bits):
-    axis = "inner" if level <= inner_bits else "group"
-    mask = {1: 1, 2: 2, 3: 4, 4: 8, 5: 1, 6: 2, 7: 4, 8: 14}[level]
-    return lax.ppermute(value, axis, [(s, s ^ mask) for s in range(lax.axis_size(axis))])
+def send(value, move):
+    pairs = []
+    for group in range(16):
+        for inner in range(16):
+            to = move(group // 2, group % 2, inner // 4, inner % 4)
+            if to is not None:
+                z, core, y, x = to
+                pairs.append((group * 16 + inner, (z * 2 + core) * 16 + y * 4 + x))
+    return lax.ppermute(value, ("group", "inner"), pairs)
+
+
+def active(core, x):
+    return (x in (1, 2)) == (core == 0)
+
+
+def exchange(value, level):
+    moves = {
+        2: lambda z, c, y, x: (z, c, y, x ^ 3),
+        3: lambda z, c, y, x: (z, c, y ^ 1, x),
+        4: lambda z, c, y, x: (z, c, y ^ 3, x),
+        5: lambda z, c, y, x: (z, c ^ 1, y, x ^ 1),
+        6: lambda z, c, y, x: (z ^ 1, c, y, x),
+        7: lambda z, c, y, x: (z ^ 2, c, y, x),
+        8: lambda z, c, y, x: (z ^ 7, c, y, x),
+    }
+    return send(value, lambda z, c, y, x: moves[level](z, c, y, x) if active(c, x) else None)
+
+
+def to_active(value):
+    return send(value, lambda z, c, y, x: None if active(c, x) else (z, c, y, x ^ 1))
+
+
+def to_passive(value):
+    return send(value, lambda z, c, y, x: (z, c, y, x ^ 1) if active(c, x) else None)
+
+
+def to_other_core(value):
+    return send(value, lambda z, c, y, x: (z, c ^ 1, y, x) if active(c, x) else None)
 
 
 def per_device(leaf_blocks, bases, targets, coupling):
-    inner_bits = lax.axis_size("inner").bit_length() - 1
-    y, z, m = call(
-        leaf_kernel, [(M, WIDTH), (M, M), (M, 128)], leaf_blocks, bases, targets,
-        scratch=[(M, M + WIDTH)], name="leaf",
-    )
-    got = exchange(y, 1, inner_bits)
-    (own,) = call(gram_kernel, [(R, offsets(1)[1])], y, name="gram")
-    (w,) = call(back_kernel, [(M, WIDTH)], y, z, m, name="back")
+    half = M // 2
+    leaf_blocks, bases, targets = (
+        pltpu.with_memory_space_constraint(a, pltpu.HBM) for a in (leaf_blocks, bases, targets)
+    )
+    ya, za, ma, rest = call(
+        leaf_kernel, [(half, WIDTH), (half, M), (half, 128), (half, half + WIDTH)], leaf_blocks, bases, targets,
+        hbm=(0, 1, 2), scratch=[(M, M + WIDTH)], sems=3, name="leaf",
+    )
+    got_a = to_active(ya)
+    yb, zb, mb = call(
+        leaf2_kernel, [(half, WIDTH), (half, half), (half, 128)], rest,
+        scratch=[(half, half + WIDTH)], name="leaf2",
+    )
+    got_b = to_active(yb)
+    (own,) = call(gram_kernel, [(R, offsets(1)[1])], ya, yb, name="gram")
+    (w,) = call(back_kernel, [(M, WIDTH)], ya, za, ma, yb, zb, mb, name="back")
+    dep, stack, folded = w, (), None
     for k in range(1, LEVELS):
         outs = [(R, width_of(k)), (R, 128), (R, offsets(k + 1)[1])]
-        kernel = first_level_kernel if k == 1 else (lambda *refs, k=k: level_kernel(k, *refs))
-        p, minv, own = call(kernel, outs, coupling, own, got, w, hbm=(3,), name="level%d" % k)
-        got = exchange(own, k + 1, inner_bits)
-        kernel = lambda *refs, k=k: apply_kernel(k, *refs)
-        (w,) = call(kernel, [(M, width_of(k + 1))], w, p, minv, name="apply%d" % k)
+        if k == 1:
+            p, minv, own = call(first_level_kernel, outs, coupling, own, got_a, got_b, dep, hbm=(4,), name="level1")
+        else:
+            kernel = lambda *refs, k=k: level_kernel(k, *refs)
+            p, minv, own = call(kernel, outs, coupling, own, got, dep, hbm=(3,), name="level%d" % k)
+        got = exchange(own, k + 1)
+        kernel = lambda *refs, k=k: stack_kernel(k, *refs)
+        rows = R * k if k <= SPLIT else R * (k - SPLIT)
+        stack = call(kernel, [(rows, width_of(k + 1))], *stack, p, minv, name="stack%d" % k)
+        dep = stack[0]
+        if k == SPLIT:
+            lower, stack = stack[0], ()
+            lower_got = to_passive(lower)
+        if k == SPLIT + 2:
+            (folded,) = call(fold_kernel, [(M, width_of(SPLIT + 1))], w, lower, lower_got, name="fold")
+            dep = folded
     kernel = lambda *refs: last_kernel(LEVELS, *refs)
-    return call(
-        kernel, [(M, NRHS)], coupling, own, got, w,
+    (z,) = call(
+        kernel, [(R * (LEVELS - SPLIT), NRHS)], coupling, own, got, stack[0], dep, hbm=(4,),
         scratch=[(R, width_of(LEVELS)), (R, 128)], name="last",
-    )[0]
+    )
+    return call(finish_kernel, [(M, NRHS)], folded, z, to_other_core(z), name="finish")[0]
 
 
 def solution(mesh):

time: 121 us -> 116 us (0.959)
  waiting for transfers between devices: 57 us -> 39 us
  starting transfers between devices: 21 us -> 37.2 us
  local copies, waits for them, and re-layouts: 2.9 us -> 0.01 us
    ppermute x8 -> x11, waiting for transfers between devices: 57 us -> 39 us  [send(): return lax.ppermute(value, ('group', 'inner'), pairs)]
    ppermute x8 -> x11, starting transfers between devices: 21 us -> 37.2 us  [send(): return lax.ppermute(value, ('group', 'inner'), pairs)]
    unnamed x8 -> x2, local copies, waits for them, and re-layouts: 2.9 us -> 0.01 us
    pallas_call x18 -> x21, Pallas kernels: 38.6 us -> 39 us  [call(): pl.pallas_call(kernel, out_shape=shapes, in_specs=[hb if i in hbm else vm...]
  transfers between devices with their start and end apart: 8 -> 11, of which waited for: 8 -> 9; matrix products, arithmetic and copies ran while one was open for 0% -> 0% of each run, Pallas kernels for 8% -> 15%
where the time goes in v3:
time: 116 us; the launch traced here: 115 us
  Pallas kernels  39 us (34%)
  waiting for transfers between devices  39 us (34%)
  starting transfers between devices  37.2 us (32%)
    pallas_call x21, Pallas kernels, call(): pl.pallas_call(kernel, out_shape=shapes, in_specs=[hb if i in hbm else vm...  39 us
    ppermute x11, waiting for transfers between devices, send(): return lax.ppermute(value, ('group', 'inner'), pairs)  39 us
    ppermute x11, starting transfers between devices, send(): return lax.ppermute(value, ('group', 'inner'), pairs)  37.2 us
  transfers between devices with their start and end apart: 11, of which 9 were waited for; matrix products, arithmetic and copies ran while one was open for 0% of the time, Pallas kernels for 15%

profile of v3, /device:TPU:2, one launch (start us, length us, event | category | flops | bytes accessed | tf_op | source)
XLA Modules:
  0.0 115.5 jit_solution(4146694441110052983)
XLA Ops:
  0.0 5.4 %leaf.1 = (f32[128,640]{1,0:T(8,128)S(1)}, f32[128,256]{1,0:T(8,128)S(1)}, f32[128,128]{1,0:T(8,128)S(1)}, f32[128,768]{1,0:T(8,128)S(1)}) custom-call(f32[256,256]{1,0:T(8,128)} %d_any.1, f32[256,512]{1,0:T(8,128)} %b_any.1, f32[256,128]{1,0:T(8,128)} %t_any.1), custom_call_target="tpu_custom_call" | custom-call | flops 10000000 | bytes 1000000 | tf_op jit(solution)/shard_map/leaf/pallas_call | solution.py:246
  5.5 1.3 %collective-permute-start = (f32[128,640]{1,0:T(8,128)S(1)}, f32[128,640]{1,0:T(8,128)S(1)}, u32[]{:S(2)}, u32[]{:S(2)}) collective-permute-start(f32[128,640]{1,0:T(8,128)S(1)} %get-tuple-element.33.ya_ref), channel_id=1, source_target_pairs={{0,1},{3,2},{4,5},{7,6},{8,9},{11,10},{12,13},{15,14},{17,16},{18,... | collective-permute-start | bytes 983048 | tf_op jit(solution)/shard_map/ppermute | solution.py:266
  6.8 3.9 %leaf2.1 = (f32[128,640]{1,0:T(8,128)S(1)}, f32[128,128]{1,0:T(8,128)S(1)}, f32[128,128]{1,0:T(8,128)S(1)}) custom-call(f32[128,768]{1,0:T(8,128)S(1)} %get-tuple-element.36.rest_ref), custom_call_target="tpu_custom_call" | custom-call | flops 10000000 | bytes 1000000 | tf_op jit(solution)/shard_map/leaf2/pallas_call | solution.py:246
  10.7 1.5 %collective-permute-start.1 = (f32[128,640]{1,0:T(8,128)S(1)}, f32[128,640]{1,0:T(8,128)S(1)}, u32[]{:S(2)}, u32[]{:S(2)}) collective-permute-start(f32[128,640]{1,0:T(8,128)S(1)} %get-tuple-element.37.yb_ref), channel_id=1, source_target_pairs={{0,1},{3,2},{4,5},{7,6},{8,9},{11,10},{12,13},{15,14},{17,16},{18,... | collective-permute-start | bytes 983048 | tf_op jit(solution)/shard_map/ppermute | solution.py:266
  12.2 1.6 %gram.1.g_ref = f32[64,3584]{1,0:T(8,128)S(1)} custom-call(f32[128,640]{1,0:T(8,128)S(1)} %get-tuple-element.33.ya_ref, f32[128,640]{1,0:T(8,128)S(1)} %get-tuple-element.37.yb_ref), custom_call_target="tpu_custom_call" | custom-call | flops 10000000 | bytes 1000000 | tf_op jit(solution)/shard_map/gram/pallas_call | solution.py:246
  13.8 0.0 copy-start
  13.8 2.3 %back.1.dep_ref.w_ref = f32[256,640]{1,0:T(8,128)S(1)} custom-call(f32[128,640]{1,0:T(8,128)S(1)} %get-tuple-element.33.ya_ref, f32[128,256]{1,0:T(8,128)S(1)} %get-tuple-element.34.za_ref, f32[128,128]{1,0:T(8,128)S(1)} %get-tuple-element.35.ma_ref, f32[128,640]{1,0:T(8,128)S(1)} %get-tuple-element.37.yb_ref, f32[128,128]{1,0:T(8,128)S(1)} %get-tuple-element.38.zb_ref, ...), custom_call_target="tpu_custom_call" | custom-call | flops 10000000 | bytes 1000000 | tf_op jit(solution)/shard_map/back/pallas_call | solution.py:246
  16.1 0.0 collective-permute-done.ya_ref
  16.1 3.6 %collective-permute-done.1.yb_ref = f32[128,640]{1,0:T(8,128)S(1)} collective-permute-done((f32[128,640]{1,0:T(8,128)S(1)}, f32[128,640]{1,0:T(8,128)S(1)}, u32[]{:S(2)}, u32[]{:S(2)}) %collective-permute-start.1) | collective-permute-done | bytes 327712 | tf_op jit(solution)/shard_map/ppermute | solution.py:266
  19.7 0.0 copy-done
  19.7 3.5 %level1.1 = (f32[64,640]{1,0:T(8,128)S(1)}, f32[64,128]{1,0:T(8,128)S(1)}, f32[64,2944]{1,0:T(8,128)S(1)}) custom-call(f32[8,64]{1,0:T(8,128)S(1)} %copy-done, f32[64,3584]{1,0:T(8,128)S(1)} %gram.1.g_ref, f32[128,640]{1,0:T(8,128)S(1)} %collective-permute-done.ya_ref, f32[128,640]{1,0:T(8,128)S(1)} %collective-permute-done.1.yb_ref, ...), custom_call_target="tpu_custom_call" | custom-call | flops 10000000 | bytes 1000000 | tf_op jit(solution)/shard_map/level1/pallas_call | solution.py:246
  23.2 3.4 %collective-permute-start.2 = (f32[64,2944]{1,0:T(8,128)S(1)}, f32[64,2944]{1,0:T(8,128)S(1)}, u32[]{:S(2)}, u32[]{:S(2)}) collective-permute-start(f32[64,2944]{1,0:T(8,128)S(1)} %get-tuple-element.42.refs_1_), channel_id=1, source_target_pairs={{1,2},{2,1},{5,6},{6,5},{9,10},{10,9},{13,14},{14,13},{16,19},{19,... | collective-permute-start | bytes 2261000 | tf_op jit(solution)/shard_map/ppermute | solution.py:266
  26.6 0.5 stack1.1.refs_3_.refs_0_
  27.1 9.6 %collective-permute-done.2.refs_2_ = f32[64,2944]{1,0:T(8,128)S(1)} collective-permute-done((f32[64,2944]{1,0:T(8,128)S(1)}, f32[64,2944]{1,0:T(8,128)S(1)}, u32[]{:S(2)}, u32[]{:S(2)}) %collective-permute-start.2) | collective-permute-done | bytes 753696 | tf_op jit(solution)/shard_map/ppermute | solution.py:266
  36.8 2.6 %level2.1 = (f32[64,640]{1,0:T(8,128)S(1)}, f32[64,128]{1,0:T(8,128)S(1)}, f32[64,2304]{1,0:T(8,128)S(1)}) custom-call(f32[8,64]{1,0:T(8,128)S(1)} %copy-done, f32[64,2944]{1,0:T(8,128)S(1)} %get-tuple-element.42.refs_1_, f32[64,2944]{1,0:T(8,128)S(1)} %collective-permute-done.2.refs_2_, f32[64,640]{1,0:T(8,128)S(1)} %stack1.1.refs_3_.refs_0_), custom_call_target="tpu_custom_call" | custom-call | flops 10000000 | bytes 1000000 | tf_op jit(solution)/shard_map/level2/pallas_call | solution.py:246
  39.4 3.5 %collective-permute-start.3 = (f32[64,2304]{1,0:T(8,128)S(1)}, f32[64,2304]{1,0:T(8,128)S(1)}, u32[]{:S(2)}, u32[]{:S(2)}) collective-permute-start(f32[64,2304]{1,0:T(8,128)S(1)} %get-tuple-element.45.refs_1_), channel_id=1, source_target_pairs={{1,5},{2,6},{5,1},{6,2},{9,13},{10,14},{13,9},{14,10},{16,20},{19,... | collective-permute-start | bytes 1769480 | tf_op jit(solution)/shard_map/ppermute | solution.py:266
  42.9 0.6 stack2.1.refs_3_.refs_0_
  43.5 7.6 %collective-permute-done.3.refs_2_ = f32[64,2304]{1,0:T(8,128)S(1)} collective-permute-done((f32[64,2304]{1,0:T(8,128)S(1)}, f32[64,2304]{1,0:T(8,128)S(1)}, u32[]{:S(2)}, u32[]{:S(2)}) %collective-permute-start.3) | collective-permute-done | bytes 589856 | tf_op jit(solution)/shard_map/ppermute | solution.py:266
  51.1 2.5 %level3.1 = (f32[64,512]{1,0:T(8,128)S(1)}, f32[64,128]{1,0:T(8,128)S(1)}, f32[64,1792]{1,0:T(8,128)S(1)}) custom-call(f32[8,64]{1,0:T(8,128)S(1)} %copy-done, f32[64,2304]{1,0:T(8,128)S(1)} %get-tuple-element.45.refs_1_, f32[64,2304]{1,0:T(8,128)S(1)} %collective-permute-done.3.refs_2_, f32[128,512]{1,0:T(8,128)S(1)} %stack2.1.refs_3_.refs_0_), custom_call_target="tpu_custom_call" | custom-call | flops 10000000 | bytes 1000000 | tf_op jit(solution)/shard_map/level3/pallas_call | solution.py:246
  53.6 5.2 %collective-permute-start.4 = (f32[64,1792]{1,0:T(8,128)S(1)}, f32[64,1792]{1,0:T(8,128)S(1)}, u32[]{:S(2)}, u32[]{:S(2)}) collective-permute-start(f32[64,1792]{1,0:T(8,128)S(1)} %get-tuple-element.48.refs_1_), channel_id=1, source_target_pairs={{1,13},{2,14},{5,9},{6,10},{9,5},{10,6},{13,1},{14,2},{16,28},{19,... | collective-permute-start | bytes 1376264 | tf_op jit(solution)/shard_map/ppermute | solution.py:266
  58.8 0.8 stack3.1.refs_3_.refs_0_
  59.6 5.7 %collective-permute-done.4.refs_2_ = f32[64,1792]{1,0:T(8,128)S(1)} collective-permute-done((f32[64,1792]{1,0:T(8,128)S(1)}, f32[64,1792]{1,0:T(8,128)S(1)}, u32[]{:S(2)}, u32[]{:S(2)}) %collective-permute-start.4) | collective-permute-done | bytes 458784 | tf_op jit(solution)/shard_map/ppermute | solution.py:266
  65.2 2.3 %level4.1 = (f32[64,512]{1,0:T(8,128)S(1)}, f32[64,128]{1,0:T(8,128)S(1)}, f32[64,1280]{1,0:T(8,128)S(1)}) custom-call(f32[8,64]{1,0:T(8,128)S(1)} %copy-done, f32[64,1792]{1,0:T(8,128)S(1)} %get-tuple-element.48.refs_1_, f32[64,1792]{1,0:T(8,128)S(1)} %collective-permute-done.4.refs_2_, f32[192,512]{1,0:T(8,128)S(1)} %stack3.1.refs_3_.refs_0_), custom_call_target="tpu_custom_call" | custom-call | flops 10000000 | bytes 1000000 | tf_op jit(solution)/shard_map/level4/pallas_call | solution.py:246
  67.6 1.9 %collective-permute-start.6 = (f32[64,1280]{1,0:T(8,128)S(1)}, f32[64,1280]{1,0:T(8,128)S(1)}, u32[]{:S(2)}, u32[]{:S(2)}) collective-permute-start(f32[64,1280]{1,0:T(8,128)S(1)} %get-tuple-element.51.refs_1_), channel_id=1, source_target_pairs={{1,16},{2,19},{5,20},{6,23},{9,24},{10,27},{13,28},{14,31},{16,1},... | collective-permute-start | bytes 983048 | tf_op jit(solution)/shard_map/ppermute | solution.py:266
  69.5 0.8 stack4.1.own_ref.refs_3_
  70.3 1.3 %collective-permute-start.5 = (f32[256,384]{1,0:T(8,128)S(1)}, f32[256,384]{1,0:T(8,128)S(1)}, u32[]{:S(2)}, u32[]{:S(2)}) collective-permute-start(f32[256,384]{1,0:T(8,128)S(1)} %stack4.1.own_ref.refs_3_), channel_id=1, source_target_pairs={{1,0},{2,3},{5,4},{6,7},{9,8},{10,11},{13,12},{14,15},{16,17},{19,... | collective-permute-start | bytes 1179656 | tf_op jit(solution)/shard_map/ppermute | solution.py:266
  71.6 4.3 %collective-permute-done.6.refs_2_ = f32[64,1280]{1,0:T(8,128)S(1)} collective-permute-done((f32[64,1280]{1,0:T(8,128)S(1)}, f32[64,1280]{1,0:T(8,128)S(1)}, u32[]{:S(2)}, u32[]{:S(2)}) %collective-permute-start.6) | collective-permute-done | bytes 327712 | tf_op jit(solution)/shard_map/ppermute | solution.py:266
  75.9 2.3 %level5.1 = (f32[64,384]{1,0:T(8,128)S(1)}, f32[64,128]{1,0:T(8,128)S(1)}, f32[64,896]{1,0:T(8,128)S(1)}) custom-call(f32[8,64]{1,0:T(8,128)S(1)} %copy-done, f32[64,1280]{1,0:T(8,128)S(1)} %get-tuple-element.51.refs_1_, f32[64,1280]{1,0:T(8,128)S(1)} %collective-permute-done.6.refs_2_, f32[256,384]{1,0:T(8,128)S(1)} %stack4.1.own_ref.refs_3_), custom_call_target="tpu_custom_call" | custom-call | flops 10000000 | bytes 1000000 | tf_op jit(solution)/shard_map/level5/pallas_call | solution.py:246
  78.2 3.8 %collective-permute-start.7 = (f32[64,896]{1,0:T(8,128)S(1)}, f32[64,896]{1,0:T(8,128)S(1)}, u32[]{:S(2)}, u32[]{:S(2)}) collective-permute-start(f32[64,896]{1,0:T(8,128)S(1)} %get-tuple-element.52.refs_1_), channel_id=1, source_target_pairs={{1,33},{2,34},{5,37},{6,38},{9,41},{10,42},{13,45},{14,46},{16,48}... | collective-permute-start | bytes 688136 | tf_op jit(solution)/shard_map/ppermute | solution.py:266
  82.1 0.4 stack5.1.refs_3_.refs_0_
  82.4 3.7 %collective-permute-done.7.refs_2_ = f32[64,896]{1,0:T(8,128)S(1)} collective-permute-done((f32[64,896]{1,0:T(8,128)S(1)}, f32[64,896]{1,0:T(8,128)S(1)}, u32[]{:S(2)}, u32[]{:S(2)}) %collective-permute-start.7) | collective-permute-done | bytes 229408 | tf_op jit(solution)/shard_map/ppermute | solution.py:266
  86.1 2.2 %level6.1 = (f32[64,384]{1,0:T(8,128)S(1)}, f32[64,128]{1,0:T(8,128)S(1)}, f32[64,512]{1,0:T(8,128)S(1)}) custom-call(f32[8,64]{1,0:T(8,128)S(1)} %copy-done, f32[64,896]{1,0:T(8,128)S(1)} %get-tuple-element.52.refs_1_, f32[64,896]{1,0:T(8,128)S(1)} %collective-permute-done.7.refs_2_, f32[64,384]{1,0:T(8,128)S(1)} %stack5.1.refs_3_.refs_0_), custom_call_target="tpu_custom_call" | custom-call | flops 10000000 | bytes 1000000 | tf_op jit(solution)/shard_map/level6/pallas_call | solution.py:246
  88.3 5.2 %collective-permute-start.8 = (f32[64,512]{1,0:T(8,128)S(1)}, f32[64,512]{1,0:T(8,128)S(1)}, u32[]{:S(2)}, u32[]{:S(2)}) collective-permute-start(f32[64,512]{1,0:T(8,128)S(1)} %get-tuple-element.55.refs_1_), channel_id=1, source_target_pairs={{1,65},{2,66},{5,69},{6,70},{9,73},{10,74},{13,77},{14,78},{16,80}... | collective-permute-start | bytes 393224 | tf_op jit(solution)/shard_map/ppermute | solution.py:266
  93.5 0.0 collective-permute-done.5.got_ref
  93.5 0.6 fold.1.refs_3_.w_ref
  94.1 2.3 %collective-permute-done.8.refs_2_ = f32[64,512]{1,0:T(8,128)S(1)} collective-permute-done((f32[64,512]{1,0:T(8,128)S(1)}, f32[64,512]{1,0:T(8,128)S(1)}, u32[]{:S(2)}, u32[]{:S(2)}) %collective-permute-start.8) | collective-permute-done | bytes 131104 | tf_op jit(solution)/shard_map/ppermute | solution.py:266
  96.4 2.1 %level7.1 = (f32[64,256]{1,0:T(8,128)S(1)}, f32[64,128]{1,0:T(8,128)S(1)}, f32[64,256]{1,0:T(8,128)S(1)}) custom-call(f32[8,64]{1,0:T(8,128)S(1)} %copy-done, f32[64,512]{1,0:T(8,128)S(1)} %get-tuple-element.55.refs_1_, f32[64,512]{1,0:T(8,128)S(1)} %collective-permute-done.8.refs_2_, f32[256,384]{1,0:T(8,128)S(1)} %fold.1.refs_3_.w_ref), custom_call_target="tpu_custom_call" | custom-call | flops 10000000 | bytes 1000000 | tf_op jit(solution)/shard_map/level7/pallas_call | solution.py:246
  98.6 8.8 %collective-permute-start.9 = (f32[64,256]{1,0:T(8,128)S(1)}, f32[64,256]{1,0:T(8,128)S(1)}, u32[]{:S(2)}, u32[]{:S(2)}) collective-permute-start(f32[64,256]{1,0:T(8,128)S(1)} %get-tuple-element.56.refs_1_), channel_id=1, source_target_pairs={{1,225},{2,226},{5,229},{6,230},{9,233},{10,234},{13,237},{14,238}... | collective-permute-start | bytes 196616 | tf_op jit(solution)/shard_map/ppermute | solution.py:266
  107.4 0.6 stack6.1.refs_0_
  108.0 0.7 stack7.1.refs_3_.refs_4_
  108.7 1.2 %collective-permute-done.9.refs_2_ = f32[64,256]{1,0:T(8,128)S(1)} collective-permute-done((f32[64,256]{1,0:T(8,128)S(1)}, f32[64,256]{1,0:T(8,128)S(1)}, u32[]{:S(2)}, u32[]{:S(2)}) %collective-permute-start.9) | collective-permute-done | bytes 65568 | tf_op jit(solution)/shard_map/ppermute | solution.py:266
  109.9 2.3 %last.1.own_ref = f32[256,128]{1,0:T(8,128)S(1)} custom-call(f32[8,64]{1,0:T(8,128)S(1)} %copy-done, f32[64,256]{1,0:T(8,128)S(1)} %get-tuple-element.56.refs_1_, f32[64,256]{1,0:T(8,128)S(1)} %collective-permute-done.9.refs_2_, f32[192,256]{1,0:T(8,128)S(1)} %stack7.1.refs_3_.refs_4_, f32[192,256]{1,0:T(8,128)S(1)} %stack7.1.refs_3_.refs_4_), custom_call_target="tpu_custom_call" | custom-call | flops 10000000 | bytes 1000000 | tf_op jit(solution)/shard_map/last/pallas_call | solution.py:246
  112.2 1.3 %collective-permute-start.10 = (f32[256,128]{1,0:T(8,128)S(1)}, f32[256,128]{1,0:T(8,128)S(1)}, u32[]{:S(2)}, u32[]{:S(2)}) collective-permute-start(f32[256,128]{1,0:T(8,128)S(1)} %last.1.own_ref), channel_id=1, source_target_pairs={{1,17},{2,18},{5,21},{6,22},{9,25},{10,26},{13,29},{14,30},{16,0},... | collective-permute-start | bytes 393224 | tf_op jit(solution)/shard_map/ppermute | solution.py:266
  113.5 1.0 collective-permute-done.10.got_ref
  114.4 1.0 finish.1
Async XLA Ops:
  5.5 10.7 %collective-permute-start = (f32[128,640]{1,0:T(8,128)S(1)}, f32[128,640]{1,0:T(8,128)S(1)}, u32[]{:S(2)}, u32[]{:S(2)}) collective-permute-start(f32[128,640]{1,0:T(8,128)S(1)} %get-tuple-element.33.ya_ref), channel_id=1, source_target_pairs={{0,1},{3,2},{4,5},{7,6},{8,9},{11,10},{12,13},{15,14},{17,16},{18,... | collective-permute-start | bytes 983048 | tf_op jit(solution)/shard_map/ppermute | solution.py:266
  10.7 9.0 %collective-permute-start.1 = (f32[128,640]{1,0:T(8,128)S(1)}, f32[128,640]{1,0:T(8,128)S(1)}, u32[]{:S(2)}, u32[]{:S(2)}) collective-permute-start(f32[128,640]{1,0:T(8,128)S(1)} %get-tuple-element.37.yb_ref), channel_id=1, source_target_pairs={{0,1},{3,2},{4,5},{7,6},{8,9},{11,10},{12,13},{15,14},{17,16},{18,... | collective-permute-start | bytes 983048 | tf_op jit(solution)/shard_map/ppermute | solution.py:266
  13.8 5.9 %copy-start = (f32[8,64]{1,0:T(8,128)S(1)}, f32[8,64]{1,0:T(8,128)}, u32[]{:S(2)}) copy-start(f32[8,64]{1,0:T(8,128)} %refs_0_.13) | copy-start | bytes 6148
  23.2 13.5 %collective-permute-start.2 = (f32[64,2944]{1,0:T(8,128)S(1)}, f32[64,2944]{1,0:T(8,128)S(1)}, u32[]{:S(2)}, u32[]{:S(2)}) collective-permute-start(f32[64,2944]{1,0:T(8,128)S(1)} %get-tuple-element.42.refs_1_), channel_id=1, source_target_pairs={{1,2},{2,1},{5,6},{6,5},{9,10},{10,9},{13,14},{14,13},{16,19},{19,... | collective-permute-start | bytes 2261000 | tf_op jit(solution)/shard_map/ppermute | solution.py:266
  39.4 11.8 %collective-permute-start.3 = (f32[64,2304]{1,0:T(8,128)S(1)}, f32[64,2304]{1,0:T(8,128)S(1)}, u32[]{:S(2)}, u32[]{:S(2)}) collective-permute-start(f32[64,2304]{1,0:T(8,128)S(1)} %get-tuple-element.45.refs_1_), channel_id=1, source_target_pairs={{1,5},{2,6},{5,1},{6,2},{9,13},{10,14},{13,9},{14,10},{16,20},{19,... | collective-permute-start | bytes 1769480 | tf_op jit(solution)/shard_map/ppermute | solution.py:266
  53.6 11.6 %collective-permute-start.4 = (f32[64,1792]{1,0:T(8,128)S(1)}, f32[64,1792]{1,0:T(8,128)S(1)}, u32[]{:S(2)}, u32[]{:S(2)}) collective-permute-start(f32[64,1792]{1,0:T(8,128)S(1)} %get-tuple-element.48.refs_1_), channel_id=1, source_target_pairs={{1,13},{2,14},{5,9},{6,10},{9,5},{10,6},{13,1},{14,2},{16,28},{19,... | collective-permute-start | bytes 1376264 | tf_op jit(solution)/shard_map/ppermute | solution.py:266
  67.6 8.4 %collective-permute-start.6 = (f32[64,1280]{1,0:T(8,128)S(1)}, f32[64,1280]{1,0:T(8,128)S(1)}, u32[]{:S(2)}, u32[]{:S(2)}) collective-permute-start(f32[64,1280]{1,0:T(8,128)S(1)} %get-tuple-element.51.refs_1_), channel_id=1, source_target_pairs={{1,16},{2,19},{5,20},{6,23},{9,24},{10,27},{13,28},{14,31},{16,1},... | collective-permute-start | bytes 983048 | tf_op jit(solution)/shard_map/ppermute | solution.py:266
  70.3 23.2 %collective-permute-start.5 = (f32[256,384]{1,0:T(8,128)S(1)}, f32[256,384]{1,0:T(8,128)S(1)}, u32[]{:S(2)}, u32[]{:S(2)}) collective-permute-start(f32[256,384]{1,0:T(8,128)S(1)} %stack4.1.own_ref.refs_3_), channel_id=1, source_target_pairs={{1,0},{2,3},{5,4},{6,7},{9,8},{10,11},{13,12},{14,15},{16,17},{19,... | collective-permute-start | bytes 1179656 | tf_op jit(solution)/shard_map/ppermute | solution.py:266
  78.2 7.9 %collective-permute-start.7 = (f32[64,896]{1,0:T(8,128)S(1)}, f32[64,896]{1,0:T(8,128)S(1)}, u32[]{:S(2)}, u32[]{:S(2)}) collective-permute-start(f32[64,896]{1,0:T(8,128)S(1)} %get-tuple-element.52.refs_1_), channel_id=1, source_target_pairs={{1,33},{2,34},{5,37},{6,38},{9,41},{10,42},{13,45},{14,46},{16,48}... | collective-permute-start | bytes 688136 | tf_op jit(solution)/shard_map/ppermute | solution.py:266
  88.3 8.1 %collective-permute-start.8 = (f32[64,512]{1,0:T(8,128)S(1)}, f32[64,512]{1,0:T(8,128)S(1)}, u32[]{:S(2)}, u32[]{:S(2)}) collective-permute-start(f32[64,512]{1,0:T(8,128)S(1)} %get-tuple-element.55.refs_1_), channel_id=1, source_target_pairs={{1,65},{2,66},{5,69},{6,70},{9,73},{10,74},{13,77},{14,78},{16,80}... | collective-permute-start | bytes 393224 | tf_op jit(solution)/shard_map/ppermute | solution.py:266
  98.6 11.3 %collective-permute-start.9 = (f32[64,256]{1,0:T(8,128)S(1)}, f32[64,256]{1,0:T(8,128)S(1)}, u32[]{:S(2)}, u32[]{:S(2)}) collective-permute-start(f32[64,256]{1,0:T(8,128)S(1)} %get-tuple-element.56.refs_1_), channel_id=1, source_target_pairs={{1,225},{2,226},{5,229},{6,230},{9,233},{10,234},{13,237},{14,238}... | collective-permute-start | bytes 196616 | tf_op jit(solution)/shard_map/ppermute | solution.py:266
  112.2 2.3 %collective-permute-start.10 = (f32[256,128]{1,0:T(8,128)S(1)}, f32[256,128]{1,0:T(8,128)S(1)}, u32[]{:S(2)}, u32[]{:S(2)}) collective-permute-start(f32[256,128]{1,0:T(8,128)S(1)} %last.1.own_ref), channel_id=1, source_target_pairs={{1,17},{2,18},{5,21},{6,22},{9,25},{10,26},{13,29},{14,30},{16,0},... | collective-permute-start | bytes 393224 | tf_op jit(solution)/shard_map/ppermute | solution.py:266

commit v4 on v2

v4 whole, which is shorter than its diff:
```python
import jax
import jax.numpy as jnp
from jax import lax
from jax.experimental import pallas as pl
from jax.experimental.pallas import tpu as pltpu
from jax.sharding import PartitionSpec as P


M = 256
R = 64
LEVELS = 8
NRHS = 128
WIDTH = LEVELS * R + NRHS
NB = 16
SPLIT = 4
F32 = jnp.float32
HI = lax.Precision.HIGHEST


def start_of(level):
    return 128 * ((level - 1) // 2)


def width_of(level):
    return WIDTH - start_of(level)


def offsets(first, last=LEVELS):
    out, at = {}, 0
    for level in range(first, last + 1):
        out[level] = at
        at += width_of(level)
    return out, at


def mm(a, b):
    return lax.dot_general(a, b, (((1,), (0,)), ((), ())), precision=HI, preferred_element_type=F32)


def mm_t(a, b):
    return lax.dot_general(a, b, (((0,), (0,)), ((), ())), precision=HI, preferred_element_type=F32)


def chol_inverse(block, at):
    sub = lax.broadcasted_iota(jnp.int32, (8, 128), 0)
    lane = lax.broadcasted_iota(jnp.int32, (8, 128), 1)
    mine = (lane >= at) & (lane < at + R)
    groups = R // 8
    tiles, pivots = [], [None] * groups
    for g in range(groups):
        eye = jnp.where(lane == sub + (8 * g + R - at), 1.0, 0.0)
        tiles.append(jnp.where(mine, block[8 * g : 8 * g + 8, :], eye))

    def spread(tile, s):
        return jnp.broadcast_to(tile[s : s + 1, :], (8, 128))

    for first in range(0, R, NB):
        cols = {}
        for r in range(first, first + NB):
            for g in range(r // 8, groups):
                cols[r, g] = jnp.broadcast_to(tiles[g][:, at + r : at + r + 1], (8, 128))
        for i in range(first, first + NB):
            gi, s = i // 8, i % 8
            pivot = spread(cols[i, gi], s)
            inv = 1.0 / pivot
            pivots[gi] = pivot if s == 0 else jnp.where(sub >= s, pivot, pivots[gi])
            row = spread(tiles[gi], s)
            below = {g: cols[i, g] for g in range(gi, groups)}
            below[gi] = jnp.where(sub > s, below[gi], 0.0)
            for r in range(i + 1, first + NB):
                mult = spread(cols[i, r // 8], r % 8) * inv
                for g in range(r // 8, groups):
                    cols[r, g] = cols[r, g] - below[g] * mult
            scaled = row * inv
            for g in range(gi, groups):
                if g > gi or s < 7:
                    tiles[g] = tiles[g] - below[g] * scaled
    out = [jnp.where(mine, 0.0, tiles[g] * lax.rsqrt(pivots[g])) for g in range(groups)]
    return jnp.concatenate(out, axis=0)


def sweep(aug, count, y_ref, z_ref, m_ref, late=()):
    rows = aug.shape[0]
    cols = aug.shape[1] - WIDTH
    for j in range(count):
        r0 = R * j
        a0 = 128 * (r0 // 128)
        minv = chol_inverse(aug[r0 : r0 + R, a0 : a0 + 128], r0 - a0)
        m_ref[r0 : r0 + R, :] = minv
        if j == 0:
            for copy in late:
                copy.wait()
        block = aug[r0 : r0 + R, a0:]
        panel = mm(minv, jnp.concatenate([block, block], axis=0))
        z_ref[r0 : r0 + R, :] = panel[:, : cols - a0]
        y_ref[r0 : r0 + R, :] = panel[:, cols - a0 :]
        for i in range(j + 1, rows // R):
            c0 = R * i
            s0 = 128 * (c0 // 128)
            aug[c0 : c0 + R, s0:] -= mm_t(panel[:, c0 - a0 : c0 - a0 + R], panel[:, s0 - a0 :])


def leaf_kernel(d_any, b_any, t_any, y_ref, z_ref, m_ref, rest_ref, aug, sem):
    at = M + LEVELS * R
    copies = [
        pltpu.make_async_copy(d_any, aug.at[:, :M], sem.at[0]),
        pltpu.make_async_copy(b_any, aug.at[:, M:at], sem.at[1]),
        pltpu.make_async_copy(t_any, aug.at[:, at:], sem.at[2]),
    ]
    for copy in copies:
        copy.start()
    copies[0].wait()
    sweep(aug, 2, y_ref, z_ref, m_ref, copies[1:])
    rest_ref[...] = aug[M // 2 :, M // 2 :]


def leaf2_kernel(rest_ref, y_ref, z_ref, m_ref, aug):
    aug[...] = rest_ref[...]
    sweep(aug, 2, y_ref, z_ref, m_ref)


def back_kernel(ya_ref, za_ref, ma_ref, yb_ref, zb_ref, mb_ref, w_ref):
    for j in range(3, -1, -1):
        y_ref, z_ref, m_ref = (ya_ref, za_ref, ma_ref) if j < 2 else (yb_ref, zb_ref, mb_ref)
        q0 = R * (j % 2)
        rhs = y_ref[q0 : q0 + R, :]
        if j < 3:
            z = z_ref[q0 : q0 + R, q0 + R :]
            rhs = rhs - mm(z, w_ref[R * (j + 1) :, :])
        w_ref[R * j : R * j + R, :] = mm_t(m_ref[q0 : q0 + R, :], rhs)[R - q0 : 2 * R - q0, :]


def gram_pair(y, pair):
    st = 128 * pair
    return mm_t(y[:, st : st + 128], y[:, st:])


def last_of(first):
    return SPLIT if first <= SPLIT else LEVELS


def row_block(grams, level):
    h = R * ((level - 1) % 2)
    return grams[(level - 1) // 2][h : h + R, :]


def put(ref, first, level, value):
    o = offsets(first)[0][level]
    ref[:, o : o + width_of(level)] = value


def get(ref, first, level):
    o = offsets(first)[0][level]
    return ref[:, o : o + width_of(level)]


def gram_pairs(ya_ref, yb_ref, pairs):
    y = jnp.concatenate([ya_ref[...], yb_ref[...]], axis=0)
    return {pair: gram_pair(y, pair) for pair in pairs}


def gram_kernel(ya_ref, yb_ref, near_ref, far_ref):
    grams = gram_pairs(ya_ref, yb_ref, range(4))
    for level in range(1, SPLIT + 1):
        put(near_ref, 1, level, row_block(grams, level))
    for level in range(SPLIT + 1, LEVELS + 1):
        put(far_ref, SPLIT + 1, level, row_block(grams, level))


def reduce_level(k, coupling_ref, rows, p_ref, m_ref):
    o = R * ((k - 1) % 2)
    ids0 = lax.broadcasted_iota(jnp.int32, (R, 128), 0)
    ids1 = lax.broadcasted_iota(jnp.int32, (R, 128), 1)
    weights = 1.0 / coupling_ref[k - 1 : k, :]
    weights = jnp.concatenate([weights, weights], axis=1)
    cap = rows[:, :128] + jnp.where(ids0 + o == ids1, jnp.broadcast_to(weights, (R, 128)), 0.0)
    minv = chol_inverse(cap, o)
    m_ref[...] = minv
    p = mm(minv, jnp.concatenate([rows, rows], axis=0))
    p_ref[...] = p
    return p


def schur(k, p, first, last):
    sk = start_of(k)
    grams = {}
    for pair in range((first - 1) // 2, (last + 1) // 2):
        st = 128 * pair
        grams[pair] = mm_t(p[:, st - sk : st - sk + 128], p[:, st - sk :])
    return grams


def next_level(k, p, trailing, n_ref):
    last = last_of(k + 1) if k != SPLIT else SPLIT
    if k < last:
        grams = schur(k, p, k + 1, last)
        for level in range(k + 1, last + 1):
            put(n_ref, k + 1, level, trailing(level) - row_block(grams, level))


def first_level_kernel(c_ref, own_ref, ya_ref, yb_ref, dep_ref, p_ref, m_ref, n_ref):
    grams = gram_pairs(ya_ref, yb_ref, range(SPLIT // 2))

    def part(level):
        return get(own_ref, 1, level) + row_block(grams, level)

    p = reduce_level(1, c_ref, part(1), p_ref, m_ref)
    next_level(1, p, part, n_ref)


def level_kernel(k, c_ref, own_ref, got_ref, dep_ref, dep2_ref, p_ref, m_ref, n_ref=None):
    def part(level):
        return get(own_ref, k, level) + get(got_ref, k, level)

    p = reduce_level(k, c_ref, part(k), p_ref, m_ref)
    next_level(k, p, part, n_ref)


def first_far_kernel(own_ref, ya_ref, yb_ref, p_ref, n_ref):
    grams = gram_pairs(ya_ref, yb_ref, range(SPLIT // 2, LEVELS // 2))
    less = schur(1, p_ref[...], SPLIT + 1, LEVELS)
    for level in range(SPLIT + 1, LEVELS + 1):
        put(n_ref, SPLIT + 1, level, get(own_ref, SPLIT + 1, level) + row_block(grams, level) - row_block(less, level))


def far_kernel(k, own_ref, got_ref, p_ref, n_ref):
    less = schur(k, p_ref[...], SPLIT + 1, LEVELS)
    for level in range(SPLIT + 1, LEVELS + 1):
        both = get(own_ref, SPLIT + 1, level) + get(got_ref, SPLIT + 1, level)
        put(n_ref, SPLIT + 1, level, both - row_block(less, level))


def apply_level(k, w, p, minv):
    o = R * ((k - 1) % 2)
    cut = (start_of(k + 1) if k < LEVELS else LEVELS * R) - start_of(k)
    coef = mm_t(minv, p[:, cut:])[R - o : 2 * R - o, :]
    return w[:, cut:] - mm(w[:, o : o + R], coef)


def apply_kernel(k, w_ref, p_ref, m_ref, o_ref):
    o_ref[...] = apply_level(k, w_ref[...], p_ref[...], m_ref[...])


def apply_two_kernel(w_ref, p_ref, m_ref, p2_ref, m2_ref, o_ref):
    two = 2 * R
    coef = mm_t(m_ref[...], p_ref[...])[R:, :]
    coef2 = mm_t(m2_ref[...], p2_ref[:, two:])[:R, :]
    coef = jnp.concatenate([coef[:, two:] - mm(coef[:, R:two], coef2), coef2], axis=0)
    o_ref[...] = w_ref[:, two:] - mm(w_ref[:, :two], coef)


def last_kernel(k, c_ref, own_ref, got_ref, w_ref, o_ref, p_ref, m_ref):
    p = reduce_level(k, c_ref, own_ref[...] + got_ref[...], p_ref, m_ref)
    o_ref[...] = apply_level(k, w_ref[...], p, m_ref[...])


def call(kernel, outs, *args, hbm=(), scratch=(), sems=0, flops=10_000_000):
    vm = pl.BlockSpec(memory_space=pltpu.VMEM)
    hb = pl.BlockSpec(memory_space=pl.ANY)
    shapes = [jax.ShapeDtypeStruct(s, F32) for s in outs]
    extra = [pltpu.SemaphoreType.DMA((sems,))] if sems else []
    return pl.pallas_call(
        kernel,
        out_shape=shapes,
        in_specs=[hb if i in hbm else vm for i in range(len(args))],
        out_specs=[vm] * len(shapes),
        scratch_shapes=[pltpu.VMEM(s, F32) for s in scratch] + extra,
        compiler_params=pltpu.CompilerParams(vmem_limit_bytes=16 << 20),
        cost_estimate=pl.CostEstimate(flops=flops, bytes_accessed=1_000_000, transcendentals=0),
    )(*args)


def exchange(value, level):
    axis = "inner" if level <= 4 else "group"
    mask = {1: 1, 2: 2, 3: 4, 4: 8, 5: 1, 6: 2, 7: 4, 8: 14}[level]
    return lax.ppermute(value, axis, [(s, s ^ mask) for s in range(lax.axis_size(axis))])


def per_device(leaf_blocks, bases, targets, coupling):
    half = M // 2
    leaf_blocks, bases, targets = (
        pltpu.with_memory_space_constraint(a, pltpu.HBM) for a in (leaf_blocks, bases, targets)
    )
    ya, za, ma, rest = call(
        leaf_kernel, [(half, WIDTH), (half, M), (half, 128), (half, half + WIDTH)], leaf_blocks, bases, targets,
        hbm=(0, 1, 2), scratch=[(M, M + WIDTH)], sems=3,
    )
    got_a = exchange(ya, 1)
    yb, zb, mb = call(
        leaf2_kernel, [(half, WIDTH), (half, half), (half, 128)], rest,
        scratch=[(half, half + WIDTH)],
    )
    got_b = exchange(yb, 1)
    far_shape = (R, offsets(SPLIT + 1)[1])
    near, far = call(gram_kernel, [(R, offsets(1, SPLIT)[1]), far_shape], ya, yb)
    (w,) = call(back_kernel, [(M, WIDTH)], ya, za, ma, yb, zb, mb)
    got = far_got = None
    for k in range(1, LEVELS):
        outs = [(R, width_of(k)), (R, 128)]
        if k != SPLIT:
            outs.append((R, offsets(k + 1, last_of(k + 1))[1]))
        if k == 1:
            p, minv, near = call(first_level_kernel, outs, coupling, near, got_a, got_b, w, hbm=(4,))
        else:
            kernel = lambda *refs, k=k: level_kernel(k, *refs)
            p, minv, *more = call(kernel, outs, coupling, near, got, w, far, hbm=(3, 4))
            near = more[0] if more else None
        if k < SPLIT:
            got = exchange(near, k + 1)
        if k == 1:
            (far,) = call(first_far_kernel, [far_shape], far, got_a, got_b, p)
        elif k <= SPLIT:
            kernel = lambda *refs, k=k: far_kernel(k, *refs)
            (far,) = call(kernel, [far_shape], far, far_got, p)
        if k < SPLIT:
            far_got = exchange(far, k + 1)
        if k == SPLIT:
            near = far
        if k >= SPLIT:
            got = exchange(near, k + 1)
        if k == LEVELS - 1:
            kernel = lambda *refs, k=k: apply_kernel(k, *refs)
            (w,) = call(kernel, [(M, width_of(k + 1))], w, p, minv)
        elif k % 2 == 0:
            (w,) = call(apply_two_kernel, [(M, width_of(k + 1))], w, *before, p, minv)
        before = (p, minv)
    kernel = lambda *refs: last_kernel(LEVELS, *refs)
    return call(
        kernel, [(M, NRHS)], coupling, near, got, w,
        scratch=[(R, width_of(LEVELS)), (R, 128)],
    )[0]


def solution(mesh):
    in_specs = (
        P(("group", "inner"), None),
        P(("group", "inner"), None),
        P(("group", "inner"), None),
        P(),
    )
    out_specs = P(("group", "inner"), None)
    return jax.shard_map(per_device, mesh=mesh, in_specs=in_specs, out_specs=out_specs, check_vma=False)
```

time: 121 us -> 116 us (0.959)
  waiting for transfers between devices: 57 us -> 53.9 us
  local copies, waits for them, and re-layouts: 2.9 us -> 0.01 us
  starting transfers between devices: 21 us -> 22.8 us
    ppermute x8 -> x12, waiting for transfers between devices: 57 us -> 53.9 us  [exchange(): lax.ppermute(value, axis, [(s, s ^ mask) for s in range(lax.axis_size(axi...]
    unnamed x8 -> x2, local copies, waits for them, and re-layouts: 2.9 us -> 0.01 us
    ppermute x8 -> x12, starting transfers between devices: 21 us -> 22.8 us  [exchange(): lax.ppermute(value, axis, [(s, s ^ mask) for s in range(lax.axis_size(axi...]
    pallas_call x18 -> x20, Pallas kernels: 38.6 us -> 38.4 us  [call(): pl.pallas_call(kernel, out_shape=shapes, in_specs=[hb if i in hbm else vm...]
  transfers between devices with their start and end apart: 8 -> 12, of which waited for: 8 -> 10; matrix products, arithmetic and copies ran while one was open for 0% -> 0% of each run, Pallas kernels for 8% -> 13%
where the time goes in v4:
time: 116 us; the launch traced here: 115 us
  waiting for transfers between devices  53.9 us (46%)
  Pallas kernels  38.4 us (33%)
  starting transfers between devices  22.8 us (20%)
    ppermute x12, waiting for transfers between devices, exchange(): lax.ppermute(value, axis, [(s, s ^ mask) for s in range(lax.axis_size(axi...  53.9 us
    pallas_call x20, Pallas kernels, call(): pl.pallas_call(kernel, out_shape=shapes, in_specs=[hb if i in hbm else vm...  38.4 us
    ppermute x12, starting transfers between devices, exchange(): lax.ppermute(value, axis, [(s, s ^ mask) for s in range(lax.axis_size(axi...  22.8 us
  transfers between devices with their start and end apart: 12, of which 10 were waited for; matrix products, arithmetic and copies ran while one was open for 0% of the time, Pallas kernels for 13%

profile of v4, /device:TPU:2, one launch (start us, length us, event | category | flops | bytes accessed | tf_op | source)
XLA Modules:
  0.0 115.3 jit_solution(5810827747570608307)
XLA Ops:
  0.0 5.4 %shard_map.46 = (f32[128,640]{1,0:T(8,128)S(1)}, f32[128,256]{1,0:T(8,128)S(1)}, f32[128,128]{1,0:T(8,128)S(1)}, f32[128,768]{1,0:T(8,128)S(1)}) custom-call(f32[256,256]{1,0:T(8,128)} %d_any.1, f32[256,512]{1,0:T(8,128)} %b_any.1, f32[256,128]{1,0:T(8,128)} %t_any.1), custom_call_target="tpu_custom_call" | custom-call | flops 10000000 | bytes 1000000 | tf_op jit(solution)/shard_map/pallas_call | solution.py:262
  5.5 3.9 %shard_map.47 = (f32[128,640]{1,0:T(8,128)S(1)}, f32[128,128]{1,0:T(8,128)S(1)}, f32[128,128]{1,0:T(8,128)S(1)}) custom-call(f32[128,768]{1,0:T(8,128)S(1)} %get-tuple-element.35.rest_ref), custom_call_target="tpu_custom_call" | custom-call | flops 10000000 | bytes 1000000 | tf_op jit(solution)/shard_map/pallas_call | solution.py:262
  9.4 2.3 %collective-permute-start.1 = (f32[128,640]{1,0:T(8,128)S(1)}, f32[128,640]{1,0:T(8,128)S(1)}, u32[]{:S(2)}, u32[]{:S(2)}) collective-permute-start(f32[128,640]{1,0:T(8,128)S(1)} %get-tuple-element.36.yb_ref), channel_id=1, source_target_pairs={{0,1},{1,0},{2,3},{3,2},{4,5},{5,4},{6,7},{7,6},{8,9},{9,8},{10,11... | collective-permute-start | bytes 983048 | tf_op jit(solution)/shard_map/ppermute | solution.py:276
  11.7 0.3 collective-permute-start
  12.0 1.1 shard_map.48
  13.1 0.0 copy-start
  13.1 2.3 %shard_map.49.dep_ref.refs_3_.w_ref = f32[256,640]{1,0:T(8,128)S(1)} custom-call(f32[128,640]{1,0:T(8,128)S(1)} %get-tuple-element.34.ya_ref, f32[128,256]{1,0:T(8,128)S(1)} %get-tuple-element.39.za_ref, f32[128,128]{1,0:T(8,128)S(1)} %get-tuple-element.40.ma_ref, f32[128,640]{1,0:T(8,128)S(1)} %get-tuple-element.36.yb_ref, ...), custom_call_target="tpu_custom_call" | custom-call | flops 10000000 | bytes 1000000 | tf_op jit(solution)/shard_map/pallas_call | solution.py:262
  15.4 4.9 %collective-permute-done.1.yb_ref = f32[128,640]{1,0:T(8,128)S(1)} collective-permute-done((f32[128,640]{1,0:T(8,128)S(1)}, f32[128,640]{1,0:T(8,128)S(1)}, u32[]{:S(2)}, u32[]{:S(2)}) %collective-permute-start.1) | collective-permute-done | bytes 327712 | tf_op jit(solution)/shard_map/ppermute | solution.py:276
  20.3 5.7 %collective-permute-done.ya_ref = f32[128,640]{1,0:T(8,128)S(1)} collective-permute-done((f32[128,640]{1,0:T(8,128)S(1)}, f32[128,640]{1,0:T(8,128)S(1)}, u32[]{:S(2)}, u32[]{:S(2)}) %collective-permute-start) | collective-permute-done | bytes 327712 | tf_op jit(solution)/shard_map/ppermute | solution.py:276
  26.0 0.0 copy-done
  26.0 3.0 %shard_map.50 = (f32[64,640]{1,0:T(8,128)S(1)}, f32[64,128]{1,0:T(8,128)S(1)}, f32[64,1664]{1,0:T(8,128)S(1)}) custom-call(f32[8,64]{1,0:T(8,128)S(1)} %copy-done, f32[64,2304]{1,0:T(8,128)S(1)} %get-tuple-element.38.own_ref, f32[128,640]{1,0:T(8,128)S(1)} %collective-permute-done.ya_ref, f32[128,640]{1,0:T(8,128)S(1)} %collective-permute-done.1.yb_ref, ...), custom_call_target="tpu_custom_call" | custom-call | flops 10000000 | bytes 1000000 | tf_op jit(solution)/shard_map/pallas_call | solution.py:262
  29.0 2.2 %collective-permute-start.3 = (f32[64,1664]{1,0:T(8,128)S(1)}, f32[64,1664]{1,0:T(8,128)S(1)}, u32[]{:S(2)}, u32[]{:S(2)}) collective-permute-start(f32[64,1664]{1,0:T(8,128)S(1)} %get-tuple-element.44.refs_1_), channel_id=1, source_target_pairs={{0,2},{1,3},{2,0},{3,1},{4,6},{5,7},{6,4},{7,5},{8,10},{9,11},{10,... | collective-permute-start | bytes 1277960 | tf_op jit(solution)/shard_map/ppermute | solution.py:276
  31.2 0.8 shard_map.51.refs_4_.refs_0_
  32.0 1.5 %collective-permute-start.2 = (f32[64,1280]{1,0:T(8,128)S(1)}, f32[64,1280]{1,0:T(8,128)S(1)}, u32[]{:S(2)}, u32[]{:S(2)}) collective-permute-start(f32[64,1280]{1,0:T(8,128)S(1)} %shard_map.51.refs_4_.refs_0_), channel_id=1, source_target_pairs={{0,2},{1,3},{2,0},{3,1},{4,6},{5,7},{6,4},{7,5},{8,10},{9,11},{10,... | collective-permute-start | bytes 983048 | tf_op jit(solution)/shard_map/ppermute | solution.py:276
  33.5 9.8 %collective-permute-done.3.refs_2_ = f32[64,1664]{1,0:T(8,128)S(1)} collective-permute-done((f32[64,1664]{1,0:T(8,128)S(1)}, f32[64,1664]{1,0:T(8,128)S(1)}, u32[]{:S(2)}, u32[]{:S(2)}) %collective-permute-start.3) | collective-permute-done | bytes 426016 | tf_op jit(solution)/shard_map/ppermute | solution.py:276
  43.2 2.3 %shard_map.52 = (f32[64,640]{1,0:T(8,128)S(1)}, f32[64,128]{1,0:T(8,128)S(1)}, f32[64,1024]{1,0:T(8,128)S(1)}) custom-call(f32[8,64]{1,0:T(8,128)S(1)} %copy-done, f32[64,1664]{1,0:T(8,128)S(1)} %get-tuple-element.44.refs_1_, f32[64,1664]{1,0:T(8,128)S(1)} %collective-permute-done.3.refs_2_, f32[256,640]{1,0:T(8,128)S(1)} %shard_map.49.dep_ref.refs_3_.w_ref, ...), custom_call_target="tpu_custom_call" | custom-call | flops 10000000 | bytes 1000000 | tf_op jit(solution)/shard_map/pallas_call | solution.py:262
  45.5 2.5 %collective-permute-done.2.refs_1_ = f32[64,1280]{1,0:T(8,128)S(1)} collective-permute-done((f32[64,1280]{1,0:T(8,128)S(1)}, f32[64,1280]{1,0:T(8,128)S(1)}, u32[]{:S(2)}, u32[]{:S(2)}) %collective-permute-start.2) | collective-permute-done | bytes 327712 | tf_op jit(solution)/shard_map/ppermute | solution.py:276
  48.1 0.5 shard_map.53.refs_4_.refs_0_
  48.5 1.9 %collective-permute-start.4 = (f32[64,1280]{1,0:T(8,128)S(1)}, f32[64,1280]{1,0:T(8,128)S(1)}, u32[]{:S(2)}, u32[]{:S(2)}) collective-permute-start(f32[64,1280]{1,0:T(8,128)S(1)} %shard_map.53.refs_4_.refs_0_), channel_id=1, source_target_pairs={{0,4},{1,5},{2,6},{3,7},{4,0},{5,1},{6,2},{7,3},{8,12},{9,13},{10,... | collective-permute-start | bytes 983048 | tf_op jit(solution)/shard_map/ppermute | solution.py:276
  50.4 0.3 collective-permute-start.5
  50.7 1.4 %shard_map.54.refs_3_.w_ref = f32[256,512]{1,0:T(8,128)S(1)} custom-call(f32[256,640]{1,0:T(8,128)S(1)} %shard_map.49.dep_ref.refs_3_.w_ref, f32[64,640]{1,0:T(8,128)S(1)} %get-tuple-element.43.p_ref, f32[64,128]{1,0:T(8,128)S(1)} %get-tuple-element.47.m_ref, f32[64,640]{1,0:T(8,128)S(1)} %get-tuple-element.45.refs_2_.p2_ref, ...), custom_call_target="tpu_custom_call" | custom-call | flops 10000000 | bytes 1000000 | tf_op jit(solution)/shard_map/pallas_call | solution.py:262
  52.2 9.9 %collective-permute-done.5.refs_2_ = f32[64,1024]{1,0:T(8,128)S(1)} collective-permute-done((f32[64,1024]{1,0:T(8,128)S(1)}, f32[64,1024]{1,0:T(8,128)S(1)}, u32[]{:S(2)}, u32[]{:S(2)}) %collective-permute-start.5) | collective-permute-done | bytes 262176 | tf_op jit(solution)/shard_map/ppermute | solution.py:276
  62.0 2.2 %shard_map.55 = (f32[64,512]{1,0:T(8,128)S(1)}, f32[64,128]{1,0:T(8,128)S(1)}, f32[64,512]{1,0:T(8,128)S(1)}) custom-call(f32[8,64]{1,0:T(8,128)S(1)} %copy-done, f32[64,1024]{1,0:T(8,128)S(1)} %get-tuple-element.46.refs_1_, f32[64,1024]{1,0:T(8,128)S(1)} %collective-permute-done.5.refs_2_, f32[256,512]{1,0:T(8,128)S(1)} %shard_map.54.refs_3_.w_ref, ...), custom_call_target="tpu_custom_call" | custom-call | flops 10000000 | bytes 1000000 | tf_op jit(solution)/shard_map/pallas_call | solution.py:262
  64.3 0.0 collective-permute-done.4.refs_1_
  64.3 0.5 shard_map.56.refs_4_.refs_0_
  64.8 3.4 %collective-permute-start.6 = (f32[64,1280]{1,0:T(8,128)S(1)}, f32[64,1280]{1,0:T(8,128)S(1)}, u32[]{:S(2)}, u32[]{:S(2)}) collective-permute-start(f32[64,1280]{1,0:T(8,128)S(1)} %shard_map.56.refs_4_.refs_0_), channel_id=1, source_target_pairs={{0,8},{1,9},{2,10},{3,11},{4,12},{5,13},{6,14},{7,15},{8,0},{9,1},... | collective-permute-start | bytes 983048 | tf_op jit(solution)/shard_map/ppermute | solution.py:276
  68.2 0.2 collective-permute-start.7
  68.4 7.7 %collective-permute-done.7.refs_2_ = f32[64,512]{1,0:T(8,128)S(1)} collective-permute-done((f32[64,512]{1,0:T(8,128)S(1)}, f32[64,512]{1,0:T(8,128)S(1)}, u32[]{:S(2)}, u32[]{:S(2)}) %collective-permute-start.7) | collective-permute-done | bytes 131104 | tf_op jit(solution)/shard_map/ppermute | solution.py:276
  76.1 1.9 %shard_map.57 = (f32[64,512]{1,0:T(8,128)S(1)}, f32[64,128]{1,0:T(8,128)S(1)}) custom-call(f32[8,64]{1,0:T(8,128)S(1)} %copy-done, f32[64,512]{1,0:T(8,128)S(1)} %get-tuple-element.50.refs_1_, f32[64,512]{1,0:T(8,128)S(1)} %collective-permute-done.7.refs_2_, f32[256,512]{1,0:T(8,128)S(1)} %shard_map.54.refs_3_.w_ref, f32[64,1280]{1,0:T(8,128)S(1)} %shard_map.56.refs_4_.refs_0_), custom_call_target="tpu_custom_call" | custom-call | flops 10000000 | bytes 1000000 | tf_op jit(solution)/shard_map/pallas_call | solution.py:262
  78.0 0.0 collective-permute-done.6.refs_1_
  78.0 0.5 shard_map.58.refs_1_.refs_4_
  78.5 0.1 collective-permute-start.8
  78.6 1.3 %shard_map.59.refs_3_.w_ref = f32[256,384]{1,0:T(8,128)S(1)} custom-call(f32[256,512]{1,0:T(8,128)S(1)} %shard_map.54.refs_3_.w_ref, f32[64,512]{1,0:T(8,128)S(1)} %get-tuple-element.49.refs_2_.p_ref, f32[64,128]{1,0:T(8,128)S(1)} %get-tuple-element.52.m_ref, f32[64,512]{1,0:T(8,128)S(1)} %get-tuple-element.51.refs_2_.p2_ref, ...), custom_call_target="tpu_custom_call" | custom-call | flops 10000000 | bytes 1000000 | tf_op jit(solution)/shard_map/pallas_call | solution.py:262
  79.9 0.3 collective-permute-done.8.refs_2_
  80.2 2.3 %shard_map.60 = (f32[64,384]{1,0:T(8,128)S(1)}, f32[64,128]{1,0:T(8,128)S(1)}, f32[64,896]{1,0:T(8,128)S(1)}) custom-call(f32[8,64]{1,0:T(8,128)S(1)} %copy-done, f32[64,1280]{1,0:T(8,128)S(1)} %shard_map.58.refs_1_.refs_4_, f32[64,1280]{1,0:T(8,128)S(1)} %collective-permute-done.8.refs_2_, f32[256,384]{1,0:T(8,128)S(1)} %shard_map.59.refs_3_.w_ref, ...), custom_call_target="tpu_custom_call" | custom-call | flops 10000000 | bytes 1000000 | tf_op jit(solution)/shard_map/pallas_call | solution.py:262
  82.5 2.1 %collective-permute-start.9 = (f32[64,896]{1,0:T(8,128)S(1)}, f32[64,896]{1,0:T(8,128)S(1)}, u32[]{:S(2)}, u32[]{:S(2)}) collective-permute-start(f32[64,896]{1,0:T(8,128)S(1)} %get-tuple-element.54.refs_1_), channel_id=1, source_target_pairs={{0,32},{16,48},{32,0},{48,16},{64,96},{80,112},{96,64},{112,80},{1... | collective-permute-start | bytes 688136 | tf_op jit(solution)/shard_map/ppermute | solution.py:276
  84.5 6.0 %collective-permute-done.9.refs_2_ = f32[64,896]{1,0:T(8,128)S(1)} collective-permute-done((f32[64,896]{1,0:T(8,128)S(1)}, f32[64,896]{1,0:T(8,128)S(1)}, u32[]{:S(2)}, u32[]{:S(2)}) %collective-permute-start.9) | collective-permute-done | bytes 229408 | tf_op jit(solution)/shard_map/ppermute | solution.py:276
  90.5 2.2 %shard_map.61 = (f32[64,384]{1,0:T(8,128)S(1)}, f32[64,128]{1,0:T(8,128)S(1)}, f32[64,512]{1,0:T(8,128)S(1)}) custom-call(f32[8,64]{1,0:T(8,128)S(1)} %copy-done, f32[64,896]{1,0:T(8,128)S(1)} %get-tuple-element.54.refs_1_, f32[64,896]{1,0:T(8,128)S(1)} %collective-permute-done.9.refs_2_, f32[256,384]{1,0:T(8,128)S(1)} %shard_map.59.refs_3_.w_ref, ...), custom_call_target="tpu_custom_call" | custom-call | flops 10000000 | bytes 1000000 | tf_op jit(solution)/shard_map/pallas_call | solution.py:262
  92.7 3.7 %collective-permute-start.10 = (f32[64,512]{1,0:T(8,128)S(1)}, f32[64,512]{1,0:T(8,128)S(1)}, u32[]{:S(2)}, u32[]{:S(2)}) collective-permute-start(f32[64,512]{1,0:T(8,128)S(1)} %get-tuple-element.55.refs_1_), channel_id=1, source_target_pairs={{0,64},{16,80},{32,96},{48,112},{64,0},{80,16},{96,32},{112,48},{1... | collective-permute-start | bytes 393224 | tf_op jit(solution)/shard_map/ppermute | solution.py:276
  96.4 1.1 shard_map.62.refs_3_.refs_0_
  97.4 5.0 %collective-permute-done.10.refs_2_ = f32[64,512]{1,0:T(8,128)S(1)} collective-permute-done((f32[64,512]{1,0:T(8,128)S(1)}, f32[64,512]{1,0:T(8,128)S(1)}, u32[]{:S(2)}, u32[]{:S(2)}) %collective-permute-start.10) | collective-permute-done | bytes 131104 | tf_op jit(solution)/shard_map/ppermute | solution.py:276
  102.4 2.1 %shard_map.63 = (f32[64,256]{1,0:T(8,128)S(1)}, f32[64,128]{1,0:T(8,128)S(1)}, f32[64,256]{1,0:T(8,128)S(1)}) custom-call(f32[8,64]{1,0:T(8,128)S(1)} %copy-done, f32[64,512]{1,0:T(8,128)S(1)} %get-tuple-element.55.refs_1_, f32[64,512]{1,0:T(8,128)S(1)} %collective-permute-done.10.refs_2_, f32[256,256]{1,0:T(8,128)S(1)} %shard_map.62.refs_3_.refs_0_, ...), custom_call_target="tpu_custom_call" | custom-call | flops 10000000 | bytes 1000000 | tf_op jit(solution)/shard_map/pallas_call | solution.py:262
  104.6 4.9 %collective-permute-start.11 = (f32[64,256]{1,0:T(8,128)S(1)}, f32[64,256]{1,0:T(8,128)S(1)}, u32[]{:S(2)}, u32[]{:S(2)}) collective-permute-start(f32[64,256]{1,0:T(8,128)S(1)} %get-tuple-element.60.refs_1_), channel_id=1, source_target_pairs={{0,224},{16,240},{32,192},{48,208},{64,160},{80,176},{96,128},{112... | collective-permute-start | bytes 196616 | tf_op jit(solution)/shard_map/ppermute | solution.py:276
  109.4 0.8 shard_map.64.refs_3_
  110.2 2.1 %collective-permute-done.11.refs_2_ = f32[64,256]{1,0:T(8,128)S(1)} collective-permute-done((f32[64,256]{1,0:T(8,128)S(1)}, f32[64,256]{1,0:T(8,128)S(1)}, u32[]{:S(2)}, u32[]{:S(2)}) %collective-permute-start.11) | collective-permute-done | bytes 65568 | tf_op jit(solution)/shard_map/ppermute | solution.py:276
  112.3 3.0 %shard_map.65 = f32[256,128]{1,0:T(8,128)} custom-call(f32[8,64]{1,0:T(8,128)S(1)} %copy-done, f32[64,256]{1,0:T(8,128)S(1)} %get-tuple-element.60.refs_1_, f32[64,256]{1,0:T(8,128)S(1)} %collective-permute-done.11.refs_2_, f32[256,256]{1,0:T(8,128)S(1)} %shard_map.64.refs_3_), custom_call_target="tpu_custom_call" | custom-call | flops 10000000 | bytes 1000000 | tf_op jit(solution)/shard_map/pallas_call | solution.py:262
Async XLA Ops:
  9.4 10.9 %collective-permute-start.1 = (f32[128,640]{1,0:T(8,128)S(1)}, f32[128,640]{1,0:T(8,128)S(1)}, u32[]{:S(2)}, u32[]{:S(2)}) collective-permute-start(f32[128,640]{1,0:T(8,128)S(1)} %get-tuple-element.36.yb_ref), channel_id=1, source_target_pairs={{0,1},{1,0},{2,3},{3,2},{4,5},{5,4},{6,7},{7,6},{8,9},{9,8},{10,11... | collective-permute-start | bytes 983048 | tf_op jit(solution)/shard_map/ppermute | solution.py:276
  11.7 14.2 %collective-permute-start = (f32[128,640]{1,0:T(8,128)S(1)}, f32[128,640]{1,0:T(8,128)S(1)}, u32[]{:S(2)}, u32[]{:S(2)}) collective-permute-start(f32[128,640]{1,0:T(8,128)S(1)} %get-tuple-element.34.ya_ref), channel_id=1, source_target_pairs={{0,1},{1,0},{2,3},{3,2},{4,5},{5,4},{6,7},{7,6},{8,9},{9,8},{10,11... | collective-permute-start | bytes 983048 | tf_op jit(solution)/shard_map/ppermute | solution.py:276
  13.1 12.9 %copy-start = (f32[8,64]{1,0:T(8,128)S(1)}, f32[8,64]{1,0:T(8,128)}, u32[]{:S(2)}) copy-start(f32[8,64]{1,0:T(8,128)} %refs_0_.13) | copy-start | bytes 6148
  29.0 14.3 %collective-permute-start.3 = (f32[64,1664]{1,0:T(8,128)S(1)}, f32[64,1664]{1,0:T(8,128)S(1)}, u32[]{:S(2)}, u32[]{:S(2)}) collective-permute-start(f32[64,1664]{1,0:T(8,128)S(1)} %get-tuple-element.44.refs_1_), channel_id=1, source_target_pairs={{0,2},{1,3},{2,0},{3,1},{4,6},{5,7},{6,4},{7,5},{8,10},{9,11},{10,... | collective-permute-start | bytes 1277960 | tf_op jit(solution)/shard_map/ppermute | solution.py:276
  32.0 16.1 %collective-permute-start.2 = (f32[64,1280]{1,0:T(8,128)S(1)}, f32[64,1280]{1,0:T(8,128)S(1)}, u32[]{:S(2)}, u32[]{:S(2)}) collective-permute-start(f32[64,1280]{1,0:T(8,128)S(1)} %shard_map.51.refs_4_.refs_0_), channel_id=1, source_target_pairs={{0,2},{1,3},{2,0},{3,1},{4,6},{5,7},{6,4},{7,5},{8,10},{9,11},{10,... | collective-permute-start | bytes 983048 | tf_op jit(solution)/shard_map/ppermute | solution.py:276
  48.5 15.7 %collective-permute-start.4 = (f32[64,1280]{1,0:T(8,128)S(1)}, f32[64,1280]{1,0:T(8,128)S(1)}, u32[]{:S(2)}, u32[]{:S(2)}) collective-permute-start(f32[64,1280]{1,0:T(8,128)S(1)} %shard_map.53.refs_4_.refs_0_), channel_id=1, source_target_pairs={{0,4},{1,5},{2,6},{3,7},{4,0},{5,1},{6,2},{7,3},{8,12},{9,13},{10,... | collective-permute-start | bytes 983048 | tf_op jit(solution)/shard_map/ppermute | solution.py:276
  50.4 11.6 %collective-permute-start.5 = (f32[64,1024]{1,0:T(8,128)S(1)}, f32[64,1024]{1,0:T(8,128)S(1)}, u32[]{:S(2)}, u32[]{:S(2)}) collective-permute-start(f32[64,1024]{1,0:T(8,128)S(1)} %get-tuple-element.46.refs_1_), channel_id=1, source_target_pairs={{0,4},{1,5},{2,6},{3,7},{4,0},{5,1},{6,2},{7,3},{8,12},{9,13},{10,... | collective-permute-start | bytes 786440 | tf_op jit(solution)/shard_map/ppermute | solution.py:276
  64.8 13.3 %collective-permute-start.6 = (f32[64,1280]{1,0:T(8,128)S(1)}, f32[64,1280]{1,0:T(8,128)S(1)}, u32[]{:S(2)}, u32[]{:S(2)}) collective-permute-start(f32[64,1280]{1,0:T(8,128)S(1)} %shard_map.56.refs_4_.refs_0_), channel_id=1, source_target_pairs={{0,8},{1,9},{2,10},{3,11},{4,12},{5,13},{6,14},{7,15},{8,0},{9,1},... | collective-permute-start | bytes 983048 | tf_op jit(solution)/shard_map/ppermute | solution.py:276
  68.2 7.9 %collective-permute-start.7 = (f32[64,512]{1,0:T(8,128)S(1)}, f32[64,512]{1,0:T(8,128)S(1)}, u32[]{:S(2)}, u32[]{:S(2)}) collective-permute-start(f32[64,512]{1,0:T(8,128)S(1)} %get-tuple-element.50.refs_1_), channel_id=1, source_target_pairs={{0,8},{1,9},{2,10},{3,11},{4,12},{5,13},{6,14},{7,15},{8,0},{9,1},... | collective-permute-start | bytes 393224 | tf_op jit(solution)/shard_map/ppermute | solution.py:276
  78.5 1.7 %collective-permute-start.8 = (f32[64,1280]{1,0:T(8,128)S(1)}, f32[64,1280]{1,0:T(8,128)S(1)}, u32[]{:S(2)}, u32[]{:S(2)}) collective-permute-start(f32[64,1280]{1,0:T(8,128)S(1)} %shard_map.58.refs_1_.refs_4_), channel_id=1, source_target_pairs={{0,16},{16,0},{32,48},{48,32},{64,80},{80,64},{96,112},{112,96},{1... | collective-permute-start | bytes 983048 | tf_op jit(solution)/shard_map/ppermute | solution.py:276
  82.5 8.0 %collective-permute-start.9 = (f32[64,896]{1,0:T(8,128)S(1)}, f32[64,896]{1,0:T(8,128)S(1)}, u32[]{:S(2)}, u32[]{:S(2)}) collective-permute-start(f32[64,896]{1,0:T(8,128)S(1)} %get-tuple-element.54.refs_1_), channel_id=1, source_target_pairs={{0,32},{16,48},{32,0},{48,16},{64,96},{80,112},{96,64},{112,80},{1... | collective-permute-start | bytes 688136 | tf_op jit(solution)/shard_map/ppermute | solution.py:276
  92.7 9.7 %collective-permute-start.10 = (f32[64,512]{1,0:T(8,128)S(1)}, f32[64,512]{1,0:T(8,128)S(1)}, u32[]{:S(2)}, u32[]{:S(2)}) collective-permute-start(f32[64,512]{1,0:T(8,128)S(1)} %get-tuple-element.55.refs_1_), channel_id=1, source_target_pairs={{0,64},{16,80},{32,96},{48,112},{64,0},{80,16},{96,32},{112,48},{1... | collective-permute-start | bytes 393224 | tf_op jit(solution)/shard_map/ppermute | solution.py:276
  104.6 7.8 %collective-permute-start.11 = (f32[64,256]{1,0:T(8,128)S(1)}, f32[64,256]{1,0:T(8,128)S(1)}, u32[]{:S(2)}, u32[]{:S(2)}) collective-permute-start(f32[64,256]{1,0:T(8,128)S(1)} %get-tuple-element.60.refs_1_), channel_id=1, source_target_pairs={{0,224},{16,240},{32,192},{48,208},{64,160},{80,176},{96,128},{112... | collective-permute-start | bytes 196616 | tf_op jit(solution)/shard_map/ppermute | solution.py:276

commit v5 on v4

--- a/solution.py
+++ b/solution.py
@@ -54,27 +54,38 @@
     def spread(tile, s):
         return jnp.broadcast_to(tile[s : s + 1, :], (8, 128))
 
-    for first in range(0, R, NB):
+    first = 0
+    while first < R:
+        last = first + NB
         cols = {}
-        for r in range(first, first + NB):
+        for r in range(first, last):
             for g in range(r // 8, groups):
                 cols[r, g] = jnp.broadcast_to(tiles[g][:, at + r : at + r + 1], (8, 128))
-        for i in range(first, first + NB):
+        for i in range(first, last, 2):
             gi, s = i // 8, i % 8
-            pivot = spread(cols[i, gi], s)
-            inv = 1.0 / pivot
-            pivots[gi] = pivot if s == 0 else jnp.where(sub >= s, pivot, pivots[gi])
+            a, b = spread(cols[i, gi], s), spread(cols[i, gi], s + 1)
+            c = spread(cols[i + 1, gi], s + 1)
+            inv_a = 1.0 / a
+            inv_c = a * (1.0 / (a * c - b * b))
+            ratio = b * inv_a
+            low = {g: cols[i, g] for g in range(gi, groups)}
+            low2 = {g: cols[i + 1, g] - low[g] * ratio for g in range(gi, groups)}
+            for r in range(i + 2, last):
+                h = r // 8
+                mult = spread(low[h], r % 8) * inv_a
+                mult2 = spread(low2[h], r % 8) * inv_c
+                for g in range(h, groups):
+                    cols[r, g] = (cols[r, g] - low[g] * mult) - low2[g] * mult2
+            pair = jnp.where(sub == s, a, c - b * ratio)
+            pivots[gi] = pair if s == 0 else jnp.where(sub >= s, pair, pivots[gi])
             row = spread(tiles[gi], s)
-            below = {g: cols[i, g] for g in range(gi, groups)}
-            below[gi] = jnp.where(sub > s, below[gi], 0.0)
-            for r in range(i + 1, first + NB):
-                mult = spread(cols[i, r // 8], r % 8) * inv
-                for g in range(r // 8, groups):
-                    cols[r, g] = cols[r, g] - below[g] * mult
-            scaled = row * inv
+            row2 = (spread(tiles[gi], s + 1) - row * ratio) * inv_c
+            row = row * inv_a
+            low[gi] = jnp.where(sub > s, low[gi], 0.0)
+            low2[gi] = jnp.where(sub > s + 1, low2[gi], 0.0)
             for g in range(gi, groups):
-                if g > gi or s < 7:
-                    tiles[g] = tiles[g] - below[g] * scaled
+                tiles[g] = (tiles[g] - low[g] * row) - low2[g] * row2
+        first = last
     out = [jnp.where(mine, 0.0, tiles[g] * lax.rsqrt(pivots[g])) for g in range(groups)]
     return jnp.concatenate(out, axis=0)
 
@@ -272,7 +283,7 @@
 
 def exchange(value, level):
     axis = "inner" if level <= 4 else "group"
-    mask = {1: 1, 2: 2, 3: 4, 4: 8, 5: 1, 6: 2, 7: 4, 8: 14}[level]
+    mask = {1: 1, 2: 3, 3: 4, 4: 12, 5: 1, 6: 2, 7: 4, 8: 14}[level]
     return lax.ppermute(value, axis, [(s, s ^ mask) for s in range(lax.axis_size(axis))])
 
 

time: 116 us -> 113 us (0.974); the launches traced: 115 us -> 111 us
  Pallas kernels: 38.4 us -> 35.4 us
  starting transfers between devices: 22.8 us -> 21 us
    pallas_call x20, Pallas kernels: 38.4 us -> 35.4 us  [call(): pl.pallas_call(kernel, out_shape=shapes, in_specs=[hb if i in hbm else vm...]
    ppermute x12, starting transfers between devices: 22.8 us -> 21 us  [exchange(): lax.ppermute(value, axis, [(s, s ^ mask) for s in range(lax.axis_size(axi...]
where the time goes in v5:
time: 113 us; the launch traced here: 111 us
  waiting for transfers between devices  54.2 us (48%)
  Pallas kernels  35.4 us (31%)
  starting transfers between devices  21 us (19%)
    ppermute x12, waiting for transfers between devices, exchange(): lax.ppermute(value, axis, [(s, s ^ mask) for s in range(lax.axis_size(axi...  54.2 us
    pallas_call x20, Pallas kernels, call(): pl.pallas_call(kernel, out_shape=shapes, in_specs=[hb if i in hbm else vm...  35.4 us
    ppermute x12, starting transfers between devices, exchange(): lax.ppermute(value, axis, [(s, s ^ mask) for s in range(lax.axis_size(axi...  21 us
  transfers between devices with their start and end apart: 12, of which 10 were waited for; matrix products, arithmetic and copies ran while one was open for 0% of the time, Pallas kernels for 13%

profile of v5, /device:TPU:2, one launch (start us, length us, event | category | flops | bytes accessed | tf_op | source)
XLA Modules:
  0.0 110.8 jit_solution(11053785485739108002)
XLA Ops:
  0.0 5.0 %shard_map.46 = (f32[128,640]{1,0:T(8,128)S(1)}, f32[128,256]{1,0:T(8,128)S(1)}, f32[128,128]{1,0:T(8,128)S(1)}, f32[128,768]{1,0:T(8,128)S(1)}) custom-call(f32[256,256]{1,0:T(8,128)} %d_any.1, f32[256,512]{1,0:T(8,128)} %b_any.1, f32[256,128]{1,0:T(8,128)} %t_any.1), custom_call_target="tpu_custom_call" | custom-call | flops 10000000 | bytes 1000000 | tf_op jit(solution)/shard_map/pallas_call | solution.py:273
  5.0 3.4 %shard_map.47 = (f32[128,640]{1,0:T(8,128)S(1)}, f32[128,128]{1,0:T(8,128)S(1)}, f32[128,128]{1,0:T(8,128)S(1)}) custom-call(f32[128,768]{1,0:T(8,128)S(1)} %get-tuple-element.35.rest_ref), custom_call_target="tpu_custom_call" | custom-call | flops 10000000 | bytes 1000000 | tf_op jit(solution)/shard_map/pallas_call | solution.py:273
  8.4 2.3 %collective-permute-start.1 = (f32[128,640]{1,0:T(8,128)S(1)}, f32[128,640]{1,0:T(8,128)S(1)}, u32[]{:S(2)}, u32[]{:S(2)}) collective-permute-start(f32[128,640]{1,0:T(8,128)S(1)} %get-tuple-element.36.yb_ref), channel_id=1, source_target_pairs={{0,1},{1,0},{2,3},{3,2},{4,5},{5,4},{6,7},{7,6},{8,9},{9,8},{10,11... | collective-permute-start | bytes 983048 | tf_op jit(solution)/shard_map/ppermute | solution.py:287
  10.7 0.3 collective-permute-start
  11.0 1.1 shard_map.48
  12.1 0.0 copy-start
  12.1 2.3 %shard_map.49.dep_ref.refs_3_.w_ref = f32[256,640]{1,0:T(8,128)S(1)} custom-call(f32[128,640]{1,0:T(8,128)S(1)} %get-tuple-element.34.ya_ref, f32[128,256]{1,0:T(8,128)S(1)} %get-tuple-element.39.za_ref, f32[128,128]{1,0:T(8,128)S(1)} %get-tuple-element.40.ma_ref, f32[128,640]{1,0:T(8,128)S(1)} %get-tuple-element.36.yb_ref, ...), custom_call_target="tpu_custom_call" | custom-call | flops 10000000 | bytes 1000000 | tf_op jit(solution)/shard_map/pallas_call | solution.py:273
  14.4 4.9 %collective-permute-done.1.yb_ref = f32[128,640]{1,0:T(8,128)S(1)} collective-permute-done((f32[128,640]{1,0:T(8,128)S(1)}, f32[128,640]{1,0:T(8,128)S(1)}, u32[]{:S(2)}, u32[]{:S(2)}) %collective-permute-start.1) | collective-permute-done | bytes 327712 | tf_op jit(solution)/shard_map/ppermute | solution.py:287
  19.3 5.7 %collective-permute-done.ya_ref = f32[128,640]{1,0:T(8,128)S(1)} collective-permute-done((f32[128,640]{1,0:T(8,128)S(1)}, f32[128,640]{1,0:T(8,128)S(1)}, u32[]{:S(2)}, u32[]{:S(2)}) %collective-permute-start) | collective-permute-done | bytes 327712 | tf_op jit(solution)/shard_map/ppermute | solution.py:287
  25.0 0.0 copy-done
  25.0 2.8 %shard_map.50 = (f32[64,640]{1,0:T(8,128)S(1)}, f32[64,128]{1,0:T(8,128)S(1)}, f32[64,1664]{1,0:T(8,128)S(1)}) custom-call(f32[8,64]{1,0:T(8,128)S(1)} %copy-done, f32[64,2304]{1,0:T(8,128)S(1)} %get-tuple-element.38.own_ref, f32[128,640]{1,0:T(8,128)S(1)} %collective-permute-done.ya_ref, f32[128,640]{1,0:T(8,128)S(1)} %collective-permute-done.1.yb_ref, ...), custom_call_target="tpu_custom_call" | custom-call | flops 10000000 | bytes 1000000 | tf_op jit(solution)/shard_map/pallas_call | solution.py:273
  27.8 1.6 %collective-permute-start.3 = (f32[64,1664]{1,0:T(8,128)S(1)}, f32[64,1664]{1,0:T(8,128)S(1)}, u32[]{:S(2)}, u32[]{:S(2)}) collective-permute-start(f32[64,1664]{1,0:T(8,128)S(1)} %get-tuple-element.44.refs_1_), channel_id=1, source_target_pairs={{0,3},{1,2},{2,1},{3,0},{4,7},{5,6},{6,5},{7,4},{8,11},{9,10},{10,... | collective-permute-start | bytes 1277960 | tf_op jit(solution)/shard_map/ppermute | solution.py:287
  29.3 0.8 shard_map.51.refs_4_.refs_0_
  30.1 0.6 collective-permute-start.2
  30.8 9.8 %collective-permute-done.3.refs_2_ = f32[64,1664]{1,0:T(8,128)S(1)} collective-permute-done((f32[64,1664]{1,0:T(8,128)S(1)}, f32[64,1664]{1,0:T(8,128)S(1)}, u32[]{:S(2)}, u32[]{:S(2)}) %collective-permute-start.3) | collective-permute-done | bytes 426016 | tf_op jit(solution)/shard_map/ppermute | solution.py:287
  40.5 2.0 %shard_map.52 = (f32[64,640]{1,0:T(8,128)S(1)}, f32[64,128]{1,0:T(8,128)S(1)}, f32[64,1024]{1,0:T(8,128)S(1)}) custom-call(f32[8,64]{1,0:T(8,128)S(1)} %copy-done, f32[64,1664]{1,0:T(8,128)S(1)} %get-tuple-element.44.refs_1_, f32[64,1664]{1,0:T(8,128)S(1)} %collective-permute-done.3.refs_2_, f32[256,640]{1,0:T(8,128)S(1)} %shard_map.49.dep_ref.refs_3_.w_ref, ...), custom_call_target="tpu_custom_call" | custom-call | flops 10000000 | bytes 1000000 | tf_op jit(solution)/shard_map/pallas_call | solution.py:273
  42.6 2.8 %collective-permute-done.2.refs_1_ = f32[64,1280]{1,0:T(8,128)S(1)} collective-permute-done((f32[64,1280]{1,0:T(8,128)S(1)}, f32[64,1280]{1,0:T(8,128)S(1)}, u32[]{:S(2)}, u32[]{:S(2)}) %collective-permute-start.2) | collective-permute-done | bytes 327712 | tf_op jit(solution)/shard_map/ppermute | solution.py:287
  45.4 0.5 shard_map.53.refs_4_.refs_0_
  45.8 1.9 %collective-permute-start.4 = (f32[64,1280]{1,0:T(8,128)S(1)}, f32[64,1280]{1,0:T(8,128)S(1)}, u32[]{:S(2)}, u32[]{:S(2)}) collective-permute-start(f32[64,1280]{1,0:T(8,128)S(1)} %shard_map.53.refs_4_.refs_0_), channel_id=1, source_target_pairs={{0,4},{1,5},{2,6},{3,7},{4,0},{5,1},{6,2},{7,3},{8,12},{9,13},{10,... | collective-permute-start | bytes 983048 | tf_op jit(solution)/shard_map/ppermute | solution.py:287
  47.7 0.3 collective-permute-start.5
  48.0 1.4 %shard_map.54.refs_3_.w_ref = f32[256,512]{1,0:T(8,128)S(1)} custom-call(f32[256,640]{1,0:T(8,128)S(1)} %shard_map.49.dep_ref.refs_3_.w_ref, f32[64,640]{1,0:T(8,128)S(1)} %get-tuple-element.43.p_ref, f32[64,128]{1,0:T(8,128)S(1)} %get-tuple-element.47.m_ref, f32[64,640]{1,0:T(8,128)S(1)} %get-tuple-element.45.refs_2_.p2_ref, ...), custom_call_target="tpu_custom_call" | custom-call | flops 10000000 | bytes 1000000 | tf_op jit(solution)/shard_map/pallas_call | solution.py:273
  49.5 9.9 %collective-permute-done.5.refs_2_ = f32[64,1024]{1,0:T(8,128)S(1)} collective-permute-done((f32[64,1024]{1,0:T(8,128)S(1)}, f32[64,1024]{1,0:T(8,128)S(1)}, u32[]{:S(2)}, u32[]{:S(2)}) %collective-permute-start.5) | collective-permute-done | bytes 262176 | tf_op jit(solution)/shard_map/ppermute | solution.py:287
  59.3 2.0 %shard_map.55 = (f32[64,512]{1,0:T(8,128)S(1)}, f32[64,128]{1,0:T(8,128)S(1)}, f32[64,512]{1,0:T(8,128)S(1)}) custom-call(f32[8,64]{1,0:T(8,128)S(1)} %copy-done, f32[64,1024]{1,0:T(8,128)S(1)} %get-tuple-element.46.refs_1_, f32[64,1024]{1,0:T(8,128)S(1)} %collective-permute-done.5.refs_2_, f32[256,512]{1,0:T(8,128)S(1)} %shard_map.54.refs_3_.w_ref, ...), custom_call_target="tpu_custom_call" | custom-call | flops 10000000 | bytes 1000000 | tf_op jit(solution)/shard_map/pallas_call | solution.py:273
  61.3 0.0 collective-permute-done.4.refs_1_
  61.4 0.5 shard_map.56.refs_4_.refs_0_
  61.8 3.3 %collective-permute-start.6 = (f32[64,1280]{1,0:T(8,128)S(1)}, f32[64,1280]{1,0:T(8,128)S(1)}, u32[]{:S(2)}, u32[]{:S(2)}) collective-permute-start(f32[64,1280]{1,0:T(8,128)S(1)} %shard_map.56.refs_4_.refs_0_), channel_id=1, source_target_pairs={{0,12},{1,13},{2,14},{3,15},{4,8},{5,9},{6,10},{7,11},{8,4},{9,5},... | collective-permute-start | bytes 983048 | tf_op jit(solution)/shard_map/ppermute | solution.py:287
  65.1 0.1 collective-permute-start.7
  65.2 7.9 %collective-permute-done.7.refs_2_ = f32[64,512]{1,0:T(8,128)S(1)} collective-permute-done((f32[64,512]{1,0:T(8,128)S(1)}, f32[64,512]{1,0:T(8,128)S(1)}, u32[]{:S(2)}, u32[]{:S(2)}) %collective-permute-start.7) | collective-permute-done | bytes 131104 | tf_op jit(solution)/shard_map/ppermute | solution.py:287
  73.1 1.6 %shard_map.57 = (f32[64,512]{1,0:T(8,128)S(1)}, f32[64,128]{1,0:T(8,128)S(1)}) custom-call(f32[8,64]{1,0:T(8,128)S(1)} %copy-done, f32[64,512]{1,0:T(8,128)S(1)} %get-tuple-element.50.refs_1_, f32[64,512]{1,0:T(8,128)S(1)} %collective-permute-done.7.refs_2_, f32[256,512]{1,0:T(8,128)S(1)} %shard_map.54.refs_3_.w_ref, f32[64,1280]{1,0:T(8,128)S(1)} %shard_map.56.refs_4_.refs_0_), custom_call_target="tpu_custom_call" | custom-call | flops 10000000 | bytes 1000000 | tf_op jit(solution)/shard_map/pallas_call | solution.py:273
  74.7 0.0 collective-permute-done.6.refs_1_
  74.7 0.5 shard_map.58.refs_1_.refs_4_
  75.2 0.1 collective-permute-start.8
  75.3 1.3 %shard_map.59.refs_3_.w_ref = f32[256,384]{1,0:T(8,128)S(1)} custom-call(f32[256,512]{1,0:T(8,128)S(1)} %shard_map.54.refs_3_.w_ref, f32[64,512]{1,0:T(8,128)S(1)} %get-tuple-element.49.refs_2_.p_ref, f32[64,128]{1,0:T(8,128)S(1)} %get-tuple-element.52.m_ref, f32[64,512]{1,0:T(8,128)S(1)} %get-tuple-element.51.refs_2_.p2_ref, ...), custom_call_target="tpu_custom_call" | custom-call | flops 10000000 | bytes 1000000 | tf_op jit(solution)/shard_map/pallas_call | solution.py:273
  76.6 0.3 collective-permute-done.8.refs_2_
  76.9 2.0 %shard_map.60 = (f32[64,384]{1,0:T(8,128)S(1)}, f32[64,128]{1,0:T(8,128)S(1)}, f32[64,896]{1,0:T(8,128)S(1)}) custom-call(f32[8,64]{1,0:T(8,128)S(1)} %copy-done, f32[64,1280]{1,0:T(8,128)S(1)} %shard_map.58.refs_1_.refs_4_, f32[64,1280]{1,0:T(8,128)S(1)} %collective-permute-done.8.refs_2_, f32[256,384]{1,0:T(8,128)S(1)} %shard_map.59.refs_3_.w_ref, ...), custom_call_target="tpu_custom_call" | custom-call | flops 10000000 | bytes 1000000 | tf_op jit(solution)/shard_map/pallas_call | solution.py:273
  78.9 2.0 %collective-permute-start.9 = (f32[64,896]{1,0:T(8,128)S(1)}, f32[64,896]{1,0:T(8,128)S(1)}, u32[]{:S(2)}, u32[]{:S(2)}) collective-permute-start(f32[64,896]{1,0:T(8,128)S(1)} %get-tuple-element.54.refs_1_), channel_id=1, source_target_pairs={{0,32},{16,48},{32,0},{48,16},{64,96},{80,112},{96,64},{112,80},{1... | collective-permute-start | bytes 688136 | tf_op jit(solution)/shard_map/ppermute | solution.py:287
  80.9 6.0 %collective-permute-done.9.refs_2_ = f32[64,896]{1,0:T(8,128)S(1)} collective-permute-done((f32[64,896]{1,0:T(8,128)S(1)}, f32[64,896]{1,0:T(8,128)S(1)}, u32[]{:S(2)}, u32[]{:S(2)}) %collective-permute-start.9) | collective-permute-done | bytes 229408 | tf_op jit(solution)/shard_map/ppermute | solution.py:287
  86.9 1.9 %shard_map.61 = (f32[64,384]{1,0:T(8,128)S(1)}, f32[64,128]{1,0:T(8,128)S(1)}, f32[64,512]{1,0:T(8,128)S(1)}) custom-call(f32[8,64]{1,0:T(8,128)S(1)} %copy-done, f32[64,896]{1,0:T(8,128)S(1)} %get-tuple-element.54.refs_1_, f32[64,896]{1,0:T(8,128)S(1)} %collective-permute-done.9.refs_2_, f32[256,384]{1,0:T(8,128)S(1)} %shard_map.59.refs_3_.w_ref, ...), custom_call_target="tpu_custom_call" | custom-call | flops 10000000 | bytes 1000000 | tf_op jit(solution)/shard_map/pallas_call | solution.py:273
  88.8 3.6 %collective-permute-start.10 = (f32[64,512]{1,0:T(8,128)S(1)}, f32[64,512]{1,0:T(8,128)S(1)}, u32[]{:S(2)}, u32[]{:S(2)}) collective-permute-start(f32[64,512]{1,0:T(8,128)S(1)} %get-tuple-element.55.refs_1_), channel_id=1, source_target_pairs={{0,64},{16,80},{32,96},{48,112},{64,0},{80,16},{96,32},{112,48},{1... | collective-permute-start | bytes 393224 | tf_op jit(solution)/shard_map/ppermute | solution.py:287
  92.4 1.1 shard_map.62.refs_3_.refs_0_
  93.5 5.0 %collective-permute-done.10.refs_2_ = f32[64,512]{1,0:T(8,128)S(1)} collective-permute-done((f32[64,512]{1,0:T(8,128)S(1)}, f32[64,512]{1,0:T(8,128)S(1)}, u32[]{:S(2)}, u32[]{:S(2)}) %collective-permute-start.10) | collective-permute-done | bytes 131104 | tf_op jit(solution)/shard_map/ppermute | solution.py:287
  98.4 1.9 %shard_map.63 = (f32[64,256]{1,0:T(8,128)S(1)}, f32[64,128]{1,0:T(8,128)S(1)}, f32[64,256]{1,0:T(8,128)S(1)}) custom-call(f32[8,64]{1,0:T(8,128)S(1)} %copy-done, f32[64,512]{1,0:T(8,128)S(1)} %get-tuple-element.55.refs_1_, f32[64,512]{1,0:T(8,128)S(1)} %collective-permute-done.10.refs_2_, f32[256,256]{1,0:T(8,128)S(1)} %shard_map.62.refs_3_.refs_0_, ...), custom_call_target="tpu_custom_call" | custom-call | flops 10000000 | bytes 1000000 | tf_op jit(solution)/shard_map/pallas_call | solution.py:273
  100.3 4.9 %collective-permute-start.11 = (f32[64,256]{1,0:T(8,128)S(1)}, f32[64,256]{1,0:T(8,128)S(1)}, u32[]{:S(2)}, u32[]{:S(2)}) collective-permute-start(f32[64,256]{1,0:T(8,128)S(1)} %get-tuple-element.60.refs_1_), channel_id=1, source_target_pairs={{0,224},{16,240},{32,192},{48,208},{64,160},{80,176},{96,128},{112... | collective-permute-start | bytes 196616 | tf_op jit(solution)/shard_map/ppermute | solution.py:287
  105.3 0.8 shard_map.64.refs_3_
  106.1 2.0 %collective-permute-done.11.refs_2_ = f32[64,256]{1,0:T(8,128)S(1)} collective-permute-done((f32[64,256]{1,0:T(8,128)S(1)}, f32[64,256]{1,0:T(8,128)S(1)}, u32[]{:S(2)}, u32[]{:S(2)}) %collective-permute-start.11) | collective-permute-done | bytes 65568 | tf_op jit(solution)/shard_map/ppermute | solution.py:287
  108.1 2.7 %shard_map.65 = f32[256,128]{1,0:T(8,128)} custom-call(f32[8,64]{1,0:T(8,128)S(1)} %copy-done, f32[64,256]{1,0:T(8,128)S(1)} %get-tuple-element.60.refs_1_, f32[64,256]{1,0:T(8,128)S(1)} %collective-permute-done.11.refs_2_, f32[256,256]{1,0:T(8,128)S(1)} %shard_map.64.refs_3_), custom_call_target="tpu_custom_call" | custom-call | flops 10000000 | bytes 1000000 | tf_op jit(solution)/shard_map/pallas_call | solution.py:273
Async XLA Ops:
  8.4 10.9 %collective-permute-start.1 = (f32[128,640]{1,0:T(8,128)S(1)}, f32[128,640]{1,0:T(8,128)S(1)}, u32[]{:S(2)}, u32[]{:S(2)}) collective-permute-start(f32[128,640]{1,0:T(8,128)S(1)} %get-tuple-element.36.yb_ref), channel_id=1, source_target_pairs={{0,1},{1,0},{2,3},{3,2},{4,5},{5,4},{6,7},{7,6},{8,9},{9,8},{10,11... | collective-permute-start | bytes 983048 | tf_op jit(solution)/shard_map/ppermute | solution.py:287
  10.7 14.2 %collective-permute-start = (f32[128,640]{1,0:T(8,128)S(1)}, f32[128,640]{1,0:T(8,128)S(1)}, u32[]{:S(2)}, u32[]{:S(2)}) collective-permute-start(f32[128,640]{1,0:T(8,128)S(1)} %get-tuple-element.34.ya_ref), channel_id=1, source_target_pairs={{0,1},{1,0},{2,3},{3,2},{4,5},{5,4},{6,7},{7,6},{8,9},{9,8},{10,11... | collective-permute-start | bytes 983048 | tf_op jit(solution)/shard_map/ppermute | solution.py:287
  12.1 12.9 %copy-start = (f32[8,64]{1,0:T(8,128)S(1)}, f32[8,64]{1,0:T(8,128)}, u32[]{:S(2)}) copy-start(f32[8,64]{1,0:T(8,128)} %refs_0_.13) | copy-start | bytes 6148
  27.8 12.8 %collective-permute-start.3 = (f32[64,1664]{1,0:T(8,128)S(1)}, f32[64,1664]{1,0:T(8,128)S(1)}, u32[]{:S(2)}, u32[]{:S(2)}) collective-permute-start(f32[64,1664]{1,0:T(8,128)S(1)} %get-tuple-element.44.refs_1_), channel_id=1, source_target_pairs={{0,3},{1,2},{2,1},{3,0},{4,7},{5,6},{6,5},{7,4},{8,11},{9,10},{10,... | collective-permute-start | bytes 1277960 | tf_op jit(solution)/shard_map/ppermute | solution.py:287
  30.1 15.2 %collective-permute-start.2 = (f32[64,1280]{1,0:T(8,128)S(1)}, f32[64,1280]{1,0:T(8,128)S(1)}, u32[]{:S(2)}, u32[]{:S(2)}) collective-permute-start(f32[64,1280]{1,0:T(8,128)S(1)} %shard_map.51.refs_4_.refs_0_), channel_id=1, source_target_pairs={{0,3},{1,2},{2,1},{3,0},{4,7},{5,6},{6,5},{7,4},{8,11},{9,10},{10,... | collective-permute-start | bytes 983048 | tf_op jit(solution)/shard_map/ppermute | solution.py:287
  45.8 15.5 %collective-permute-start.4 = (f32[64,1280]{1,0:T(8,128)S(1)}, f32[64,1280]{1,0:T(8,128)S(1)}, u32[]{:S(2)}, u32[]{:S(2)}) collective-permute-start(f32[64,1280]{1,0:T(8,128)S(1)} %shard_map.53.refs_4_.refs_0_), channel_id=1, source_target_pairs={{0,4},{1,5},{2,6},{3,7},{4,0},{5,1},{6,2},{7,3},{8,12},{9,13},{10,... | collective-permute-start | bytes 983048 | tf_op jit(solution)/shard_map/ppermute | solution.py:287
  47.7 11.6 %collective-permute-start.5 = (f32[64,1024]{1,0:T(8,128)S(1)}, f32[64,1024]{1,0:T(8,128)S(1)}, u32[]{:S(2)}, u32[]{:S(2)}) collective-permute-start(f32[64,1024]{1,0:T(8,128)S(1)} %get-tuple-element.46.refs_1_), channel_id=1, source_target_pairs={{0,4},{1,5},{2,6},{3,7},{4,0},{5,1},{6,2},{7,3},{8,12},{9,13},{10,... | collective-permute-start | bytes 786440 | tf_op jit(solution)/shard_map/ppermute | solution.py:287
  61.8 12.9 %collective-permute-start.6 = (f32[64,1280]{1,0:T(8,128)S(1)}, f32[64,1280]{1,0:T(8,128)S(1)}, u32[]{:S(2)}, u32[]{:S(2)}) collective-permute-start(f32[64,1280]{1,0:T(8,128)S(1)} %shard_map.56.refs_4_.refs_0_), channel_id=1, source_target_pairs={{0,12},{1,13},{2,14},{3,15},{4,8},{5,9},{6,10},{7,11},{8,4},{9,5},... | collective-permute-start | bytes 983048 | tf_op jit(solution)/shard_map/ppermute | solution.py:287
  65.1 8.0 %collective-permute-start.7 = (f32[64,512]{1,0:T(8,128)S(1)}, f32[64,512]{1,0:T(8,128)S(1)}, u32[]{:S(2)}, u32[]{:S(2)}) collective-permute-start(f32[64,512]{1,0:T(8,128)S(1)} %get-tuple-element.50.refs_1_), channel_id=1, source_target_pairs={{0,12},{1,13},{2,14},{3,15},{4,8},{5,9},{6,10},{7,11},{8,4},{9,5},... | collective-permute-start | bytes 393224 | tf_op jit(solution)/shard_map/ppermute | solution.py:287
  75.2 1.7 %collective-permute-start.8 = (f32[64,1280]{1,0:T(8,128)S(1)}, f32[64,1280]{1,0:T(8,128)S(1)}, u32[]{:S(2)}, u32[]{:S(2)}) collective-permute-start(f32[64,1280]{1,0:T(8,128)S(1)} %shard_map.58.refs_1_.refs_4_), channel_id=1, source_target_pairs={{0,16},{16,0},{32,48},{48,32},{64,80},{80,64},{96,112},{112,96},{1... | collective-permute-start | bytes 983048 | tf_op jit(solution)/shard_map/ppermute | solution.py:287
  78.9 8.0 %collective-permute-start.9 = (f32[64,896]{1,0:T(8,128)S(1)}, f32[64,896]{1,0:T(8,128)S(1)}, u32[]{:S(2)}, u32[]{:S(2)}) collective-permute-start(f32[64,896]{1,0:T(8,128)S(1)} %get-tuple-element.54.refs_1_), channel_id=1, source_target_pairs={{0,32},{16,48},{32,0},{48,16},{64,96},{80,112},{96,64},{112,80},{1... | collective-permute-start | bytes 688136 | tf_op jit(solution)/shard_map/ppermute | solution.py:287
  88.8 9.6 %collective-permute-start.10 = (f32[64,512]{1,0:T(8,128)S(1)}, f32[64,512]{1,0:T(8,128)S(1)}, u32[]{:S(2)}, u32[]{:S(2)}) collective-permute-start(f32[64,512]{1,0:T(8,128)S(1)} %get-tuple-element.55.refs_1_), channel_id=1, source_target_pairs={{0,64},{16,80},{32,96},{48,112},{64,0},{80,16},{96,32},{112,48},{1... | collective-permute-start | bytes 393224 | tf_op jit(solution)/shard_map/ppermute | solution.py:287
  100.3 7.8 %collective-permute-start.11 = (f32[64,256]{1,0:T(8,128)S(1)}, f32[64,256]{1,0:T(8,128)S(1)}, u32[]{:S(2)}, u32[]{:S(2)}) collective-permute-start(f32[64,256]{1,0:T(8,128)S(1)} %get-tuple-element.60.refs_1_), channel_id=1, source_target_pairs={{0,224},{16,240},{32,192},{48,208},{64,160},{80,176},{96,128},{112... | collective-permute-start | bytes 196616 | tf_op jit(solution)/shard_map/ppermute | solution.py:287

commit v6 on v5

--- a/solution.py
+++ b/solution.py
@@ -90,25 +90,31 @@
     return jnp.concatenate(out, axis=0)
 
 
-def sweep(aug, count, y_ref, z_ref, m_ref, late=()):
-    rows = aug.shape[0]
-    cols = aug.shape[1] - WIDTH
-    for j in range(count):
-        r0 = R * j
-        a0 = 128 * (r0 // 128)
-        minv = chol_inverse(aug[r0 : r0 + R, a0 : a0 + 128], r0 - a0)
+def lanes_from(j):
+    return 128 * (R * j // 128)
+
+
+def sweep(aug, first, count, y_ref, z_ref, m_ref, late=()):
+    base = lanes_from(first)
+    for j in range(first, first + count):
+        r0 = R * (j - first)
+        a0 = lanes_from(j) - base
+        at = R * j - lanes_from(j)
+        split = M - lanes_from(j)
+        minv = chol_inverse(aug[r0 : r0 + R, a0 : a0 + 128], at)
         m_ref[r0 : r0 + R, :] = minv
-        if j == 0:
-            for copy in late:
-                copy.wait()
+        for copy in late:
+            copy.wait()
+        late = ()
         block = aug[r0 : r0 + R, a0:]
         panel = mm(minv, jnp.concatenate([block, block], axis=0))
-        z_ref[r0 : r0 + R, :] = panel[:, : cols - a0]
-        y_ref[r0 : r0 + R, :] = panel[:, cols - a0 :]
-        for i in range(j + 1, rows // R):
-            c0 = R * i
-            s0 = 128 * (c0 // 128)
-            aug[c0 : c0 + R, s0:] -= mm_t(panel[:, c0 - a0 : c0 - a0 + R], panel[:, s0 - a0 :])
+        z_ref[r0 : r0 + R, :] = panel[:, :split]
+        y_ref[r0 : r0 + R, :] = panel[:, split:]
+        for i in range(j + 1, 4):
+            c0 = R * i - lanes_from(j)
+            s0 = lanes_from(i) - lanes_from(j)
+            q0 = R * (i - first)
+            aug[q0 : q0 + R, a0 + s0 :] -= mm_t(panel[:, c0 : c0 + R], panel[:, s0:])
 
 
 def leaf_kernel(d_any, b_any, t_any, y_ref, z_ref, m_ref, rest_ref, aug, sem):
@@ -121,24 +127,31 @@
     for copy in copies:
         copy.start()
     copies[0].wait()
-    sweep(aug, 2, y_ref, z_ref, m_ref, copies[1:])
-    rest_ref[...] = aug[M // 2 :, M // 2 :]
-
-
-def leaf2_kernel(rest_ref, y_ref, z_ref, m_ref, aug):
-    aug[...] = rest_ref[...]
-    sweep(aug, 2, y_ref, z_ref, m_ref)
-
-
-def back_kernel(ya_ref, za_ref, ma_ref, yb_ref, zb_ref, mb_ref, w_ref):
+    sweep(aug, 0, 1, y_ref, z_ref, m_ref, copies[1:])
+    rest_ref[...] = aug[R:, :]
+
+
+def leaf2_kernel(aug_ref, y_ref, z_ref, m_ref, rest_ref, aug):
+    aug[...] = aug_ref[...]
+    sweep(aug, 1, 1, y_ref, z_ref, m_ref)
+    rest_ref[...] = aug[R:, 2 * R :]
+
+
+def leaf3_kernel(aug_ref, y_ref, z_ref, m_ref, aug):
+    aug[...] = aug_ref[...]
+    sweep(aug, 2, 2, y_ref, z_ref, m_ref)
+
+
+def back_kernel(*refs):
+    ys, zs, ms, w_ref = refs[:3], refs[3:6], refs[6:9], refs[9]
     for j in range(3, -1, -1):
-        y_ref, z_ref, m_ref = (ya_ref, za_ref, ma_ref) if j < 2 else (yb_ref, zb_ref, mb_ref)
-        q0 = R * (j % 2)
-        rhs = y_ref[q0 : q0 + R, :]
+        part, q0 = min(j, 2), R * max(j - 2, 0)
+        o = R - (R * j - lanes_from(j))
+        rhs = ys[part][q0 : q0 + R, :]
         if j < 3:
-            z = z_ref[q0 : q0 + R, q0 + R :]
+            z = zs[part][q0 : q0 + R, R * (j + 1) - lanes_from(j) :]
             rhs = rhs - mm(z, w_ref[R * (j + 1) :, :])
-        w_ref[R * j : R * j + R, :] = mm_t(m_ref[q0 : q0 + R, :], rhs)[R - q0 : 2 * R - q0, :]
+        w_ref[R * j : R * j + R, :] = mm_t(ms[part][q0 : q0 + R, :], rhs)[o : o + R, :]
 
 
 def gram_pair(y, pair):
@@ -165,13 +178,13 @@
     return ref[:, o : o + width_of(level)]
 
 
-def gram_pairs(ya_ref, yb_ref, pairs):
-    y = jnp.concatenate([ya_ref[...], yb_ref[...]], axis=0)
+def gram_pairs(y_refs, pairs):
+    y = jnp.concatenate([y_ref[...] for y_ref in y_refs], axis=0)
     return {pair: gram_pair(y, pair) for pair in pairs}
 
 
-def gram_kernel(ya_ref, yb_ref, near_ref, far_ref):
-    grams = gram_pairs(ya_ref, yb_ref, range(4))
+def gram_kernel(ya_ref, yb_ref, yc_ref, near_ref, far_ref):
+    grams = gram_pairs((ya_ref, yb_ref, yc_ref), range(4))
     for level in range(1, SPLIT + 1):
         put(near_ref, 1, level, row_block(grams, level))
     for level in range(SPLIT + 1, LEVELS + 1):
@@ -209,8 +222,8 @@
             put(n_ref, k + 1, level, trailing(level) - row_block(grams, level))
 
 
-def first_level_kernel(c_ref, own_ref, ya_ref, yb_ref, dep_ref, p_ref, m_ref, n_ref):
-    grams = gram_pairs(ya_ref, yb_ref, range(SPLIT // 2))
+def first_level_kernel(c_ref, own_ref, ya_ref, yb_ref, yc_ref, dep_ref, p_ref, m_ref, n_ref):
+    grams = gram_pairs((ya_ref, yb_ref, yc_ref), range(SPLIT // 2))
 
     def part(level):
         return get(own_ref, 1, level) + row_block(grams, level)
@@ -227,8 +240,8 @@
     next_level(k, p, part, n_ref)
 
 
-def first_far_kernel(own_ref, ya_ref, yb_ref, p_ref, n_ref):
-    grams = gram_pairs(ya_ref, yb_ref, range(SPLIT // 2, LEVELS // 2))
+def first_far_kernel(own_ref, ya_ref, yb_ref, yc_ref, p_ref, n_ref):
+    grams = gram_pairs((ya_ref, yb_ref, yc_ref), range(SPLIT // 2, LEVELS // 2))
     less = schur(1, p_ref[...], SPLIT + 1, LEVELS)
     for level in range(SPLIT + 1, LEVELS + 1):
         put(n_ref, SPLIT + 1, level, get(own_ref, SPLIT + 1, level) + row_block(grams, level) - row_block(less, level))
@@ -293,33 +306,39 @@
         pltpu.with_memory_space_constraint(a, pltpu.HBM) for a in (leaf_blocks, bases, targets)
     )
     ya, za, ma, rest = call(
-        leaf_kernel, [(half, WIDTH), (half, M), (half, 128), (half, half + WIDTH)], leaf_blocks, bases, targets,
+        leaf_kernel, [(R, WIDTH), (R, M), (R, 128), (3 * R, M + WIDTH)], leaf_blocks, bases, targets,
         hbm=(0, 1, 2), scratch=[(M, M + WIDTH)], sems=3,
     )
     got_a = exchange(ya, 1)
-    yb, zb, mb = call(
-        leaf2_kernel, [(half, WIDTH), (half, half), (half, 128)], rest,
+    yb, zb, mb, rest = call(
+        leaf2_kernel, [(R, WIDTH), (R, M), (R, 128), (half, half + WIDTH)], rest,
+        scratch=[(3 * R, M + WIDTH)],
+    )
+    got_b = exchange(yb, 1)
+    yc, zc, mc = call(
+        leaf3_kernel, [(half, WIDTH), (half, half), (half, 128)], rest,
         scratch=[(half, half + WIDTH)],
     )
-    got_b = exchange(yb, 1)
+    got_y = (got_a, got_b, exchange(yc, 1))
     far_shape = (R, offsets(SPLIT + 1)[1])
-    near, far = call(gram_kernel, [(R, offsets(1, SPLIT)[1]), far_shape], ya, yb)
-    (w,) = call(back_kernel, [(M, WIDTH)], ya, za, ma, yb, zb, mb)
+    near, far = call(gram_kernel, [(R, offsets(1, SPLIT)[1]), far_shape], ya, yb, yc)
+    (w,) = call(back_kernel, [(M, WIDTH)], ya, yb, yc, za, zb, zc, ma, mb, mc)
     got = far_got = None
+    dep = w
     for k in range(1, LEVELS):
         outs = [(R, width_of(k)), (R, 128)]
         if k != SPLIT:
             outs.append((R, offsets(k + 1, last_of(k + 1))[1]))
         if k == 1:
-            p, minv, near = call(first_level_kernel, outs, coupling, near, got_a, got_b, w, hbm=(4,))
+            p, minv, near = call(first_level_kernel, outs, coupling, near, *got_y, w, hbm=(5,))
         else:
             kernel = lambda *refs, k=k: level_kernel(k, *refs)
-            p, minv, *more = call(kernel, outs, coupling, near, got, w, far, hbm=(3, 4))
+            p, minv, *more = call(kernel, outs, coupling, near, got, dep, far, hbm=(3, 4))
             near = more[0] if more else None
         if k < SPLIT:
             got = exchange(near, k + 1)
         if k == 1:
-            (far,) = call(first_far_kernel, [far_shape], far, got_a, got_b, p)
+            (far,) = call(first_far_kernel, [far_shape], far, *got_y, p)
         elif k <= SPLIT:
             kernel = lambda *refs, k=k: far_kernel(k, *refs)
             (far,) = call(kernel, [far_shape], far, far_got, p)
@@ -335,6 +354,8 @@
         elif k % 2 == 0:
             (w,) = call(apply_two_kernel, [(M, width_of(k + 1))], w, *before, p, minv)
         before = (p, minv)
+        if k != SPLIT:
+            dep = w
     kernel = lambda *refs: last_kernel(LEVELS, *refs)
     return call(
         kernel, [(M, NRHS)], coupling, near, got, w,

time: 113 us -> 113 us (level)
  waiting for transfers between devices: 54.2 us -> 52.3 us
  starting transfers between devices: 21 us -> 22.7 us
    ppermute x12 -> x13, waiting for transfers between devices: 54.2 us -> 52.3 us  [exchange(): lax.ppermute(value, axis, [(s, s ^ mask) for s in range(lax.axis_size(axi...]
    ppermute x12 -> x13, starting transfers between devices: 21 us -> 22.7 us  [exchange(): lax.ppermute(value, axis, [(s, s ^ mask) for s in range(lax.axis_size(axi...]
    pallas_call x20 -> x21, Pallas kernels: 35.4 us -> 35.7 us  [call(): pl.pallas_call(kernel, out_shape=shapes, in_specs=[hb if i in hbm else vm...]
  transfers between devices with their start and end apart: 12 -> 13, of which waited for: 10 -> 10; matrix products, arithmetic and copies ran while one was open for 0% -> 0% of each run, Pallas kernels for 13% -> 13%
where the time goes in v6:
time: 113 us; the launch traced here: 111 us
  waiting for transfers between devices  52.3 us (46%)
  Pallas kernels  35.7 us (32%)
  starting transfers between devices  22.7 us (20%)
    ppermute x13, waiting for transfers between devices, exchange(): lax.ppermute(value, axis, [(s, s ^ mask) for s in range(lax.axis_size(axi...  52.3 us
    pallas_call x21, Pallas kernels, call(): pl.pallas_call(kernel, out_shape=shapes, in_specs=[hb if i in hbm else vm...  35.7 us
    ppermute x13, starting transfers between devices, exchange(): lax.ppermute(value, axis, [(s, s ^ mask) for s in range(lax.axis_size(axi...  22.7 us
  transfers between devices with their start and end apart: 13, of which 10 were waited for; matrix products, arithmetic and copies ran while one was open for 0% of the time, Pallas kernels for 13%

profile of v6, /device:TPU:2, one launch (start us, length us, event | category | flops | bytes accessed | tf_op | source)
XLA Modules:
  0.0 111.0 jit_solution(17252195150899098306)
XLA Ops:
  0.0 3.2 %shard_map.46 = (f32[64,640]{1,0:T(8,128)S(1)}, f32[64,256]{1,0:T(8,128)S(1)}, f32[64,128]{1,0:T(8,128)S(1)}, f32[192,896]{1,0:T(8,128)S(1)}) custom-call(f32[256,256]{1,0:T(8,128)} %d_any.1, f32[256,512]{1,0:T(8,128)} %b_any.1, f32[256,128]{1,0:T(8,128)} %t_any.1), custom_call_target="tpu_custom_call" | custom-call | flops 10000000 | bytes 1000000 | tf_op jit(solution)/shard_map/pallas_call | solution.py:286
  3.2 2.0 %shard_map.47 = (f32[64,640]{1,0:T(8,128)S(1)}, f32[64,256]{1,0:T(8,128)S(1)}, f32[64,128]{1,0:T(8,128)S(1)}, f32[128,768]{1,0:T(8,128)S(1)}) custom-call(f32[192,896]{1,0:T(8,128)S(1)} %get-tuple-element.39.aug_ref), custom_call_target="tpu_custom_call" | custom-call | flops 10000000 | bytes 1000000 | tf_op jit(solution)/shard_map/pallas_call | solution.py:286
  5.3 3.4 %shard_map.48 = (f32[128,640]{1,0:T(8,128)S(1)}, f32[128,128]{1,0:T(8,128)S(1)}, f32[128,128]{1,0:T(8,128)S(1)}) custom-call(f32[128,768]{1,0:T(8,128)S(1)} %get-tuple-element.41.aug_ref), custom_call_target="tpu_custom_call" | custom-call | flops 10000000 | bytes 1000000 | tf_op jit(solution)/shard_map/pallas_call | solution.py:286
  8.7 2.3 %collective-permute-start.2 = (f32[128,640]{1,0:T(8,128)S(1)}, f32[128,640]{1,0:T(8,128)S(1)}, u32[]{:S(2)}, u32[]{:S(2)}) collective-permute-start(f32[128,640]{1,0:T(8,128)S(1)} %get-tuple-element.42.yc_ref.refs_2_), channel_id=1, source_target_pairs={{0,1},{1,0},{2,3},{3,2},{4,5},{5,4},{6,7},{7,6},{8,9},{9,8},{10,11... | collective-permute-start | bytes 983048 | tf_op jit(solution)/shard_map/ppermute | solution.py:300
  11.0 0.1 collective-permute-start.1
  11.1 1.9 %collective-permute-start = (f32[64,640]{1,0:T(8,128)S(1)}, f32[64,640]{1,0:T(8,128)S(1)}, u32[]{:S(2)}, u32[]{:S(2)}) collective-permute-start(f32[64,640]{1,0:T(8,128)S(1)} %get-tuple-element.38.ya_ref.refs_0_), channel_id=1, source_target_pairs={{0,1},{1,0},{2,3},{3,2},{4,5},{5,4},{6,7},{7,6},{8,9},{9,8},{10,11... | collective-permute-start | bytes 491528 | tf_op jit(solution)/shard_map/ppermute | solution.py:300
  13.1 1.1 shard_map.49
  14.1 0.0 copy-start
  14.1 2.3 %shard_map.50.dep_ref.refs_3_.w_ref = f32[256,640]{1,0:T(8,128)S(1)} custom-call(f32[64,640]{1,0:T(8,128)S(1)} %get-tuple-element.38.ya_ref.refs_0_, f32[64,640]{1,0:T(8,128)S(1)} %get-tuple-element.40.yb_ref.refs_1_, f32[128,640]{1,0:T(8,128)S(1)} %get-tuple-element.42.yc_ref.refs_2_, f32[64,256]{1,0:T(8,128)S(1)} %get-tuple-element.45.refs_3_, ...), custom_call_target="tpu_custom_call" | custom-call | flops 10000000 | bytes 1000000 | tf_op jit(solution)/shard_map/pallas_call | solution.py:286
  16.4 6.7 %collective-permute-done.1.yb_ref = f32[64,640]{1,0:T(8,128)S(1)} collective-permute-done((f32[64,640]{1,0:T(8,128)S(1)}, f32[64,640]{1,0:T(8,128)S(1)}, u32[]{:S(2)}, u32[]{:S(2)}) %collective-permute-start.1) | collective-permute-done | bytes 163872 | tf_op jit(solution)/shard_map/ppermute | solution.py:300
  23.1 2.2 %collective-permute-done.ya_ref = f32[64,640]{1,0:T(8,128)S(1)} collective-permute-done((f32[64,640]{1,0:T(8,128)S(1)}, f32[64,640]{1,0:T(8,128)S(1)}, u32[]{:S(2)}, u32[]{:S(2)}) %collective-permute-start) | collective-permute-done | bytes 163872 | tf_op jit(solution)/shard_map/ppermute | solution.py:300
  25.3 0.0 collective-permute-done.2.yc_ref
  25.3 0.0 copy-done
  25.3 2.8 %shard_map.51 = (f32[64,640]{1,0:T(8,128)S(1)}, f32[64,128]{1,0:T(8,128)S(1)}, f32[64,1664]{1,0:T(8,128)S(1)}) custom-call(f32[8,64]{1,0:T(8,128)S(1)} %copy-done, f32[64,2304]{1,0:T(8,128)S(1)} %get-tuple-element.44.own_ref, f32[64,640]{1,0:T(8,128)S(1)} %collective-permute-done.ya_ref, f32[64,640]{1,0:T(8,128)S(1)} %collective-permute-done.1.yb_ref, ...), custom_call_target="tpu_custom_call" | custom-call | flops 10000000 | bytes 1000000 | tf_op jit(solution)/shard_map/pallas_call | solution.py:286
  28.1 1.6 %collective-permute-start.4 = (f32[64,1664]{1,0:T(8,128)S(1)}, f32[64,1664]{1,0:T(8,128)S(1)}, u32[]{:S(2)}, u32[]{:S(2)}) collective-permute-start(f32[64,1664]{1,0:T(8,128)S(1)} %get-tuple-element.52.refs_1_), channel_id=1, source_target_pairs={{0,3},{1,2},{2,1},{3,0},{4,7},{5,6},{6,5},{7,4},{8,11},{9,10},{10,... | collective-permute-start | bytes 1277960 | tf_op jit(solution)/shard_map/ppermute | solution.py:300
  29.6 0.8 shard_map.52.refs_4_.refs_0_
  30.4 0.6 collective-permute-start.3
  31.1 9.8 %collective-permute-done.4.refs_2_ = f32[64,1664]{1,0:T(8,128)S(1)} collective-permute-done((f32[64,1664]{1,0:T(8,128)S(1)}, f32[64,1664]{1,0:T(8,128)S(1)}, u32[]{:S(2)}, u32[]{:S(2)}) %collective-permute-start.4) | collective-permute-done | bytes 426016 | tf_op jit(solution)/shard_map/ppermute | solution.py:300
  40.8 2.0 %shard_map.53 = (f32[64,640]{1,0:T(8,128)S(1)}, f32[64,128]{1,0:T(8,128)S(1)}, f32[64,1024]{1,0:T(8,128)S(1)}) custom-call(f32[8,64]{1,0:T(8,128)S(1)} %copy-done, f32[64,1664]{1,0:T(8,128)S(1)} %get-tuple-element.52.refs_1_, f32[64,1664]{1,0:T(8,128)S(1)} %collective-permute-done.4.refs_2_, f32[256,640]{1,0:T(8,128)S(1)} %shard_map.50.dep_ref.refs_3_.w_ref, ...), custom_call_target="tpu_custom_call" | custom-call | flops 10000000 | bytes 1000000 | tf_op jit(solution)/shard_map/pallas_call | solution.py:286
  42.9 2.8 %collective-permute-done.3.refs_1_ = f32[64,1280]{1,0:T(8,128)S(1)} collective-permute-done((f32[64,1280]{1,0:T(8,128)S(1)}, f32[64,1280]{1,0:T(8,128)S(1)}, u32[]{:S(2)}, u32[]{:S(2)}) %collective-permute-start.3) | collective-permute-done | bytes 327712 | tf_op jit(solution)/shard_map/ppermute | solution.py:300
  45.7 0.5 shard_map.54.refs_4_.refs_0_
  46.1 1.9 %collective-permute-start.5 = (f32[64,1280]{1,0:T(8,128)S(1)}, f32[64,1280]{1,0:T(8,128)S(1)}, u32[]{:S(2)}, u32[]{:S(2)}) collective-permute-start(f32[64,1280]{1,0:T(8,128)S(1)} %shard_map.54.refs_4_.refs_0_), channel_id=1, source_target_pairs={{0,4},{1,5},{2,6},{3,7},{4,0},{5,1},{6,2},{7,3},{8,12},{9,13},{10,... | collective-permute-start | bytes 983048 | tf_op jit(solution)/shard_map/ppermute | solution.py:300
  48.0 0.3 collective-permute-start.6
  48.4 1.4 %shard_map.55.refs_3_.w_ref = f32[256,512]{1,0:T(8,128)S(1)} custom-call(f32[256,640]{1,0:T(8,128)S(1)} %shard_map.50.dep_ref.refs_3_.w_ref, f32[64,640]{1,0:T(8,128)S(1)} %get-tuple-element.51.p_ref, f32[64,128]{1,0:T(8,128)S(1)} %get-tuple-element.55.m_ref, f32[64,640]{1,0:T(8,128)S(1)} %get-tuple-element.53.refs_2_.p2_ref, ...), custom_call_target="tpu_custom_call" | custom-call | flops 10000000 | bytes 1000000 | tf_op jit(solution)/shard_map/pallas_call | solution.py:286
  49.8 9.9 %collective-permute-done.6.refs_2_ = f32[64,1024]{1,0:T(8,128)S(1)} collective-permute-done((f32[64,1024]{1,0:T(8,128)S(1)}, f32[64,1024]{1,0:T(8,128)S(1)}, u32[]{:S(2)}, u32[]{:S(2)}) %collective-permute-start.6) | collective-permute-done | bytes 262176 | tf_op jit(solution)/shard_map/ppermute | solution.py:300
  59.7 2.0 %shard_map.56 = (f32[64,512]{1,0:T(8,128)S(1)}, f32[64,128]{1,0:T(8,128)S(1)}, f32[64,512]{1,0:T(8,128)S(1)}) custom-call(f32[8,64]{1,0:T(8,128)S(1)} %copy-done, f32[64,1024]{1,0:T(8,128)S(1)} %get-tuple-element.54.refs_1_, f32[64,1024]{1,0:T(8,128)S(1)} %collective-permute-done.6.refs_2_, f32[256,512]{1,0:T(8,128)S(1)} %shard_map.55.refs_3_.w_ref, ...), custom_call_target="tpu_custom_call" | custom-call | flops 10000000 | bytes 1000000 | tf_op jit(solution)/shard_map/pallas_call | solution.py:286
  61.7 0.0 collective-permute-done.5.refs_1_
  61.7 0.5 shard_map.57.refs_4_.refs_0_
  62.2 3.2 %collective-permute-start.7 = (f32[64,1280]{1,0:T(8,128)S(1)}, f32[64,1280]{1,0:T(8,128)S(1)}, u32[]{:S(2)}, u32[]{:S(2)}) collective-permute-start(f32[64,1280]{1,0:T(8,128)S(1)} %shard_map.57.refs_4_.refs_0_), channel_id=1, source_target_pairs={{0,12},{1,13},{2,14},{3,15},{4,8},{5,9},{6,10},{7,11},{8,4},{9,5},... | collective-permute-start | bytes 983048 | tf_op jit(solution)/shard_map/ppermute | solution.py:300
  65.4 0.1 collective-permute-start.8
  65.5 7.9 %collective-permute-done.8.refs_2_ = f32[64,512]{1,0:T(8,128)S(1)} collective-permute-done((f32[64,512]{1,0:T(8,128)S(1)}, f32[64,512]{1,0:T(8,128)S(1)}, u32[]{:S(2)}, u32[]{:S(2)}) %collective-permute-start.8) | collective-permute-done | bytes 131104 | tf_op jit(solution)/shard_map/ppermute | solution.py:300
  73.4 1.6 %shard_map.58 = (f32[64,512]{1,0:T(8,128)S(1)}, f32[64,128]{1,0:T(8,128)S(1)}) custom-call(f32[8,64]{1,0:T(8,128)S(1)} %copy-done, f32[64,512]{1,0:T(8,128)S(1)} %get-tuple-element.58.refs_1_, f32[64,512]{1,0:T(8,128)S(1)} %collective-permute-done.8.refs_2_, f32[256,512]{1,0:T(8,128)S(1)} %shard_map.55.refs_3_.w_ref, f32[64,1280]{1,0:T(8,128)S(1)} %shard_map.57.refs_4_.refs_0_), custom_call_target="tpu_custom_call" | custom-call | flops 10000000 | bytes 1000000 | tf_op jit(solution)/shard_map/pallas_call | solution.py:286
  75.0 0.0 collective-permute-done.7.refs_1_
  75.0 0.5 shard_map.59.refs_1_.refs_4_
  75.5 0.1 collective-permute-start.9
  75.6 1.6 %collective-permute-done.9.refs_2_ = f32[64,1280]{1,0:T(8,128)S(1)} collective-permute-done((f32[64,1280]{1,0:T(8,128)S(1)}, f32[64,1280]{1,0:T(8,128)S(1)}, u32[]{:S(2)}, u32[]{:S(2)}) %collective-permute-start.9) | collective-permute-done | bytes 327712 | tf_op jit(solution)/shard_map/ppermute | solution.py:300
  77.2 2.0 %shard_map.60 = (f32[64,384]{1,0:T(8,128)S(1)}, f32[64,128]{1,0:T(8,128)S(1)}, f32[64,896]{1,0:T(8,128)S(1)}) custom-call(f32[8,64]{1,0:T(8,128)S(1)} %copy-done, f32[64,1280]{1,0:T(8,128)S(1)} %shard_map.59.refs_1_.refs_4_, f32[64,1280]{1,0:T(8,128)S(1)} %collective-permute-done.9.refs_2_, f32[256,512]{1,0:T(8,128)S(1)} %shard_map.55.refs_3_.w_ref, ...), custom_call_target="tpu_custom_call" | custom-call | flops 10000000 | bytes 1000000 | tf_op jit(solution)/shard_map/pallas_call | solution.py:286
  79.2 2.0 %collective-permute-start.10 = (f32[64,896]{1,0:T(8,128)S(1)}, f32[64,896]{1,0:T(8,128)S(1)}, u32[]{:S(2)}, u32[]{:S(2)}) collective-permute-start(f32[64,896]{1,0:T(8,128)S(1)} %get-tuple-element.60.refs_1_), channel_id=1, source_target_pairs={{0,32},{16,48},{32,0},{48,16},{64,96},{80,112},{96,64},{112,80},{1... | collective-permute-start | bytes 688136 | tf_op jit(solution)/shard_map/ppermute | solution.py:300
  81.2 1.3 %shard_map.61.refs_3_.w_ref = f32[256,384]{1,0:T(8,128)S(1)} custom-call(f32[256,512]{1,0:T(8,128)S(1)} %shard_map.55.refs_3_.w_ref, f32[64,512]{1,0:T(8,128)S(1)} %get-tuple-element.57.refs_2_.p_ref, f32[64,128]{1,0:T(8,128)S(1)} %get-tuple-element.61.m_ref, f32[64,512]{1,0:T(8,128)S(1)} %get-tuple-element.59.refs_2_.p2_ref, ...), custom_call_target="tpu_custom_call" | custom-call | flops 10000000 | bytes 1000000 | tf_op jit(solution)/shard_map/pallas_call | solution.py:286
  82.5 4.6 %collective-permute-done.10.refs_2_ = f32[64,896]{1,0:T(8,128)S(1)} collective-permute-done((f32[64,896]{1,0:T(8,128)S(1)}, f32[64,896]{1,0:T(8,128)S(1)}, u32[]{:S(2)}, u32[]{:S(2)}) %collective-permute-start.10) | collective-permute-done | bytes 229408 | tf_op jit(solution)/shard_map/ppermute | solution.py:300
  87.1 1.9 %shard_map.62 = (f32[64,384]{1,0:T(8,128)S(1)}, f32[64,128]{1,0:T(8,128)S(1)}, f32[64,512]{1,0:T(8,128)S(1)}) custom-call(f32[8,64]{1,0:T(8,128)S(1)} %copy-done, f32[64,896]{1,0:T(8,128)S(1)} %get-tuple-element.60.refs_1_, f32[64,896]{1,0:T(8,128)S(1)} %collective-permute-done.10.refs_2_, f32[256,384]{1,0:T(8,128)S(1)} %shard_map.61.refs_3_.w_ref, ...), custom_call_target="tpu_custom_call" | custom-call | flops 10000000 | bytes 1000000 | tf_op jit(solution)/shard_map/pallas_call | solution.py:286
  89.0 3.7 %collective-permute-start.11 = (f32[64,512]{1,0:T(8,128)S(1)}, f32[64,512]{1,0:T(8,128)S(1)}, u32[]{:S(2)}, u32[]{:S(2)}) collective-permute-start(f32[64,512]{1,0:T(8,128)S(1)} %get-tuple-element.63.refs_1_), channel_id=1, source_target_pairs={{0,64},{16,80},{32,96},{48,112},{64,0},{80,16},{96,32},{112,48},{1... | collective-permute-start | bytes 393224 | tf_op jit(solution)/shard_map/ppermute | solution.py:300
  92.6 1.1 shard_map.63.refs_3_.refs_0_
  93.7 4.9 %collective-permute-done.11.refs_2_ = f32[64,512]{1,0:T(8,128)S(1)} collective-permute-done((f32[64,512]{1,0:T(8,128)S(1)}, f32[64,512]{1,0:T(8,128)S(1)}, u32[]{:S(2)}, u32[]{:S(2)}) %collective-permute-start.11) | collective-permute-done | bytes 131104 | tf_op jit(solution)/shard_map/ppermute | solution.py:300
  98.6 1.9 %shard_map.64 = (f32[64,256]{1,0:T(8,128)S(1)}, f32[64,128]{1,0:T(8,128)S(1)}, f32[64,256]{1,0:T(8,128)S(1)}) custom-call(f32[8,64]{1,0:T(8,128)S(1)} %copy-done, f32[64,512]{1,0:T(8,128)S(1)} %get-tuple-element.63.refs_1_, f32[64,512]{1,0:T(8,128)S(1)} %collective-permute-done.11.refs_2_, f32[256,256]{1,0:T(8,128)S(1)} %shard_map.63.refs_3_.refs_0_, ...), custom_call_target="tpu_custom_call" | custom-call | flops 10000000 | bytes 1000000 | tf_op jit(solution)/shard_map/pallas_call | solution.py:286
  100.6 4.9 %collective-permute-start.12 = (f32[64,256]{1,0:T(8,128)S(1)}, f32[64,256]{1,0:T(8,128)S(1)}, u32[]{:S(2)}, u32[]{:S(2)}) collective-permute-start(f32[64,256]{1,0:T(8,128)S(1)} %get-tuple-element.68.refs_1_), channel_id=1, source_target_pairs={{0,224},{16,240},{32,192},{48,208},{64,160},{80,176},{96,128},{112... | collective-permute-start | bytes 196616 | tf_op jit(solution)/shard_map/ppermute | solution.py:300
  105.4 0.8 shard_map.65.refs_3_
  106.3 2.1 %collective-permute-done.12.refs_2_ = f32[64,256]{1,0:T(8,128)S(1)} collective-permute-done((f32[64,256]{1,0:T(8,128)S(1)}, f32[64,256]{1,0:T(8,128)S(1)}, u32[]{:S(2)}, u32[]{:S(2)}) %collective-permute-start.12) | collective-permute-done | bytes 65568 | tf_op jit(solution)/shard_map/ppermute | solution.py:300
  108.3 2.7 %shard_map.66 = f32[256,128]{1,0:T(8,128)} custom-call(f32[8,64]{1,0:T(8,128)S(1)} %copy-done, f32[64,256]{1,0:T(8,128)S(1)} %get-tuple-element.68.refs_1_, f32[64,256]{1,0:T(8,128)S(1)} %collective-permute-done.12.refs_2_, f32[256,256]{1,0:T(8,128)S(1)} %shard_map.65.refs_3_), custom_call_target="tpu_custom_call" | custom-call | flops 10000000 | bytes 1000000 | tf_op jit(solution)/shard_map/pallas_call | solution.py:286
Async XLA Ops:
  8.7 16.6 %collective-permute-start.2 = (f32[128,640]{1,0:T(8,128)S(1)}, f32[128,640]{1,0:T(8,128)S(1)}, u32[]{:S(2)}, u32[]{:S(2)}) collective-permute-start(f32[128,640]{1,0:T(8,128)S(1)} %get-tuple-element.42.yc_ref.refs_2_), channel_id=1, source_target_pairs={{0,1},{1,0},{2,3},{3,2},{4,5},{5,4},{6,7},{7,6},{8,9},{9,8},{10,11... | collective-permute-start | bytes 983048 | tf_op jit(solution)/shard_map/ppermute | solution.py:300
  11.0 12.1 %collective-permute-start.1 = (f32[64,640]{1,0:T(8,128)S(1)}, f32[64,640]{1,0:T(8,128)S(1)}, u32[]{:S(2)}, u32[]{:S(2)}) collective-permute-start(f32[64,640]{1,0:T(8,128)S(1)} %get-tuple-element.40.yb_ref.refs_1_), channel_id=1, source_target_pairs={{0,1},{1,0},{2,3},{3,2},{4,5},{5,4},{6,7},{7,6},{8,9},{9,8},{10,11... | collective-permute-start | bytes 491528 | tf_op jit(solution)/shard_map/ppermute | solution.py:300
  11.1 14.1 %collective-permute-start = (f32[64,640]{1,0:T(8,128)S(1)}, f32[64,640]{1,0:T(8,128)S(1)}, u32[]{:S(2)}, u32[]{:S(2)}) collective-permute-start(f32[64,640]{1,0:T(8,128)S(1)} %get-tuple-element.38.ya_ref.refs_0_), channel_id=1, source_target_pairs={{0,1},{1,0},{2,3},{3,2},{4,5},{5,4},{6,7},{7,6},{8,9},{9,8},{10,11... | collective-permute-start | bytes 491528 | tf_op jit(solution)/shard_map/ppermute | solution.py:300
  14.1 11.1 %copy-start = (f32[8,64]{1,0:T(8,128)S(1)}, f32[8,64]{1,0:T(8,128)}, u32[]{:S(2)}) copy-start(f32[8,64]{1,0:T(8,128)} %refs_0_.13) | copy-start | bytes 6148
  28.1 12.8 %collective-permute-start.4 = (f32[64,1664]{1,0:T(8,128)S(1)}, f32[64,1664]{1,0:T(8,128)S(1)}, u32[]{:S(2)}, u32[]{:S(2)}) collective-permute-start(f32[64,1664]{1,0:T(8,128)S(1)} %get-tuple-element.52.refs_1_), channel_id=1, source_target_pairs={{0,3},{1,2},{2,1},{3,0},{4,7},{5,6},{6,5},{7,4},{8,11},{9,10},{10,... | collective-permute-start | bytes 1277960 | tf_op jit(solution)/shard_map/ppermute | solution.py:300
  30.4 15.2 %collective-permute-start.3 = (f32[64,1280]{1,0:T(8,128)S(1)}, f32[64,1280]{1,0:T(8,128)S(1)}, u32[]{:S(2)}, u32[]{:S(2)}) collective-permute-start(f32[64,1280]{1,0:T(8,128)S(1)} %shard_map.52.refs_4_.refs_0_), channel_id=1, source_target_pairs={{0,3},{1,2},{2,1},{3,0},{4,7},{5,6},{6,5},{7,4},{8,11},{9,10},{10,... | collective-permute-start | bytes 983048 | tf_op jit(solution)/shard_map/ppermute | solution.py:300
  46.1 15.5 %collective-permute-start.5 = (f32[64,1280]{1,0:T(8,128)S(1)}, f32[64,1280]{1,0:T(8,128)S(1)}, u32[]{:S(2)}, u32[]{:S(2)}) collective-permute-start(f32[64,1280]{1,0:T(8,128)S(1)} %shard_map.54.refs_4_.refs_0_), channel_id=1, source_target_pairs={{0,4},{1,5},{2,6},{3,7},{4,0},{5,1},{6,2},{7,3},{8,12},{9,13},{10,... | collective-permute-start | bytes 983048 | tf_op jit(solution)/shard_map/ppermute | solution.py:300
  48.0 11.6 %collective-permute-start.6 = (f32[64,1024]{1,0:T(8,128)S(1)}, f32[64,1024]{1,0:T(8,128)S(1)}, u32[]{:S(2)}, u32[]{:S(2)}) collective-permute-start(f32[64,1024]{1,0:T(8,128)S(1)} %get-tuple-element.54.refs_1_), channel_id=1, source_target_pairs={{0,4},{1,5},{2,6},{3,7},{4,0},{5,1},{6,2},{7,3},{8,12},{9,13},{10,... | collective-permute-start | bytes 786440 | tf_op jit(solution)/shard_map/ppermute | solution.py:300
  62.2 12.8 %collective-permute-start.7 = (f32[64,1280]{1,0:T(8,128)S(1)}, f32[64,1280]{1,0:T(8,128)S(1)}, u32[]{:S(2)}, u32[]{:S(2)}) collective-permute-start(f32[64,1280]{1,0:T(8,128)S(1)} %shard_map.57.refs_4_.refs_0_), channel_id=1, source_target_pairs={{0,12},{1,13},{2,14},{3,15},{4,8},{5,9},{6,10},{7,11},{8,4},{9,5},... | collective-permute-start | bytes 983048 | tf_op jit(solution)/shard_map/ppermute | solution.py:300
  65.4 8.0 %collective-permute-start.8 = (f32[64,512]{1,0:T(8,128)S(1)}, f32[64,512]{1,0:T(8,128)S(1)}, u32[]{:S(2)}, u32[]{:S(2)}) collective-permute-start(f32[64,512]{1,0:T(8,128)S(1)} %get-tuple-element.58.refs_1_), channel_id=1, source_target_pairs={{0,12},{1,13},{2,14},{3,15},{4,8},{5,9},{6,10},{7,11},{8,4},{9,5},... | collective-permute-start | bytes 393224 | tf_op jit(solution)/shard_map/ppermute | solution.py:300
  75.5 1.7 %collective-permute-start.9 = (f32[64,1280]{1,0:T(8,128)S(1)}, f32[64,1280]{1,0:T(8,128)S(1)}, u32[]{:S(2)}, u32[]{:S(2)}) collective-permute-start(f32[64,1280]{1,0:T(8,128)S(1)} %shard_map.59.refs_1_.refs_4_), channel_id=1, source_target_pairs={{0,16},{16,0},{32,48},{48,32},{64,80},{80,64},{96,112},{112,96},{1... | collective-permute-start | bytes 983048 | tf_op jit(solution)/shard_map/ppermute | solution.py:300
  79.2 7.9 %collective-permute-start.10 = (f32[64,896]{1,0:T(8,128)S(1)}, f32[64,896]{1,0:T(8,128)S(1)}, u32[]{:S(2)}, u32[]{:S(2)}) collective-permute-start(f32[64,896]{1,0:T(8,128)S(1)} %get-tuple-element.60.refs_1_), channel_id=1, source_target_pairs={{0,32},{16,48},{32,0},{48,16},{64,96},{80,112},{96,64},{112,80},{1... | collective-permute-start | bytes 688136 | tf_op jit(solution)/shard_map/ppermute | solution.py:300
  89.0 9.6 %collective-permute-start.11 = (f32[64,512]{1,0:T(8,128)S(1)}, f32[64,512]{1,0:T(8,128)S(1)}, u32[]{:S(2)}, u32[]{:S(2)}) collective-permute-start(f32[64,512]{1,0:T(8,128)S(1)} %get-tuple-element.63.refs_1_), channel_id=1, source_target_pairs={{0,64},{16,80},{32,96},{48,112},{64,0},{80,16},{96,32},{112,48},{1... | collective-permute-start | bytes 393224 | tf_op jit(solution)/shard_map/ppermute | solution.py:300
  100.6 7.8 %collective-permute-start.12 = (f32[64,256]{1,0:T(8,128)S(1)}, f32[64,256]{1,0:T(8,128)S(1)}, u32[]{:S(2)}, u32[]{:S(2)}) collective-permute-start(f32[64,256]{1,0:T(8,128)S(1)} %get-tuple-element.68.refs_1_), channel_id=1, source_target_pairs={{0,224},{16,240},{32,192},{48,208},{64,160},{80,176},{96,128},{112... | collective-permute-start | bytes 196616 | tf_op jit(solution)/shard_map/ppermute | solution.py:300

commit v7 on v6

--- a/solution.py
+++ b/solution.py
@@ -13,6 +13,7 @@
 WIDTH = LEVELS * R + NRHS
 NB = 16
 SPLIT = 4
+HALVED = (6, 7)
 F32 = jnp.float32
 HI = lax.Precision.HIGHEST
 
@@ -25,12 +26,24 @@
     return WIDTH - start_of(level)
 
 
-def offsets(first, last=LEVELS):
+def shared(first):
+    return {2: (2, 4), 5: (6, 8), 6: (6, 8)}.get(first, (0, 0))
+
+
+def last_of(first):
+    return SPLIT if first <= SPLIT else LEVELS
+
+
+def offsets(first):
     out, at = {}, 0
-    for level in range(first, last + 1):
+    for level in range(first, last_of(first) + 1):
         out[level] = at
-        at += width_of(level)
+        at += width_in(first, level)
     return out, at
+
+
+def width_in(first, level):
+    return width_of(level) - (128 if level == shared(first)[1] else 0)
 
 
 def mm(a, b):
@@ -159,23 +172,38 @@
     return mm_t(y[:, st : st + 128], y[:, st:])
 
 
-def last_of(first):
-    return SPLIT if first <= SPLIT else LEVELS
-
-
 def row_block(grams, level):
     h = R * ((level - 1) % 2)
     return grams[(level - 1) // 2][h : h + R, :]
 
 
+def pack(first, blocks):
+    host, guest = shared(first)
+    out = dict(blocks)
+    if host:
+        lane = lax.broadcasted_iota(jnp.int32, (R, 128), 1)
+        moved = pltpu.roll(blocks[guest][:, :128], R, 1)
+        tile = jnp.where(lane < R, moved, blocks[host][:, :128])
+        out[host] = jnp.concatenate([tile, blocks[host][:, 128:]], axis=1)
+        out[guest] = blocks[guest][:, 128:]
+    return out
+
+
+def packed(first, value, level):
+    o = offsets(first)[0][level]
+    return value[:, o : o + width_in(first, level)]
+
+
+def unpack(first, value, level):
+    host, guest = shared(first)
+    if level != guest:
+        return value(level)
+    return jnp.concatenate([pltpu.roll(value(host)[:, :128], R, 1), value(level)], axis=1)
+
+
 def put(ref, first, level, value):
     o = offsets(first)[0][level]
-    ref[:, o : o + width_of(level)] = value
-
-
-def get(ref, first, level):
-    o = offsets(first)[0][level]
-    return ref[:, o : o + width_of(level)]
+    ref[:, o : o + width_in(first, level)] = value
 
 
 def gram_pairs(y_refs, pairs):
@@ -187,8 +215,10 @@
     grams = gram_pairs((ya_ref, yb_ref, yc_ref), range(4))
     for level in range(1, SPLIT + 1):
         put(near_ref, 1, level, row_block(grams, level))
-    for level in range(SPLIT + 1, LEVELS + 1):
-        put(far_ref, SPLIT + 1, level, row_block(grams, level))
+    first = SPLIT + 1
+    blocks = pack(first, {level: row_block(grams, level) for level in range(first, LEVELS + 1)})
+    for level, value in blocks.items():
+        put(far_ref, first, level, value)
 
 
 def reduce_level(k, coupling_ref, rows, p_ref, m_ref):
@@ -215,43 +245,77 @@
 
 
 def next_level(k, p, trailing, n_ref):
-    last = last_of(k + 1) if k != SPLIT else SPLIT
-    if k < last:
-        grams = schur(k, p, k + 1, last)
-        for level in range(k + 1, last + 1):
-            put(n_ref, k + 1, level, trailing(level) - row_block(grams, level))
+    first, last = k + 1, last_of(k)
+    if k >= last:
+        return
+    grams = schur(k, p, first, last)
+    less = {level: row_block(grams, level) for level in range(first, last + 1)}
+    if shared(first)[0] and shared(first) == shared(k):
+        less = pack(first, less)
+        blocks = {level: trailing(level) - less[level] for level in less}
+    else:
+        blocks = pack(first, {level: unpack(k, trailing, level) - less[level] for level in less})
+    for level, value in blocks.items():
+        put(n_ref, first, level, value)
+
+
+def on_core0():
+    return lax.rem(lax.axis_index("group"), 2) == 0
+
+
+def next_half(n_ref, h_ref):
+    h_ref[...] = jnp.where(on_core0(), n_ref[: R // 2, :], n_ref[R // 2 :, :])
 
 
 def first_level_kernel(c_ref, own_ref, ya_ref, yb_ref, yc_ref, dep_ref, p_ref, m_ref, n_ref):
     grams = gram_pairs((ya_ref, yb_ref, yc_ref), range(SPLIT // 2))
 
     def part(level):
-        return get(own_ref, 1, level) + row_block(grams, level)
+        return packed(1, own_ref, level) + row_block(grams, level)
 
     p = reduce_level(1, c_ref, part(1), p_ref, m_ref)
     next_level(1, p, part, n_ref)
 
 
-def level_kernel(k, c_ref, own_ref, got_ref, dep_ref, dep2_ref, p_ref, m_ref, n_ref=None):
+def level_kernel(k, c_ref, own_ref, got_ref, dep_ref, dep2_ref, p_ref, m_ref, n_ref=None, h_ref=None):
     def part(level):
-        return get(own_ref, k, level) + get(got_ref, k, level)
+        return packed(k, own_ref, level) + packed(k, got_ref, level)
 
     p = reduce_level(k, c_ref, part(k), p_ref, m_ref)
     next_level(k, p, part, n_ref)
+    if h_ref is not None:
+        next_half(n_ref, h_ref)
+
+
+def halves_level_kernel(k, c_ref, own_ref, got_ref, other_ref, dep_ref, p_ref, m_ref, n_ref, h_ref=None):
+    core0 = on_core0()
+
+    def part(level):
+        mine, theirs = packed(k, got_ref, level), packed(k, other_ref, level)
+        got = [jnp.where(core0, mine, theirs), jnp.where(core0, theirs, mine)]
+        return packed(k, own_ref, level) + jnp.concatenate(got, axis=0)
+
+    p = reduce_level(k, c_ref, part(k), p_ref, m_ref)
+    next_level(k, p, part, n_ref)
+    if h_ref is not None:
+        next_half(n_ref, h_ref)
 
 
 def first_far_kernel(own_ref, ya_ref, yb_ref, yc_ref, p_ref, n_ref):
+    first = SPLIT + 1
     grams = gram_pairs((ya_ref, yb_ref, yc_ref), range(SPLIT // 2, LEVELS // 2))
-    less = schur(1, p_ref[...], SPLIT + 1, LEVELS)
-    for level in range(SPLIT + 1, LEVELS + 1):
-        put(n_ref, SPLIT + 1, level, get(own_ref, SPLIT + 1, level) + row_block(grams, level) - row_block(less, level))
+    less = schur(1, p_ref[...], first, LEVELS)
+    more = {level: row_block(grams, level) - row_block(less, level) for level in range(first, LEVELS + 1)}
+    for level, value in pack(first, more).items():
+        put(n_ref, first, level, packed(first, own_ref, level) + value)
 
 
 def far_kernel(k, own_ref, got_ref, p_ref, n_ref):
-    less = schur(k, p_ref[...], SPLIT + 1, LEVELS)
-    for level in range(SPLIT + 1, LEVELS + 1):
-        both = get(own_ref, SPLIT + 1, level) + get(got_ref, SPLIT + 1, level)
-        put(n_ref, SPLIT + 1, level, both - row_block(less, level))
+    first = SPLIT + 1
+    less = schur(k, p_ref[...], first, LEVELS)
+    for level, value in pack(first, {level: row_block(less, level) for level in range(first, LEVELS + 1)}).items():
+        both = packed(first, own_ref, level) + packed(first, got_ref, level)
+        put(n_ref, first, level, both - value)
 
 
 def apply_level(k, w, p, minv):
@@ -321,20 +385,26 @@
     )
     got_y = (got_a, got_b, exchange(yc, 1))
     far_shape = (R, offsets(SPLIT + 1)[1])
-    near, far = call(gram_kernel, [(R, offsets(1, SPLIT)[1]), far_shape], ya, yb, yc)
+    near, far = call(gram_kernel, [(R, offsets(1)[1]), far_shape], ya, yb, yc)
     (w,) = call(back_kernel, [(M, WIDTH)], ya, yb, yc, za, zb, zc, ma, mb, mc)
     got = far_got = None
     dep = w
     for k in range(1, LEVELS):
         outs = [(R, width_of(k)), (R, 128)]
         if k != SPLIT:
-            outs.append((R, offsets(k + 1, last_of(k + 1))[1]))
+            outs.append((R, offsets(k + 1)[1]))
+        if k + 1 in HALVED:
+            outs.append((R // 2, offsets(k + 1)[1]))
         if k == 1:
-            p, minv, near = call(first_level_kernel, outs, coupling, near, *got_y, w, hbm=(5,))
+            p, minv, near = call(first_level_kernel, outs, coupling, near, *got_y, dep, hbm=(5,))
+            more = [near]
+        elif k in HALVED:
+            kernel = lambda *refs, k=k: halves_level_kernel(k, *refs)
+            p, minv, *more = call(kernel, outs, coupling, near, got, other, dep, hbm=(4,))
         else:
             kernel = lambda *refs, k=k: level_kernel(k, *refs)
             p, minv, *more = call(kernel, outs, coupling, near, got, dep, far, hbm=(3, 4))
-            near = more[0] if more else None
+        near = more[0] if more else None
         if k < SPLIT:
             got = exchange(near, k + 1)
         if k == 1:
@@ -346,7 +416,10 @@
             far_got = exchange(far, k + 1)
         if k == SPLIT:
             near = far
-        if k >= SPLIT:
+        if k + 1 in HALVED:
+            got = exchange(more[1], k + 1)
+            other = exchange(got, SPLIT + 1)
+        elif k >= SPLIT:
             got = exchange(near, k + 1)
         if k == LEVELS - 1:
             kernel = lambda *refs, k=k: apply_kernel(k, *refs)

time: 113 us -> 109 us (0.965)
  the two profiles are of different devices: /device:TPU:2 before, /device:TPU:1 now
where the time goes in v7:
time: 109 us
  waiting for transfers between devices  43.6 us (40%)
  Pallas kernels  36.1 us (33%)
  starting transfers between devices  29 us (27%)
    ppermute x15, waiting for transfers between devices, exchange(): lax.ppermute(value, axis, [(s, s ^ mask) for s in range(lax.axis_size(axi...  43.6 us
    pallas_call x21, Pallas kernels, call(): pl.pallas_call(kernel, out_shape=shapes, in_specs=[hb if i in hbm else vm...  36.1 us
    ppermute x15, starting transfers between devices, exchange(): lax.ppermute(value, axis, [(s, s ^ mask) for s in range(lax.axis_size(axi...  29 us
  transfers between devices with their start and end apart: 15, of which 10 were waited for; matrix products, arithmetic and copies ran while one was open for 0% of the time, Pallas kernels for 13%

profile of v7, /device:TPU:1, one launch (start us, length us, event | category | flops | bytes accessed | tf_op | source)
XLA Modules:
  0.0 108.9 jit_solution(5842491506444680449)
XLA Ops:
  0.0 3.2 %shard_map.46 = (f32[64,640]{1,0:T(8,128)S(1)}, f32[64,256]{1,0:T(8,128)S(1)}, f32[64,128]{1,0:T(8,128)S(1)}, f32[192,896]{1,0:T(8,128)S(1)}) custom-call(f32[256,256]{1,0:T(8,128)} %d_any.1, f32[256,512]{1,0:T(8,128)} %b_any.1, f32[256,128]{1,0:T(8,128)} %t_any.1), custom_call_target="tpu_custom_call" | custom-call | flops 10000000 | bytes 1000000 | tf_op jit(solution)/shard_map/pallas_call | solution.py:350
  3.2 2.0 %shard_map.47 = (f32[64,640]{1,0:T(8,128)S(1)}, f32[64,256]{1,0:T(8,128)S(1)}, f32[64,128]{1,0:T(8,128)S(1)}, f32[128,768]{1,0:T(8,128)S(1)}) custom-call(f32[192,896]{1,0:T(8,128)S(1)} %get-tuple-element.41.aug_ref), custom_call_target="tpu_custom_call" | custom-call | flops 10000000 | bytes 1000000 | tf_op jit(solution)/shard_map/pallas_call | solution.py:350
  5.3 3.4 %shard_map.48 = (f32[128,640]{1,0:T(8,128)S(1)}, f32[128,128]{1,0:T(8,128)S(1)}, f32[128,128]{1,0:T(8,128)S(1)}) custom-call(f32[128,768]{1,0:T(8,128)S(1)} %get-tuple-element.43.aug_ref), custom_call_target="tpu_custom_call" | custom-call | flops 10000000 | bytes 1000000 | tf_op jit(solution)/shard_map/pallas_call | solution.py:350
  8.7 2.1 %collective-permute-start.2 = (f32[128,640]{1,0:T(8,128)S(1)}, f32[128,640]{1,0:T(8,128)S(1)}, u32[]{:S(2)}, u32[]{:S(2)}) collective-permute-start(f32[128,640]{1,0:T(8,128)S(1)} %get-tuple-element.44.yc_ref.refs_2_), channel_id=1, source_target_pairs={{0,1},{1,0},{2,3},{3,2},{4,5},{5,4},{6,7},{7,6},{8,9},{9,8},{10,11... | collective-permute-start | bytes 983048 | tf_op jit(solution)/shard_map/ppermute | solution.py:364
  10.8 0.1 collective-permute-start.1
  10.9 1.4 %collective-permute-start = (f32[64,640]{1,0:T(8,128)S(1)}, f32[64,640]{1,0:T(8,128)S(1)}, u32[]{:S(2)}, u32[]{:S(2)}) collective-permute-start(f32[64,640]{1,0:T(8,128)S(1)} %get-tuple-element.40.ya_ref.refs_0_), channel_id=1, source_target_pairs={{0,1},{1,0},{2,3},{3,2},{4,5},{5,4},{6,7},{7,6},{8,9},{9,8},{10,11... | collective-permute-start | bytes 491528 | tf_op jit(solution)/shard_map/ppermute | solution.py:364
  12.3 1.1 %shard_map.49 = (f32[64,2304]{1,0:T(8,128)S(1)}, f32[64,1152]{1,0:T(8,128)S(1)}) custom-call(f32[64,640]{1,0:T(8,128)S(1)} %get-tuple-element.40.ya_ref.refs_0_, f32[64,640]{1,0:T(8,128)S(1)} %get-tuple-element.42.yb_ref.refs_1_, f32[128,640]{1,0:T(8,128)S(1)} %get-tuple-element.44.yc_ref.refs_2_), custom_call_target="tpu_custom_call" | custom-call | flops 10000000 | bytes 1000000 | tf_op jit(solution)/shard_map/pallas_call | solution.py:350
  13.4 0.0 copy-start
  13.4 2.3 %shard_map.50.dep_ref.refs_3_.w_ref = f32[256,640]{1,0:T(8,128)S(1)} custom-call(f32[64,640]{1,0:T(8,128)S(1)} %get-tuple-element.40.ya_ref.refs_0_, f32[64,640]{1,0:T(8,128)S(1)} %get-tuple-element.42.yb_ref.refs_1_, f32[128,640]{1,0:T(8,128)S(1)} %get-tuple-element.44.yc_ref.refs_2_, f32[64,256]{1,0:T(8,128)S(1)} %get-tuple-element.47.refs_3_, ...), custom_call_target="tpu_custom_call" | custom-call | flops 10000000 | bytes 1000000 | tf_op jit(solution)/shard_map/pallas_call | solution.py:350
  15.7 4.8 %collective-permute-done.1.yb_ref = f32[64,640]{1,0:T(8,128)S(1)} collective-permute-done((f32[64,640]{1,0:T(8,128)S(1)}, f32[64,640]{1,0:T(8,128)S(1)}, u32[]{:S(2)}, u32[]{:S(2)}) %collective-permute-start.1) | collective-permute-done | bytes 163872 | tf_op jit(solution)/shard_map/ppermute | solution.py:364
  20.5 3.5 %collective-permute-done.ya_ref = f32[64,640]{1,0:T(8,128)S(1)} collective-permute-done((f32[64,640]{1,0:T(8,128)S(1)}, f32[64,640]{1,0:T(8,128)S(1)}, u32[]{:S(2)}, u32[]{:S(2)}) %collective-permute-start) | collective-permute-done | bytes 163872 | tf_op jit(solution)/shard_map/ppermute | solution.py:364
  24.0 0.0 collective-permute-done.2.yc_ref
  24.0 0.0 copy-done
  24.0 2.8 %shard_map.51 = (f32[64,640]{1,0:T(8,128)S(1)}, f32[64,128]{1,0:T(8,128)S(1)}, f32[64,1536]{1,0:T(8,128)S(1)}) custom-call(f32[8,64]{1,0:T(8,128)S(1)} %copy-done, f32[64,2304]{1,0:T(8,128)S(1)} %get-tuple-element.46.own_ref, f32[64,640]{1,0:T(8,128)S(1)} %collective-permute-done.ya_ref, f32[64,640]{1,0:T(8,128)S(1)} %collective-permute-done.1.yb_ref, ...), custom_call_target="tpu_custom_call" | custom-call | flops 10000000 | bytes 1000000 | tf_op jit(solution)/shard_map/pallas_call | solution.py:350
  26.8 3.8 %collective-permute-start.4 = (f32[64,1536]{1,0:T(8,128)S(1)}, f32[64,1536]{1,0:T(8,128)S(1)}, u32[]{:S(2)}, u32[]{:S(2)}) collective-permute-start(f32[64,1536]{1,0:T(8,128)S(1)} %get-tuple-element.54.refs_1_), channel_id=1, source_target_pairs={{0,3},{1,2},{2,1},{3,0},{4,7},{5,6},{6,5},{7,4},{8,11},{9,10},{10,... | collective-permute-start | bytes 1179656 | tf_op jit(solution)/shard_map/ppermute | solution.py:364
  30.6 0.8 shard_map.52.refs_4_.refs_0_
  31.4 0.1 collective-permute-start.3
  31.5 6.8 %collective-permute-done.4.refs_2_ = f32[64,1536]{1,0:T(8,128)S(1)} collective-permute-done((f32[64,1536]{1,0:T(8,128)S(1)}, f32[64,1536]{1,0:T(8,128)S(1)}, u32[]{:S(2)}, u32[]{:S(2)}) %collective-permute-start.4) | collective-permute-done | bytes 393248 | tf_op jit(solution)/shard_map/ppermute | solution.py:364
  38.3 2.0 %shard_map.53 = (f32[64,640]{1,0:T(8,128)S(1)}, f32[64,128]{1,0:T(8,128)S(1)}, f32[64,1024]{1,0:T(8,128)S(1)}) custom-call(f32[8,64]{1,0:T(8,128)S(1)} %copy-done, f32[64,1536]{1,0:T(8,128)S(1)} %get-tuple-element.54.refs_1_, f32[64,1536]{1,0:T(8,128)S(1)} %collective-permute-done.4.refs_2_, f32[256,640]{1,0:T(8,128)S(1)} %shard_map.50.dep_ref.refs_3_.w_ref, ...), custom_call_target="tpu_custom_call" | custom-call | flops 10000000 | bytes 1000000 | tf_op jit(solution)/shard_map/pallas_call | solution.py:350
  40.3 4.3 %collective-permute-done.3.refs_1_ = f32[64,1152]{1,0:T(8,128)S(1)} collective-permute-done((f32[64,1152]{1,0:T(8,128)S(1)}, f32[64,1152]{1,0:T(8,128)S(1)}, u32[]{:S(2)}, u32[]{:S(2)}) %collective-permute-start.3) | collective-permute-done | bytes 294944 | tf_op jit(solution)/shard_map/ppermute | solution.py:364
  44.6 0.5 shard_map.54.refs_4_.refs_0_
  45.2 1.5 %collective-permute-start.5 = (f32[64,1152]{1,0:T(8,128)S(1)}, f32[64,1152]{1,0:T(8,128)S(1)}, u32[]{:S(2)}, u32[]{:S(2)}) collective-permute-start(f32[64,1152]{1,0:T(8,128)S(1)} %shard_map.54.refs_4_.refs_0_), channel_id=1, source_target_pairs={{0,4},{1,5},{2,6},{3,7},{4,0},{5,1},{6,2},{7,3},{8,12},{9,13},{10,... | collective-permute-start | bytes 884744 | tf_op jit(solution)/shard_map/ppermute | solution.py:364
  46.7 0.3 collective-permute-start.6
  47.0 1.4 %shard_map.55.refs_3_.w_ref = f32[256,512]{1,0:T(8,128)S(1)} custom-call(f32[256,640]{1,0:T(8,128)S(1)} %shard_map.50.dep_ref.refs_3_.w_ref, f32[64,640]{1,0:T(8,128)S(1)} %get-tuple-element.53.p_ref, f32[64,128]{1,0:T(8,128)S(1)} %get-tuple-element.57.m_ref, f32[64,640]{1,0:T(8,128)S(1)} %get-tuple-element.55.refs_2_.p2_ref, ...), custom_call_target="tpu_custom_call" | custom-call | flops 10000000 | bytes 1000000 | tf_op jit(solution)/shard_map/pallas_call | solution.py:350
  48.4 8.7 %collective-permute-done.6.refs_2_ = f32[64,1024]{1,0:T(8,128)S(1)} collective-permute-done((f32[64,1024]{1,0:T(8,128)S(1)}, f32[64,1024]{1,0:T(8,128)S(1)}, u32[]{:S(2)}, u32[]{:S(2)}) %collective-permute-start.6) | collective-permute-done | bytes 262176 | tf_op jit(solution)/shard_map/ppermute | solution.py:364
  57.1 2.0 %shard_map.56 = (f32[64,512]{1,0:T(8,128)S(1)}, f32[64,128]{1,0:T(8,128)S(1)}, f32[64,512]{1,0:T(8,128)S(1)}) custom-call(f32[8,64]{1,0:T(8,128)S(1)} %copy-done, f32[64,1024]{1,0:T(8,128)S(1)} %get-tuple-element.56.refs_1_, f32[64,1024]{1,0:T(8,128)S(1)} %collective-permute-done.6.refs_2_, f32[256,512]{1,0:T(8,128)S(1)} %shard_map.55.refs_3_.w_ref, ...), custom_call_target="tpu_custom_call" | custom-call | flops 10000000 | bytes 1000000 | tf_op jit(solution)/shard_map/pallas_call | solution.py:350
  59.1 0.0 collective-permute-done.5.refs_1_
  59.1 0.5 shard_map.57.refs_4_.refs_0_
  59.7 2.9 %collective-permute-start.7 = (f32[64,1152]{1,0:T(8,128)S(1)}, f32[64,1152]{1,0:T(8,128)S(1)}, u32[]{:S(2)}, u32[]{:S(2)}) collective-permute-start(f32[64,1152]{1,0:T(8,128)S(1)} %shard_map.57.refs_4_.refs_0_), channel_id=1, source_target_pairs={{0,12},{1,13},{2,14},{3,15},{4,8},{5,9},{6,10},{7,11},{8,4},{9,5},... | collective-permute-start | bytes 884744 | tf_op jit(solution)/shard_map/ppermute | solution.py:364
  62.6 0.1 collective-permute-start.8
  62.7 6.8 %collective-permute-done.8.refs_2_ = f32[64,512]{1,0:T(8,128)S(1)} collective-permute-done((f32[64,512]{1,0:T(8,128)S(1)}, f32[64,512]{1,0:T(8,128)S(1)}, u32[]{:S(2)}, u32[]{:S(2)}) %collective-permute-start.8) | collective-permute-done | bytes 131104 | tf_op jit(solution)/shard_map/ppermute | solution.py:364
  69.4 1.6 %shard_map.58 = (f32[64,512]{1,0:T(8,128)S(1)}, f32[64,128]{1,0:T(8,128)S(1)}) custom-call(f32[8,64]{1,0:T(8,128)S(1)} %copy-done, f32[64,512]{1,0:T(8,128)S(1)} %get-tuple-element.60.refs_1_, f32[64,512]{1,0:T(8,128)S(1)} %collective-permute-done.8.refs_2_, f32[256,512]{1,0:T(8,128)S(1)} %shard_map.55.refs_3_.w_ref, f32[64,1152]{1,0:T(8,128)S(1)} %shard_map.57.refs_4_.refs_0_), custom_call_target="tpu_custom_call" | custom-call | flops 10000000 | bytes 1000000 | tf_op jit(solution)/shard_map/pallas_call | solution.py:350
  71.0 0.0 collective-permute-done.7.refs_1_
  71.1 0.5 shard_map.59.refs_1_.refs_4_
  71.6 4.0 %collective-permute-start.9 = (f32[64,1152]{1,0:T(8,128)S(1)}, f32[64,1152]{1,0:T(8,128)S(1)}, u32[]{:S(2)}, u32[]{:S(2)}) collective-permute-start(f32[64,1152]{1,0:T(8,128)S(1)} %shard_map.59.refs_1_.refs_4_), channel_id=1, source_target_pairs={{0,16},{16,0},{32,48},{48,32},{64,80},{80,64},{96,112},{112,96},{1... | collective-permute-start | bytes 884744 | tf_op jit(solution)/shard_map/ppermute | solution.py:364
  75.6 1.2 %collective-permute-done.9.refs_2_ = f32[64,1152]{1,0:T(8,128)S(1)} collective-permute-done((f32[64,1152]{1,0:T(8,128)S(1)}, f32[64,1152]{1,0:T(8,128)S(1)}, u32[]{:S(2)}, u32[]{:S(2)}) %collective-permute-start.9) | collective-permute-done | bytes 294944 | tf_op jit(solution)/shard_map/ppermute | solution.py:364
  76.8 2.1 %shard_map.60 = (f32[64,384]{1,0:T(8,128)S(1)}, f32[64,128]{1,0:T(8,128)S(1)}, f32[64,768]{1,0:T(8,128)S(1)}, f32[32,768]{1,0:T(8,128)S(1)}) custom-call(f32[8,64]{1,0:T(8,128)S(1)} %copy-done, f32[64,1152]{1,0:T(8,128)S(1)} %shard_map.59.refs_1_.refs_4_, f32[64,1152]{1,0:T(8,128)S(1)} %collective-permute-done.9.refs_2_, ...), custom_call_target="tpu_custom_call" | custom-call | flops 10000000 | bytes 1000000 | tf_op jit(solution)/shard_map/pallas_call | solution.py:350
  78.9 1.8 %collective-permute-start.10 = (f32[32,768]{1,0:T(8,128)S(1)}, f32[32,768]{1,0:T(8,128)S(1)}, u32[]{:S(2)}, u32[]{:S(2)}) collective-permute-start(f32[32,768]{1,0:T(8,128)S(1)} %get-tuple-element.63), channel_id=1, source_target_pairs={{0,32},{16,48},{32,0},{48,16},{64,96},{80,112},{96,64},{112,80},{1... | collective-permute-start | bytes 294920 | tf_op jit(solution)/shard_map/ppermute | solution.py:364
  80.7 2.8 %collective-permute-done.10.refs_2_ = f32[32,768]{1,0:T(8,128)S(1)} collective-permute-done((f32[32,768]{1,0:T(8,128)S(1)}, f32[32,768]{1,0:T(8,128)S(1)}, u32[]{:S(2)}, u32[]{:S(2)}) %collective-permute-start.10) | collective-permute-done | bytes 98336 | tf_op jit(solution)/shard_map/ppermute | solution.py:364
  83.5 1.0 collective-permute-start.11
  84.5 1.3 %shard_map.61.refs_4_.w_ref = f32[256,384]{1,0:T(8,128)S(1)} custom-call(f32[256,512]{1,0:T(8,128)S(1)} %shard_map.55.refs_3_.w_ref, f32[64,512]{1,0:T(8,128)S(1)} %get-tuple-element.59.refs_2_.p_ref, f32[64,128]{1,0:T(8,128)S(1)} %get-tuple-element.64.m_ref, f32[64,512]{1,0:T(8,128)S(1)} %get-tuple-element.61.refs_2_.p2_ref, ...), custom_call_target="tpu_custom_call" | custom-call | flops 10000000 | bytes 1000000 | tf_op jit(solution)/shard_map/pallas_call | solution.py:350
  85.8 0.0 collective-permute-done.11.refs_3_
  85.8 1.9 %shard_map.62 = (f32[64,384]{1,0:T(8,128)S(1)}, f32[64,128]{1,0:T(8,128)S(1)}, f32[64,512]{1,0:T(8,128)S(1)}, f32[32,512]{1,0:T(8,128)S(1)}) custom-call(f32[8,64]{1,0:T(8,128)S(1)} %copy-done, f32[64,768]{1,0:T(8,128)S(1)} %get-tuple-element.62.refs_1_, f32[32,768]{1,0:T(8,128)S(1)} %collective-permute-done.10.refs_2_, ...), custom_call_target="tpu_custom_call" | custom-call | flops 10000000 | bytes 1000000 | tf_op jit(solution)/shard_map/pallas_call | solution.py:350
  87.7 3.0 %collective-permute-start.12 = (f32[32,512]{1,0:T(8,128)S(1)}, f32[32,512]{1,0:T(8,128)S(1)}, u32[]{:S(2)}, u32[]{:S(2)}) collective-permute-start(f32[32,512]{1,0:T(8,128)S(1)} %get-tuple-element.67), channel_id=1, source_target_pairs={{0,64},{16,80},{32,96},{48,112},{64,0},{80,16},{96,32},{112,48},{1... | collective-permute-start | bytes 196616 | tf_op jit(solution)/shard_map/ppermute | solution.py:364
  90.7 2.5 %collective-permute-done.12.refs_2_ = f32[32,512]{1,0:T(8,128)S(1)} collective-permute-done((f32[32,512]{1,0:T(8,128)S(1)}, f32[32,512]{1,0:T(8,128)S(1)}, u32[]{:S(2)}, u32[]{:S(2)}) %collective-permute-start.12) | collective-permute-done | bytes 65568 | tf_op jit(solution)/shard_map/ppermute | solution.py:364
  93.2 2.0 %collective-permute-start.13 = (f32[32,512]{1,0:T(8,128)S(1)}, f32[32,512]{1,0:T(8,128)S(1)}, u32[]{:S(2)}, u32[]{:S(2)}) collective-permute-start(f32[32,512]{1,0:T(8,128)S(1)} %collective-permute-done.12.refs_2_), channel_id=1, source_target_pairs={{0,16},{16,0},{32,48},{48,32},{64,80},{80,64},{96,112},{112,96},{1... | collective-permute-start | bytes 196616 | tf_op jit(solution)/shard_map/ppermute | solution.py:364
  95.2 1.1 shard_map.63.refs_4_.refs_0_
  96.2 0.0 collective-permute-done.13.refs_3_
  96.2 1.9 %shard_map.64 = (f32[64,256]{1,0:T(8,128)S(1)}, f32[64,128]{1,0:T(8,128)S(1)}, f32[64,256]{1,0:T(8,128)S(1)}) custom-call(f32[8,64]{1,0:T(8,128)S(1)} %copy-done, f32[64,512]{1,0:T(8,128)S(1)} %get-tuple-element.66.refs_1_, f32[32,512]{1,0:T(8,128)S(1)} %collective-permute-done.12.refs_2_, f32[32,512]{1,0:T(8,128)S(1)} %collective-permute-done.13.refs_3_, ...), custom_call_target="tpu_custom_call" | custom-call | flops 10000000 | bytes 1000000 | tf_op jit(solution)/shard_map/pallas_call | solution.py:350
  98.2 4.9 %collective-permute-start.14 = (f32[64,256]{1,0:T(8,128)S(1)}, f32[64,256]{1,0:T(8,128)S(1)}, u32[]{:S(2)}, u32[]{:S(2)}) collective-permute-start(f32[64,256]{1,0:T(8,128)S(1)} %get-tuple-element.72.refs_1_), channel_id=1, source_target_pairs={{0,224},{16,240},{32,192},{48,208},{64,160},{80,176},{96,128},{112... | collective-permute-start | bytes 196616 | tf_op jit(solution)/shard_map/ppermute | solution.py:364
  103.1 0.8 shard_map.65.refs_3_
  103.9 2.3 %collective-permute-done.14.refs_2_ = f32[64,256]{1,0:T(8,128)S(1)} collective-permute-done((f32[64,256]{1,0:T(8,128)S(1)}, f32[64,256]{1,0:T(8,128)S(1)}, u32[]{:S(2)}, u32[]{:S(2)}) %collective-permute-start.14) | collective-permute-done | bytes 65568 | tf_op jit(solution)/shard_map/ppermute | solution.py:364
  106.2 2.7 %shard_map.66 = f32[256,128]{1,0:T(8,128)} custom-call(f32[8,64]{1,0:T(8,128)S(1)} %copy-done, f32[64,256]{1,0:T(8,128)S(1)} %get-tuple-element.72.refs_1_, f32[64,256]{1,0:T(8,128)S(1)} %collective-permute-done.14.refs_2_, f32[256,256]{1,0:T(8,128)S(1)} %shard_map.65.refs_3_), custom_call_target="tpu_custom_call" | custom-call | flops 10000000 | bytes 1000000 | tf_op jit(solution)/shard_map/pallas_call | solution.py:350
Async XLA Ops:
  8.7 15.3 %collective-permute-start.2 = (f32[128,640]{1,0:T(8,128)S(1)}, f32[128,640]{1,0:T(8,128)S(1)}, u32[]{:S(2)}, u32[]{:S(2)}) collective-permute-start(f32[128,640]{1,0:T(8,128)S(1)} %get-tuple-element.44.yc_ref.refs_2_), channel_id=1, source_target_pairs={{0,1},{1,0},{2,3},{3,2},{4,5},{5,4},{6,7},{7,6},{8,9},{9,8},{10,11... | collective-permute-start | bytes 983048 | tf_op jit(solution)/shard_map/ppermute | solution.py:364
  10.8 9.7 %collective-permute-start.1 = (f32[64,640]{1,0:T(8,128)S(1)}, f32[64,640]{1,0:T(8,128)S(1)}, u32[]{:S(2)}, u32[]{:S(2)}) collective-permute-start(f32[64,640]{1,0:T(8,128)S(1)} %get-tuple-element.42.yb_ref.refs_1_), channel_id=1, source_target_pairs={{0,1},{1,0},{2,3},{3,2},{4,5},{5,4},{6,7},{7,6},{8,9},{9,8},{10,11... | collective-permute-start | bytes 491528 | tf_op jit(solution)/shard_map/ppermute | solution.py:364
  10.9 13.1 %collective-permute-start = (f32[64,640]{1,0:T(8,128)S(1)}, f32[64,640]{1,0:T(8,128)S(1)}, u32[]{:S(2)}, u32[]{:S(2)}) collective-permute-start(f32[64,640]{1,0:T(8,128)S(1)} %get-tuple-element.40.ya_ref.refs_0_), channel_id=1, source_target_pairs={{0,1},{1,0},{2,3},{3,2},{4,5},{5,4},{6,7},{7,6},{8,9},{9,8},{10,11... | collective-permute-start | bytes 491528 | tf_op jit(solution)/shard_map/ppermute | solution.py:364
  13.4 10.6 %copy-start = (f32[8,64]{1,0:T(8,128)S(1)}, f32[8,64]{1,0:T(8,128)}, u32[]{:S(2)}) copy-start(f32[8,64]{1,0:T(8,128)} %refs_0_.13) | copy-start | bytes 6148
  26.8 11.5 %collective-permute-start.4 = (f32[64,1536]{1,0:T(8,128)S(1)}, f32[64,1536]{1,0:T(8,128)S(1)}, u32[]{:S(2)}, u32[]{:S(2)}) collective-permute-start(f32[64,1536]{1,0:T(8,128)S(1)} %get-tuple-element.54.refs_1_), channel_id=1, source_target_pairs={{0,3},{1,2},{2,1},{3,0},{4,7},{5,6},{6,5},{7,4},{8,11},{9,10},{10,... | collective-permute-start | bytes 1179656 | tf_op jit(solution)/shard_map/ppermute | solution.py:364
  31.4 13.2 %collective-permute-start.3 = (f32[64,1152]{1,0:T(8,128)S(1)}, f32[64,1152]{1,0:T(8,128)S(1)}, u32[]{:S(2)}, u32[]{:S(2)}) collective-permute-start(f32[64,1152]{1,0:T(8,128)S(1)} %shard_map.52.refs_4_.refs_0_), channel_id=1, source_target_pairs={{0,3},{1,2},{2,1},{3,0},{4,7},{5,6},{6,5},{7,4},{8,11},{9,10},{10,... | collective-permute-start | bytes 884744 | tf_op jit(solution)/shard_map/ppermute | solution.py:364
  45.2 13.9 %collective-permute-start.5 = (f32[64,1152]{1,0:T(8,128)S(1)}, f32[64,1152]{1,0:T(8,128)S(1)}, u32[]{:S(2)}, u32[]{:S(2)}) collective-permute-start(f32[64,1152]{1,0:T(8,128)S(1)} %shard_map.54.refs_4_.refs_0_), channel_id=1, source_target_pairs={{0,4},{1,5},{2,6},{3,7},{4,0},{5,1},{6,2},{7,3},{8,12},{9,13},{10,... | collective-permute-start | bytes 884744 | tf_op jit(solution)/shard_map/ppermute | solution.py:364
  46.7 10.4 %collective-permute-start.6 = (f32[64,1024]{1,0:T(8,128)S(1)}, f32[64,1024]{1,0:T(8,128)S(1)}, u32[]{:S(2)}, u32[]{:S(2)}) collective-permute-start(f32[64,1024]{1,0:T(8,128)S(1)} %get-tuple-element.56.refs_1_), channel_id=1, source_target_pairs={{0,4},{1,5},{2,6},{3,7},{4,0},{5,1},{6,2},{7,3},{8,12},{9,13},{10,... | collective-permute-start | bytes 786440 | tf_op jit(solution)/shard_map/ppermute | solution.py:364
  59.7 11.4 %collective-permute-start.7 = (f32[64,1152]{1,0:T(8,128)S(1)}, f32[64,1152]{1,0:T(8,128)S(1)}, u32[]{:S(2)}, u32[]{:S(2)}) collective-permute-start(f32[64,1152]{1,0:T(8,128)S(1)} %shard_map.57.refs_4_.refs_0_), channel_id=1, source_target_pairs={{0,12},{1,13},{2,14},{3,15},{4,8},{5,9},{6,10},{7,11},{8,4},{9,5},... | collective-permute-start | bytes 884744 | tf_op jit(solution)/shard_map/ppermute | solution.py:364
  62.6 6.9 %collective-permute-start.8 = (f32[64,512]{1,0:T(8,128)S(1)}, f32[64,512]{1,0:T(8,128)S(1)}, u32[]{:S(2)}, u32[]{:S(2)}) collective-permute-start(f32[64,512]{1,0:T(8,128)S(1)} %get-tuple-element.60.refs_1_), channel_id=1, source_target_pairs={{0,12},{1,13},{2,14},{3,15},{4,8},{5,9},{6,10},{7,11},{8,4},{9,5},... | collective-permute-start | bytes 393224 | tf_op jit(solution)/shard_map/ppermute | solution.py:364
  71.6 5.2 %collective-permute-start.9 = (f32[64,1152]{1,0:T(8,128)S(1)}, f32[64,1152]{1,0:T(8,128)S(1)}, u32[]{:S(2)}, u32[]{:S(2)}) collective-permute-start(f32[64,1152]{1,0:T(8,128)S(1)} %shard_map.59.refs_1_.refs_4_), channel_id=1, source_target_pairs={{0,16},{16,0},{32,48},{48,32},{64,80},{80,64},{96,112},{112,96},{1... | collective-permute-start | bytes 884744 | tf_op jit(solution)/shard_map/ppermute | solution.py:364
  78.9 4.5 %collective-permute-start.10 = (f32[32,768]{1,0:T(8,128)S(1)}, f32[32,768]{1,0:T(8,128)S(1)}, u32[]{:S(2)}, u32[]{:S(2)}) collective-permute-start(f32[32,768]{1,0:T(8,128)S(1)} %get-tuple-element.63), channel_id=1, source_target_pairs={{0,32},{16,48},{32,0},{48,16},{64,96},{80,112},{96,64},{112,80},{1... | collective-permute-start | bytes 294920 | tf_op jit(solution)/shard_map/ppermute | solution.py:364
  83.5 2.3 %collective-permute-start.11 = (f32[32,768]{1,0:T(8,128)S(1)}, f32[32,768]{1,0:T(8,128)S(1)}, u32[]{:S(2)}, u32[]{:S(2)}) collective-permute-start(f32[32,768]{1,0:T(8,128)S(1)} %collective-permute-done.10.refs_2_), channel_id=1, source_target_pairs={{0,16},{16,0},{32,48},{48,32},{64,80},{80,64},{96,112},{112,96},{1... | collective-permute-start | bytes 294920 | tf_op jit(solution)/shard_map/ppermute | solution.py:364
  87.7 5.5 %collective-permute-start.12 = (f32[32,512]{1,0:T(8,128)S(1)}, f32[32,512]{1,0:T(8,128)S(1)}, u32[]{:S(2)}, u32[]{:S(2)}) collective-permute-start(f32[32,512]{1,0:T(8,128)S(1)} %get-tuple-element.67), channel_id=1, source_target_pairs={{0,64},{16,80},{32,96},{48,112},{64,0},{80,16},{96,32},{112,48},{1... | collective-permute-start | bytes 196616 | tf_op jit(solution)/shard_map/ppermute | solution.py:364
  93.2 3.1 %collective-permute-start.13 = (f32[32,512]{1,0:T(8,128)S(1)}, f32[32,512]{1,0:T(8,128)S(1)}, u32[]{:S(2)}, u32[]{:S(2)}) collective-permute-start(f32[32,512]{1,0:T(8,128)S(1)} %collective-permute-done.12.refs_2_), channel_id=1, source_target_pairs={{0,16},{16,0},{32,48},{48,32},{64,80},{80,64},{96,112},{112,96},{1... | collective-permute-start | bytes 196616 | tf_op jit(solution)/shard_map/ppermute | solution.py:364
  98.2 8.0 %collective-permute-start.14 = (f32[64,256]{1,0:T(8,128)S(1)}, f32[64,256]{1,0:T(8,128)S(1)}, u32[]{:S(2)}, u32[]{:S(2)}) collective-permute-start(f32[64,256]{1,0:T(8,128)S(1)} %get-tuple-element.72.refs_1_), channel_id=1, source_target_pairs={{0,224},{16,240},{32,192},{48,208},{64,160},{80,176},{96,128},{112... | collective-permute-start | bytes 196616 | tf_op jit(solution)/shard_map/ppermute | solution.py:364

commit v8 on v7

--- a/solution.py
+++ b/solution.py
@@ -107,64 +107,53 @@
     return 128 * (R * j // 128)
 
 
-def sweep(aug, first, count, y_ref, z_ref, m_ref, late=()):
-    base = lanes_from(first)
-    for j in range(first, first + count):
-        r0 = R * (j - first)
-        a0 = lanes_from(j) - base
-        at = R * j - lanes_from(j)
-        split = M - lanes_from(j)
-        minv = chol_inverse(aug[r0 : r0 + R, a0 : a0 + 128], at)
-        m_ref[r0 : r0 + R, :] = minv
-        for copy in late:
-            copy.wait()
-        late = ()
-        block = aug[r0 : r0 + R, a0:]
-        panel = mm(minv, jnp.concatenate([block, block], axis=0))
-        z_ref[r0 : r0 + R, :] = panel[:, :split]
-        y_ref[r0 : r0 + R, :] = panel[:, split:]
-        for i in range(j + 1, 4):
-            c0 = R * i - lanes_from(j)
-            s0 = lanes_from(i) - lanes_from(j)
-            q0 = R * (i - first)
-            aug[q0 : q0 + R, a0 + s0 :] -= mm_t(panel[:, c0 : c0 + R], panel[:, s0:])
-
-
-def leaf_kernel(d_any, b_any, t_any, y_ref, z_ref, m_ref, rest_ref, aug, sem):
+def panel_out(rows, j, y_ref, z_ref, m_ref):
+    split = M - lanes_from(j)
+    minv = chol_inverse(rows[:, :128], R * j - lanes_from(j))
+    m_ref[...] = minv
+    panel = mm(minv, jnp.concatenate([rows, rows], axis=0))
+    z_ref[...] = panel[:, :split]
+    y_ref[...] = panel[:, split:]
+
+
+def leaf_kernel(d_any, b_any, t_any, y_ref, z_ref, m_ref, rest_ref, head, sem):
     at = M + LEVELS * R
-    copies = [
-        pltpu.make_async_copy(d_any, aug.at[:, :M], sem.at[0]),
-        pltpu.make_async_copy(b_any, aug.at[:, M:at], sem.at[1]),
-        pltpu.make_async_copy(t_any, aug.at[:, at:], sem.at[2]),
-    ]
+    parts = ((d_any, 0, M), (b_any, M, at), (t_any, at, M + WIDTH))
+    copies = []
+    for n, (rows, dest) in enumerate((((0, R), head), ((R, M), rest_ref))):
+        for i, (src, lo, hi) in enumerate(parts):
+            copies.append(
+                pltpu.make_async_copy(src.at[rows[0] : rows[1], :], dest.at[:, lo:hi], sem.at[3 * n + i])
+            )
     for copy in copies:
         copy.start()
-    copies[0].wait()
-    sweep(aug, 0, 1, y_ref, z_ref, m_ref, copies[1:])
-    rest_ref[...] = aug[R:, :]
-
-
-def leaf2_kernel(aug_ref, y_ref, z_ref, m_ref, rest_ref, aug):
-    aug[...] = aug_ref[...]
-    sweep(aug, 1, 1, y_ref, z_ref, m_ref)
-    rest_ref[...] = aug[R:, 2 * R :]
-
-
-def leaf3_kernel(aug_ref, y_ref, z_ref, m_ref, aug):
-    aug[...] = aug_ref[...]
-    sweep(aug, 2, 2, y_ref, z_ref, m_ref)
+    for copy in copies[:3]:
+        copy.wait()
+    panel_out(head[...], 0, y_ref, z_ref, m_ref)
+    for copy in copies[3:]:
+        copy.wait()
+
+
+def leaf_next_kernel(j, rest_ref, *refs):
+    ys, zs, outs = refs[:j], refs[j : 2 * j], refs[2 * j :]
+    base = lanes_from(j)
+    before = jnp.concatenate(
+        [jnp.concatenate([zs[i][:, base - lanes_from(i) :], ys[i][...]], axis=1) for i in range(j)], axis=0
+    )
+    c0 = R * j - base
+    rows = rest_ref[R * (j - 1) : R * j, base:] - mm_t(before[:, c0 : c0 + R], before)
+    panel_out(rows, j, *outs)
 
 
 def back_kernel(*refs):
-    ys, zs, ms, w_ref = refs[:3], refs[3:6], refs[6:9], refs[9]
+    ys, zs, ms, w_ref = refs[:4], refs[4:8], refs[8:12], refs[12]
     for j in range(3, -1, -1):
-        part, q0 = min(j, 2), R * max(j - 2, 0)
         o = R - (R * j - lanes_from(j))
-        rhs = ys[part][q0 : q0 + R, :]
+        rhs = ys[j][...]
         if j < 3:
-            z = zs[part][q0 : q0 + R, R * (j + 1) - lanes_from(j) :]
+            z = zs[j][:, R * (j + 1) - lanes_from(j) :]
             rhs = rhs - mm(z, w_ref[R * (j + 1) :, :])
-        w_ref[R * j : R * j + R, :] = mm_t(ms[part][q0 : q0 + R, :], rhs)[o : o + R, :]
+        w_ref[R * j : R * j + R, :] = mm_t(ms[j][...], rhs)[o : o + R, :]
 
 
 def gram_pair(y, pair):
@@ -211,8 +200,9 @@
     return {pair: gram_pair(y, pair) for pair in pairs}
 
 
-def gram_kernel(ya_ref, yb_ref, yc_ref, near_ref, far_ref):
-    grams = gram_pairs((ya_ref, yb_ref, yc_ref), range(4))
+def gram_kernel(*refs):
+    *y_refs, near_ref, far_ref = refs
+    grams = gram_pairs(y_refs, range(4))
     for level in range(1, SPLIT + 1):
         put(near_ref, 1, level, row_block(grams, level))
     first = SPLIT + 1
@@ -267,8 +257,9 @@
     h_ref[...] = jnp.where(on_core0(), n_ref[: R // 2, :], n_ref[R // 2 :, :])
 
 
-def first_level_kernel(c_ref, own_ref, ya_ref, yb_ref, yc_ref, dep_ref, p_ref, m_ref, n_ref):
-    grams = gram_pairs((ya_ref, yb_ref, yc_ref), range(SPLIT // 2))
+def first_level_kernel(c_ref, own_ref, *refs):
+    *y_refs, dep_ref, p_ref, m_ref, n_ref = refs
+    grams = gram_pairs(y_refs, range(SPLIT // 2))
 
     def part(level):
         return packed(1, own_ref, level) + row_block(grams, level)
@@ -301,9 +292,10 @@
         next_half(n_ref, h_ref)
 
 
-def first_far_kernel(own_ref, ya_ref, yb_ref, yc_ref, p_ref, n_ref):
+def first_far_kernel(own_ref, *refs):
+    *y_refs, p_ref, n_ref = refs
     first = SPLIT + 1
-    grams = gram_pairs((ya_ref, yb_ref, yc_ref), range(SPLIT // 2, LEVELS // 2))
+    grams = gram_pairs(y_refs, range(SPLIT // 2, LEVELS // 2))
     less = schur(1, p_ref[...], first, LEVELS)
     more = {level: row_block(grams, level) - row_block(less, level) for level in range(first, LEVELS + 1)}
     for level, value in pack(first, more).items():
@@ -360,33 +352,32 @@
 
 def exchange(value, level):
     axis = "inner" if level <= 4 else "group"
-    mask = {1: 1, 2: 3, 3: 4, 4: 12, 5: 1, 6: 2, 7: 4, 8: 14}[level]
+    mask = {1: 1, 2: 3, 3: 4, 4: 12, 5: 1, 6: 2, 7: 4, 8: 12}[level]
     return lax.ppermute(value, axis, [(s, s ^ mask) for s in range(lax.axis_size(axis))])
 
 
 def per_device(leaf_blocks, bases, targets, coupling):
-    half = M // 2
     leaf_blocks, bases, targets = (
         pltpu.with_memory_space_constraint(a, pltpu.HBM) for a in (leaf_blocks, bases, targets)
     )
-    ya, za, ma, rest = call(
-        leaf_kernel, [(R, WIDTH), (R, M), (R, 128), (3 * R, M + WIDTH)], leaf_blocks, bases, targets,
-        hbm=(0, 1, 2), scratch=[(M, M + WIDTH)], sems=3,
-    )
-    got_a = exchange(ya, 1)
-    yb, zb, mb, rest = call(
-        leaf2_kernel, [(R, WIDTH), (R, M), (R, 128), (half, half + WIDTH)], rest,
-        scratch=[(3 * R, M + WIDTH)],
-    )
-    got_b = exchange(yb, 1)
-    yc, zc, mc = call(
-        leaf3_kernel, [(half, WIDTH), (half, half), (half, 128)], rest,
-        scratch=[(half, half + WIDTH)],
-    )
-    got_y = (got_a, got_b, exchange(yc, 1))
+    ys, zs, ms, got_y = [], [], [], []
+    for j in range(4):
+        outs = [(R, WIDTH), (R, M - lanes_from(j)), (R, 128)]
+        if j == 0:
+            y, z, m, rest = call(
+                leaf_kernel, outs + [(M - R, M + WIDTH)], leaf_blocks, bases, targets,
+                hbm=(0, 1, 2), scratch=[(R, M + WIDTH)], sems=6,
+            )
+        else:
+            kernel = lambda *refs, j=j: leaf_next_kernel(j, *refs)
+            y, z, m = call(kernel, outs, rest, *ys, *zs)
+        ys.append(y)
+        zs.append(z)
+        ms.append(m)
+        got_y.append(exchange(y, 1))
     far_shape = (R, offsets(SPLIT + 1)[1])
-    near, far = call(gram_kernel, [(R, offsets(1)[1]), far_shape], ya, yb, yc)
-    (w,) = call(back_kernel, [(M, WIDTH)], ya, yb, yc, za, zb, zc, ma, mb, mc)
+    near, far = call(gram_kernel, [(R, offsets(1)[1]), far_shape], *ys)
+    (w,) = call(back_kernel, [(M, WIDTH)], *ys, *zs, *ms)
     got = far_got = None
     dep = w
     for k in range(1, LEVELS):
@@ -396,7 +387,7 @@
         if k + 1 in HALVED:
             outs.append((R // 2, offsets(k + 1)[1]))
         if k == 1:
-            p, minv, near = call(first_level_kernel, outs, coupling, near, *got_y, dep, hbm=(5,))
+            p, minv, near = call(first_level_kernel, outs, coupling, near, *got_y, dep, hbm=(6,))
             more = [near]
         elif k in HALVED:
             kernel = lambda *refs, k=k: halves_level_kernel(k, *refs)

time: 109 us -> 100 us (0.917)
  the two profiles are of different devices: /device:TPU:1 before, /device:TPU:39 now
where the time goes in v8:
time: 100 us
  waiting for transfers between devices  38.5 us (38%)
  Pallas kernels  36 us (36%)
  starting transfers between devices  25.7 us (26%)
    ppermute x16, waiting for transfers between devices, exchange(): lax.ppermute(value, axis, [(s, s ^ mask) for s in range(lax.axis_size(axi...  38.5 us
    pallas_call x22, Pallas kernels, call(): pl.pallas_call(kernel, out_shape=shapes, in_specs=[hb if i in hbm else vm...  36 us
    ppermute x16, starting transfers between devices, exchange(): lax.ppermute(value, axis, [(s, s ^ mask) for s in range(lax.axis_size(axi...  25.7 us
  transfers between devices with their start and end apart: 16, of which 9 were waited for; matrix products, arithmetic and copies ran while one was open for 0% of the time, Pallas kernels for 20%

profile of v8, /device:TPU:39, one launch (start us, length us, event | category | flops | bytes accessed | tf_op | source)
XLA Modules:
  0.0 100.4 jit_solution(9643862161457588473)
XLA Ops:
  0.0 2.6 %shard_map.46 = (f32[64,640]{1,0:T(8,128)S(1)}, f32[64,256]{1,0:T(8,128)S(1)}, f32[64,128]{1,0:T(8,128)S(1)}, f32[192,896]{1,0:T(8,128)S(1)}) custom-call(f32[256,256]{1,0:T(8,128)} %d_any.1, f32[256,512]{1,0:T(8,128)} %b_any.1, f32[256,128]{1,0:T(8,128)} %t_any.1), custom_call_target="tpu_custom_call" | custom-call | flops 10000000 | bytes 1000000 | tf_op jit(solution)/shard_map/pallas_call | solution.py:342
  2.6 0.6 collective-permute-start
  3.3 2.0 %shard_map.47 = (f32[64,640]{1,0:T(8,128)S(1)}, f32[64,256]{1,0:T(8,128)S(1)}, f32[64,128]{1,0:T(8,128)S(1)}) custom-call(f32[192,896]{1,0:T(8,128)S(1)} %get-tuple-element.43.refs_0_, f32[64,640]{1,0:T(8,128)S(1)} %get-tuple-element.42.refs_1_.refs_0_, f32[64,256]{1,0:T(8,128)S(1)} %get-tuple-element.44.refs_2_.refs_3_.refs_4_), custom_call_target="tpu_custom_call" | custom-call | flops 10000000 | bytes 1000000 | tf_op jit(solution)/shard_map/pallas_call | solution.py:342
  5.2 1.0 collective-permute-start.1
  6.2 1.9 %shard_map.48 = (f32[64,640]{1,0:T(8,128)S(1)}, f32[64,128]{1,0:T(8,128)S(1)}, f32[64,128]{1,0:T(8,128)S(1)}) custom-call(f32[192,896]{1,0:T(8,128)S(1)} %get-tuple-element.43.refs_0_, f32[64,640]{1,0:T(8,128)S(1)} %get-tuple-element.42.refs_1_.refs_0_, f32[64,640]{1,0:T(8,128)S(1)} %get-tuple-element.45.refs_2_.refs_1_, ...), custom_call_target="tpu_custom_call" | custom-call | flops 10000000 | bytes 1000000 | tf_op jit(solution)/shard_map/pallas_call | solution.py:342
  8.1 2.1 %shard_map.49 = (f32[64,640]{1,0:T(8,128)S(1)}, f32[64,128]{1,0:T(8,128)S(1)}, f32[64,128]{1,0:T(8,128)S(1)}) custom-call(f32[192,896]{1,0:T(8,128)S(1)} %get-tuple-element.43.refs_0_, f32[64,640]{1,0:T(8,128)S(1)} %get-tuple-element.42.refs_1_.refs_0_, f32[64,640]{1,0:T(8,128)S(1)} %get-tuple-element.45.refs_2_.refs_1_, ...), custom_call_target="tpu_custom_call" | custom-call | flops 10000000 | bytes 1000000 | tf_op jit(solution)/shard_map/pallas_call | solution.py:342
  10.2 0.6 collective-permute-start.3
  10.8 0.9 collective-permute-start.2
  11.7 1.1 %shard_map.50 = (f32[64,2304]{1,0:T(8,128)S(1)}, f32[64,1152]{1,0:T(8,128)S(1)}) custom-call(f32[64,640]{1,0:T(8,128)S(1)} %get-tuple-element.42.refs_1_.refs_0_, f32[64,640]{1,0:T(8,128)S(1)} %get-tuple-element.45.refs_2_.refs_1_, f32[64,640]{1,0:T(8,128)S(1)} %get-tuple-element.47.refs_3_.refs_2_, f32[64,640]{1,0:T(8,128)S(1)} %get-tuple-element.49.refs_3_), custom_call_target="tpu_custom_call" | custom-call | flops 10000000 | bytes 1000000 | tf_op jit(solution)/shard_map/pallas_call | solution.py:342
  12.9 0.0 copy-start
  12.9 2.3 %shard_map.51.refs_4_.refs_3_.w_ref = f32[256,640]{1,0:T(8,128)S(1)} custom-call(f32[64,640]{1,0:T(8,128)S(1)} %get-tuple-element.42.refs_1_.refs_0_, f32[64,640]{1,0:T(8,128)S(1)} %get-tuple-element.45.refs_2_.refs_1_, f32[64,640]{1,0:T(8,128)S(1)} %get-tuple-element.47.refs_3_.refs_2_, f32[64,640]{1,0:T(8,128)S(1)} %get-tuple-element.49.refs_3_, ...), custom_call_target="tpu_custom_call" | custom-call | flops 10000000 | bytes 1000000 | tf_op jit(solution)/shard_map/pallas_call | solution.py:342
  15.1 0.0 collective-permute-done.refs_0_
  15.2 0.0 collective-permute-done.1.refs_1_
  15.2 0.0 collective-permute-done.3.refs_3_
  15.2 3.1 %collective-permute-done.2.refs_2_ = f32[64,640]{1,0:T(8,128)S(1)} collective-permute-done((f32[64,640]{1,0:T(8,128)S(1)}, f32[64,640]{1,0:T(8,128)S(1)}, u32[]{:S(2)}, u32[]{:S(2)}) %collective-permute-start.2) | collective-permute-done | bytes 163872 | tf_op jit(solution)/shard_map/ppermute | solution.py:356
  18.3 0.0 copy-done
  18.3 2.8 %shard_map.52 = (f32[64,640]{1,0:T(8,128)S(1)}, f32[64,128]{1,0:T(8,128)S(1)}, f32[64,1536]{1,0:T(8,128)S(1)}) custom-call(f32[8,64]{1,0:T(8,128)S(1)} %copy-done, f32[64,2304]{1,0:T(8,128)S(1)} %get-tuple-element.51.own_ref, f32[64,640]{1,0:T(8,128)S(1)} %collective-permute-done.refs_0_, f32[64,640]{1,0:T(8,128)S(1)} %collective-permute-done.1.refs_1_, ...), custom_call_target="tpu_custom_call" | custom-call | flops 10000000 | bytes 1000000 | tf_op jit(solution)/shard_map/pallas_call | solution.py:342
  21.1 0.3 collective-permute-start.5
  21.4 0.8 shard_map.53.refs_4_.refs_0_
  22.2 2.6 %collective-permute-start.4 = (f32[64,1152]{1,0:T(8,128)S(1)}, f32[64,1152]{1,0:T(8,128)S(1)}, u32[]{:S(2)}, u32[]{:S(2)}) collective-permute-start(f32[64,1152]{1,0:T(8,128)S(1)} %shard_map.53.refs_4_.refs_0_), channel_id=1, source_target_pairs={{0,3},{1,2},{2,1},{3,0},{4,7},{5,6},{6,5},{7,4},{8,11},{9,10},{10,... | collective-permute-start | bytes 884744 | tf_op jit(solution)/shard_map/ppermute | solution.py:356
  24.8 6.2 %collective-permute-done.5.refs_2_ = f32[64,1536]{1,0:T(8,128)S(1)} collective-permute-done((f32[64,1536]{1,0:T(8,128)S(1)}, f32[64,1536]{1,0:T(8,128)S(1)}, u32[]{:S(2)}, u32[]{:S(2)}) %collective-permute-start.5) | collective-permute-done | bytes 393248 | tf_op jit(solution)/shard_map/ppermute | solution.py:356
  31.0 2.0 %shard_map.54 = (f32[64,640]{1,0:T(8,128)S(1)}, f32[64,128]{1,0:T(8,128)S(1)}, f32[64,1024]{1,0:T(8,128)S(1)}) custom-call(f32[8,64]{1,0:T(8,128)S(1)} %copy-done, f32[64,1536]{1,0:T(8,128)S(1)} %get-tuple-element.58.refs_1_, f32[64,1536]{1,0:T(8,128)S(1)} %collective-permute-done.5.refs_2_, f32[256,640]{1,0:T(8,128)S(1)} %shard_map.51.refs_4_.refs_3_.w_ref, ...), custom_call_target="tpu_custom_call" | custom-call | flops 10000000 | bytes 1000000 | tf_op jit(solution)/shard_map/pallas_call | solution.py:342
  33.0 4.3 %collective-permute-done.4.refs_1_ = f32[64,1152]{1,0:T(8,128)S(1)} collective-permute-done((f32[64,1152]{1,0:T(8,128)S(1)}, f32[64,1152]{1,0:T(8,128)S(1)}, u32[]{:S(2)}, u32[]{:S(2)}) %collective-permute-start.4) | collective-permute-done | bytes 294944 | tf_op jit(solution)/shard_map/ppermute | solution.py:356
  37.3 0.5 shard_map.55.refs_4_.refs_0_
  37.8 1.4 %collective-permute-start.6 = (f32[64,1152]{1,0:T(8,128)S(1)}, f32[64,1152]{1,0:T(8,128)S(1)}, u32[]{:S(2)}, u32[]{:S(2)}) collective-permute-start(f32[64,1152]{1,0:T(8,128)S(1)} %shard_map.55.refs_4_.refs_0_), channel_id=1, source_target_pairs={{0,4},{1,5},{2,6},{3,7},{4,0},{5,1},{6,2},{7,3},{8,12},{9,13},{10,... | collective-permute-start | bytes 884744 | tf_op jit(solution)/shard_map/ppermute | solution.py:356
  39.2 0.3 collective-permute-start.7
  39.5 1.4 %shard_map.56.refs_3_.w_ref = f32[256,512]{1,0:T(8,128)S(1)} custom-call(f32[256,640]{1,0:T(8,128)S(1)} %shard_map.51.refs_4_.refs_3_.w_ref, f32[64,640]{1,0:T(8,128)S(1)} %get-tuple-element.57.refs_4_.p_ref, f32[64,128]{1,0:T(8,128)S(1)} %get-tuple-element.61.m_ref, f32[64,640]{1,0:T(8,128)S(1)} %get-tuple-element.59.refs_2_.p2_ref, ...), custom_call_target="tpu_custom_call" | custom-call | flops 10000000 | bytes 1000000 | tf_op jit(solution)/shard_map/pallas_call | solution.py:342
  40.9 8.2 %collective-permute-done.7.refs_2_ = f32[64,1024]{1,0:T(8,128)S(1)} collective-permute-done((f32[64,1024]{1,0:T(8,128)S(1)}, f32[64,1024]{1,0:T(8,128)S(1)}, u32[]{:S(2)}, u32[]{:S(2)}) %collective-permute-start.7) | collective-permute-done | bytes 262176 | tf_op jit(solution)/shard_map/ppermute | solution.py:356
  49.2 2.0 %shard_map.57 = (f32[64,512]{1,0:T(8,128)S(1)}, f32[64,128]{1,0:T(8,128)S(1)}, f32[64,512]{1,0:T(8,128)S(1)}) custom-call(f32[8,64]{1,0:T(8,128)S(1)} %copy-done, f32[64,1024]{1,0:T(8,128)S(1)} %get-tuple-element.60.refs_1_, f32[64,1024]{1,0:T(8,128)S(1)} %collective-permute-done.7.refs_2_, f32[256,512]{1,0:T(8,128)S(1)} %shard_map.56.refs_3_.w_ref, ...), custom_call_target="tpu_custom_call" | custom-call | flops 10000000 | bytes 1000000 | tf_op jit(solution)/shard_map/pallas_call | solution.py:342
  51.2 0.0 collective-permute-done.6.refs_1_
  51.2 0.5 shard_map.58.refs_4_.refs_0_
  51.7 2.8 %collective-permute-start.8 = (f32[64,1152]{1,0:T(8,128)S(1)}, f32[64,1152]{1,0:T(8,128)S(1)}, u32[]{:S(2)}, u32[]{:S(2)}) collective-permute-start(f32[64,1152]{1,0:T(8,128)S(1)} %shard_map.58.refs_4_.refs_0_), channel_id=1, source_target_pairs={{0,12},{1,13},{2,14},{3,15},{4,8},{5,9},{6,10},{7,11},{8,4},{9,5},... | collective-permute-start | bytes 884744 | tf_op jit(solution)/shard_map/ppermute | solution.py:356
  54.5 0.1 collective-permute-start.9
  54.6 6.0 %collective-permute-done.9.refs_2_ = f32[64,512]{1,0:T(8,128)S(1)} collective-permute-done((f32[64,512]{1,0:T(8,128)S(1)}, f32[64,512]{1,0:T(8,128)S(1)}, u32[]{:S(2)}, u32[]{:S(2)}) %collective-permute-start.9) | collective-permute-done | bytes 131104 | tf_op jit(solution)/shard_map/ppermute | solution.py:356
  60.7 1.6 %shard_map.59 = (f32[64,512]{1,0:T(8,128)S(1)}, f32[64,128]{1,0:T(8,128)S(1)}) custom-call(f32[8,64]{1,0:T(8,128)S(1)} %copy-done, f32[64,512]{1,0:T(8,128)S(1)} %get-tuple-element.64.refs_1_, f32[64,512]{1,0:T(8,128)S(1)} %collective-permute-done.9.refs_2_, f32[256,512]{1,0:T(8,128)S(1)} %shard_map.56.refs_3_.w_ref, f32[64,1152]{1,0:T(8,128)S(1)} %shard_map.58.refs_4_.refs_0_), custom_call_target="tpu_custom_call" | custom-call | flops 10000000 | bytes 1000000 | tf_op jit(solution)/shard_map/pallas_call | solution.py:342
  62.3 0.0 collective-permute-done.8.refs_1_
  62.3 0.5 shard_map.60.refs_1_.refs_4_
  62.8 4.7 %collective-permute-start.10 = (f32[64,1152]{1,0:T(8,128)S(1)}, f32[64,1152]{1,0:T(8,128)S(1)}, u32[]{:S(2)}, u32[]{:S(2)}) collective-permute-start(f32[64,1152]{1,0:T(8,128)S(1)} %shard_map.60.refs_1_.refs_4_), channel_id=1, source_target_pairs={{0,16},{16,0},{32,48},{48,32},{64,80},{80,64},{96,112},{112,96},{1... | collective-permute-start | bytes 884744 | tf_op jit(solution)/shard_map/ppermute | solution.py:356
  67.6 1.2 %collective-permute-done.10.refs_2_ = f32[64,1152]{1,0:T(8,128)S(1)} collective-permute-done((f32[64,1152]{1,0:T(8,128)S(1)}, f32[64,1152]{1,0:T(8,128)S(1)}, u32[]{:S(2)}, u32[]{:S(2)}) %collective-permute-start.10) | collective-permute-done | bytes 294944 | tf_op jit(solution)/shard_map/ppermute | solution.py:356
  68.8 2.1 %shard_map.61 = (f32[64,384]{1,0:T(8,128)S(1)}, f32[64,128]{1,0:T(8,128)S(1)}, f32[64,768]{1,0:T(8,128)S(1)}, f32[32,768]{1,0:T(8,128)S(1)}) custom-call(f32[8,64]{1,0:T(8,128)S(1)} %copy-done, f32[64,1152]{1,0:T(8,128)S(1)} %shard_map.60.refs_1_.refs_4_, f32[64,1152]{1,0:T(8,128)S(1)} %collective-permute-done.10.refs_2_, ...), custom_call_target="tpu_custom_call" | custom-call | flops 10000000 | bytes 1000000 | tf_op jit(solution)/shard_map/pallas_call | solution.py:342
  70.9 0.1 collective-permute-start.11
  71.0 4.0 %collective-permute-done.11.refs_2_ = f32[32,768]{1,0:T(8,128)S(1)} collective-permute-done((f32[32,768]{1,0:T(8,128)S(1)}, f32[32,768]{1,0:T(8,128)S(1)}, u32[]{:S(2)}, u32[]{:S(2)}) %collective-permute-start.11) | collective-permute-done | bytes 98336 | tf_op jit(solution)/shard_map/ppermute | solution.py:356
  74.9 1.2 %collective-permute-start.12 = (f32[32,768]{1,0:T(8,128)S(1)}, f32[32,768]{1,0:T(8,128)S(1)}, u32[]{:S(2)}, u32[]{:S(2)}) collective-permute-start(f32[32,768]{1,0:T(8,128)S(1)} %collective-permute-done.11.refs_2_), channel_id=1, source_target_pairs={{0,16},{16,0},{32,48},{48,32},{64,80},{80,64},{96,112},{112,96},{1... | collective-permute-start | bytes 294920 | tf_op jit(solution)/shard_map/ppermute | solution.py:356
  76.2 1.3 %shard_map.62.refs_4_.w_ref = f32[256,384]{1,0:T(8,128)S(1)} custom-call(f32[256,512]{1,0:T(8,128)S(1)} %shard_map.56.refs_3_.w_ref, f32[64,512]{1,0:T(8,128)S(1)} %get-tuple-element.63.refs_2_.p_ref, f32[64,128]{1,0:T(8,128)S(1)} %get-tuple-element.68.m_ref, f32[64,512]{1,0:T(8,128)S(1)} %get-tuple-element.65.refs_2_.p2_ref, ...), custom_call_target="tpu_custom_call" | custom-call | flops 10000000 | bytes 1000000 | tf_op jit(solution)/shard_map/pallas_call | solution.py:342
  77.5 0.0 collective-permute-done.12.refs_3_
  77.5 1.9 %shard_map.63 = (f32[64,384]{1,0:T(8,128)S(1)}, f32[64,128]{1,0:T(8,128)S(1)}, f32[64,512]{1,0:T(8,128)S(1)}, f32[32,512]{1,0:T(8,128)S(1)}) custom-call(f32[8,64]{1,0:T(8,128)S(1)} %copy-done, f32[64,768]{1,0:T(8,128)S(1)} %get-tuple-element.66.refs_1_, f32[32,768]{1,0:T(8,128)S(1)} %collective-permute-done.11.refs_2_, ...), custom_call_target="tpu_custom_call" | custom-call | flops 10000000 | bytes 1000000 | tf_op jit(solution)/shard_map/pallas_call | solution.py:342
  79.4 3.1 %collective-permute-start.13 = (f32[32,512]{1,0:T(8,128)S(1)}, f32[32,512]{1,0:T(8,128)S(1)}, u32[]{:S(2)}, u32[]{:S(2)}) collective-permute-start(f32[32,512]{1,0:T(8,128)S(1)} %get-tuple-element.71), channel_id=1, source_target_pairs={{0,64},{16,80},{32,96},{48,112},{64,0},{80,16},{96,32},{112,48},{1... | collective-permute-start | bytes 196616 | tf_op jit(solution)/shard_map/ppermute | solution.py:356
  82.5 3.0 %collective-permute-done.13.refs_2_ = f32[32,512]{1,0:T(8,128)S(1)} collective-permute-done((f32[32,512]{1,0:T(8,128)S(1)}, f32[32,512]{1,0:T(8,128)S(1)}, u32[]{:S(2)}, u32[]{:S(2)}) %collective-permute-start.13) | collective-permute-done | bytes 65568 | tf_op jit(solution)/shard_map/ppermute | solution.py:356
  85.5 0.5 collective-permute-start.14
  85.9 1.1 %shard_map.64.refs_4_.refs_0_ = f32[256,256]{1,0:T(8,128)S(1)} custom-call(f32[256,384]{1,0:T(8,128)S(1)} %shard_map.62.refs_4_.w_ref, f32[64,384]{1,0:T(8,128)S(1)} %get-tuple-element.72.p_ref, f32[64,128]{1,0:T(8,128)S(1)} %get-tuple-element.73.m_ref, f32[64,384]{1,0:T(8,128)S(1)} %get-tuple-element.74.p2_ref, f32[64,128]{1,0:T(8,128)S(1)} %get-tuple-element.75.m2_ref), custom_call_target="tpu_custom_call" | custom-call | flops 10000000 | bytes 1000000 | tf_op jit(solution)/shard_map/pallas_call | solution.py:342
  87.0 0.0 collective-permute-done.14.refs_3_
  87.0 1.9 %shard_map.65 = (f32[64,256]{1,0:T(8,128)S(1)}, f32[64,128]{1,0:T(8,128)S(1)}, f32[64,256]{1,0:T(8,128)S(1)}) custom-call(f32[8,64]{1,0:T(8,128)S(1)} %copy-done, f32[64,512]{1,0:T(8,128)S(1)} %get-tuple-element.70.refs_1_, f32[32,512]{1,0:T(8,128)S(1)} %collective-permute-done.13.refs_2_, f32[32,512]{1,0:T(8,128)S(1)} %collective-permute-done.14.refs_3_, ...), custom_call_target="tpu_custom_call" | custom-call | flops 10000000 | bytes 1000000 | tf_op jit(solution)/shard_map/pallas_call | solution.py:342
  88.9 5.5 %collective-permute-start.15 = (f32[64,256]{1,0:T(8,128)S(1)}, f32[64,256]{1,0:T(8,128)S(1)}, u32[]{:S(2)}, u32[]{:S(2)}) collective-permute-start(f32[64,256]{1,0:T(8,128)S(1)} %get-tuple-element.76.refs_1_), channel_id=1, source_target_pairs={{0,192},{16,208},{32,224},{48,240},{64,128},{80,144},{96,160},{112... | collective-permute-start | bytes 196616 | tf_op jit(solution)/shard_map/ppermute | solution.py:356
  94.5 0.8 shard_map.66.refs_3_
  95.3 2.4 %collective-permute-done.15.refs_2_ = f32[64,256]{1,0:T(8,128)S(1)} collective-permute-done((f32[64,256]{1,0:T(8,128)S(1)}, f32[64,256]{1,0:T(8,128)S(1)}, u32[]{:S(2)}, u32[]{:S(2)}) %collective-permute-start.15) | collective-permute-done | bytes 65568 | tf_op jit(solution)/shard_map/ppermute | solution.py:356
  97.7 2.7 %shard_map.67 = f32[256,128]{1,0:T(8,128)} custom-call(f32[8,64]{1,0:T(8,128)S(1)} %copy-done, f32[64,256]{1,0:T(8,128)S(1)} %get-tuple-element.76.refs_1_, f32[64,256]{1,0:T(8,128)S(1)} %collective-permute-done.15.refs_2_, f32[256,256]{1,0:T(8,128)S(1)} %shard_map.66.refs_3_), custom_call_target="tpu_custom_call" | custom-call | flops 10000000 | bytes 1000000 | tf_op jit(solution)/shard_map/pallas_call | solution.py:342
Async XLA Ops:
  2.6 12.5 %collective-permute-start = (f32[64,640]{1,0:T(8,128)S(1)}, f32[64,640]{1,0:T(8,128)S(1)}, u32[]{:S(2)}, u32[]{:S(2)}) collective-permute-start(f32[64,640]{1,0:T(8,128)S(1)} %get-tuple-element.42.refs_1_.refs_0_), channel_id=1, source_target_pairs={{0,1},{1,0},{2,3},{3,2},{4,5},{5,4},{6,7},{7,6},{8,9},{9,8},{10,11... | collective-permute-start | bytes 491528 | tf_op jit(solution)/shard_map/ppermute | solution.py:356
  5.2 9.9 %collective-permute-start.1 = (f32[64,640]{1,0:T(8,128)S(1)}, f32[64,640]{1,0:T(8,128)S(1)}, u32[]{:S(2)}, u32[]{:S(2)}) collective-permute-start(f32[64,640]{1,0:T(8,128)S(1)} %get-tuple-element.45.refs_2_.refs_1_), channel_id=1, source_target_pairs={{0,1},{1,0},{2,3},{3,2},{4,5},{5,4},{6,7},{7,6},{8,9},{9,8},{10,11... | collective-permute-start | bytes 491528 | tf_op jit(solution)/shard_map/ppermute | solution.py:356
  10.2 5.0 %collective-permute-start.3 = (f32[64,640]{1,0:T(8,128)S(1)}, f32[64,640]{1,0:T(8,128)S(1)}, u32[]{:S(2)}, u32[]{:S(2)}) collective-permute-start(f32[64,640]{1,0:T(8,128)S(1)} %get-tuple-element.49.refs_3_), channel_id=1, source_target_pairs={{0,1},{1,0},{2,3},{3,2},{4,5},{5,4},{6,7},{7,6},{8,9},{9,8},{10,11... | collective-permute-start | bytes 491528 | tf_op jit(solution)/shard_map/ppermute | solution.py:356
  10.8 7.5 %collective-permute-start.2 = (f32[64,640]{1,0:T(8,128)S(1)}, f32[64,640]{1,0:T(8,128)S(1)}, u32[]{:S(2)}, u32[]{:S(2)}) collective-permute-start(f32[64,640]{1,0:T(8,128)S(1)} %get-tuple-element.47.refs_3_.refs_2_), channel_id=1, source_target_pairs={{0,1},{1,0},{2,3},{3,2},{4,5},{5,4},{6,7},{7,6},{8,9},{9,8},{10,11... | collective-permute-start | bytes 491528 | tf_op jit(solution)/shard_map/ppermute | solution.py:356
  12.9 5.4 %copy-start = (f32[8,64]{1,0:T(8,128)S(1)}, f32[8,64]{1,0:T(8,128)}, u32[]{:S(2)}) copy-start(f32[8,64]{1,0:T(8,128)} %refs_0_.13) | copy-start | bytes 6148
  21.1 9.9 %collective-permute-start.5 = (f32[64,1536]{1,0:T(8,128)S(1)}, f32[64,1536]{1,0:T(8,128)S(1)}, u32[]{:S(2)}, u32[]{:S(2)}) collective-permute-start(f32[64,1536]{1,0:T(8,128)S(1)} %get-tuple-element.58.refs_1_), channel_id=1, source_target_pairs={{0,3},{1,2},{2,1},{3,0},{4,7},{5,6},{6,5},{7,4},{8,11},{9,10},{10,... | collective-permute-start | bytes 1179656 | tf_op jit(solution)/shard_map/ppermute | solution.py:356
  22.2 15.1 %collective-permute-start.4 = (f32[64,1152]{1,0:T(8,128)S(1)}, f32[64,1152]{1,0:T(8,128)S(1)}, u32[]{:S(2)}, u32[]{:S(2)}) collective-permute-start(f32[64,1152]{1,0:T(8,128)S(1)} %shard_map.53.refs_4_.refs_0_), channel_id=1, source_target_pairs={{0,3},{1,2},{2,1},{3,0},{4,7},{5,6},{6,5},{7,4},{8,11},{9,10},{10,... | collective-permute-start | bytes 884744 | tf_op jit(solution)/shard_map/ppermute | solution.py:356
  37.8 13.3 %collective-permute-start.6 = (f32[64,1152]{1,0:T(8,128)S(1)}, f32[64,1152]{1,0:T(8,128)S(1)}, u32[]{:S(2)}, u32[]{:S(2)}) collective-permute-start(f32[64,1152]{1,0:T(8,128)S(1)} %shard_map.55.refs_4_.refs_0_), channel_id=1, source_target_pairs={{0,4},{1,5},{2,6},{3,7},{4,0},{5,1},{6,2},{7,3},{8,12},{9,13},{10,... | collective-permute-start | bytes 884744 | tf_op jit(solution)/shard_map/ppermute | solution.py:356
  39.2 10.0 %collective-permute-start.7 = (f32[64,1024]{1,0:T(8,128)S(1)}, f32[64,1024]{1,0:T(8,128)S(1)}, u32[]{:S(2)}, u32[]{:S(2)}) collective-permute-start(f32[64,1024]{1,0:T(8,128)S(1)} %get-tuple-element.60.refs_1_), channel_id=1, source_target_pairs={{0,4},{1,5},{2,6},{3,7},{4,0},{5,1},{6,2},{7,3},{8,12},{9,13},{10,... | collective-permute-start | bytes 786440 | tf_op jit(solution)/shard_map/ppermute | solution.py:356
  51.7 10.5 %collective-permute-start.8 = (f32[64,1152]{1,0:T(8,128)S(1)}, f32[64,1152]{1,0:T(8,128)S(1)}, u32[]{:S(2)}, u32[]{:S(2)}) collective-permute-start(f32[64,1152]{1,0:T(8,128)S(1)} %shard_map.58.refs_4_.refs_0_), channel_id=1, source_target_pairs={{0,12},{1,13},{2,14},{3,15},{4,8},{5,9},{6,10},{7,11},{8,4},{9,5},... | collective-permute-start | bytes 884744 | tf_op jit(solution)/shard_map/ppermute | solution.py:356
  54.5 6.1 %collective-permute-start.9 = (f32[64,512]{1,0:T(8,128)S(1)}, f32[64,512]{1,0:T(8,128)S(1)}, u32[]{:S(2)}, u32[]{:S(2)}) collective-permute-start(f32[64,512]{1,0:T(8,128)S(1)} %get-tuple-element.64.refs_1_), channel_id=1, source_target_pairs={{0,12},{1,13},{2,14},{3,15},{4,8},{5,9},{6,10},{7,11},{8,4},{9,5},... | collective-permute-start | bytes 393224 | tf_op jit(solution)/shard_map/ppermute | solution.py:356
  62.8 5.9 %collective-permute-start.10 = (f32[64,1152]{1,0:T(8,128)S(1)}, f32[64,1152]{1,0:T(8,128)S(1)}, u32[]{:S(2)}, u32[]{:S(2)}) collective-permute-start(f32[64,1152]{1,0:T(8,128)S(1)} %shard_map.60.refs_1_.refs_4_), channel_id=1, source_target_pairs={{0,16},{16,0},{32,48},{48,32},{64,80},{80,64},{96,112},{112,96},{1... | collective-permute-start | bytes 884744 | tf_op jit(solution)/shard_map/ppermute | solution.py:356
  70.9 4.1 %collective-permute-start.11 = (f32[32,768]{1,0:T(8,128)S(1)}, f32[32,768]{1,0:T(8,128)S(1)}, u32[]{:S(2)}, u32[]{:S(2)}) collective-permute-start(f32[32,768]{1,0:T(8,128)S(1)} %get-tuple-element.67), channel_id=1, source_target_pairs={{0,32},{16,48},{32,0},{48,16},{64,96},{80,112},{96,64},{112,80},{1... | collective-permute-start | bytes 294920 | tf_op jit(solution)/shard_map/ppermute | solution.py:356
  74.9 2.5 %collective-permute-start.12 = (f32[32,768]{1,0:T(8,128)S(1)}, f32[32,768]{1,0:T(8,128)S(1)}, u32[]{:S(2)}, u32[]{:S(2)}) collective-permute-start(f32[32,768]{1,0:T(8,128)S(1)} %collective-permute-done.11.refs_2_), channel_id=1, source_target_pairs={{0,16},{16,0},{32,48},{48,32},{64,80},{80,64},{96,112},{112,96},{1... | collective-permute-start | bytes 294920 | tf_op jit(solution)/shard_map/ppermute | solution.py:356
  79.4 6.1 %collective-permute-start.13 = (f32[32,512]{1,0:T(8,128)S(1)}, f32[32,512]{1,0:T(8,128)S(1)}, u32[]{:S(2)}, u32[]{:S(2)}) collective-permute-start(f32[32,512]{1,0:T(8,128)S(1)} %get-tuple-element.71), channel_id=1, source_target_pairs={{0,64},{16,80},{32,96},{48,112},{64,0},{80,16},{96,32},{112,48},{1... | collective-permute-start | bytes 196616 | tf_op jit(solution)/shard_map/ppermute | solution.py:356
  85.5 1.6 %collective-permute-start.14 = (f32[32,512]{1,0:T(8,128)S(1)}, f32[32,512]{1,0:T(8,128)S(1)}, u32[]{:S(2)}, u32[]{:S(2)}) collective-permute-start(f32[32,512]{1,0:T(8,128)S(1)} %collective-permute-done.13.refs_2_), channel_id=1, source_target_pairs={{0,16},{16,0},{32,48},{48,32},{64,80},{80,64},{96,112},{112,96},{1... | collective-permute-start | bytes 196616 | tf_op jit(solution)/shard_map/ppermute | solution.py:356
  88.9 8.8 %collective-permute-start.15 = (f32[64,256]{1,0:T(8,128)S(1)}, f32[64,256]{1,0:T(8,128)S(1)}, u32[]{:S(2)}, u32[]{:S(2)}) collective-permute-start(f32[64,256]{1,0:T(8,128)S(1)} %get-tuple-element.76.refs_1_), channel_id=1, source_target_pairs={{0,192},{16,208},{32,224},{48,240},{64,128},{80,144},{96,160},{112... | collective-permute-start | bytes 196616 | tf_op jit(solution)/shard_map/ppermute | solution.py:356

commit v9 on v8

--- a/solution.py
+++ b/solution.py
@@ -11,7 +11,7 @@
 LEVELS = 8
 NRHS = 128
 WIDTH = LEVELS * R + NRHS
-NB = 16
+BLOCKS = (8, 8, 16, 16, 16)
 SPLIT = 4
 HALVED = (6, 7)
 F32 = jnp.float32
@@ -68,12 +68,12 @@
         return jnp.broadcast_to(tile[s : s + 1, :], (8, 128))
 
     first = 0
-    while first < R:
-        last = first + NB
+    for size in BLOCKS:
+        last = first + size
         cols = {}
         for r in range(first, last):
             for g in range(r // 8, groups):
-                cols[r, g] = jnp.broadcast_to(tiles[g][:, at + r : at + r + 1], (8, 128))
+                cols[r, g] = jnp.take_along_axis(tiles[g], jnp.full((8, 128), at + r, jnp.int32), axis=1)
         for i in range(first, last, 2):
             gi, s = i // 8, i % 8
             a, b = spread(cols[i, gi], s), spread(cols[i, gi], s + 1)
@@ -211,14 +211,18 @@
         put(far_ref, first, level, value)
 
 
-def reduce_level(k, coupling_ref, rows, p_ref, m_ref):
+def factor(k, coupling_ref, rows):
     o = R * ((k - 1) % 2)
     ids0 = lax.broadcasted_iota(jnp.int32, (R, 128), 0)
     ids1 = lax.broadcasted_iota(jnp.int32, (R, 128), 1)
     weights = 1.0 / coupling_ref[k - 1 : k, :]
     weights = jnp.concatenate([weights, weights], axis=1)
     cap = rows[:, :128] + jnp.where(ids0 + o == ids1, jnp.broadcast_to(weights, (R, 128)), 0.0)
-    minv = chol_inverse(cap, o)
+    return chol_inverse(cap, o)
+
+
+def reduce_level(k, coupling_ref, rows, p_ref, m_ref):
+    minv = factor(k, coupling_ref, rows)
     m_ref[...] = minv
     p = mm(minv, jnp.concatenate([rows, rows], axis=0))
     p_ref[...] = p
@@ -329,9 +333,14 @@
     o_ref[...] = w_ref[:, two:] - mm(w_ref[:, :two], coef)
 
 
-def last_kernel(k, c_ref, own_ref, got_ref, w_ref, o_ref, p_ref, m_ref):
-    p = reduce_level(k, c_ref, own_ref[...] + got_ref[...], p_ref, m_ref)
-    o_ref[...] = apply_level(k, w_ref[...], p, m_ref[...])
+def last_kernel(k, c_ref, own_ref, got_ref, w_ref, o_ref):
+    o = R * ((k - 1) % 2)
+    rows = own_ref[...] + got_ref[...]
+    minv = factor(k, c_ref, rows)[:, R - o : 2 * R - o]
+    left = lax.dot_general(
+        w_ref[:, o : o + R], minv, (((1,), (1,)), ((), ())), precision=HI, preferred_element_type=F32
+    )
+    o_ref[...] = w_ref[:, 128:] - mm(left, mm(minv, rows[:, 128:]))
 
 
 def call(kernel, outs, *args, hbm=(), scratch=(), sems=0, flops=10_000_000):
@@ -376,7 +385,7 @@
         ms.append(m)
         got_y.append(exchange(y, 1))
     far_shape = (R, offsets(SPLIT + 1)[1])
-    near, far = call(gram_kernel, [(R, offsets(1)[1]), far_shape], *ys)
+    near, far = call(gram_kernel, [(R, offsets(1)[1]), far_shape], *ys, *got_y[:3])
     (w,) = call(back_kernel, [(M, WIDTH)], *ys, *zs, *ms)
     got = far_got = None
     dep = w
@@ -387,7 +396,7 @@
         if k + 1 in HALVED:
             outs.append((R // 2, offsets(k + 1)[1]))
         if k == 1:
-            p, minv, near = call(first_level_kernel, outs, coupling, near, *got_y, dep, hbm=(6,))
+            p, minv, near = call(first_level_kernel, outs, coupling, near, *got_y[3:], dep, hbm=(3,))
             more = [near]
         elif k in HALVED:
             kernel = lambda *refs, k=k: halves_level_kernel(k, *refs)
@@ -399,7 +408,7 @@
         if k < SPLIT:
             got = exchange(near, k + 1)
         if k == 1:
-            (far,) = call(first_far_kernel, [far_shape], far, *got_y, p)
+            (far,) = call(first_far_kernel, [far_shape], far, *got_y[3:], p)
         elif k <= SPLIT:
             kernel = lambda *refs, k=k: far_kernel(k, *refs)
             (far,) = call(kernel, [far_shape], far, far_got, p)
@@ -421,10 +430,7 @@
         if k != SPLIT:
             dep = w
     kernel = lambda *refs: last_kernel(LEVELS, *refs)
-    return call(
-        kernel, [(M, NRHS)], coupling, near, got, w,
-        scratch=[(R, width_of(LEVELS)), (R, 128)],
-    )[0]
+    return call(kernel, [(M, NRHS)], coupling, near, got, w)[0]
 
 
 def solution(mesh):

time: 100 us -> 100 us (level)
  the two profiles are of different devices: /device:TPU:39 before, /device:TPU:33 now
where the time goes in v9:
time: 100 us
  waiting for transfers between devices  40.4 us (40%)
  Pallas kernels  34.5 us (34%)
  starting transfers between devices  25.3 us (25%)
    ppermute x16, waiting for transfers between devices, exchange(): lax.ppermute(value, axis, [(s, s ^ mask) for s in range(lax.axis_size(axi...  40.4 us
    pallas_call x22, Pallas kernels, call(): pl.pallas_call(kernel, out_shape=shapes, in_specs=[hb if i in hbm else vm...  34.5 us
    ppermute x16, starting transfers between devices, exchange(): lax.ppermute(value, axis, [(s, s ^ mask) for s in range(lax.axis_size(axi...  25.3 us
  transfers between devices with their start and end apart: 16, of which 10 were waited for; matrix products, arithmetic and copies ran while one was open for 0% of the time, Pallas kernels for 20%

profile of v9, /device:TPU:33, one launch (start us, length us, event | category | flops | bytes accessed | tf_op | source)
XLA Modules:
  0.0 100.4 jit_solution(18141270578772669860)
XLA Ops:
  0.0 2.4 %shard_map.46 = (f32[64,640]{1,0:T(8,128)S(1)}, f32[64,256]{1,0:T(8,128)S(1)}, f32[64,128]{1,0:T(8,128)S(1)}, f32[192,896]{1,0:T(8,128)S(1)}) custom-call(f32[256,256]{1,0:T(8,128)} %d_any.1, f32[256,512]{1,0:T(8,128)} %b_any.1, f32[256,128]{1,0:T(8,128)} %t_any.1), custom_call_target="tpu_custom_call" | custom-call | flops 10000000 | bytes 1000000 | tf_op jit(solution)/shard_map/pallas_call | solution.py:351
  2.4 1.3 %collective-permute-start = (f32[64,640]{1,0:T(8,128)S(1)}, f32[64,640]{1,0:T(8,128)S(1)}, u32[]{:S(2)}, u32[]{:S(2)}) collective-permute-start(f32[64,640]{1,0:T(8,128)S(1)} %get-tuple-element.42.refs_1_.refs_0_), channel_id=1, source_target_pairs={{0,1},{1,0},{2,3},{3,2},{4,5},{5,4},{6,7},{7,6},{8,9},{9,8},{10,11... | collective-permute-start | bytes 491528 | tf_op jit(solution)/shard_map/ppermute | solution.py:365
  3.7 1.8 %shard_map.47 = (f32[64,640]{1,0:T(8,128)S(1)}, f32[64,256]{1,0:T(8,128)S(1)}, f32[64,128]{1,0:T(8,128)S(1)}) custom-call(f32[192,896]{1,0:T(8,128)S(1)} %get-tuple-element.43.refs_0_, f32[64,640]{1,0:T(8,128)S(1)} %get-tuple-element.42.refs_1_.refs_0_, f32[64,256]{1,0:T(8,128)S(1)} %get-tuple-element.44.refs_2_.refs_3_.refs_4_), custom_call_target="tpu_custom_call" | custom-call | flops 10000000 | bytes 1000000 | tf_op jit(solution)/shard_map/pallas_call | solution.py:351
  5.5 0.3 collective-permute-start.1
  5.8 1.8 %shard_map.48 = (f32[64,640]{1,0:T(8,128)S(1)}, f32[64,128]{1,0:T(8,128)S(1)}, f32[64,128]{1,0:T(8,128)S(1)}) custom-call(f32[192,896]{1,0:T(8,128)S(1)} %get-tuple-element.43.refs_0_, f32[64,640]{1,0:T(8,128)S(1)} %get-tuple-element.42.refs_1_.refs_0_, f32[64,640]{1,0:T(8,128)S(1)} %get-tuple-element.45.refs_2_.refs_1_, ...), custom_call_target="tpu_custom_call" | custom-call | flops 10000000 | bytes 1000000 | tf_op jit(solution)/shard_map/pallas_call | solution.py:351
  7.6 1.3 %collective-permute-start.2 = (f32[64,640]{1,0:T(8,128)S(1)}, f32[64,640]{1,0:T(8,128)S(1)}, u32[]{:S(2)}, u32[]{:S(2)}) collective-permute-start(f32[64,640]{1,0:T(8,128)S(1)} %get-tuple-element.47.refs_3_.refs_2_), channel_id=1, source_target_pairs={{0,1},{1,0},{2,3},{3,2},{4,5},{5,4},{6,7},{7,6},{8,9},{9,8},{10,11... | collective-permute-start | bytes 491528 | tf_op jit(solution)/shard_map/ppermute | solution.py:365
  8.9 1.8 %shard_map.49 = (f32[64,640]{1,0:T(8,128)S(1)}, f32[64,128]{1,0:T(8,128)S(1)}, f32[64,128]{1,0:T(8,128)S(1)}) custom-call(f32[192,896]{1,0:T(8,128)S(1)} %get-tuple-element.43.refs_0_, f32[64,640]{1,0:T(8,128)S(1)} %get-tuple-element.42.refs_1_.refs_0_, f32[64,640]{1,0:T(8,128)S(1)} %get-tuple-element.45.refs_2_.refs_1_, ...), custom_call_target="tpu_custom_call" | custom-call | flops 10000000 | bytes 1000000 | tf_op jit(solution)/shard_map/pallas_call | solution.py:351
  10.7 0.5 collective-permute-start.3
  11.3 2.3 %shard_map.51.refs_1_.refs_3_.w_ref = f32[256,640]{1,0:T(8,128)S(1)} custom-call(f32[64,640]{1,0:T(8,128)S(1)} %get-tuple-element.42.refs_1_.refs_0_, f32[64,640]{1,0:T(8,128)S(1)} %get-tuple-element.45.refs_2_.refs_1_, f32[64,640]{1,0:T(8,128)S(1)} %get-tuple-element.47.refs_3_.refs_2_, f32[64,640]{1,0:T(8,128)S(1)} %get-tuple-element.49.refs_3_, ...), custom_call_target="tpu_custom_call" | custom-call | flops 10000000 | bytes 1000000 | tf_op jit(solution)/shard_map/pallas_call | solution.py:351
  13.5 1.2 %collective-permute-done.2.refs_6_ = f32[64,640]{1,0:T(8,128)S(1)} collective-permute-done((f32[64,640]{1,0:T(8,128)S(1)}, f32[64,640]{1,0:T(8,128)S(1)}, u32[]{:S(2)}, u32[]{:S(2)}) %collective-permute-start.2) | collective-permute-done | bytes 163872 | tf_op jit(solution)/shard_map/ppermute | solution.py:365
  14.8 0.0 collective-permute-done.1.refs_5_
  14.8 0.0 collective-permute-done.refs_4_
  14.8 0.0 copy-start
  14.8 2.0 %shard_map.50 = (f32[64,2304]{1,0:T(8,128)S(1)}, f32[64,1152]{1,0:T(8,128)S(1)}) custom-call(f32[64,640]{1,0:T(8,128)S(1)} %get-tuple-element.42.refs_1_.refs_0_, f32[64,640]{1,0:T(8,128)S(1)} %get-tuple-element.45.refs_2_.refs_1_, f32[64,640]{1,0:T(8,128)S(1)} %get-tuple-element.47.refs_3_.refs_2_, f32[64,640]{1,0:T(8,128)S(1)} %get-tuple-element.49.refs_3_, ...), custom_call_target="tpu_custom_call" | custom-call | flops 10000000 | bytes 1000000 | tf_op jit(solution)/shard_map/pallas_call | solution.py:351
  16.8 1.5 %collective-permute-done.3.refs_0_ = f32[64,640]{1,0:T(8,128)S(1)} collective-permute-done((f32[64,640]{1,0:T(8,128)S(1)}, f32[64,640]{1,0:T(8,128)S(1)}, u32[]{:S(2)}, u32[]{:S(2)}) %collective-permute-start.3) | collective-permute-done | bytes 163872 | tf_op jit(solution)/shard_map/ppermute | solution.py:365
  18.3 0.0 copy-done
  18.3 2.4 %shard_map.52 = (f32[64,640]{1,0:T(8,128)S(1)}, f32[64,128]{1,0:T(8,128)S(1)}, f32[64,1536]{1,0:T(8,128)S(1)}) custom-call(f32[8,64]{1,0:T(8,128)S(1)} %copy-done, f32[64,2304]{1,0:T(8,128)S(1)} %get-tuple-element.51.own_ref, f32[64,640]{1,0:T(8,128)S(1)} %collective-permute-done.3.refs_0_, f32[256,640]{1,0:T(8,128)S(1)} %shard_map.51.refs_1_.refs_3_.w_ref), custom_call_target="tpu_custom_call" | custom-call | flops 10000000 | bytes 1000000 | tf_op jit(solution)/shard_map/pallas_call | solution.py:351
  20.7 2.4 %collective-permute-start.5 = (f32[64,1536]{1,0:T(8,128)S(1)}, f32[64,1536]{1,0:T(8,128)S(1)}, u32[]{:S(2)}, u32[]{:S(2)}) collective-permute-start(f32[64,1536]{1,0:T(8,128)S(1)} %get-tuple-element.58.refs_1_), channel_id=1, source_target_pairs={{0,3},{1,2},{2,1},{3,0},{4,7},{5,6},{6,5},{7,4},{8,11},{9,10},{10,... | collective-permute-start | bytes 1179656 | tf_op jit(solution)/shard_map/ppermute | solution.py:365
  23.1 0.8 shard_map.53.refs_4_.refs_0_
  23.9 0.4 collective-permute-start.4
  24.3 7.0 %collective-permute-done.5.refs_2_ = f32[64,1536]{1,0:T(8,128)S(1)} collective-permute-done((f32[64,1536]{1,0:T(8,128)S(1)}, f32[64,1536]{1,0:T(8,128)S(1)}, u32[]{:S(2)}, u32[]{:S(2)}) %collective-permute-start.5) | collective-permute-done | bytes 393248 | tf_op jit(solution)/shard_map/ppermute | solution.py:365
  31.3 1.8 %shard_map.54 = (f32[64,640]{1,0:T(8,128)S(1)}, f32[64,128]{1,0:T(8,128)S(1)}, f32[64,1024]{1,0:T(8,128)S(1)}) custom-call(f32[8,64]{1,0:T(8,128)S(1)} %copy-done, f32[64,1536]{1,0:T(8,128)S(1)} %get-tuple-element.58.refs_1_, f32[64,1536]{1,0:T(8,128)S(1)} %collective-permute-done.5.refs_2_, f32[256,640]{1,0:T(8,128)S(1)} %shard_map.51.refs_1_.refs_3_.w_ref, ...), custom_call_target="tpu_custom_call" | custom-call | flops 10000000 | bytes 1000000 | tf_op jit(solution)/shard_map/pallas_call | solution.py:351
  33.1 4.5 %collective-permute-done.4.refs_1_ = f32[64,1152]{1,0:T(8,128)S(1)} collective-permute-done((f32[64,1152]{1,0:T(8,128)S(1)}, f32[64,1152]{1,0:T(8,128)S(1)}, u32[]{:S(2)}, u32[]{:S(2)}) %collective-permute-start.4) | collective-permute-done | bytes 294944 | tf_op jit(solution)/shard_map/ppermute | solution.py:365
  37.6 0.5 shard_map.55.refs_4_.refs_0_
  38.1 1.4 %collective-permute-start.6 = (f32[64,1152]{1,0:T(8,128)S(1)}, f32[64,1152]{1,0:T(8,128)S(1)}, u32[]{:S(2)}, u32[]{:S(2)}) collective-permute-start(f32[64,1152]{1,0:T(8,128)S(1)} %shard_map.55.refs_4_.refs_0_), channel_id=1, source_target_pairs={{0,4},{1,5},{2,6},{3,7},{4,0},{5,1},{6,2},{7,3},{8,12},{9,13},{10,... | collective-permute-start | bytes 884744 | tf_op jit(solution)/shard_map/ppermute | solution.py:365
  39.5 0.3 collective-permute-start.7
  39.8 1.4 %shard_map.56.refs_3_.w_ref = f32[256,512]{1,0:T(8,128)S(1)} custom-call(f32[256,640]{1,0:T(8,128)S(1)} %shard_map.51.refs_1_.refs_3_.w_ref, f32[64,640]{1,0:T(8,128)S(1)} %get-tuple-element.57.refs_1_.p_ref, f32[64,128]{1,0:T(8,128)S(1)} %get-tuple-element.61.m_ref, f32[64,640]{1,0:T(8,128)S(1)} %get-tuple-element.59.refs_2_.p2_ref, ...), custom_call_target="tpu_custom_call" | custom-call | flops 10000000 | bytes 1000000 | tf_op jit(solution)/shard_map/pallas_call | solution.py:351
  41.3 8.9 %collective-permute-done.7.refs_2_ = f32[64,1024]{1,0:T(8,128)S(1)} collective-permute-done((f32[64,1024]{1,0:T(8,128)S(1)}, f32[64,1024]{1,0:T(8,128)S(1)}, u32[]{:S(2)}, u32[]{:S(2)}) %collective-permute-start.7) | collective-permute-done | bytes 262176 | tf_op jit(solution)/shard_map/ppermute | solution.py:365
  50.2 1.8 %shard_map.57 = (f32[64,512]{1,0:T(8,128)S(1)}, f32[64,128]{1,0:T(8,128)S(1)}, f32[64,512]{1,0:T(8,128)S(1)}) custom-call(f32[8,64]{1,0:T(8,128)S(1)} %copy-done, f32[64,1024]{1,0:T(8,128)S(1)} %get-tuple-element.60.refs_1_, f32[64,1024]{1,0:T(8,128)S(1)} %collective-permute-done.7.refs_2_, f32[256,512]{1,0:T(8,128)S(1)} %shard_map.56.refs_3_.w_ref, ...), custom_call_target="tpu_custom_call" | custom-call | flops 10000000 | bytes 1000000 | tf_op jit(solution)/shard_map/pallas_call | solution.py:351
  52.0 0.0 collective-permute-done.6.refs_1_
  52.1 0.5 shard_map.58.refs_4_.refs_0_
  52.6 2.8 %collective-permute-start.8 = (f32[64,1152]{1,0:T(8,128)S(1)}, f32[64,1152]{1,0:T(8,128)S(1)}, u32[]{:S(2)}, u32[]{:S(2)}) collective-permute-start(f32[64,1152]{1,0:T(8,128)S(1)} %shard_map.58.refs_4_.refs_0_), channel_id=1, source_target_pairs={{0,12},{1,13},{2,14},{3,15},{4,8},{5,9},{6,10},{7,11},{8,4},{9,5},... | collective-permute-start | bytes 884744 | tf_op jit(solution)/shard_map/ppermute | solution.py:365
  55.4 0.1 collective-permute-start.9
  55.5 6.8 %collective-permute-done.9.refs_2_ = f32[64,512]{1,0:T(8,128)S(1)} collective-permute-done((f32[64,512]{1,0:T(8,128)S(1)}, f32[64,512]{1,0:T(8,128)S(1)}, u32[]{:S(2)}, u32[]{:S(2)}) %collective-permute-start.9) | collective-permute-done | bytes 131104 | tf_op jit(solution)/shard_map/ppermute | solution.py:365
  62.3 1.4 %shard_map.59 = (f32[64,512]{1,0:T(8,128)S(1)}, f32[64,128]{1,0:T(8,128)S(1)}) custom-call(f32[8,64]{1,0:T(8,128)S(1)} %copy-done, f32[64,512]{1,0:T(8,128)S(1)} %get-tuple-element.64.refs_1_, f32[64,512]{1,0:T(8,128)S(1)} %collective-permute-done.9.refs_2_, f32[256,512]{1,0:T(8,128)S(1)} %shard_map.56.refs_3_.w_ref, f32[64,1152]{1,0:T(8,128)S(1)} %shard_map.58.refs_4_.refs_0_), custom_call_target="tpu_custom_call" | custom-call | flops 10000000 | bytes 1000000 | tf_op jit(solution)/shard_map/pallas_call | solution.py:351
  63.7 0.0 collective-permute-done.8.refs_1_
  63.7 0.5 shard_map.60.refs_1_.refs_4_
  64.3 4.0 %collective-permute-start.10 = (f32[64,1152]{1,0:T(8,128)S(1)}, f32[64,1152]{1,0:T(8,128)S(1)}, u32[]{:S(2)}, u32[]{:S(2)}) collective-permute-start(f32[64,1152]{1,0:T(8,128)S(1)} %shard_map.60.refs_1_.refs_4_), channel_id=1, source_target_pairs={{0,16},{16,0},{32,48},{48,32},{64,80},{80,64},{96,112},{112,96},{1... | collective-permute-start | bytes 884744 | tf_op jit(solution)/shard_map/ppermute | solution.py:365
  68.3 1.2 %collective-permute-done.10.refs_2_ = f32[64,1152]{1,0:T(8,128)S(1)} collective-permute-done((f32[64,1152]{1,0:T(8,128)S(1)}, f32[64,1152]{1,0:T(8,128)S(1)}, u32[]{:S(2)}, u32[]{:S(2)}) %collective-permute-start.10) | collective-permute-done | bytes 294944 | tf_op jit(solution)/shard_map/ppermute | solution.py:365
  69.5 1.9 %shard_map.61 = (f32[64,384]{1,0:T(8,128)S(1)}, f32[64,128]{1,0:T(8,128)S(1)}, f32[64,768]{1,0:T(8,128)S(1)}, f32[32,768]{1,0:T(8,128)S(1)}) custom-call(f32[8,64]{1,0:T(8,128)S(1)} %copy-done, f32[64,1152]{1,0:T(8,128)S(1)} %shard_map.60.refs_1_.refs_4_, f32[64,1152]{1,0:T(8,128)S(1)} %collective-permute-done.10.refs_2_, ...), custom_call_target="tpu_custom_call" | custom-call | flops 10000000 | bytes 1000000 | tf_op jit(solution)/shard_map/pallas_call | solution.py:351
  71.4 0.1 collective-permute-start.11
  71.5 4.0 %collective-permute-done.11.refs_2_ = f32[32,768]{1,0:T(8,128)S(1)} collective-permute-done((f32[32,768]{1,0:T(8,128)S(1)}, f32[32,768]{1,0:T(8,128)S(1)}, u32[]{:S(2)}, u32[]{:S(2)}) %collective-permute-start.11) | collective-permute-done | bytes 98336 | tf_op jit(solution)/shard_map/ppermute | solution.py:365
  75.5 1.2 %collective-permute-start.12 = (f32[32,768]{1,0:T(8,128)S(1)}, f32[32,768]{1,0:T(8,128)S(1)}, u32[]{:S(2)}, u32[]{:S(2)}) collective-permute-start(f32[32,768]{1,0:T(8,128)S(1)} %collective-permute-done.11.refs_2_), channel_id=1, source_target_pairs={{0,16},{16,0},{32,48},{48,32},{64,80},{80,64},{96,112},{112,96},{1... | collective-permute-start | bytes 294920 | tf_op jit(solution)/shard_map/ppermute | solution.py:365
  76.7 1.3 %shard_map.62.refs_4_.w_ref = f32[256,384]{1,0:T(8,128)S(1)} custom-call(f32[256,512]{1,0:T(8,128)S(1)} %shard_map.56.refs_3_.w_ref, f32[64,512]{1,0:T(8,128)S(1)} %get-tuple-element.63.refs_2_.p_ref, f32[64,128]{1,0:T(8,128)S(1)} %get-tuple-element.68.m_ref, f32[64,512]{1,0:T(8,128)S(1)} %get-tuple-element.65.refs_2_.p2_ref, ...), custom_call_target="tpu_custom_call" | custom-call | flops 10000000 | bytes 1000000 | tf_op jit(solution)/shard_map/pallas_call | solution.py:351
  78.0 0.0 collective-permute-done.12.refs_3_
  78.0 1.7 %shard_map.63 = (f32[64,384]{1,0:T(8,128)S(1)}, f32[64,128]{1,0:T(8,128)S(1)}, f32[64,512]{1,0:T(8,128)S(1)}, f32[32,512]{1,0:T(8,128)S(1)}) custom-call(f32[8,64]{1,0:T(8,128)S(1)} %copy-done, f32[64,768]{1,0:T(8,128)S(1)} %get-tuple-element.66.refs_1_, f32[32,768]{1,0:T(8,128)S(1)} %collective-permute-done.11.refs_2_, ...), custom_call_target="tpu_custom_call" | custom-call | flops 10000000 | bytes 1000000 | tf_op jit(solution)/shard_map/pallas_call | solution.py:351
  79.8 3.1 %collective-permute-start.13 = (f32[32,512]{1,0:T(8,128)S(1)}, f32[32,512]{1,0:T(8,128)S(1)}, u32[]{:S(2)}, u32[]{:S(2)}) collective-permute-start(f32[32,512]{1,0:T(8,128)S(1)} %get-tuple-element.71), channel_id=1, source_target_pairs={{0,64},{16,80},{32,96},{48,112},{64,0},{80,16},{96,32},{112,48},{1... | collective-permute-start | bytes 196616 | tf_op jit(solution)/shard_map/ppermute | solution.py:365
  82.9 3.0 %collective-permute-done.13.refs_2_ = f32[32,512]{1,0:T(8,128)S(1)} collective-permute-done((f32[32,512]{1,0:T(8,128)S(1)}, f32[32,512]{1,0:T(8,128)S(1)}, u32[]{:S(2)}, u32[]{:S(2)}) %collective-permute-start.13) | collective-permute-done | bytes 65568 | tf_op jit(solution)/shard_map/ppermute | solution.py:365
  85.9 0.5 collective-permute-start.14
  86.3 1.1 %shard_map.64.refs_4_.refs_0_ = f32[256,256]{1,0:T(8,128)S(1)} custom-call(f32[256,384]{1,0:T(8,128)S(1)} %shard_map.62.refs_4_.w_ref, f32[64,384]{1,0:T(8,128)S(1)} %get-tuple-element.72.p_ref, f32[64,128]{1,0:T(8,128)S(1)} %get-tuple-element.73.m_ref, f32[64,384]{1,0:T(8,128)S(1)} %get-tuple-element.74.p2_ref, f32[64,128]{1,0:T(8,128)S(1)} %get-tuple-element.75.m2_ref), custom_call_target="tpu_custom_call" | custom-call | flops 10000000 | bytes 1000000 | tf_op jit(solution)/shard_map/pallas_call | solution.py:351
  87.4 0.0 collective-permute-done.14.refs_3_
  87.4 1.8 %shard_map.65 = (f32[64,256]{1,0:T(8,128)S(1)}, f32[64,128]{1,0:T(8,128)S(1)}, f32[64,256]{1,0:T(8,128)S(1)}) custom-call(f32[8,64]{1,0:T(8,128)S(1)} %copy-done, f32[64,512]{1,0:T(8,128)S(1)} %get-tuple-element.70.refs_1_, f32[32,512]{1,0:T(8,128)S(1)} %collective-permute-done.13.refs_2_, f32[32,512]{1,0:T(8,128)S(1)} %collective-permute-done.14.refs_3_, ...), custom_call_target="tpu_custom_call" | custom-call | flops 10000000 | bytes 1000000 | tf_op jit(solution)/shard_map/pallas_call | solution.py:351
  89.2 5.5 %collective-permute-start.15 = (f32[64,256]{1,0:T(8,128)S(1)}, f32[64,256]{1,0:T(8,128)S(1)}, u32[]{:S(2)}, u32[]{:S(2)}) collective-permute-start(f32[64,256]{1,0:T(8,128)S(1)} %get-tuple-element.76.refs_1_), channel_id=1, source_target_pairs={{0,192},{16,208},{32,224},{48,240},{64,128},{80,144},{96,160},{112... | collective-permute-start | bytes 196616 | tf_op jit(solution)/shard_map/ppermute | solution.py:365
  94.7 0.8 shard_map.66.refs_3_
  95.6 2.4 %collective-permute-done.15.refs_2_ = f32[64,256]{1,0:T(8,128)S(1)} collective-permute-done((f32[64,256]{1,0:T(8,128)S(1)}, f32[64,256]{1,0:T(8,128)S(1)}, u32[]{:S(2)}, u32[]{:S(2)}) %collective-permute-start.15) | collective-permute-done | bytes 65568 | tf_op jit(solution)/shard_map/ppermute | solution.py:365
  97.9 2.5 %shard_map.67 = f32[256,128]{1,0:T(8,128)} custom-call(f32[8,64]{1,0:T(8,128)S(1)} %copy-done, f32[64,256]{1,0:T(8,128)S(1)} %get-tuple-element.76.refs_1_, f32[64,256]{1,0:T(8,128)S(1)} %collective-permute-done.15.refs_2_, f32[256,256]{1,0:T(8,128)S(1)} %shard_map.66.refs_3_), custom_call_target="tpu_custom_call" | custom-call | flops 10000000 | bytes 1000000 | tf_op jit(solution)/shard_map/pallas_call | solution.py:351
Async XLA Ops:
  2.4 12.4 %collective-permute-start = (f32[64,640]{1,0:T(8,128)S(1)}, f32[64,640]{1,0:T(8,128)S(1)}, u32[]{:S(2)}, u32[]{:S(2)}) collective-permute-start(f32[64,640]{1,0:T(8,128)S(1)} %get-tuple-element.42.refs_1_.refs_0_), channel_id=1, source_target_pairs={{0,1},{1,0},{2,3},{3,2},{4,5},{5,4},{6,7},{7,6},{8,9},{9,8},{10,11... | collective-permute-start | bytes 491528 | tf_op jit(solution)/shard_map/ppermute | solution.py:365
  5.5 9.3 %collective-permute-start.1 = (f32[64,640]{1,0:T(8,128)S(1)}, f32[64,640]{1,0:T(8,128)S(1)}, u32[]{:S(2)}, u32[]{:S(2)}) collective-permute-start(f32[64,640]{1,0:T(8,128)S(1)} %get-tuple-element.45.refs_2_.refs_1_), channel_id=1, source_target_pairs={{0,1},{1,0},{2,3},{3,2},{4,5},{5,4},{6,7},{7,6},{8,9},{9,8},{10,11... | collective-permute-start | bytes 491528 | tf_op jit(solution)/shard_map/ppermute | solution.py:365
  7.6 7.2 %collective-permute-start.2 = (f32[64,640]{1,0:T(8,128)S(1)}, f32[64,640]{1,0:T(8,128)S(1)}, u32[]{:S(2)}, u32[]{:S(2)}) collective-permute-start(f32[64,640]{1,0:T(8,128)S(1)} %get-tuple-element.47.refs_3_.refs_2_), channel_id=1, source_target_pairs={{0,1},{1,0},{2,3},{3,2},{4,5},{5,4},{6,7},{7,6},{8,9},{9,8},{10,11... | collective-permute-start | bytes 491528 | tf_op jit(solution)/shard_map/ppermute | solution.py:365
  10.7 7.6 %collective-permute-start.3 = (f32[64,640]{1,0:T(8,128)S(1)}, f32[64,640]{1,0:T(8,128)S(1)}, u32[]{:S(2)}, u32[]{:S(2)}) collective-permute-start(f32[64,640]{1,0:T(8,128)S(1)} %get-tuple-element.49.refs_3_), channel_id=1, source_target_pairs={{0,1},{1,0},{2,3},{3,2},{4,5},{5,4},{6,7},{7,6},{8,9},{9,8},{10,11... | collective-permute-start | bytes 491528 | tf_op jit(solution)/shard_map/ppermute | solution.py:365
  14.8 3.5 %copy-start = (f32[8,64]{1,0:T(8,128)S(1)}, f32[8,64]{1,0:T(8,128)}, u32[]{:S(2)}) copy-start(f32[8,64]{1,0:T(8,128)} %refs_0_.13) | copy-start | bytes 6148
  20.7 10.6 %collective-permute-start.5 = (f32[64,1536]{1,0:T(8,128)S(1)}, f32[64,1536]{1,0:T(8,128)S(1)}, u32[]{:S(2)}, u32[]{:S(2)}) collective-permute-start(f32[64,1536]{1,0:T(8,128)S(1)} %get-tuple-element.58.refs_1_), channel_id=1, source_target_pairs={{0,3},{1,2},{2,1},{3,0},{4,7},{5,6},{6,5},{7,4},{8,11},{9,10},{10,... | collective-permute-start | bytes 1179656 | tf_op jit(solution)/shard_map/ppermute | solution.py:365
  23.9 13.7 %collective-permute-start.4 = (f32[64,1152]{1,0:T(8,128)S(1)}, f32[64,1152]{1,0:T(8,128)S(1)}, u32[]{:S(2)}, u32[]{:S(2)}) collective-permute-start(f32[64,1152]{1,0:T(8,128)S(1)} %shard_map.53.refs_4_.refs_0_), channel_id=1, source_target_pairs={{0,3},{1,2},{2,1},{3,0},{4,7},{5,6},{6,5},{7,4},{8,11},{9,10},{10,... | collective-permute-start | bytes 884744 | tf_op jit(solution)/shard_map/ppermute | solution.py:365
  38.1 13.9 %collective-permute-start.6 = (f32[64,1152]{1,0:T(8,128)S(1)}, f32[64,1152]{1,0:T(8,128)S(1)}, u32[]{:S(2)}, u32[]{:S(2)}) collective-permute-start(f32[64,1152]{1,0:T(8,128)S(1)} %shard_map.55.refs_4_.refs_0_), channel_id=1, source_target_pairs={{0,4},{1,5},{2,6},{3,7},{4,0},{5,1},{6,2},{7,3},{8,12},{9,13},{10,... | collective-permute-start | bytes 884744 | tf_op jit(solution)/shard_map/ppermute | solution.py:365
  39.5 10.7 %collective-permute-start.7 = (f32[64,1024]{1,0:T(8,128)S(1)}, f32[64,1024]{1,0:T(8,128)S(1)}, u32[]{:S(2)}, u32[]{:S(2)}) collective-permute-start(f32[64,1024]{1,0:T(8,128)S(1)} %get-tuple-element.60.refs_1_), channel_id=1, source_target_pairs={{0,4},{1,5},{2,6},{3,7},{4,0},{5,1},{6,2},{7,3},{8,12},{9,13},{10,... | collective-permute-start | bytes 786440 | tf_op jit(solution)/shard_map/ppermute | solution.py:365
  52.6 11.1 %collective-permute-start.8 = (f32[64,1152]{1,0:T(8,128)S(1)}, f32[64,1152]{1,0:T(8,128)S(1)}, u32[]{:S(2)}, u32[]{:S(2)}) collective-permute-start(f32[64,1152]{1,0:T(8,128)S(1)} %shard_map.58.refs_4_.refs_0_), channel_id=1, source_target_pairs={{0,12},{1,13},{2,14},{3,15},{4,8},{5,9},{6,10},{7,11},{8,4},{9,5},... | collective-permute-start | bytes 884744 | tf_op jit(solution)/shard_map/ppermute | solution.py:365
  55.4 6.9 %collective-permute-start.9 = (f32[64,512]{1,0:T(8,128)S(1)}, f32[64,512]{1,0:T(8,128)S(1)}, u32[]{:S(2)}, u32[]{:S(2)}) collective-permute-start(f32[64,512]{1,0:T(8,128)S(1)} %get-tuple-element.64.refs_1_), channel_id=1, source_target_pairs={{0,12},{1,13},{2,14},{3,15},{4,8},{5,9},{6,10},{7,11},{8,4},{9,5},... | collective-permute-start | bytes 393224 | tf_op jit(solution)/shard_map/ppermute | solution.py:365
  64.3 5.2 %collective-permute-start.10 = (f32[64,1152]{1,0:T(8,128)S(1)}, f32[64,1152]{1,0:T(8,128)S(1)}, u32[]{:S(2)}, u32[]{:S(2)}) collective-permute-start(f32[64,1152]{1,0:T(8,128)S(1)} %shard_map.60.refs_1_.refs_4_), channel_id=1, source_target_pairs={{0,16},{16,0},{32,48},{48,32},{64,80},{80,64},{96,112},{112,96},{1... | collective-permute-start | bytes 884744 | tf_op jit(solution)/shard_map/ppermute | solution.py:365
  71.4 4.1 %collective-permute-start.11 = (f32[32,768]{1,0:T(8,128)S(1)}, f32[32,768]{1,0:T(8,128)S(1)}, u32[]{:S(2)}, u32[]{:S(2)}) collective-permute-start(f32[32,768]{1,0:T(8,128)S(1)} %get-tuple-element.67), channel_id=1, source_target_pairs={{0,32},{16,48},{32,0},{48,16},{64,96},{80,112},{96,64},{112,80},{1... | collective-permute-start | bytes 294920 | tf_op jit(solution)/shard_map/ppermute | solution.py:365
  75.5 2.6 %collective-permute-start.12 = (f32[32,768]{1,0:T(8,128)S(1)}, f32[32,768]{1,0:T(8,128)S(1)}, u32[]{:S(2)}, u32[]{:S(2)}) collective-permute-start(f32[32,768]{1,0:T(8,128)S(1)} %collective-permute-done.11.refs_2_), channel_id=1, source_target_pairs={{0,16},{16,0},{32,48},{48,32},{64,80},{80,64},{96,112},{112,96},{1... | collective-permute-start | bytes 294920 | tf_op jit(solution)/shard_map/ppermute | solution.py:365
  79.8 6.1 %collective-permute-start.13 = (f32[32,512]{1,0:T(8,128)S(1)}, f32[32,512]{1,0:T(8,128)S(1)}, u32[]{:S(2)}, u32[]{:S(2)}) collective-permute-start(f32[32,512]{1,0:T(8,128)S(1)} %get-tuple-element.71), channel_id=1, source_target_pairs={{0,64},{16,80},{32,96},{48,112},{64,0},{80,16},{96,32},{112,48},{1... | collective-permute-start | bytes 196616 | tf_op jit(solution)/shard_map/ppermute | solution.py:365
  85.9 1.6 %collective-permute-start.14 = (f32[32,512]{1,0:T(8,128)S(1)}, f32[32,512]{1,0:T(8,128)S(1)}, u32[]{:S(2)}, u32[]{:S(2)}) collective-permute-start(f32[32,512]{1,0:T(8,128)S(1)} %collective-permute-done.13.refs_2_), channel_id=1, source_target_pairs={{0,16},{16,0},{32,48},{48,32},{64,80},{80,64},{96,112},{112,96},{1... | collective-permute-start | bytes 196616 | tf_op jit(solution)/shard_map/ppermute | solution.py:365
  89.2 8.7 %collective-permute-start.15 = (f32[64,256]{1,0:T(8,128)S(1)}, f32[64,256]{1,0:T(8,128)S(1)}, u32[]{:S(2)}, u32[]{:S(2)}) collective-permute-start(f32[64,256]{1,0:T(8,128)S(1)} %get-tuple-element.76.refs_1_), channel_id=1, source_target_pairs={{0,192},{16,208},{32,224},{48,240},{64,128},{80,144},{96,160},{112... | collective-permute-start | bytes 196616 | tf_op jit(solution)/shard_map/ppermute | solution.py:365

commit v10 on v9

--- a/solution.py
+++ b/solution.py
@@ -306,12 +306,15 @@
         put(n_ref, first, level, packed(first, own_ref, level) + value)
 
 
-def far_kernel(k, own_ref, got_ref, p_ref, n_ref):
+def less_kernel(k, own_ref, p_ref, n_ref):
     first = SPLIT + 1
     less = schur(k, p_ref[...], first, LEVELS)
     for level, value in pack(first, {level: row_block(less, level) for level in range(first, LEVELS + 1)}).items():
-        both = packed(first, own_ref, level) + packed(first, got_ref, level)
-        put(n_ref, first, level, both - value)
+        put(n_ref, first, level, packed(first, own_ref, level) - value)
+
+
+def add_kernel(own_ref, got_ref, n_ref):
+    n_ref[...] = own_ref[...] + got_ref[...]
 
 
 def apply_level(k, w, p, minv):
@@ -410,8 +413,9 @@
         if k == 1:
             (far,) = call(first_far_kernel, [far_shape], far, *got_y[3:], p)
         elif k <= SPLIT:
-            kernel = lambda *refs, k=k: far_kernel(k, *refs)
-            (far,) = call(kernel, [far_shape], far, far_got, p)
+            kernel = lambda *refs, k=k: less_kernel(k, *refs)
+            (far,) = call(kernel, [far_shape], far, p)
+            (far,) = call(add_kernel, [far_shape], far, far_got)
         if k < SPLIT:
             far_got = exchange(far, k + 1)
         if k == SPLIT:

time: 100 us -> 100 us (level)
    pallas_call x22 -> x25, Pallas kernels: 34.5 us -> 34.6 us  [call(): pl.pallas_call(kernel, out_shape=shapes, in_specs=[hb if i in hbm else vm...]
  transfers between devices with their start and end apart: 16 -> 16, of which waited for: 10 -> 10; matrix products, arithmetic and copies ran while one was open for 0% -> 0% of each run, Pallas kernels for 20% -> 22%
where the time goes in v10:
time: 100 us
  waiting for transfers between devices  39.9 us (40%)
  Pallas kernels  34.6 us (35%)
  starting transfers between devices  25.3 us (25%)
    ppermute x16, waiting for transfers between devices, exchange(): lax.ppermute(value, axis, [(s, s ^ mask) for s in range(lax.axis_size(axi...  39.9 us
    pallas_call x25, Pallas kernels, call(): pl.pallas_call(kernel, out_shape=shapes, in_specs=[hb if i in hbm else vm...  34.6 us
    ppermute x16, starting transfers between devices, exchange(): lax.ppermute(value, axis, [(s, s ^ mask) for s in range(lax.axis_size(axi...  25.3 us
  transfers between devices with their start and end apart: 16, of which 10 were waited for; matrix products, arithmetic and copies ran while one was open for 0% of the time, Pallas kernels for 22%

profile of v10, /device:TPU:33, one launch (start us, length us, event | category | flops | bytes accessed | tf_op | source)
XLA Modules:
  0.0 100.0 jit_solution(14796614842906562671)
XLA Ops:
  0.0 2.4 %shard_map.46 = (f32[64,640]{1,0:T(8,128)S(1)}, f32[64,256]{1,0:T(8,128)S(1)}, f32[64,128]{1,0:T(8,128)S(1)}, f32[192,896]{1,0:T(8,128)S(1)}) custom-call(f32[256,256]{1,0:T(8,128)} %d_any.1, f32[256,512]{1,0:T(8,128)} %b_any.1, f32[256,128]{1,0:T(8,128)} %t_any.1), custom_call_target="tpu_custom_call" | custom-call | flops 10000000 | bytes 1000000 | tf_op jit(solution)/shard_map/pallas_call | solution.py:354
  2.4 1.3 %collective-permute-start = (f32[64,640]{1,0:T(8,128)S(1)}, f32[64,640]{1,0:T(8,128)S(1)}, u32[]{:S(2)}, u32[]{:S(2)}) collective-permute-start(f32[64,640]{1,0:T(8,128)S(1)} %get-tuple-element.42.refs_1_.refs_0_), channel_id=1, source_target_pairs={{0,1},{1,0},{2,3},{3,2},{4,5},{5,4},{6,7},{7,6},{8,9},{9,8},{10,11... | collective-permute-start | bytes 491528 | tf_op jit(solution)/shard_map/ppermute | solution.py:368
  3.7 1.8 %shard_map.47 = (f32[64,640]{1,0:T(8,128)S(1)}, f32[64,256]{1,0:T(8,128)S(1)}, f32[64,128]{1,0:T(8,128)S(1)}) custom-call(f32[192,896]{1,0:T(8,128)S(1)} %get-tuple-element.43.refs_0_, f32[64,640]{1,0:T(8,128)S(1)} %get-tuple-element.42.refs_1_.refs_0_, f32[64,256]{1,0:T(8,128)S(1)} %get-tuple-element.44.refs_2_.refs_3_.refs_4_), custom_call_target="tpu_custom_call" | custom-call | flops 10000000 | bytes 1000000 | tf_op jit(solution)/shard_map/pallas_call | solution.py:354
  5.5 0.3 collective-permute-start.1
  5.8 1.8 %shard_map.48 = (f32[64,640]{1,0:T(8,128)S(1)}, f32[64,128]{1,0:T(8,128)S(1)}, f32[64,128]{1,0:T(8,128)S(1)}) custom-call(f32[192,896]{1,0:T(8,128)S(1)} %get-tuple-element.43.refs_0_, f32[64,640]{1,0:T(8,128)S(1)} %get-tuple-element.42.refs_1_.refs_0_, f32[64,640]{1,0:T(8,128)S(1)} %get-tuple-element.45.refs_2_.refs_1_, ...), custom_call_target="tpu_custom_call" | custom-call | flops 10000000 | bytes 1000000 | tf_op jit(solution)/shard_map/pallas_call | solution.py:354
  7.6 1.3 %collective-permute-start.2 = (f32[64,640]{1,0:T(8,128)S(1)}, f32[64,640]{1,0:T(8,128)S(1)}, u32[]{:S(2)}, u32[]{:S(2)}) collective-permute-start(f32[64,640]{1,0:T(8,128)S(1)} %get-tuple-element.47.refs_3_.refs_2_), channel_id=1, source_target_pairs={{0,1},{1,0},{2,3},{3,2},{4,5},{5,4},{6,7},{7,6},{8,9},{9,8},{10,11... | collective-permute-start | bytes 491528 | tf_op jit(solution)/shard_map/ppermute | solution.py:368
  8.9 1.8 %shard_map.49 = (f32[64,640]{1,0:T(8,128)S(1)}, f32[64,128]{1,0:T(8,128)S(1)}, f32[64,128]{1,0:T(8,128)S(1)}) custom-call(f32[192,896]{1,0:T(8,128)S(1)} %get-tuple-element.43.refs_0_, f32[64,640]{1,0:T(8,128)S(1)} %get-tuple-element.42.refs_1_.refs_0_, f32[64,640]{1,0:T(8,128)S(1)} %get-tuple-element.45.refs_2_.refs_1_, ...), custom_call_target="tpu_custom_call" | custom-call | flops 10000000 | bytes 1000000 | tf_op jit(solution)/shard_map/pallas_call | solution.py:354
  10.7 0.5 collective-permute-start.3
  11.3 2.3 %shard_map.51.refs_1_.refs_3_.w_ref = f32[256,640]{1,0:T(8,128)S(1)} custom-call(f32[64,640]{1,0:T(8,128)S(1)} %get-tuple-element.42.refs_1_.refs_0_, f32[64,640]{1,0:T(8,128)S(1)} %get-tuple-element.45.refs_2_.refs_1_, f32[64,640]{1,0:T(8,128)S(1)} %get-tuple-element.47.refs_3_.refs_2_, f32[64,640]{1,0:T(8,128)S(1)} %get-tuple-element.49.refs_3_, ...), custom_call_target="tpu_custom_call" | custom-call | flops 10000000 | bytes 1000000 | tf_op jit(solution)/shard_map/pallas_call | solution.py:354
  13.5 0.0 collective-permute-done.refs_4_
  13.6 0.0 collective-permute-done.1.refs_5_
  13.6 1.2 %collective-permute-done.2.refs_6_ = f32[64,640]{1,0:T(8,128)S(1)} collective-permute-done((f32[64,640]{1,0:T(8,128)S(1)}, f32[64,640]{1,0:T(8,128)S(1)}, u32[]{:S(2)}, u32[]{:S(2)}) %collective-permute-start.2) | collective-permute-done | bytes 163872 | tf_op jit(solution)/shard_map/ppermute | solution.py:368
  14.8 0.0 copy-start
  14.8 2.0 %shard_map.50 = (f32[64,2304]{1,0:T(8,128)S(1)}, f32[64,1152]{1,0:T(8,128)S(1)}) custom-call(f32[64,640]{1,0:T(8,128)S(1)} %get-tuple-element.42.refs_1_.refs_0_, f32[64,640]{1,0:T(8,128)S(1)} %get-tuple-element.45.refs_2_.refs_1_, f32[64,640]{1,0:T(8,128)S(1)} %get-tuple-element.47.refs_3_.refs_2_, f32[64,640]{1,0:T(8,128)S(1)} %get-tuple-element.49.refs_3_, ...), custom_call_target="tpu_custom_call" | custom-call | flops 10000000 | bytes 1000000 | tf_op jit(solution)/shard_map/pallas_call | solution.py:354
  16.8 1.5 %collective-permute-done.3.refs_0_ = f32[64,640]{1,0:T(8,128)S(1)} collective-permute-done((f32[64,640]{1,0:T(8,128)S(1)}, f32[64,640]{1,0:T(8,128)S(1)}, u32[]{:S(2)}, u32[]{:S(2)}) %collective-permute-start.3) | collective-permute-done | bytes 163872 | tf_op jit(solution)/shard_map/ppermute | solution.py:368
  18.3 0.0 copy-done
  18.3 2.4 %shard_map.52 = (f32[64,640]{1,0:T(8,128)S(1)}, f32[64,128]{1,0:T(8,128)S(1)}, f32[64,1536]{1,0:T(8,128)S(1)}) custom-call(f32[8,64]{1,0:T(8,128)S(1)} %copy-done, f32[64,2304]{1,0:T(8,128)S(1)} %get-tuple-element.51.own_ref, f32[64,640]{1,0:T(8,128)S(1)} %collective-permute-done.3.refs_0_, f32[256,640]{1,0:T(8,128)S(1)} %shard_map.51.refs_1_.refs_3_.w_ref), custom_call_target="tpu_custom_call" | custom-call | flops 10000000 | bytes 1000000 | tf_op jit(solution)/shard_map/pallas_call | solution.py:354
  20.7 2.4 %collective-permute-start.4 = (f32[64,1536]{1,0:T(8,128)S(1)}, f32[64,1536]{1,0:T(8,128)S(1)}, u32[]{:S(2)}, u32[]{:S(2)}) collective-permute-start(f32[64,1536]{1,0:T(8,128)S(1)} %get-tuple-element.58.refs_1_), channel_id=1, source_target_pairs={{0,3},{1,2},{2,1},{3,0},{4,7},{5,6},{6,5},{7,4},{8,11},{9,10},{10,... | collective-permute-start | bytes 1179656 | tf_op jit(solution)/shard_map/ppermute | solution.py:368
  23.1 0.8 shard_map.53.refs_4_.refs_0_
  23.9 0.4 collective-permute-start.5
  24.3 7.0 %collective-permute-done.4.refs_2_ = f32[64,1536]{1,0:T(8,128)S(1)} collective-permute-done((f32[64,1536]{1,0:T(8,128)S(1)}, f32[64,1536]{1,0:T(8,128)S(1)}, u32[]{:S(2)}, u32[]{:S(2)}) %collective-permute-start.4) | collective-permute-done | bytes 393248 | tf_op jit(solution)/shard_map/ppermute | solution.py:368
  31.3 1.8 %shard_map.54 = (f32[64,640]{1,0:T(8,128)S(1)}, f32[64,128]{1,0:T(8,128)S(1)}, f32[64,1024]{1,0:T(8,128)S(1)}) custom-call(f32[8,64]{1,0:T(8,128)S(1)} %copy-done, f32[64,1536]{1,0:T(8,128)S(1)} %get-tuple-element.58.refs_1_, f32[64,1536]{1,0:T(8,128)S(1)} %collective-permute-done.4.refs_2_, f32[256,640]{1,0:T(8,128)S(1)} %shard_map.51.refs_1_.refs_3_.w_ref, ...), custom_call_target="tpu_custom_call" | custom-call | flops 10000000 | bytes 1000000 | tf_op jit(solution)/shard_map/pallas_call | solution.py:354
  33.1 0.5 shard_map.55.own_ref
  33.7 3.9 %collective-permute-done.5.got_ref = f32[64,1152]{1,0:T(8,128)S(1)} collective-permute-done((f32[64,1152]{1,0:T(8,128)S(1)}, f32[64,1152]{1,0:T(8,128)S(1)}, u32[]{:S(2)}, u32[]{:S(2)}) %collective-permute-start.5) | collective-permute-done | bytes 294944 | tf_op jit(solution)/shard_map/ppermute | solution.py:368
  37.6 1.4 %collective-permute-start.7 = (f32[64,1152]{1,0:T(8,128)S(1)}, f32[64,1152]{1,0:T(8,128)S(1)}, u32[]{:S(2)}, u32[]{:S(2)}) collective-permute-start(f32[64,1152]{1,0:T(8,128)S(1)} %shard_map.56.refs_4_.refs_0_), channel_id=1, source_target_pairs={{0,4},{1,5},{2,6},{3,7},{4,0},{5,1},{6,2},{7,3},{8,12},{9,13},{10,... | collective-permute-start | bytes 884744 | tf_op jit(solution)/shard_map/ppermute | solution.py:368
  39.0 0.3 collective-permute-start.6
  39.3 1.4 %shard_map.57.refs_3_.w_ref = f32[256,512]{1,0:T(8,128)S(1)} custom-call(f32[256,640]{1,0:T(8,128)S(1)} %shard_map.51.refs_1_.refs_3_.w_ref, f32[64,640]{1,0:T(8,128)S(1)} %get-tuple-element.57.refs_1_.p_ref, f32[64,128]{1,0:T(8,128)S(1)} %get-tuple-element.61.m_ref, f32[64,640]{1,0:T(8,128)S(1)} %get-tuple-element.59.refs_1_.p2_ref, ...), custom_call_target="tpu_custom_call" | custom-call | flops 10000000 | bytes 1000000 | tf_op jit(solution)/shard_map/pallas_call | solution.py:354
  40.8 8.9 %collective-permute-done.6.refs_2_ = f32[64,1024]{1,0:T(8,128)S(1)} collective-permute-done((f32[64,1024]{1,0:T(8,128)S(1)}, f32[64,1024]{1,0:T(8,128)S(1)}, u32[]{:S(2)}, u32[]{:S(2)}) %collective-permute-start.6) | collective-permute-done | bytes 262176 | tf_op jit(solution)/shard_map/ppermute | solution.py:368
  49.7 1.8 %shard_map.58 = (f32[64,512]{1,0:T(8,128)S(1)}, f32[64,128]{1,0:T(8,128)S(1)}, f32[64,512]{1,0:T(8,128)S(1)}) custom-call(f32[8,64]{1,0:T(8,128)S(1)} %copy-done, f32[64,1024]{1,0:T(8,128)S(1)} %get-tuple-element.60.refs_1_, f32[64,1024]{1,0:T(8,128)S(1)} %collective-permute-done.6.refs_2_, f32[256,512]{1,0:T(8,128)S(1)} %shard_map.57.refs_3_.w_ref, ...), custom_call_target="tpu_custom_call" | custom-call | flops 10000000 | bytes 1000000 | tf_op jit(solution)/shard_map/pallas_call | solution.py:354
  51.5 0.5 shard_map.59.own_ref
  52.1 0.0 collective-permute-done.7.got_ref
  52.1 2.8 %collective-permute-start.9 = (f32[64,1152]{1,0:T(8,128)S(1)}, f32[64,1152]{1,0:T(8,128)S(1)}, u32[]{:S(2)}, u32[]{:S(2)}) collective-permute-start(f32[64,1152]{1,0:T(8,128)S(1)} %shard_map.60.refs_4_.refs_0_), channel_id=1, source_target_pairs={{0,12},{1,13},{2,14},{3,15},{4,8},{5,9},{6,10},{7,11},{8,4},{9,5},... | collective-permute-start | bytes 884744 | tf_op jit(solution)/shard_map/ppermute | solution.py:368
  54.9 0.1 collective-permute-start.8
  55.0 6.8 %collective-permute-done.8.refs_2_ = f32[64,512]{1,0:T(8,128)S(1)} collective-permute-done((f32[64,512]{1,0:T(8,128)S(1)}, f32[64,512]{1,0:T(8,128)S(1)}, u32[]{:S(2)}, u32[]{:S(2)}) %collective-permute-start.8) | collective-permute-done | bytes 131104 | tf_op jit(solution)/shard_map/ppermute | solution.py:368
  61.8 1.4 %shard_map.61 = (f32[64,512]{1,0:T(8,128)S(1)}, f32[64,128]{1,0:T(8,128)S(1)}) custom-call(f32[8,64]{1,0:T(8,128)S(1)} %copy-done, f32[64,512]{1,0:T(8,128)S(1)} %get-tuple-element.64.refs_1_, f32[64,512]{1,0:T(8,128)S(1)} %collective-permute-done.8.refs_2_, f32[256,512]{1,0:T(8,128)S(1)} %shard_map.57.refs_3_.w_ref, f32[64,1152]{1,0:T(8,128)S(1)} %shard_map.60.refs_4_.refs_0_), custom_call_target="tpu_custom_call" | custom-call | flops 10000000 | bytes 1000000 | tf_op jit(solution)/shard_map/pallas_call | solution.py:354
  63.3 0.5 shard_map.62.own_ref
  63.8 0.0 collective-permute-done.9.got_ref
  63.9 4.0 %collective-permute-start.10 = (f32[64,1152]{1,0:T(8,128)S(1)}, f32[64,1152]{1,0:T(8,128)S(1)}, u32[]{:S(2)}, u32[]{:S(2)}) collective-permute-start(f32[64,1152]{1,0:T(8,128)S(1)} %shard_map.63.refs_1_.refs_4_), channel_id=1, source_target_pairs={{0,16},{16,0},{32,48},{48,32},{64,80},{80,64},{96,112},{112,96},{1... | collective-permute-start | bytes 884744 | tf_op jit(solution)/shard_map/ppermute | solution.py:368
  67.8 1.2 %collective-permute-done.10.refs_2_ = f32[64,1152]{1,0:T(8,128)S(1)} collective-permute-done((f32[64,1152]{1,0:T(8,128)S(1)}, f32[64,1152]{1,0:T(8,128)S(1)}, u32[]{:S(2)}, u32[]{:S(2)}) %collective-permute-start.10) | collective-permute-done | bytes 294944 | tf_op jit(solution)/shard_map/ppermute | solution.py:368
  69.1 1.9 %shard_map.64 = (f32[64,384]{1,0:T(8,128)S(1)}, f32[64,128]{1,0:T(8,128)S(1)}, f32[64,768]{1,0:T(8,128)S(1)}, f32[32,768]{1,0:T(8,128)S(1)}) custom-call(f32[8,64]{1,0:T(8,128)S(1)} %copy-done, f32[64,1152]{1,0:T(8,128)S(1)} %shard_map.63.refs_1_.refs_4_, f32[64,1152]{1,0:T(8,128)S(1)} %collective-permute-done.10.refs_2_, ...), custom_call_target="tpu_custom_call" | custom-call | flops 10000000 | bytes 1000000 | tf_op jit(solution)/shard_map/pallas_call | solution.py:354
  71.0 0.1 collective-permute-start.11
  71.1 4.0 %collective-permute-done.11.refs_2_ = f32[32,768]{1,0:T(8,128)S(1)} collective-permute-done((f32[32,768]{1,0:T(8,128)S(1)}, f32[32,768]{1,0:T(8,128)S(1)}, u32[]{:S(2)}, u32[]{:S(2)}) %collective-permute-start.11) | collective-permute-done | bytes 98336 | tf_op jit(solution)/shard_map/ppermute | solution.py:368
  75.1 1.2 %collective-permute-start.12 = (f32[32,768]{1,0:T(8,128)S(1)}, f32[32,768]{1,0:T(8,128)S(1)}, u32[]{:S(2)}, u32[]{:S(2)}) collective-permute-start(f32[32,768]{1,0:T(8,128)S(1)} %collective-permute-done.11.refs_2_), channel_id=1, source_target_pairs={{0,16},{16,0},{32,48},{48,32},{64,80},{80,64},{96,112},{112,96},{1... | collective-permute-start | bytes 294920 | tf_op jit(solution)/shard_map/ppermute | solution.py:368
  76.3 1.3 %shard_map.65.refs_4_.w_ref = f32[256,384]{1,0:T(8,128)S(1)} custom-call(f32[256,512]{1,0:T(8,128)S(1)} %shard_map.57.refs_3_.w_ref, f32[64,512]{1,0:T(8,128)S(1)} %get-tuple-element.63.refs_1_.p_ref, f32[64,128]{1,0:T(8,128)S(1)} %get-tuple-element.68.m_ref, f32[64,512]{1,0:T(8,128)S(1)} %get-tuple-element.65.refs_1_.p2_ref, ...), custom_call_target="tpu_custom_call" | custom-call | flops 10000000 | bytes 1000000 | tf_op jit(solution)/shard_map/pallas_call | solution.py:354
  77.6 0.0 collective-permute-done.12.refs_3_
  77.6 1.7 %shard_map.66 = (f32[64,384]{1,0:T(8,128)S(1)}, f32[64,128]{1,0:T(8,128)S(1)}, f32[64,512]{1,0:T(8,128)S(1)}, f32[32,512]{1,0:T(8,128)S(1)}) custom-call(f32[8,64]{1,0:T(8,128)S(1)} %copy-done, f32[64,768]{1,0:T(8,128)S(1)} %get-tuple-element.66.refs_1_, f32[32,768]{1,0:T(8,128)S(1)} %collective-permute-done.11.refs_2_, ...), custom_call_target="tpu_custom_call" | custom-call | flops 10000000 | bytes 1000000 | tf_op jit(solution)/shard_map/pallas_call | solution.py:354
  79.4 3.1 %collective-permute-start.13 = (f32[32,512]{1,0:T(8,128)S(1)}, f32[32,512]{1,0:T(8,128)S(1)}, u32[]{:S(2)}, u32[]{:S(2)}) collective-permute-start(f32[32,512]{1,0:T(8,128)S(1)} %get-tuple-element.71), channel_id=1, source_target_pairs={{0,64},{16,80},{32,96},{48,112},{64,0},{80,16},{96,32},{112,48},{1... | collective-permute-start | bytes 196616 | tf_op jit(solution)/shard_map/ppermute | solution.py:368
  82.4 3.0 %collective-permute-done.13.refs_2_ = f32[32,512]{1,0:T(8,128)S(1)} collective-permute-done((f32[32,512]{1,0:T(8,128)S(1)}, f32[32,512]{1,0:T(8,128)S(1)}, u32[]{:S(2)}, u32[]{:S(2)}) %collective-permute-start.13) | collective-permute-done | bytes 65568 | tf_op jit(solution)/shard_map/ppermute | solution.py:368
  85.4 0.5 collective-permute-start.14
  85.9 1.1 %shard_map.67.refs_4_.refs_0_ = f32[256,256]{1,0:T(8,128)S(1)} custom-call(f32[256,384]{1,0:T(8,128)S(1)} %shard_map.65.refs_4_.w_ref, f32[64,384]{1,0:T(8,128)S(1)} %get-tuple-element.72.p_ref, f32[64,128]{1,0:T(8,128)S(1)} %get-tuple-element.73.m_ref, f32[64,384]{1,0:T(8,128)S(1)} %get-tuple-element.74.p2_ref, f32[64,128]{1,0:T(8,128)S(1)} %get-tuple-element.75.m2_ref), custom_call_target="tpu_custom_call" | custom-call | flops 10000000 | bytes 1000000 | tf_op jit(solution)/shard_map/pallas_call | solution.py:354
  87.0 0.0 collective-permute-done.14.refs_3_
  87.0 1.8 %shard_map.68 = (f32[64,256]{1,0:T(8,128)S(1)}, f32[64,128]{1,0:T(8,128)S(1)}, f32[64,256]{1,0:T(8,128)S(1)}) custom-call(f32[8,64]{1,0:T(8,128)S(1)} %copy-done, f32[64,512]{1,0:T(8,128)S(1)} %get-tuple-element.70.refs_1_, f32[32,512]{1,0:T(8,128)S(1)} %collective-permute-done.13.refs_2_, f32[32,512]{1,0:T(8,128)S(1)} %collective-permute-done.14.refs_3_, ...), custom_call_target="tpu_custom_call" | custom-call | flops 10000000 | bytes 1000000 | tf_op jit(solution)/shard_map/pallas_call | solution.py:354
  88.8 5.6 %collective-permute-start.15 = (f32[64,256]{1,0:T(8,128)S(1)}, f32[64,256]{1,0:T(8,128)S(1)}, u32[]{:S(2)}, u32[]{:S(2)}) collective-permute-start(f32[64,256]{1,0:T(8,128)S(1)} %get-tuple-element.76.refs_1_), channel_id=1, source_target_pairs={{0,192},{16,208},{32,224},{48,240},{64,128},{80,144},{96,160},{112... | collective-permute-start | bytes 196616 | tf_op jit(solution)/shard_map/ppermute | solution.py:368
  94.3 0.8 shard_map.69.refs_3_
  95.1 2.4 %collective-permute-done.15.refs_2_ = f32[64,256]{1,0:T(8,128)S(1)} collective-permute-done((f32[64,256]{1,0:T(8,128)S(1)}, f32[64,256]{1,0:T(8,128)S(1)}, u32[]{:S(2)}, u32[]{:S(2)}) %collective-permute-start.15) | collective-permute-done | bytes 65568 | tf_op jit(solution)/shard_map/ppermute | solution.py:368
  97.5 2.5 %shard_map.70 = f32[256,128]{1,0:T(8,128)} custom-call(f32[8,64]{1,0:T(8,128)S(1)} %copy-done, f32[64,256]{1,0:T(8,128)S(1)} %get-tuple-element.76.refs_1_, f32[64,256]{1,0:T(8,128)S(1)} %collective-permute-done.15.refs_2_, f32[256,256]{1,0:T(8,128)S(1)} %shard_map.69.refs_3_), custom_call_target="tpu_custom_call" | custom-call | flops 10000000 | bytes 1000000 | tf_op jit(solution)/shard_map/pallas_call | solution.py:354
  (3 shorter events, 0.1 us)
Async XLA Ops:
  2.4 11.1 %collective-permute-start = (f32[64,640]{1,0:T(8,128)S(1)}, f32[64,640]{1,0:T(8,128)S(1)}, u32[]{:S(2)}, u32[]{:S(2)}) collective-permute-start(f32[64,640]{1,0:T(8,128)S(1)} %get-tuple-element.42.refs_1_.refs_0_), channel_id=1, source_target_pairs={{0,1},{1,0},{2,3},{3,2},{4,5},{5,4},{6,7},{7,6},{8,9},{9,8},{10,11... | collective-permute-start | bytes 491528 | tf_op jit(solution)/shard_map/ppermute | solution.py:368
  5.5 8.1 %collective-permute-start.1 = (f32[64,640]{1,0:T(8,128)S(1)}, f32[64,640]{1,0:T(8,128)S(1)}, u32[]{:S(2)}, u32[]{:S(2)}) collective-permute-start(f32[64,640]{1,0:T(8,128)S(1)} %get-tuple-element.45.refs_2_.refs_1_), channel_id=1, source_target_pairs={{0,1},{1,0},{2,3},{3,2},{4,5},{5,4},{6,7},{7,6},{8,9},{9,8},{10,11... | collective-permute-start | bytes 491528 | tf_op jit(solution)/shard_map/ppermute | solution.py:368
  7.6 7.2 %collective-permute-start.2 = (f32[64,640]{1,0:T(8,128)S(1)}, f32[64,640]{1,0:T(8,128)S(1)}, u32[]{:S(2)}, u32[]{:S(2)}) collective-permute-start(f32[64,640]{1,0:T(8,128)S(1)} %get-tuple-element.47.refs_3_.refs_2_), channel_id=1, source_target_pairs={{0,1},{1,0},{2,3},{3,2},{4,5},{5,4},{6,7},{7,6},{8,9},{9,8},{10,11... | collective-permute-start | bytes 491528 | tf_op jit(solution)/shard_map/ppermute | solution.py:368
  10.7 7.6 %collective-permute-start.3 = (f32[64,640]{1,0:T(8,128)S(1)}, f32[64,640]{1,0:T(8,128)S(1)}, u32[]{:S(2)}, u32[]{:S(2)}) collective-permute-start(f32[64,640]{1,0:T(8,128)S(1)} %get-tuple-element.49.refs_3_), channel_id=1, source_target_pairs={{0,1},{1,0},{2,3},{3,2},{4,5},{5,4},{6,7},{7,6},{8,9},{9,8},{10,11... | collective-permute-start | bytes 491528 | tf_op jit(solution)/shard_map/ppermute | solution.py:368
  14.8 3.5 %copy-start = (f32[8,64]{1,0:T(8,128)S(1)}, f32[8,64]{1,0:T(8,128)}, u32[]{:S(2)}) copy-start(f32[8,64]{1,0:T(8,128)} %refs_0_.13) | copy-start | bytes 6148
  20.7 10.6 %collective-permute-start.4 = (f32[64,1536]{1,0:T(8,128)S(1)}, f32[64,1536]{1,0:T(8,128)S(1)}, u32[]{:S(2)}, u32[]{:S(2)}) collective-permute-start(f32[64,1536]{1,0:T(8,128)S(1)} %get-tuple-element.58.refs_1_), channel_id=1, source_target_pairs={{0,3},{1,2},{2,1},{3,0},{4,7},{5,6},{6,5},{7,4},{8,11},{9,10},{10,... | collective-permute-start | bytes 1179656 | tf_op jit(solution)/shard_map/ppermute | solution.py:368
  23.9 13.7 %collective-permute-start.5 = (f32[64,1152]{1,0:T(8,128)S(1)}, f32[64,1152]{1,0:T(8,128)S(1)}, u32[]{:S(2)}, u32[]{:S(2)}) collective-permute-start(f32[64,1152]{1,0:T(8,128)S(1)} %shard_map.53.refs_4_.refs_0_), channel_id=1, source_target_pairs={{0,3},{1,2},{2,1},{3,0},{4,7},{5,6},{6,5},{7,4},{8,11},{9,10},{10,... | collective-permute-start | bytes 884744 | tf_op jit(solution)/shard_map/ppermute | solution.py:368
  37.6 14.4 %collective-permute-start.7 = (f32[64,1152]{1,0:T(8,128)S(1)}, f32[64,1152]{1,0:T(8,128)S(1)}, u32[]{:S(2)}, u32[]{:S(2)}) collective-permute-start(f32[64,1152]{1,0:T(8,128)S(1)} %shard_map.56.refs_4_.refs_0_), channel_id=1, source_target_pairs={{0,4},{1,5},{2,6},{3,7},{4,0},{5,1},{6,2},{7,3},{8,12},{9,13},{10,... | collective-permute-start | bytes 884744 | tf_op jit(solution)/shard_map/ppermute | solution.py:368
  39.0 10.7 %collective-permute-start.6 = (f32[64,1024]{1,0:T(8,128)S(1)}, f32[64,1024]{1,0:T(8,128)S(1)}, u32[]{:S(2)}, u32[]{:S(2)}) collective-permute-start(f32[64,1024]{1,0:T(8,128)S(1)} %get-tuple-element.60.refs_1_), channel_id=1, source_target_pairs={{0,4},{1,5},{2,6},{3,7},{4,0},{5,1},{6,2},{7,3},{8,12},{9,13},{10,... | collective-permute-start | bytes 786440 | tf_op jit(solution)/shard_map/ppermute | solution.py:368
  52.1 11.7 %collective-permute-start.9 = (f32[64,1152]{1,0:T(8,128)S(1)}, f32[64,1152]{1,0:T(8,128)S(1)}, u32[]{:S(2)}, u32[]{:S(2)}) collective-permute-start(f32[64,1152]{1,0:T(8,128)S(1)} %shard_map.60.refs_4_.refs_0_), channel_id=1, source_target_pairs={{0,12},{1,13},{2,14},{3,15},{4,8},{5,9},{6,10},{7,11},{8,4},{9,5},... | collective-permute-start | bytes 884744 | tf_op jit(solution)/shard_map/ppermute | solution.py:368
  54.9 6.9 %collective-permute-start.8 = (f32[64,512]{1,0:T(8,128)S(1)}, f32[64,512]{1,0:T(8,128)S(1)}, u32[]{:S(2)}, u32[]{:S(2)}) collective-permute-start(f32[64,512]{1,0:T(8,128)S(1)} %get-tuple-element.64.refs_1_), channel_id=1, source_target_pairs={{0,12},{1,13},{2,14},{3,15},{4,8},{5,9},{6,10},{7,11},{8,4},{9,5},... | collective-permute-start | bytes 393224 | tf_op jit(solution)/shard_map/ppermute | solution.py:368
  63.9 5.2 %collective-permute-start.10 = (f32[64,1152]{1,0:T(8,128)S(1)}, f32[64,1152]{1,0:T(8,128)S(1)}, u32[]{:S(2)}, u32[]{:S(2)}) collective-permute-start(f32[64,1152]{1,0:T(8,128)S(1)} %shard_map.63.refs_1_.refs_4_), channel_id=1, source_target_pairs={{0,16},{16,0},{32,48},{48,32},{64,80},{80,64},{96,112},{112,96},{1... | collective-permute-start | bytes 884744 | tf_op jit(solution)/shard_map/ppermute | solution.py:368
  71.0 4.1 %collective-permute-start.11 = (f32[32,768]{1,0:T(8,128)S(1)}, f32[32,768]{1,0:T(8,128)S(1)}, u32[]{:S(2)}, u32[]{:S(2)}) collective-permute-start(f32[32,768]{1,0:T(8,128)S(1)} %get-tuple-element.67), channel_id=1, source_target_pairs={{0,32},{16,48},{32,0},{48,16},{64,96},{80,112},{96,64},{112,80},{1... | collective-permute-start | bytes 294920 | tf_op jit(solution)/shard_map/ppermute | solution.py:368
  75.1 2.6 %collective-permute-start.12 = (f32[32,768]{1,0:T(8,128)S(1)}, f32[32,768]{1,0:T(8,128)S(1)}, u32[]{:S(2)}, u32[]{:S(2)}) collective-permute-start(f32[32,768]{1,0:T(8,128)S(1)} %collective-permute-done.11.refs_2_), channel_id=1, source_target_pairs={{0,16},{16,0},{32,48},{48,32},{64,80},{80,64},{96,112},{112,96},{1... | collective-permute-start | bytes 294920 | tf_op jit(solution)/shard_map/ppermute | solution.py:368
  79.4 6.1 %collective-permute-start.13 = (f32[32,512]{1,0:T(8,128)S(1)}, f32[32,512]{1,0:T(8,128)S(1)}, u32[]{:S(2)}, u32[]{:S(2)}) collective-permute-start(f32[32,512]{1,0:T(8,128)S(1)} %get-tuple-element.71), channel_id=1, source_target_pairs={{0,64},{16,80},{32,96},{48,112},{64,0},{80,16},{96,32},{112,48},{1... | collective-permute-start | bytes 196616 | tf_op jit(solution)/shard_map/ppermute | solution.py:368
  85.4 1.6 %collective-permute-start.14 = (f32[32,512]{1,0:T(8,128)S(1)}, f32[32,512]{1,0:T(8,128)S(1)}, u32[]{:S(2)}, u32[]{:S(2)}) collective-permute-start(f32[32,512]{1,0:T(8,128)S(1)} %collective-permute-done.13.refs_2_), channel_id=1, source_target_pairs={{0,16},{16,0},{32,48},{48,32},{64,80},{80,64},{96,112},{112,96},{1... | collective-permute-start | bytes 196616 | tf_op jit(solution)/shard_map/ppermute | solution.py:368
  88.8 8.7 %collective-permute-start.15 = (f32[64,256]{1,0:T(8,128)S(1)}, f32[64,256]{1,0:T(8,128)S(1)}, u32[]{:S(2)}, u32[]{:S(2)}) collective-permute-start(f32[64,256]{1,0:T(8,128)S(1)} %get-tuple-element.76.refs_1_), channel_id=1, source_target_pairs={{0,192},{16,208},{32,224},{48,240},{64,128},{80,144},{96,160},{112... | collective-permute-start | bytes 196616 | tf_op jit(solution)/shard_map/ppermute | solution.py:368

commit v11 on v10

--- a/solution.py
+++ b/solution.py
@@ -180,6 +180,10 @@
 
 def packed(first, value, level):
     o = offsets(first)[0][level]
+    if isinstance(value, tuple):
+        if level == first:
+            return value[0][...]
+        value, o = value[1], o - width_in(first, first)
     return value[:, o : o + width_in(first, level)]
 
 
@@ -192,6 +196,11 @@
 
 def put(ref, first, level, value):
     o = offsets(first)[0][level]
+    if isinstance(ref, tuple):
+        if level == first:
+            ref[0][...] = value
+            return
+        ref, o = ref[1], o - width_in(first, first)
     ref[:, o : o + width_in(first, level)] = value
 
 
@@ -262,14 +271,14 @@
 
 
 def first_level_kernel(c_ref, own_ref, *refs):
-    *y_refs, dep_ref, p_ref, m_ref, n_ref = refs
+    *y_refs, dep_ref, p_ref, m_ref, n_ref, n2_ref = refs
     grams = gram_pairs(y_refs, range(SPLIT // 2))
 
     def part(level):
         return packed(1, own_ref, level) + row_block(grams, level)
 
     p = reduce_level(1, c_ref, part(1), p_ref, m_ref)
-    next_level(1, p, part, n_ref)
+    next_level(1, p, part, (n_ref, n2_ref))
 
 
 def level_kernel(k, c_ref, own_ref, got_ref, dep_ref, dep2_ref, p_ref, m_ref, n_ref=None, h_ref=None):
@@ -280,6 +289,17 @@
     next_level(k, p, part, n_ref)
     if h_ref is not None:
         next_half(n_ref, h_ref)
+
+
+def head_kernel(k, c_ref, own_ref, got_ref, dep_ref, dep2_ref, p_ref, m_ref):
+    reduce_level(k, c_ref, own_ref[...] + got_ref[...], p_ref, m_ref)
+
+
+def tail_kernel(k, own_ref, own2_ref, got_ref, got2_ref, p_ref, *n_refs):
+    def part(level):
+        return packed(k, (own_ref, own2_ref), level) + packed(k, (got_ref, got2_ref), level)
+
+    next_level(k, p_ref[...], part, n_refs if len(n_refs) > 1 else n_refs[0])
 
 
 def halves_level_kernel(k, c_ref, own_ref, got_ref, other_ref, dep_ref, p_ref, m_ref, n_ref, h_ref=None):
@@ -394,22 +414,29 @@
     dep = w
     for k in range(1, LEVELS):
         outs = [(R, width_of(k)), (R, 128)]
+        following = []
         if k != SPLIT:
-            outs.append((R, offsets(k + 1)[1]))
+            head, total = width_in(k + 1, k + 1), offsets(k + 1)[1]
+            following = [(R, head), (R, total - head)] if k + 1 < SPLIT else [(R, total)]
         if k + 1 in HALVED:
-            outs.append((R // 2, offsets(k + 1)[1]))
+            following.append((R // 2, offsets(k + 1)[1]))
         if k == 1:
-            p, minv, near = call(first_level_kernel, outs, coupling, near, *got_y[3:], dep, hbm=(3,))
-            more = [near]
+            p, minv, *near = call(first_level_kernel, outs + following, coupling, near, *got_y[3:], dep, hbm=(3,))
+        elif k < SPLIT:
+            kernel = lambda *refs, k=k: head_kernel(k, *refs)
+            p, minv = call(kernel, outs, coupling, near[0], got[0], dep, far, hbm=(3, 4))
+            kernel = lambda *refs, k=k: tail_kernel(k, *refs)
+            near = call(kernel, following, *near, *got, p)
         elif k in HALVED:
             kernel = lambda *refs, k=k: halves_level_kernel(k, *refs)
-            p, minv, *more = call(kernel, outs, coupling, near, got, other, dep, hbm=(4,))
+            p, minv, *near = call(kernel, outs + following, coupling, near[0], got, other, dep, hbm=(4,))
         else:
             kernel = lambda *refs, k=k: level_kernel(k, *refs)
-            p, minv, *more = call(kernel, outs, coupling, near, got, dep, far, hbm=(3, 4))
-        near = more[0] if more else None
-        if k < SPLIT:
-            got = exchange(near, k + 1)
+            p, minv, *near = call(kernel, outs + following, coupling, near[0], got, dep, far, hbm=(3, 4))
+        if k + 1 < SPLIT:
+            got = [exchange(near[0], k + 1), exchange(near[1], k + 1)]
+        elif k + 1 == SPLIT:
+            got = exchange(near[0], k + 1)
         if k == 1:
             (far,) = call(first_far_kernel, [far_shape], far, *got_y[3:], p)
         elif k <= SPLIT:
@@ -419,22 +446,22 @@
         if k < SPLIT:
             far_got = exchange(far, k + 1)
         if k == SPLIT:
-            near = far
+            near = [far]
         if k + 1 in HALVED:
-            got = exchange(more[1], k + 1)
+            got = exchange(near[1], k + 1)
             other = exchange(got, SPLIT + 1)
         elif k >= SPLIT:
-            got = exchange(near, k + 1)
+            got = exchange(near[0], k + 1)
         if k == LEVELS - 1:
             kernel = lambda *refs, k=k: apply_kernel(k, *refs)
             (w,) = call(kernel, [(M, width_of(k + 1))], w, p, minv)
         elif k % 2 == 0:
             (w,) = call(apply_two_kernel, [(M, width_of(k + 1))], w, *before, p, minv)
         before = (p, minv)
-        if k != SPLIT:
+        if k > SPLIT:
             dep = w
     kernel = lambda *refs: last_kernel(LEVELS, *refs)
-    return call(kernel, [(M, NRHS)], coupling, near, got, w)[0]
+    return call(kernel, [(M, NRHS)], coupling, near[0], got, w)[0]
 
 
 def solution(mesh):

time: 100 us -> 101 us (1.010)
  starting transfers between devices: 25.3 us -> 30.9 us
  waiting for transfers between devices: 39.9 us -> 34.9 us
    ppermute x16 -> x18, starting transfers between devices: 25.3 us -> 30.9 us  [exchange(): lax.ppermute(value, axis, [(s, s ^ mask) for s in range(lax.axis_size(axi...]
    ppermute x16 -> x18, waiting for transfers between devices: 39.9 us -> 34.9 us  [exchange(): lax.ppermute(value, axis, [(s, s ^ mask) for s in range(lax.axis_size(axi...]
    pallas_call x25 -> x27, Pallas kernels: 34.6 us -> 34.6 us  [call(): pl.pallas_call(kernel, out_shape=shapes, in_specs=[hb if i in hbm else vm...]
  transfers between devices with their start and end apart: 16 -> 18, of which waited for: 10 -> 11; matrix products, arithmetic and copies ran while one was open for 0% -> 0% of each run, Pallas kernels for 22% -> 21%
where the time goes in v11:
time: 101 us
  waiting for transfers between devices  34.9 us (35%)
  Pallas kernels  34.6 us (34%)
  starting transfers between devices  30.9 us (31%)
    ppermute x18, waiting for transfers between devices, exchange(): lax.ppermute(value, axis, [(s, s ^ mask) for s in range(lax.axis_size(axi...  34.9 us
    pallas_call x27, Pallas kernels, call(): pl.pallas_call(kernel, out_shape=shapes, in_specs=[hb if i in hbm else vm...  34.6 us
    ppermute x18, starting transfers between devices, exchange(): lax.ppermute(value, axis, [(s, s ^ mask) for s in range(lax.axis_size(axi...  30.9 us
  transfers between devices with their start and end apart: 18, of which 11 were waited for; matrix products, arithmetic and copies ran while one was open for 0% of the time, Pallas kernels for 21%

profile of v11, /device:TPU:33, one launch (start us, length us, event | category | flops | bytes accessed | tf_op | source)
XLA Modules:
  0.0 100.7 jit_solution(3021621048254945144)
XLA Ops:
  0.0 2.4 %shard_map.46 = (f32[64,640]{1,0:T(8,128)S(1)}, f32[64,256]{1,0:T(8,128)S(1)}, f32[64,128]{1,0:T(8,128)S(1)}, f32[192,896]{1,0:T(8,128)S(1)}) custom-call(f32[256,256]{1,0:T(8,128)} %d_any.1, f32[256,512]{1,0:T(8,128)} %b_any.1, f32[256,128]{1,0:T(8,128)} %t_any.1), custom_call_target="tpu_custom_call" | custom-call | flops 10000000 | bytes 1000000 | tf_op jit(solution)/shard_map/pallas_call | solution.py:374
  2.4 1.3 %collective-permute-start = (f32[64,640]{1,0:T(8,128)S(1)}, f32[64,640]{1,0:T(8,128)S(1)}, u32[]{:S(2)}, u32[]{:S(2)}) collective-permute-start(f32[64,640]{1,0:T(8,128)S(1)} %get-tuple-element.43.refs_1_.refs_0_), channel_id=1, source_target_pairs={{0,1},{1,0},{2,3},{3,2},{4,5},{5,4},{6,7},{7,6},{8,9},{9,8},{10,11... | collective-permute-start | bytes 491528 | tf_op jit(solution)/shard_map/ppermute | solution.py:388
  3.7 1.8 %shard_map.47 = (f32[64,640]{1,0:T(8,128)S(1)}, f32[64,256]{1,0:T(8,128)S(1)}, f32[64,128]{1,0:T(8,128)S(1)}) custom-call(f32[192,896]{1,0:T(8,128)S(1)} %get-tuple-element.44.refs_0_, f32[64,640]{1,0:T(8,128)S(1)} %get-tuple-element.43.refs_1_.refs_0_, f32[64,256]{1,0:T(8,128)S(1)} %get-tuple-element.45.refs_2_.refs_3_.refs_4_), custom_call_target="tpu_custom_call" | custom-call | flops 10000000 | bytes 1000000 | tf_op jit(solution)/shard_map/pallas_call | solution.py:374
  5.5 0.3 collective-permute-start.1
  5.8 1.8 %shard_map.48 = (f32[64,640]{1,0:T(8,128)S(1)}, f32[64,128]{1,0:T(8,128)S(1)}, f32[64,128]{1,0:T(8,128)S(1)}) custom-call(f32[192,896]{1,0:T(8,128)S(1)} %get-tuple-element.44.refs_0_, f32[64,640]{1,0:T(8,128)S(1)} %get-tuple-element.43.refs_1_.refs_0_, f32[64,640]{1,0:T(8,128)S(1)} %get-tuple-element.46.refs_2_.refs_1_, ...), custom_call_target="tpu_custom_call" | custom-call | flops 10000000 | bytes 1000000 | tf_op jit(solution)/shard_map/pallas_call | solution.py:374
  7.6 1.3 %collective-permute-start.2 = (f32[64,640]{1,0:T(8,128)S(1)}, f32[64,640]{1,0:T(8,128)S(1)}, u32[]{:S(2)}, u32[]{:S(2)}) collective-permute-start(f32[64,640]{1,0:T(8,128)S(1)} %get-tuple-element.48.refs_3_.refs_2_), channel_id=1, source_target_pairs={{0,1},{1,0},{2,3},{3,2},{4,5},{5,4},{6,7},{7,6},{8,9},{9,8},{10,11... | collective-permute-start | bytes 491528 | tf_op jit(solution)/shard_map/ppermute | solution.py:388
  8.9 1.8 %shard_map.49 = (f32[64,640]{1,0:T(8,128)S(1)}, f32[64,128]{1,0:T(8,128)S(1)}, f32[64,128]{1,0:T(8,128)S(1)}) custom-call(f32[192,896]{1,0:T(8,128)S(1)} %get-tuple-element.44.refs_0_, f32[64,640]{1,0:T(8,128)S(1)} %get-tuple-element.43.refs_1_.refs_0_, f32[64,640]{1,0:T(8,128)S(1)} %get-tuple-element.46.refs_2_.refs_1_, ...), custom_call_target="tpu_custom_call" | custom-call | flops 10000000 | bytes 1000000 | tf_op jit(solution)/shard_map/pallas_call | solution.py:374
  10.7 0.5 collective-permute-start.3
  11.3 2.3 %shard_map.51.refs_1_.refs_3_.w_ref = f32[256,640]{1,0:T(8,128)S(1)} custom-call(f32[64,640]{1,0:T(8,128)S(1)} %get-tuple-element.43.refs_1_.refs_0_, f32[64,640]{1,0:T(8,128)S(1)} %get-tuple-element.46.refs_2_.refs_1_, f32[64,640]{1,0:T(8,128)S(1)} %get-tuple-element.48.refs_3_.refs_2_, f32[64,640]{1,0:T(8,128)S(1)} %get-tuple-element.50.refs_3_, ...), custom_call_target="tpu_custom_call" | custom-call | flops 10000000 | bytes 1000000 | tf_op jit(solution)/shard_map/pallas_call | solution.py:374
  13.5 0.0 collective-permute-done.refs_4_
  13.5 0.0 collective-permute-done.1.refs_5_
  13.6 1.2 %collective-permute-done.2.refs_6_ = f32[64,640]{1,0:T(8,128)S(1)} collective-permute-done((f32[64,640]{1,0:T(8,128)S(1)}, f32[64,640]{1,0:T(8,128)S(1)}, u32[]{:S(2)}, u32[]{:S(2)}) %collective-permute-start.2) | collective-permute-done | bytes 163872 | tf_op jit(solution)/shard_map/ppermute | solution.py:388
  14.8 0.0 copy-start
  14.8 2.0 %shard_map.50 = (f32[64,2304]{1,0:T(8,128)S(1)}, f32[64,1152]{1,0:T(8,128)S(1)}) custom-call(f32[64,640]{1,0:T(8,128)S(1)} %get-tuple-element.43.refs_1_.refs_0_, f32[64,640]{1,0:T(8,128)S(1)} %get-tuple-element.46.refs_2_.refs_1_, f32[64,640]{1,0:T(8,128)S(1)} %get-tuple-element.48.refs_3_.refs_2_, f32[64,640]{1,0:T(8,128)S(1)} %get-tuple-element.50.refs_3_, ...), custom_call_target="tpu_custom_call" | custom-call | flops 10000000 | bytes 1000000 | tf_op jit(solution)/shard_map/pallas_call | solution.py:374
  16.8 1.5 %collective-permute-done.3.refs_0_ = f32[64,640]{1,0:T(8,128)S(1)} collective-permute-done((f32[64,640]{1,0:T(8,128)S(1)}, f32[64,640]{1,0:T(8,128)S(1)}, u32[]{:S(2)}, u32[]{:S(2)}) %collective-permute-start.3) | collective-permute-done | bytes 163872 | tf_op jit(solution)/shard_map/ppermute | solution.py:388
  18.3 0.0 copy-done
  18.3 2.4 %shard_map.52 = (f32[64,640]{1,0:T(8,128)S(1)}, f32[64,128]{1,0:T(8,128)S(1)}, f32[64,640]{1,0:T(8,128)S(1)}, f32[64,896]{1,0:T(8,128)S(1)}) custom-call(f32[8,64]{1,0:T(8,128)S(1)} %copy-done, f32[64,2304]{1,0:T(8,128)S(1)} %get-tuple-element.52.own_ref, f32[64,640]{1,0:T(8,128)S(1)} %collective-permute-done.3.refs_0_, ...), custom_call_target="tpu_custom_call" | custom-call | flops 10000000 | bytes 1000000 | tf_op jit(solution)/shard_map/pallas_call | solution.py:374
  20.7 0.8 shard_map.53.refs_4_.refs_0_
  21.5 2.4 %collective-permute-start.5 = (f32[64,1152]{1,0:T(8,128)S(1)}, f32[64,1152]{1,0:T(8,128)S(1)}, u32[]{:S(2)}, u32[]{:S(2)}) collective-permute-start(f32[64,1152]{1,0:T(8,128)S(1)} %shard_map.53.refs_4_.refs_0_), channel_id=1, source_target_pairs={{0,3},{1,2},{2,1},{3,0},{4,7},{5,6},{6,5},{7,4},{8,11},{9,10},{10,... | collective-permute-start | bytes 884744 | tf_op jit(solution)/shard_map/ppermute | solution.py:388
  23.9 0.3 collective-permute-start.4
  24.2 2.3 %collective-permute-start.6 = (f32[64,896]{1,0:T(8,128)S(1)}, f32[64,896]{1,0:T(8,128)S(1)}, u32[]{:S(2)}, u32[]{:S(2)}) collective-permute-start(f32[64,896]{1,0:T(8,128)S(1)} %get-tuple-element.61.refs_1_), channel_id=1, source_target_pairs={{0,3},{1,2},{2,1},{3,0},{4,7},{5,6},{6,5},{7,4},{8,11},{9,10},{10,... | collective-permute-start | bytes 688136 | tf_op jit(solution)/shard_map/ppermute | solution.py:388
  26.6 6.9 %collective-permute-done.4.refs_2_ = f32[64,640]{1,0:T(8,128)S(1)} collective-permute-done((f32[64,640]{1,0:T(8,128)S(1)}, f32[64,640]{1,0:T(8,128)S(1)}, u32[]{:S(2)}, u32[]{:S(2)}) %collective-permute-start.4) | collective-permute-done | bytes 163872 | tf_op jit(solution)/shard_map/ppermute | solution.py:388
  33.5 1.5 %shard_map.54 = (f32[64,640]{1,0:T(8,128)S(1)}, f32[64,128]{1,0:T(8,128)S(1)}) custom-call(f32[8,64]{1,0:T(8,128)S(1)} %copy-done, f32[64,640]{1,0:T(8,128)S(1)} %get-tuple-element.59.refs_1_.refs_0_, f32[64,640]{1,0:T(8,128)S(1)} %collective-permute-done.4.refs_2_, f32[256,640]{1,0:T(8,128)S(1)} %shard_map.51.refs_1_.refs_3_.w_ref, ...), custom_call_target="tpu_custom_call" | custom-call | flops 10000000 | bytes 1000000 | tf_op jit(solution)/shard_map/pallas_call | solution.py:374
  34.9 0.5 shard_map.55.own_ref
  35.5 0.0 collective-permute-done.5.got_ref
  35.5 1.4 %collective-permute-start.8 = (f32[64,1152]{1,0:T(8,128)S(1)}, f32[64,1152]{1,0:T(8,128)S(1)}, u32[]{:S(2)}, u32[]{:S(2)}) collective-permute-start(f32[64,1152]{1,0:T(8,128)S(1)} %shard_map.56.refs_4_.refs_0_), channel_id=1, source_target_pairs={{0,4},{1,5},{2,6},{3,7},{4,0},{5,1},{6,2},{7,3},{8,12},{9,13},{10,... | collective-permute-start | bytes 884744 | tf_op jit(solution)/shard_map/ppermute | solution.py:388
  36.9 1.5 %collective-permute-done.6.refs_3_ = f32[64,896]{1,0:T(8,128)S(1)} collective-permute-done((f32[64,896]{1,0:T(8,128)S(1)}, f32[64,896]{1,0:T(8,128)S(1)}, u32[]{:S(2)}, u32[]{:S(2)}) %collective-permute-start.6) | collective-permute-done | bytes 229408 | tf_op jit(solution)/shard_map/ppermute | solution.py:388
  38.4 0.4 shard_map.57
  38.8 1.6 %collective-permute-start.7 = (f32[64,512]{1,0:T(8,128)S(1)}, f32[64,512]{1,0:T(8,128)S(1)}, u32[]{:S(2)}, u32[]{:S(2)}) collective-permute-start(f32[64,512]{1,0:T(8,128)S(1)} %get-tuple-element.62.refs_1_.refs_0_), channel_id=1, source_target_pairs={{0,4},{1,5},{2,6},{3,7},{4,0},{5,1},{6,2},{7,3},{8,12},{9,13},{10,... | collective-permute-start | bytes 393224 | tf_op jit(solution)/shard_map/ppermute | solution.py:388
  40.4 3.2 %collective-permute-done.7.refs_2_ = f32[64,512]{1,0:T(8,128)S(1)} collective-permute-done((f32[64,512]{1,0:T(8,128)S(1)}, f32[64,512]{1,0:T(8,128)S(1)}, u32[]{:S(2)}, u32[]{:S(2)}) %collective-permute-start.7) | collective-permute-done | bytes 131104 | tf_op jit(solution)/shard_map/ppermute | solution.py:388
  43.6 1.4 %shard_map.58 = (f32[64,512]{1,0:T(8,128)S(1)}, f32[64,128]{1,0:T(8,128)S(1)}) custom-call(f32[8,64]{1,0:T(8,128)S(1)} %copy-done, f32[64,512]{1,0:T(8,128)S(1)} %get-tuple-element.62.refs_1_.refs_0_, f32[64,512]{1,0:T(8,128)S(1)} %collective-permute-done.7.refs_2_, f32[256,640]{1,0:T(8,128)S(1)} %shard_map.51.refs_1_.refs_3_.w_ref, ...), custom_call_target="tpu_custom_call" | custom-call | flops 10000000 | bytes 1000000 | tf_op jit(solution)/shard_map/pallas_call | solution.py:374
  45.1 0.5 shard_map.59.own_ref
  45.6 0.0 collective-permute-done.8.got_ref
  45.7 2.8 %collective-permute-start.11 = (f32[64,1152]{1,0:T(8,128)S(1)}, f32[64,1152]{1,0:T(8,128)S(1)}, u32[]{:S(2)}, u32[]{:S(2)}) collective-permute-start(f32[64,1152]{1,0:T(8,128)S(1)} %shard_map.60.refs_4_.refs_0_), channel_id=1, source_target_pairs={{0,12},{1,13},{2,14},{3,15},{4,8},{5,9},{6,10},{7,11},{8,4},{9,5},... | collective-permute-start | bytes 884744 | tf_op jit(solution)/shard_map/ppermute | solution.py:388
  48.4 0.0 collective-permute-start.9
  48.4 3.8 %collective-permute-done.9.refs_3_ = f32[64,512]{1,0:T(8,128)S(1)} collective-permute-done((f32[64,512]{1,0:T(8,128)S(1)}, f32[64,512]{1,0:T(8,128)S(1)}, u32[]{:S(2)}, u32[]{:S(2)}) %collective-permute-start.9) | collective-permute-done | bytes 131104 | tf_op jit(solution)/shard_map/ppermute | solution.py:388
  52.2 0.4 shard_map.61.refs_1_
  52.7 0.2 collective-permute-start.10
  52.9 6.2 %collective-permute-done.10.refs_2_ = f32[64,512]{1,0:T(8,128)S(1)} collective-permute-done((f32[64,512]{1,0:T(8,128)S(1)}, f32[64,512]{1,0:T(8,128)S(1)}, u32[]{:S(2)}, u32[]{:S(2)}) %collective-permute-start.10) | collective-permute-done | bytes 131104 | tf_op jit(solution)/shard_map/ppermute | solution.py:388
  59.1 1.4 %shard_map.62 = (f32[64,512]{1,0:T(8,128)S(1)}, f32[64,128]{1,0:T(8,128)S(1)}) custom-call(f32[8,64]{1,0:T(8,128)S(1)} %copy-done, f32[64,512]{1,0:T(8,128)S(1)} %shard_map.61.refs_1_, f32[64,512]{1,0:T(8,128)S(1)} %collective-permute-done.10.refs_2_, f32[256,640]{1,0:T(8,128)S(1)} %shard_map.51.refs_1_.refs_3_.w_ref, f32[64,1152]{1,0:T(8,128)S(1)} %shard_map.60.refs_4_.refs_0_), custom_call_target="tpu_custom_call" | custom-call | flops 10000000 | bytes 1000000 | tf_op jit(solution)/shard_map/pallas_call | solution.py:374
  60.5 0.5 shard_map.63.own_ref
  61.0 0.0 collective-permute-done.11.got_ref
  61.1 6.0 %collective-permute-start.12 = (f32[64,1152]{1,0:T(8,128)S(1)}, f32[64,1152]{1,0:T(8,128)S(1)}, u32[]{:S(2)}, u32[]{:S(2)}) collective-permute-start(f32[64,1152]{1,0:T(8,128)S(1)} %shard_map.64.refs_1_.refs_4_), channel_id=1, source_target_pairs={{0,16},{16,0},{32,48},{48,32},{64,80},{80,64},{96,112},{112,96},{1... | collective-permute-start | bytes 884744 | tf_op jit(solution)/shard_map/ppermute | solution.py:388
  67.1 1.2 %collective-permute-done.12.refs_2_ = f32[64,1152]{1,0:T(8,128)S(1)} collective-permute-done((f32[64,1152]{1,0:T(8,128)S(1)}, f32[64,1152]{1,0:T(8,128)S(1)}, u32[]{:S(2)}, u32[]{:S(2)}) %collective-permute-start.12) | collective-permute-done | bytes 294944 | tf_op jit(solution)/shard_map/ppermute | solution.py:388
  68.3 1.9 %shard_map.65 = (f32[64,384]{1,0:T(8,128)S(1)}, f32[64,128]{1,0:T(8,128)S(1)}, f32[64,768]{1,0:T(8,128)S(1)}, f32[32,768]{1,0:T(8,128)S(1)}) custom-call(f32[8,64]{1,0:T(8,128)S(1)} %copy-done, f32[64,1152]{1,0:T(8,128)S(1)} %shard_map.64.refs_1_.refs_4_, f32[64,1152]{1,0:T(8,128)S(1)} %collective-permute-done.12.refs_2_, ...), custom_call_target="tpu_custom_call" | custom-call | flops 10000000 | bytes 1000000 | tf_op jit(solution)/shard_map/pallas_call | solution.py:374
  70.2 0.1 collective-permute-start.13
  70.3 4.0 %collective-permute-done.13.refs_2_ = f32[32,768]{1,0:T(8,128)S(1)} collective-permute-done((f32[32,768]{1,0:T(8,128)S(1)}, f32[32,768]{1,0:T(8,128)S(1)}, u32[]{:S(2)}, u32[]{:S(2)}) %collective-permute-start.13) | collective-permute-done | bytes 98336 | tf_op jit(solution)/shard_map/ppermute | solution.py:388
  74.3 1.2 %collective-permute-start.14 = (f32[32,768]{1,0:T(8,128)S(1)}, f32[32,768]{1,0:T(8,128)S(1)}, u32[]{:S(2)}, u32[]{:S(2)}) collective-permute-start(f32[32,768]{1,0:T(8,128)S(1)} %collective-permute-done.13.refs_2_), channel_id=1, source_target_pairs={{0,16},{16,0},{32,48},{48,32},{64,80},{80,64},{96,112},{112,96},{1... | collective-permute-start | bytes 294920 | tf_op jit(solution)/shard_map/ppermute | solution.py:388
  75.5 1.4 %shard_map.66.w_ref = f32[256,512]{1,0:T(8,128)S(1)} custom-call(f32[256,640]{1,0:T(8,128)S(1)} %shard_map.51.refs_1_.refs_3_.w_ref, f32[64,640]{1,0:T(8,128)S(1)} %get-tuple-element.58.refs_1_.p_ref, f32[64,128]{1,0:T(8,128)S(1)} %get-tuple-element.68.m_ref, f32[64,640]{1,0:T(8,128)S(1)} %get-tuple-element.60.refs_1_.refs_4_.p2_ref, ...), custom_call_target="tpu_custom_call" | custom-call | flops 10000000 | bytes 1000000 | tf_op jit(solution)/shard_map/pallas_call | solution.py:374
  77.0 1.3 %shard_map.67.refs_4_.w_ref = f32[256,384]{1,0:T(8,128)S(1)} custom-call(f32[256,512]{1,0:T(8,128)S(1)} %shard_map.66.w_ref, f32[64,512]{1,0:T(8,128)S(1)} %get-tuple-element.63.refs_1_.refs_4_.p_ref, f32[64,128]{1,0:T(8,128)S(1)} %get-tuple-element.70.m_ref, f32[64,512]{1,0:T(8,128)S(1)} %get-tuple-element.65.refs_1_.p2_ref, ...), custom_call_target="tpu_custom_call" | custom-call | flops 10000000 | bytes 1000000 | tf_op jit(solution)/shard_map/pallas_call | solution.py:374
  78.3 0.0 collective-permute-done.14.refs_3_
  78.3 1.7 %shard_map.68 = (f32[64,384]{1,0:T(8,128)S(1)}, f32[64,128]{1,0:T(8,128)S(1)}, f32[64,512]{1,0:T(8,128)S(1)}, f32[32,512]{1,0:T(8,128)S(1)}) custom-call(f32[8,64]{1,0:T(8,128)S(1)} %copy-done, f32[64,768]{1,0:T(8,128)S(1)} %get-tuple-element.66.refs_1_, f32[32,768]{1,0:T(8,128)S(1)} %collective-permute-done.13.refs_2_, ...), custom_call_target="tpu_custom_call" | custom-call | flops 10000000 | bytes 1000000 | tf_op jit(solution)/shard_map/pallas_call | solution.py:374
  80.0 3.1 %collective-permute-start.15 = (f32[32,512]{1,0:T(8,128)S(1)}, f32[32,512]{1,0:T(8,128)S(1)}, u32[]{:S(2)}, u32[]{:S(2)}) collective-permute-start(f32[32,512]{1,0:T(8,128)S(1)} %get-tuple-element.73), channel_id=1, source_target_pairs={{0,64},{16,80},{32,96},{48,112},{64,0},{80,16},{96,32},{112,48},{1... | collective-permute-start | bytes 196616 | tf_op jit(solution)/shard_map/ppermute | solution.py:388
  83.1 3.0 %collective-permute-done.15.refs_2_ = f32[32,512]{1,0:T(8,128)S(1)} collective-permute-done((f32[32,512]{1,0:T(8,128)S(1)}, f32[32,512]{1,0:T(8,128)S(1)}, u32[]{:S(2)}, u32[]{:S(2)}) %collective-permute-start.15) | collective-permute-done | bytes 65568 | tf_op jit(solution)/shard_map/ppermute | solution.py:388
  86.1 0.5 collective-permute-start.16
  86.6 1.1 %shard_map.69.refs_4_.refs_0_ = f32[256,256]{1,0:T(8,128)S(1)} custom-call(f32[256,384]{1,0:T(8,128)S(1)} %shard_map.67.refs_4_.w_ref, f32[64,384]{1,0:T(8,128)S(1)} %get-tuple-element.74.p_ref, f32[64,128]{1,0:T(8,128)S(1)} %get-tuple-element.75.m_ref, f32[64,384]{1,0:T(8,128)S(1)} %get-tuple-element.76.p2_ref, f32[64,128]{1,0:T(8,128)S(1)} %get-tuple-element.77.m2_ref), custom_call_target="tpu_custom_call" | custom-call | flops 10000000 | bytes 1000000 | tf_op jit(solution)/shard_map/pallas_call | solution.py:374
  87.6 0.0 collective-permute-done.16.refs_3_
  87.6 1.8 %shard_map.70 = (f32[64,256]{1,0:T(8,128)S(1)}, f32[64,128]{1,0:T(8,128)S(1)}, f32[64,256]{1,0:T(8,128)S(1)}) custom-call(f32[8,64]{1,0:T(8,128)S(1)} %copy-done, f32[64,512]{1,0:T(8,128)S(1)} %get-tuple-element.72.refs_1_, f32[32,512]{1,0:T(8,128)S(1)} %collective-permute-done.15.refs_2_, f32[32,512]{1,0:T(8,128)S(1)} %collective-permute-done.16.refs_3_, ...), custom_call_target="tpu_custom_call" | custom-call | flops 10000000 | bytes 1000000 | tf_op jit(solution)/shard_map/pallas_call | solution.py:374
  89.4 5.6 %collective-permute-start.17 = (f32[64,256]{1,0:T(8,128)S(1)}, f32[64,256]{1,0:T(8,128)S(1)}, u32[]{:S(2)}, u32[]{:S(2)}) collective-permute-start(f32[64,256]{1,0:T(8,128)S(1)} %get-tuple-element.78.refs_1_), channel_id=1, source_target_pairs={{0,192},{16,208},{32,224},{48,240},{64,128},{80,144},{96,160},{112... | collective-permute-start | bytes 196616 | tf_op jit(solution)/shard_map/ppermute | solution.py:388
  95.0 0.8 shard_map.71.refs_3_
  95.8 2.4 %collective-permute-done.17.refs_2_ = f32[64,256]{1,0:T(8,128)S(1)} collective-permute-done((f32[64,256]{1,0:T(8,128)S(1)}, f32[64,256]{1,0:T(8,128)S(1)}, u32[]{:S(2)}, u32[]{:S(2)}) %collective-permute-start.17) | collective-permute-done | bytes 65568 | tf_op jit(solution)/shard_map/ppermute | solution.py:388
  98.2 2.5 %shard_map.72 = f32[256,128]{1,0:T(8,128)} custom-call(f32[8,64]{1,0:T(8,128)S(1)} %copy-done, f32[64,256]{1,0:T(8,128)S(1)} %get-tuple-element.78.refs_1_, f32[64,256]{1,0:T(8,128)S(1)} %collective-permute-done.17.refs_2_, f32[256,256]{1,0:T(8,128)S(1)} %shard_map.71.refs_3_), custom_call_target="tpu_custom_call" | custom-call | flops 10000000 | bytes 1000000 | tf_op jit(solution)/shard_map/pallas_call | solution.py:374
  (3 shorter events, 0.1 us)
Async XLA Ops:
  2.4 11.1 %collective-permute-start = (f32[64,640]{1,0:T(8,128)S(1)}, f32[64,640]{1,0:T(8,128)S(1)}, u32[]{:S(2)}, u32[]{:S(2)}) collective-permute-start(f32[64,640]{1,0:T(8,128)S(1)} %get-tuple-element.43.refs_1_.refs_0_), channel_id=1, source_target_pairs={{0,1},{1,0},{2,3},{3,2},{4,5},{5,4},{6,7},{7,6},{8,9},{9,8},{10,11... | collective-permute-start | bytes 491528 | tf_op jit(solution)/shard_map/ppermute | solution.py:388
  5.5 8.1 %collective-permute-start.1 = (f32[64,640]{1,0:T(8,128)S(1)}, f32[64,640]{1,0:T(8,128)S(1)}, u32[]{:S(2)}, u32[]{:S(2)}) collective-permute-start(f32[64,640]{1,0:T(8,128)S(1)} %get-tuple-element.46.refs_2_.refs_1_), channel_id=1, source_target_pairs={{0,1},{1,0},{2,3},{3,2},{4,5},{5,4},{6,7},{7,6},{8,9},{9,8},{10,11... | collective-permute-start | bytes 491528 | tf_op jit(solution)/shard_map/ppermute | solution.py:388
  7.6 7.2 %collective-permute-start.2 = (f32[64,640]{1,0:T(8,128)S(1)}, f32[64,640]{1,0:T(8,128)S(1)}, u32[]{:S(2)}, u32[]{:S(2)}) collective-permute-start(f32[64,640]{1,0:T(8,128)S(1)} %get-tuple-element.48.refs_3_.refs_2_), channel_id=1, source_target_pairs={{0,1},{1,0},{2,3},{3,2},{4,5},{5,4},{6,7},{7,6},{8,9},{9,8},{10,11... | collective-permute-start | bytes 491528 | tf_op jit(solution)/shard_map/ppermute | solution.py:388
  10.7 7.6 %collective-permute-start.3 = (f32[64,640]{1,0:T(8,128)S(1)}, f32[64,640]{1,0:T(8,128)S(1)}, u32[]{:S(2)}, u32[]{:S(2)}) collective-permute-start(f32[64,640]{1,0:T(8,128)S(1)} %get-tuple-element.50.refs_3_), channel_id=1, source_target_pairs={{0,1},{1,0},{2,3},{3,2},{4,5},{5,4},{6,7},{7,6},{8,9},{9,8},{10,11... | collective-permute-start | bytes 491528 | tf_op jit(solution)/shard_map/ppermute | solution.py:388
  14.8 3.5 %copy-start = (f32[8,64]{1,0:T(8,128)S(1)}, f32[8,64]{1,0:T(8,128)}, u32[]{:S(2)}) copy-start(f32[8,64]{1,0:T(8,128)} %refs_0_.13) | copy-start | bytes 6148
  21.5 14.0 %collective-permute-start.5 = (f32[64,1152]{1,0:T(8,128)S(1)}, f32[64,1152]{1,0:T(8,128)S(1)}, u32[]{:S(2)}, u32[]{:S(2)}) collective-permute-start(f32[64,1152]{1,0:T(8,128)S(1)} %shard_map.53.refs_4_.refs_0_), channel_id=1, source_target_pairs={{0,3},{1,2},{2,1},{3,0},{4,7},{5,6},{6,5},{7,4},{8,11},{9,10},{10,... | collective-permute-start | bytes 884744 | tf_op jit(solution)/shard_map/ppermute | solution.py:388
  23.9 9.6 %collective-permute-start.4 = (f32[64,640]{1,0:T(8,128)S(1)}, f32[64,640]{1,0:T(8,128)S(1)}, u32[]{:S(2)}, u32[]{:S(2)}) collective-permute-start(f32[64,640]{1,0:T(8,128)S(1)} %get-tuple-element.59.refs_1_.refs_0_), channel_id=1, source_target_pairs={{0,3},{1,2},{2,1},{3,0},{4,7},{5,6},{6,5},{7,4},{8,11},{9,10},{10,... | collective-permute-start | bytes 491528 | tf_op jit(solution)/shard_map/ppermute | solution.py:388
  24.2 14.2 %collective-permute-start.6 = (f32[64,896]{1,0:T(8,128)S(1)}, f32[64,896]{1,0:T(8,128)S(1)}, u32[]{:S(2)}, u32[]{:S(2)}) collective-permute-start(f32[64,896]{1,0:T(8,128)S(1)} %get-tuple-element.61.refs_1_), channel_id=1, source_target_pairs={{0,3},{1,2},{2,1},{3,0},{4,7},{5,6},{6,5},{7,4},{8,11},{9,10},{10,... | collective-permute-start | bytes 688136 | tf_op jit(solution)/shard_map/ppermute | solution.py:388
  35.5 10.1 %collective-permute-start.8 = (f32[64,1152]{1,0:T(8,128)S(1)}, f32[64,1152]{1,0:T(8,128)S(1)}, u32[]{:S(2)}, u32[]{:S(2)}) collective-permute-start(f32[64,1152]{1,0:T(8,128)S(1)} %shard_map.56.refs_4_.refs_0_), channel_id=1, source_target_pairs={{0,4},{1,5},{2,6},{3,7},{4,0},{5,1},{6,2},{7,3},{8,12},{9,13},{10,... | collective-permute-start | bytes 884744 | tf_op jit(solution)/shard_map/ppermute | solution.py:388
  38.8 4.8 %collective-permute-start.7 = (f32[64,512]{1,0:T(8,128)S(1)}, f32[64,512]{1,0:T(8,128)S(1)}, u32[]{:S(2)}, u32[]{:S(2)}) collective-permute-start(f32[64,512]{1,0:T(8,128)S(1)} %get-tuple-element.62.refs_1_.refs_0_), channel_id=1, source_target_pairs={{0,4},{1,5},{2,6},{3,7},{4,0},{5,1},{6,2},{7,3},{8,12},{9,13},{10,... | collective-permute-start | bytes 393224 | tf_op jit(solution)/shard_map/ppermute | solution.py:388
  45.7 15.4 %collective-permute-start.11 = (f32[64,1152]{1,0:T(8,128)S(1)}, f32[64,1152]{1,0:T(8,128)S(1)}, u32[]{:S(2)}, u32[]{:S(2)}) collective-permute-start(f32[64,1152]{1,0:T(8,128)S(1)} %shard_map.60.refs_4_.refs_0_), channel_id=1, source_target_pairs={{0,12},{1,13},{2,14},{3,15},{4,8},{5,9},{6,10},{7,11},{8,4},{9,5},... | collective-permute-start | bytes 884744 | tf_op jit(solution)/shard_map/ppermute | solution.py:388
  48.4 3.8 %collective-permute-start.9 = (f32[64,512]{1,0:T(8,128)S(1)}, f32[64,512]{1,0:T(8,128)S(1)}, u32[]{:S(2)}, u32[]{:S(2)}) collective-permute-start(f32[64,512]{1,0:T(8,128)S(1)} %get-tuple-element.64.refs_1_), channel_id=1, source_target_pairs={{0,4},{1,5},{2,6},{3,7},{4,0},{5,1},{6,2},{7,3},{8,12},{9,13},{10,... | collective-permute-start | bytes 393224 | tf_op jit(solution)/shard_map/ppermute | solution.py:388
  52.7 6.4 %collective-permute-start.10 = (f32[64,512]{1,0:T(8,128)S(1)}, f32[64,512]{1,0:T(8,128)S(1)}, u32[]{:S(2)}, u32[]{:S(2)}) collective-permute-start(f32[64,512]{1,0:T(8,128)S(1)} %shard_map.61.refs_1_), channel_id=1, source_target_pairs={{0,12},{1,13},{2,14},{3,15},{4,8},{5,9},{6,10},{7,11},{8,4},{9,5},... | collective-permute-start | bytes 393224 | tf_op jit(solution)/shard_map/ppermute | solution.py:388
  61.1 7.2 %collective-permute-start.12 = (f32[64,1152]{1,0:T(8,128)S(1)}, f32[64,1152]{1,0:T(8,128)S(1)}, u32[]{:S(2)}, u32[]{:S(2)}) collective-permute-start(f32[64,1152]{1,0:T(8,128)S(1)} %shard_map.64.refs_1_.refs_4_), channel_id=1, source_target_pairs={{0,16},{16,0},{32,48},{48,32},{64,80},{80,64},{96,112},{112,96},{1... | collective-permute-start | bytes 884744 | tf_op jit(solution)/shard_map/ppermute | solution.py:388
  70.2 4.1 %collective-permute-start.13 = (f32[32,768]{1,0:T(8,128)S(1)}, f32[32,768]{1,0:T(8,128)S(1)}, u32[]{:S(2)}, u32[]{:S(2)}) collective-permute-start(f32[32,768]{1,0:T(8,128)S(1)} %get-tuple-element.67), channel_id=1, source_target_pairs={{0,32},{16,48},{32,0},{48,16},{64,96},{80,112},{96,64},{112,80},{1... | collective-permute-start | bytes 294920 | tf_op jit(solution)/shard_map/ppermute | solution.py:388
  74.3 4.0 %collective-permute-start.14 = (f32[32,768]{1,0:T(8,128)S(1)}, f32[32,768]{1,0:T(8,128)S(1)}, u32[]{:S(2)}, u32[]{:S(2)}) collective-permute-start(f32[32,768]{1,0:T(8,128)S(1)} %collective-permute-done.13.refs_2_), channel_id=1, source_target_pairs={{0,16},{16,0},{32,48},{48,32},{64,80},{80,64},{96,112},{112,96},{1... | collective-permute-start | bytes 294920 | tf_op jit(solution)/shard_map/ppermute | solution.py:388
  80.0 6.1 %collective-permute-start.15 = (f32[32,512]{1,0:T(8,128)S(1)}, f32[32,512]{1,0:T(8,128)S(1)}, u32[]{:S(2)}, u32[]{:S(2)}) collective-permute-start(f32[32,512]{1,0:T(8,128)S(1)} %get-tuple-element.73), channel_id=1, source_target_pairs={{0,64},{16,80},{32,96},{48,112},{64,0},{80,16},{96,32},{112,48},{1... | collective-permute-start | bytes 196616 | tf_op jit(solution)/shard_map/ppermute | solution.py:388
  86.1 1.5 %collective-permute-start.16 = (f32[32,512]{1,0:T(8,128)S(1)}, f32[32,512]{1,0:T(8,128)S(1)}, u32[]{:S(2)}, u32[]{:S(2)}) collective-permute-start(f32[32,512]{1,0:T(8,128)S(1)} %collective-permute-done.15.refs_2_), channel_id=1, source_target_pairs={{0,16},{16,0},{32,48},{48,32},{64,80},{80,64},{96,112},{112,96},{1... | collective-permute-start | bytes 196616 | tf_op jit(solution)/shard_map/ppermute | solution.py:388
  89.4 8.8 %collective-permute-start.17 = (f32[64,256]{1,0:T(8,128)S(1)}, f32[64,256]{1,0:T(8,128)S(1)}, u32[]{:S(2)}, u32[]{:S(2)}) collective-permute-start(f32[64,256]{1,0:T(8,128)S(1)} %get-tuple-element.78.refs_1_), channel_id=1, source_target_pairs={{0,192},{16,208},{32,224},{48,240},{64,128},{80,144},{96,160},{112... | collective-permute-start | bytes 196616 | tf_op jit(solution)/shard_map/ppermute | solution.py:388

commit v12 on v11

--- a/solution.py
+++ b/solution.py
@@ -408,7 +408,7 @@
         ms.append(m)
         got_y.append(exchange(y, 1))
     far_shape = (R, offsets(SPLIT + 1)[1])
-    near, far = call(gram_kernel, [(R, offsets(1)[1]), far_shape], *ys, *got_y[:3])
+    near, far = call(gram_kernel, [(R, offsets(1)[1]), far_shape], *ys, *got_y[:2])
     (w,) = call(back_kernel, [(M, WIDTH)], *ys, *zs, *ms)
     got = far_got = None
     dep = w
@@ -421,7 +421,7 @@
         if k + 1 in HALVED:
             following.append((R // 2, offsets(k + 1)[1]))
         if k == 1:
-            p, minv, *near = call(first_level_kernel, outs + following, coupling, near, *got_y[3:], dep, hbm=(3,))
+            p, minv, *near = call(first_level_kernel, outs + following, coupling, near, *got_y[2:], dep, hbm=(4,))
         elif k < SPLIT:
             kernel = lambda *refs, k=k: head_kernel(k, *refs)
             p, minv = call(kernel, outs, coupling, near[0], got[0], dep, far, hbm=(3, 4))
@@ -438,7 +438,7 @@
         elif k + 1 == SPLIT:
             got = exchange(near[0], k + 1)
         if k == 1:
-            (far,) = call(first_far_kernel, [far_shape], far, *got_y[3:], p)
+            (far,) = call(first_far_kernel, [far_shape], far, *got_y[2:], p)
         elif k <= SPLIT:
             kernel = lambda *refs, k=k: less_kernel(k, *refs)
             (far,) = call(kernel, [far_shape], far, p)

time: 101 us -> 101 us (level)
  the two profiles are of different devices: /device:TPU:33 before, /device:TPU:39 now
where the time goes in v12:
time: 101 us
  Pallas kernels  34.5 us (34%)
  waiting for transfers between devices  34.5 us (34%)
  starting transfers between devices  31.8 us (31%)
    pallas_call x27, Pallas kernels, call(): pl.pallas_call(kernel, out_shape=shapes, in_specs=[hb if i in hbm else vm...  34.5 us
    ppermute x18, waiting for transfers between devices, exchange(): lax.ppermute(value, axis, [(s, s ^ mask) for s in range(lax.axis_size(axi...  34.5 us
    ppermute x18, starting transfers between devices, exchange(): lax.ppermute(value, axis, [(s, s ^ mask) for s in range(lax.axis_size(axi...  31.8 us
  transfers between devices with their start and end apart: 18, of which 10 were waited for; matrix products, arithmetic and copies ran while one was open for 0% of the time, Pallas kernels for 21%

profile of v12, /device:TPU:39, one launch (start us, length us, event | category | flops | bytes accessed | tf_op | source)
XLA Modules:
  0.0 101.0 jit_solution(15980662080721359420)
XLA Ops:
  0.0 2.4 %shard_map.46 = (f32[64,640]{1,0:T(8,128)S(1)}, f32[64,256]{1,0:T(8,128)S(1)}, f32[64,128]{1,0:T(8,128)S(1)}, f32[192,896]{1,0:T(8,128)S(1)}) custom-call(f32[256,256]{1,0:T(8,128)} %d_any.1, f32[256,512]{1,0:T(8,128)} %b_any.1, f32[256,128]{1,0:T(8,128)} %t_any.1), custom_call_target="tpu_custom_call" | custom-call | flops 10000000 | bytes 1000000 | tf_op jit(solution)/shard_map/pallas_call | solution.py:374
  2.4 0.6 collective-permute-start
  3.1 1.8 %shard_map.47 = (f32[64,640]{1,0:T(8,128)S(1)}, f32[64,256]{1,0:T(8,128)S(1)}, f32[64,128]{1,0:T(8,128)S(1)}) custom-call(f32[192,896]{1,0:T(8,128)S(1)} %get-tuple-element.44.refs_0_, f32[64,640]{1,0:T(8,128)S(1)} %get-tuple-element.43.refs_1_.refs_0_, f32[64,256]{1,0:T(8,128)S(1)} %get-tuple-element.45.refs_2_.refs_3_.refs_4_), custom_call_target="tpu_custom_call" | custom-call | flops 10000000 | bytes 1000000 | tf_op jit(solution)/shard_map/pallas_call | solution.py:374
  4.8 1.0 collective-permute-start.1
  5.8 1.8 %shard_map.48 = (f32[64,640]{1,0:T(8,128)S(1)}, f32[64,128]{1,0:T(8,128)S(1)}, f32[64,128]{1,0:T(8,128)S(1)}) custom-call(f32[192,896]{1,0:T(8,128)S(1)} %get-tuple-element.44.refs_0_, f32[64,640]{1,0:T(8,128)S(1)} %get-tuple-element.43.refs_1_.refs_0_, f32[64,640]{1,0:T(8,128)S(1)} %get-tuple-element.46.refs_2_.refs_1_, ...), custom_call_target="tpu_custom_call" | custom-call | flops 10000000 | bytes 1000000 | tf_op jit(solution)/shard_map/pallas_call | solution.py:374
  7.6 1.8 %shard_map.49 = (f32[64,640]{1,0:T(8,128)S(1)}, f32[64,128]{1,0:T(8,128)S(1)}, f32[64,128]{1,0:T(8,128)S(1)}) custom-call(f32[192,896]{1,0:T(8,128)S(1)} %get-tuple-element.44.refs_0_, f32[64,640]{1,0:T(8,128)S(1)} %get-tuple-element.43.refs_1_.refs_0_, f32[64,640]{1,0:T(8,128)S(1)} %get-tuple-element.46.refs_2_.refs_1_, ...), custom_call_target="tpu_custom_call" | custom-call | flops 10000000 | bytes 1000000 | tf_op jit(solution)/shard_map/pallas_call | solution.py:374
  9.5 0.6 collective-permute-start.3
  10.1 0.9 collective-permute-start.2
  11.0 2.3 %shard_map.51.refs_2_.refs_3_.w_ref = f32[256,640]{1,0:T(8,128)S(1)} custom-call(f32[64,640]{1,0:T(8,128)S(1)} %get-tuple-element.43.refs_1_.refs_0_, f32[64,640]{1,0:T(8,128)S(1)} %get-tuple-element.46.refs_2_.refs_1_, f32[64,640]{1,0:T(8,128)S(1)} %get-tuple-element.48.refs_3_.refs_2_, f32[64,640]{1,0:T(8,128)S(1)} %get-tuple-element.50.refs_3_, ...), custom_call_target="tpu_custom_call" | custom-call | flops 10000000 | bytes 1000000 | tf_op jit(solution)/shard_map/pallas_call | solution.py:374
  13.3 0.0 collective-permute-done.1.refs_5_
  13.3 0.0 collective-permute-done.refs_4_
  13.3 0.0 copy-start
  13.3 1.9 %shard_map.50 = (f32[64,2304]{1,0:T(8,128)S(1)}, f32[64,1152]{1,0:T(8,128)S(1)}) custom-call(f32[64,640]{1,0:T(8,128)S(1)} %get-tuple-element.43.refs_1_.refs_0_, f32[64,640]{1,0:T(8,128)S(1)} %get-tuple-element.46.refs_2_.refs_1_, f32[64,640]{1,0:T(8,128)S(1)} %get-tuple-element.48.refs_3_.refs_2_, f32[64,640]{1,0:T(8,128)S(1)} %get-tuple-element.50.refs_3_, ...), custom_call_target="tpu_custom_call" | custom-call | flops 10000000 | bytes 1000000 | tf_op jit(solution)/shard_map/pallas_call | solution.py:374
  15.2 0.0 collective-permute-done.3.refs_1_
  15.2 2.4 %collective-permute-done.2.refs_0_ = f32[64,640]{1,0:T(8,128)S(1)} collective-permute-done((f32[64,640]{1,0:T(8,128)S(1)}, f32[64,640]{1,0:T(8,128)S(1)}, u32[]{:S(2)}, u32[]{:S(2)}) %collective-permute-start.2) | collective-permute-done | bytes 163872 | tf_op jit(solution)/shard_map/ppermute | solution.py:388
  17.6 0.0 copy-done
  17.6 2.3 %shard_map.52 = (f32[64,640]{1,0:T(8,128)S(1)}, f32[64,128]{1,0:T(8,128)S(1)}, f32[64,640]{1,0:T(8,128)S(1)}, f32[64,896]{1,0:T(8,128)S(1)}) custom-call(f32[8,64]{1,0:T(8,128)S(1)} %copy-done, f32[64,2304]{1,0:T(8,128)S(1)} %get-tuple-element.52.own_ref, f32[64,640]{1,0:T(8,128)S(1)} %collective-permute-done.2.refs_0_, ...), custom_call_target="tpu_custom_call" | custom-call | flops 10000000 | bytes 1000000 | tf_op jit(solution)/shard_map/pallas_call | solution.py:374
  19.9 0.8 shard_map.53.refs_4_.refs_0_
  20.7 0.3 collective-permute-start.5
  21.0 2.5 %collective-permute-start.4 = (f32[64,640]{1,0:T(8,128)S(1)}, f32[64,640]{1,0:T(8,128)S(1)}, u32[]{:S(2)}, u32[]{:S(2)}) collective-permute-start(f32[64,640]{1,0:T(8,128)S(1)} %get-tuple-element.59.refs_1_.refs_0_), channel_id=1, source_target_pairs={{0,3},{1,2},{2,1},{3,0},{4,7},{5,6},{6,5},{7,4},{8,11},{9,10},{10,... | collective-permute-start | bytes 491528 | tf_op jit(solution)/shard_map/ppermute | solution.py:388
  23.5 0.2 collective-permute-start.6
  23.7 8.3 %collective-permute-done.4.refs_2_ = f32[64,640]{1,0:T(8,128)S(1)} collective-permute-done((f32[64,640]{1,0:T(8,128)S(1)}, f32[64,640]{1,0:T(8,128)S(1)}, u32[]{:S(2)}, u32[]{:S(2)}) %collective-permute-start.4) | collective-permute-done | bytes 163872 | tf_op jit(solution)/shard_map/ppermute | solution.py:388
  32.0 1.5 %shard_map.54 = (f32[64,640]{1,0:T(8,128)S(1)}, f32[64,128]{1,0:T(8,128)S(1)}) custom-call(f32[8,64]{1,0:T(8,128)S(1)} %copy-done, f32[64,640]{1,0:T(8,128)S(1)} %get-tuple-element.59.refs_1_.refs_0_, f32[64,640]{1,0:T(8,128)S(1)} %collective-permute-done.4.refs_2_, f32[256,640]{1,0:T(8,128)S(1)} %shard_map.51.refs_2_.refs_3_.w_ref, ...), custom_call_target="tpu_custom_call" | custom-call | flops 10000000 | bytes 1000000 | tf_op jit(solution)/shard_map/pallas_call | solution.py:374
  33.5 0.5 shard_map.55.own_ref
  34.0 0.0 collective-permute-done.5.got_ref
  34.1 1.4 %collective-permute-start.8 = (f32[64,1152]{1,0:T(8,128)S(1)}, f32[64,1152]{1,0:T(8,128)S(1)}, u32[]{:S(2)}, u32[]{:S(2)}) collective-permute-start(f32[64,1152]{1,0:T(8,128)S(1)} %shard_map.56.refs_4_.refs_0_), channel_id=1, source_target_pairs={{0,4},{1,5},{2,6},{3,7},{4,0},{5,1},{6,2},{7,3},{8,12},{9,13},{10,... | collective-permute-start | bytes 884744 | tf_op jit(solution)/shard_map/ppermute | solution.py:388
  35.5 1.5 %collective-permute-done.6.refs_3_ = f32[64,896]{1,0:T(8,128)S(1)} collective-permute-done((f32[64,896]{1,0:T(8,128)S(1)}, f32[64,896]{1,0:T(8,128)S(1)}, u32[]{:S(2)}, u32[]{:S(2)}) %collective-permute-start.6) | collective-permute-done | bytes 229408 | tf_op jit(solution)/shard_map/ppermute | solution.py:388
  36.9 0.4 shard_map.57
  37.3 1.6 %collective-permute-start.7 = (f32[64,512]{1,0:T(8,128)S(1)}, f32[64,512]{1,0:T(8,128)S(1)}, u32[]{:S(2)}, u32[]{:S(2)}) collective-permute-start(f32[64,512]{1,0:T(8,128)S(1)} %get-tuple-element.62.refs_1_.refs_0_), channel_id=1, source_target_pairs={{0,4},{1,5},{2,6},{3,7},{4,0},{5,1},{6,2},{7,3},{8,12},{9,13},{10,... | collective-permute-start | bytes 393224 | tf_op jit(solution)/shard_map/ppermute | solution.py:388
  39.0 2.5 %collective-permute-done.7.refs_2_ = f32[64,512]{1,0:T(8,128)S(1)} collective-permute-done((f32[64,512]{1,0:T(8,128)S(1)}, f32[64,512]{1,0:T(8,128)S(1)}, u32[]{:S(2)}, u32[]{:S(2)}) %collective-permute-start.7) | collective-permute-done | bytes 131104 | tf_op jit(solution)/shard_map/ppermute | solution.py:388
  41.5 1.4 %shard_map.58 = (f32[64,512]{1,0:T(8,128)S(1)}, f32[64,128]{1,0:T(8,128)S(1)}) custom-call(f32[8,64]{1,0:T(8,128)S(1)} %copy-done, f32[64,512]{1,0:T(8,128)S(1)} %get-tuple-element.62.refs_1_.refs_0_, f32[64,512]{1,0:T(8,128)S(1)} %collective-permute-done.7.refs_2_, f32[256,640]{1,0:T(8,128)S(1)} %shard_map.51.refs_2_.refs_3_.w_ref, ...), custom_call_target="tpu_custom_call" | custom-call | flops 10000000 | bytes 1000000 | tf_op jit(solution)/shard_map/pallas_call | solution.py:374
  42.9 0.5 shard_map.59.own_ref
  43.5 0.0 collective-permute-done.8.got_ref
  43.5 2.8 %collective-permute-start.11 = (f32[64,1152]{1,0:T(8,128)S(1)}, f32[64,1152]{1,0:T(8,128)S(1)}, u32[]{:S(2)}, u32[]{:S(2)}) collective-permute-start(f32[64,1152]{1,0:T(8,128)S(1)} %shard_map.60.refs_4_.refs_0_), channel_id=1, source_target_pairs={{0,12},{1,13},{2,14},{3,15},{4,8},{5,9},{6,10},{7,11},{8,4},{9,5},... | collective-permute-start | bytes 884744 | tf_op jit(solution)/shard_map/ppermute | solution.py:388
  46.3 0.0 collective-permute-start.9
  46.3 3.8 %collective-permute-done.9.refs_3_ = f32[64,512]{1,0:T(8,128)S(1)} collective-permute-done((f32[64,512]{1,0:T(8,128)S(1)}, f32[64,512]{1,0:T(8,128)S(1)}, u32[]{:S(2)}, u32[]{:S(2)}) %collective-permute-start.9) | collective-permute-done | bytes 131104 | tf_op jit(solution)/shard_map/ppermute | solution.py:388
  50.2 0.4 shard_map.61.refs_1_
  50.6 1.1 %collective-permute-start.10 = (f32[64,512]{1,0:T(8,128)S(1)}, f32[64,512]{1,0:T(8,128)S(1)}, u32[]{:S(2)}, u32[]{:S(2)}) collective-permute-start(f32[64,512]{1,0:T(8,128)S(1)} %shard_map.61.refs_1_), channel_id=1, source_target_pairs={{0,12},{1,13},{2,14},{3,15},{4,8},{5,9},{6,10},{7,11},{8,4},{9,5},... | collective-permute-start | bytes 393224 | tf_op jit(solution)/shard_map/ppermute | solution.py:388
  51.6 5.4 %collective-permute-done.10.refs_2_ = f32[64,512]{1,0:T(8,128)S(1)} collective-permute-done((f32[64,512]{1,0:T(8,128)S(1)}, f32[64,512]{1,0:T(8,128)S(1)}, u32[]{:S(2)}, u32[]{:S(2)}) %collective-permute-start.10) | collective-permute-done | bytes 131104 | tf_op jit(solution)/shard_map/ppermute | solution.py:388
  57.1 1.4 %shard_map.62 = (f32[64,512]{1,0:T(8,128)S(1)}, f32[64,128]{1,0:T(8,128)S(1)}) custom-call(f32[8,64]{1,0:T(8,128)S(1)} %copy-done, f32[64,512]{1,0:T(8,128)S(1)} %shard_map.61.refs_1_, f32[64,512]{1,0:T(8,128)S(1)} %collective-permute-done.10.refs_2_, f32[256,640]{1,0:T(8,128)S(1)} %shard_map.51.refs_2_.refs_3_.w_ref, f32[64,1152]{1,0:T(8,128)S(1)} %shard_map.60.refs_4_.refs_0_), custom_call_target="tpu_custom_call" | custom-call | flops 10000000 | bytes 1000000 | tf_op jit(solution)/shard_map/pallas_call | solution.py:374
  58.5 0.5 shard_map.63.own_ref
  59.1 0.0 collective-permute-done.11.got_ref
  59.1 8.4 %collective-permute-start.12 = (f32[64,1152]{1,0:T(8,128)S(1)}, f32[64,1152]{1,0:T(8,128)S(1)}, u32[]{:S(2)}, u32[]{:S(2)}) collective-permute-start(f32[64,1152]{1,0:T(8,128)S(1)} %shard_map.64.refs_1_.refs_4_), channel_id=1, source_target_pairs={{0,16},{16,0},{32,48},{48,32},{64,80},{80,64},{96,112},{112,96},{1... | collective-permute-start | bytes 884744 | tf_op jit(solution)/shard_map/ppermute | solution.py:388
  67.5 1.2 %collective-permute-done.12.refs_2_ = f32[64,1152]{1,0:T(8,128)S(1)} collective-permute-done((f32[64,1152]{1,0:T(8,128)S(1)}, f32[64,1152]{1,0:T(8,128)S(1)}, u32[]{:S(2)}, u32[]{:S(2)}) %collective-permute-start.12) | collective-permute-done | bytes 294944 | tf_op jit(solution)/shard_map/ppermute | solution.py:388
  68.7 1.9 %shard_map.65 = (f32[64,384]{1,0:T(8,128)S(1)}, f32[64,128]{1,0:T(8,128)S(1)}, f32[64,768]{1,0:T(8,128)S(1)}, f32[32,768]{1,0:T(8,128)S(1)}) custom-call(f32[8,64]{1,0:T(8,128)S(1)} %copy-done, f32[64,1152]{1,0:T(8,128)S(1)} %shard_map.64.refs_1_.refs_4_, f32[64,1152]{1,0:T(8,128)S(1)} %collective-permute-done.12.refs_2_, ...), custom_call_target="tpu_custom_call" | custom-call | flops 10000000 | bytes 1000000 | tf_op jit(solution)/shard_map/pallas_call | solution.py:374
  70.7 0.1 collective-permute-start.13
  70.8 4.0 %collective-permute-done.13.refs_2_ = f32[32,768]{1,0:T(8,128)S(1)} collective-permute-done((f32[32,768]{1,0:T(8,128)S(1)}, f32[32,768]{1,0:T(8,128)S(1)}, u32[]{:S(2)}, u32[]{:S(2)}) %collective-permute-start.13) | collective-permute-done | bytes 98336 | tf_op jit(solution)/shard_map/ppermute | solution.py:388
  74.7 1.2 %collective-permute-start.14 = (f32[32,768]{1,0:T(8,128)S(1)}, f32[32,768]{1,0:T(8,128)S(1)}, u32[]{:S(2)}, u32[]{:S(2)}) collective-permute-start(f32[32,768]{1,0:T(8,128)S(1)} %collective-permute-done.13.refs_2_), channel_id=1, source_target_pairs={{0,16},{16,0},{32,48},{48,32},{64,80},{80,64},{96,112},{112,96},{1... | collective-permute-start | bytes 294920 | tf_op jit(solution)/shard_map/ppermute | solution.py:388
  76.0 1.4 %shard_map.66.w_ref = f32[256,512]{1,0:T(8,128)S(1)} custom-call(f32[256,640]{1,0:T(8,128)S(1)} %shard_map.51.refs_2_.refs_3_.w_ref, f32[64,640]{1,0:T(8,128)S(1)} %get-tuple-element.58.refs_2_.p_ref, f32[64,128]{1,0:T(8,128)S(1)} %get-tuple-element.68.m_ref, f32[64,640]{1,0:T(8,128)S(1)} %get-tuple-element.60.refs_1_.refs_4_.p2_ref, ...), custom_call_target="tpu_custom_call" | custom-call | flops 10000000 | bytes 1000000 | tf_op jit(solution)/shard_map/pallas_call | solution.py:374
  77.4 1.3 %shard_map.67.refs_4_.w_ref = f32[256,384]{1,0:T(8,128)S(1)} custom-call(f32[256,512]{1,0:T(8,128)S(1)} %shard_map.66.w_ref, f32[64,512]{1,0:T(8,128)S(1)} %get-tuple-element.63.refs_1_.refs_4_.p_ref, f32[64,128]{1,0:T(8,128)S(1)} %get-tuple-element.70.m_ref, f32[64,512]{1,0:T(8,128)S(1)} %get-tuple-element.65.refs_1_.p2_ref, ...), custom_call_target="tpu_custom_call" | custom-call | flops 10000000 | bytes 1000000 | tf_op jit(solution)/shard_map/pallas_call | solution.py:374
  78.7 0.0 collective-permute-done.14.refs_3_
  78.7 1.7 %shard_map.68 = (f32[64,384]{1,0:T(8,128)S(1)}, f32[64,128]{1,0:T(8,128)S(1)}, f32[64,512]{1,0:T(8,128)S(1)}, f32[32,512]{1,0:T(8,128)S(1)}) custom-call(f32[8,64]{1,0:T(8,128)S(1)} %copy-done, f32[64,768]{1,0:T(8,128)S(1)} %get-tuple-element.66.refs_1_, f32[32,768]{1,0:T(8,128)S(1)} %collective-permute-done.13.refs_2_, ...), custom_call_target="tpu_custom_call" | custom-call | flops 10000000 | bytes 1000000 | tf_op jit(solution)/shard_map/pallas_call | solution.py:374
  80.4 3.1 %collective-permute-start.15 = (f32[32,512]{1,0:T(8,128)S(1)}, f32[32,512]{1,0:T(8,128)S(1)}, u32[]{:S(2)}, u32[]{:S(2)}) collective-permute-start(f32[32,512]{1,0:T(8,128)S(1)} %get-tuple-element.73), channel_id=1, source_target_pairs={{0,64},{16,80},{32,96},{48,112},{64,0},{80,16},{96,32},{112,48},{1... | collective-permute-start | bytes 196616 | tf_op jit(solution)/shard_map/ppermute | solution.py:388
  83.5 3.0 %collective-permute-done.15.refs_2_ = f32[32,512]{1,0:T(8,128)S(1)} collective-permute-done((f32[32,512]{1,0:T(8,128)S(1)}, f32[32,512]{1,0:T(8,128)S(1)}, u32[]{:S(2)}, u32[]{:S(2)}) %collective-permute-start.15) | collective-permute-done | bytes 65568 | tf_op jit(solution)/shard_map/ppermute | solution.py:388
  86.5 0.5 collective-permute-start.16
  87.0 1.1 %shard_map.69.refs_4_.refs_0_ = f32[256,256]{1,0:T(8,128)S(1)} custom-call(f32[256,384]{1,0:T(8,128)S(1)} %shard_map.67.refs_4_.w_ref, f32[64,384]{1,0:T(8,128)S(1)} %get-tuple-element.74.p_ref, f32[64,128]{1,0:T(8,128)S(1)} %get-tuple-element.75.m_ref, f32[64,384]{1,0:T(8,128)S(1)} %get-tuple-element.76.p2_ref, f32[64,128]{1,0:T(8,128)S(1)} %get-tuple-element.77.m2_ref), custom_call_target="tpu_custom_call" | custom-call | flops 10000000 | bytes 1000000 | tf_op jit(solution)/shard_map/pallas_call | solution.py:374
  88.0 0.0 collective-permute-done.16.refs_3_
  88.1 1.8 %shard_map.70 = (f32[64,256]{1,0:T(8,128)S(1)}, f32[64,128]{1,0:T(8,128)S(1)}, f32[64,256]{1,0:T(8,128)S(1)}) custom-call(f32[8,64]{1,0:T(8,128)S(1)} %copy-done, f32[64,512]{1,0:T(8,128)S(1)} %get-tuple-element.72.refs_1_, f32[32,512]{1,0:T(8,128)S(1)} %collective-permute-done.15.refs_2_, f32[32,512]{1,0:T(8,128)S(1)} %collective-permute-done.16.refs_3_, ...), custom_call_target="tpu_custom_call" | custom-call | flops 10000000 | bytes 1000000 | tf_op jit(solution)/shard_map/pallas_call | solution.py:374
  89.8 5.6 %collective-permute-start.17 = (f32[64,256]{1,0:T(8,128)S(1)}, f32[64,256]{1,0:T(8,128)S(1)}, u32[]{:S(2)}, u32[]{:S(2)}) collective-permute-start(f32[64,256]{1,0:T(8,128)S(1)} %get-tuple-element.78.refs_1_), channel_id=1, source_target_pairs={{0,192},{16,208},{32,224},{48,240},{64,128},{80,144},{96,160},{112... | collective-permute-start | bytes 196616 | tf_op jit(solution)/shard_map/ppermute | solution.py:388
  95.4 0.8 shard_map.71.refs_3_
  96.2 2.4 %collective-permute-done.17.refs_2_ = f32[64,256]{1,0:T(8,128)S(1)} collective-permute-done((f32[64,256]{1,0:T(8,128)S(1)}, f32[64,256]{1,0:T(8,128)S(1)}, u32[]{:S(2)}, u32[]{:S(2)}) %collective-permute-start.17) | collective-permute-done | bytes 65568 | tf_op jit(solution)/shard_map/ppermute | solution.py:388
  98.6 2.5 %shard_map.72 = f32[256,128]{1,0:T(8,128)} custom-call(f32[8,64]{1,0:T(8,128)S(1)} %copy-done, f32[64,256]{1,0:T(8,128)S(1)} %get-tuple-element.78.refs_1_, f32[64,256]{1,0:T(8,128)S(1)} %collective-permute-done.17.refs_2_, f32[256,256]{1,0:T(8,128)S(1)} %shard_map.71.refs_3_), custom_call_target="tpu_custom_call" | custom-call | flops 10000000 | bytes 1000000 | tf_op jit(solution)/shard_map/pallas_call | solution.py:374
  (3 shorter events, 0.1 us)
Async XLA Ops:
  2.4 10.9 %collective-permute-start = (f32[64,640]{1,0:T(8,128)S(1)}, f32[64,640]{1,0:T(8,128)S(1)}, u32[]{:S(2)}, u32[]{:S(2)}) collective-permute-start(f32[64,640]{1,0:T(8,128)S(1)} %get-tuple-element.43.refs_1_.refs_0_), channel_id=1, source_target_pairs={{0,1},{1,0},{2,3},{3,2},{4,5},{5,4},{6,7},{7,6},{8,9},{9,8},{10,11... | collective-permute-start | bytes 491528 | tf_op jit(solution)/shard_map/ppermute | solution.py:388
  4.8 8.4 %collective-permute-start.1 = (f32[64,640]{1,0:T(8,128)S(1)}, f32[64,640]{1,0:T(8,128)S(1)}, u32[]{:S(2)}, u32[]{:S(2)}) collective-permute-start(f32[64,640]{1,0:T(8,128)S(1)} %get-tuple-element.46.refs_2_.refs_1_), channel_id=1, source_target_pairs={{0,1},{1,0},{2,3},{3,2},{4,5},{5,4},{6,7},{7,6},{8,9},{9,8},{10,11... | collective-permute-start | bytes 491528 | tf_op jit(solution)/shard_map/ppermute | solution.py:388
  9.5 5.7 %collective-permute-start.3 = (f32[64,640]{1,0:T(8,128)S(1)}, f32[64,640]{1,0:T(8,128)S(1)}, u32[]{:S(2)}, u32[]{:S(2)}) collective-permute-start(f32[64,640]{1,0:T(8,128)S(1)} %get-tuple-element.50.refs_3_), channel_id=1, source_target_pairs={{0,1},{1,0},{2,3},{3,2},{4,5},{5,4},{6,7},{7,6},{8,9},{9,8},{10,11... | collective-permute-start | bytes 491528 | tf_op jit(solution)/shard_map/ppermute | solution.py:388
  10.1 7.5 %collective-permute-start.2 = (f32[64,640]{1,0:T(8,128)S(1)}, f32[64,640]{1,0:T(8,128)S(1)}, u32[]{:S(2)}, u32[]{:S(2)}) collective-permute-start(f32[64,640]{1,0:T(8,128)S(1)} %get-tuple-element.48.refs_3_.refs_2_), channel_id=1, source_target_pairs={{0,1},{1,0},{2,3},{3,2},{4,5},{5,4},{6,7},{7,6},{8,9},{9,8},{10,11... | collective-permute-start | bytes 491528 | tf_op jit(solution)/shard_map/ppermute | solution.py:388
  13.3 4.3 %copy-start = (f32[8,64]{1,0:T(8,128)S(1)}, f32[8,64]{1,0:T(8,128)}, u32[]{:S(2)}) copy-start(f32[8,64]{1,0:T(8,128)} %refs_0_.13) | copy-start | bytes 6148
  20.7 13.3 %collective-permute-start.5 = (f32[64,1152]{1,0:T(8,128)S(1)}, f32[64,1152]{1,0:T(8,128)S(1)}, u32[]{:S(2)}, u32[]{:S(2)}) collective-permute-start(f32[64,1152]{1,0:T(8,128)S(1)} %shard_map.53.refs_4_.refs_0_), channel_id=1, source_target_pairs={{0,3},{1,2},{2,1},{3,0},{4,7},{5,6},{6,5},{7,4},{8,11},{9,10},{10,... | collective-permute-start | bytes 884744 | tf_op jit(solution)/shard_map/ppermute | solution.py:388
  21.0 11.0 %collective-permute-start.4 = (f32[64,640]{1,0:T(8,128)S(1)}, f32[64,640]{1,0:T(8,128)S(1)}, u32[]{:S(2)}, u32[]{:S(2)}) collective-permute-start(f32[64,640]{1,0:T(8,128)S(1)} %get-tuple-element.59.refs_1_.refs_0_), channel_id=1, source_target_pairs={{0,3},{1,2},{2,1},{3,0},{4,7},{5,6},{6,5},{7,4},{8,11},{9,10},{10,... | collective-permute-start | bytes 491528 | tf_op jit(solution)/shard_map/ppermute | solution.py:388
  23.5 13.4 %collective-permute-start.6 = (f32[64,896]{1,0:T(8,128)S(1)}, f32[64,896]{1,0:T(8,128)S(1)}, u32[]{:S(2)}, u32[]{:S(2)}) collective-permute-start(f32[64,896]{1,0:T(8,128)S(1)} %get-tuple-element.61.refs_1_), channel_id=1, source_target_pairs={{0,3},{1,2},{2,1},{3,0},{4,7},{5,6},{6,5},{7,4},{8,11},{9,10},{10,... | collective-permute-start | bytes 688136 | tf_op jit(solution)/shard_map/ppermute | solution.py:388
  34.1 9.4 %collective-permute-start.8 = (f32[64,1152]{1,0:T(8,128)S(1)}, f32[64,1152]{1,0:T(8,128)S(1)}, u32[]{:S(2)}, u32[]{:S(2)}) collective-permute-start(f32[64,1152]{1,0:T(8,128)S(1)} %shard_map.56.refs_4_.refs_0_), channel_id=1, source_target_pairs={{0,4},{1,5},{2,6},{3,7},{4,0},{5,1},{6,2},{7,3},{8,12},{9,13},{10,... | collective-permute-start | bytes 884744 | tf_op jit(solution)/shard_map/ppermute | solution.py:388
  37.3 4.1 %collective-permute-start.7 = (f32[64,512]{1,0:T(8,128)S(1)}, f32[64,512]{1,0:T(8,128)S(1)}, u32[]{:S(2)}, u32[]{:S(2)}) collective-permute-start(f32[64,512]{1,0:T(8,128)S(1)} %get-tuple-element.62.refs_1_.refs_0_), channel_id=1, source_target_pairs={{0,4},{1,5},{2,6},{3,7},{4,0},{5,1},{6,2},{7,3},{8,12},{9,13},{10,... | collective-permute-start | bytes 393224 | tf_op jit(solution)/shard_map/ppermute | solution.py:388
  43.5 15.6 %collective-permute-start.11 = (f32[64,1152]{1,0:T(8,128)S(1)}, f32[64,1152]{1,0:T(8,128)S(1)}, u32[]{:S(2)}, u32[]{:S(2)}) collective-permute-start(f32[64,1152]{1,0:T(8,128)S(1)} %shard_map.60.refs_4_.refs_0_), channel_id=1, source_target_pairs={{0,12},{1,13},{2,14},{3,15},{4,8},{5,9},{6,10},{7,11},{8,4},{9,5},... | collective-permute-start | bytes 884744 | tf_op jit(solution)/shard_map/ppermute | solution.py:388
  46.3 3.8 %collective-permute-start.9 = (f32[64,512]{1,0:T(8,128)S(1)}, f32[64,512]{1,0:T(8,128)S(1)}, u32[]{:S(2)}, u32[]{:S(2)}) collective-permute-start(f32[64,512]{1,0:T(8,128)S(1)} %get-tuple-element.64.refs_1_), channel_id=1, source_target_pairs={{0,4},{1,5},{2,6},{3,7},{4,0},{5,1},{6,2},{7,3},{8,12},{9,13},{10,... | collective-permute-start | bytes 393224 | tf_op jit(solution)/shard_map/ppermute | solution.py:388
  50.6 6.5 %collective-permute-start.10 = (f32[64,512]{1,0:T(8,128)S(1)}, f32[64,512]{1,0:T(8,128)S(1)}, u32[]{:S(2)}, u32[]{:S(2)}) collective-permute-start(f32[64,512]{1,0:T(8,128)S(1)} %shard_map.61.refs_1_), channel_id=1, source_target_pairs={{0,12},{1,13},{2,14},{3,15},{4,8},{5,9},{6,10},{7,11},{8,4},{9,5},... | collective-permute-start | bytes 393224 | tf_op jit(solution)/shard_map/ppermute | solution.py:388
  59.1 9.6 %collective-permute-start.12 = (f32[64,1152]{1,0:T(8,128)S(1)}, f32[64,1152]{1,0:T(8,128)S(1)}, u32[]{:S(2)}, u32[]{:S(2)}) collective-permute-start(f32[64,1152]{1,0:T(8,128)S(1)} %shard_map.64.refs_1_.refs_4_), channel_id=1, source_target_pairs={{0,16},{16,0},{32,48},{48,32},{64,80},{80,64},{96,112},{112,96},{1... | collective-permute-start | bytes 884744 | tf_op jit(solution)/shard_map/ppermute | solution.py:388
  70.7 4.1 %collective-permute-start.13 = (f32[32,768]{1,0:T(8,128)S(1)}, f32[32,768]{1,0:T(8,128)S(1)}, u32[]{:S(2)}, u32[]{:S(2)}) collective-permute-start(f32[32,768]{1,0:T(8,128)S(1)} %get-tuple-element.67), channel_id=1, source_target_pairs={{0,32},{16,48},{32,0},{48,16},{64,96},{80,112},{96,64},{112,80},{1... | collective-permute-start | bytes 294920 | tf_op jit(solution)/shard_map/ppermute | solution.py:388
  74.7 4.0 %collective-permute-start.14 = (f32[32,768]{1,0:T(8,128)S(1)}, f32[32,768]{1,0:T(8,128)S(1)}, u32[]{:S(2)}, u32[]{:S(2)}) collective-permute-start(f32[32,768]{1,0:T(8,128)S(1)} %collective-permute-done.13.refs_2_), channel_id=1, source_target_pairs={{0,16},{16,0},{32,48},{48,32},{64,80},{80,64},{96,112},{112,96},{1... | collective-permute-start | bytes 294920 | tf_op jit(solution)/shard_map/ppermute | solution.py:388
  80.4 6.1 %collective-permute-start.15 = (f32[32,512]{1,0:T(8,128)S(1)}, f32[32,512]{1,0:T(8,128)S(1)}, u32[]{:S(2)}, u32[]{:S(2)}) collective-permute-start(f32[32,512]{1,0:T(8,128)S(1)} %get-tuple-element.73), channel_id=1, source_target_pairs={{0,64},{16,80},{32,96},{48,112},{64,0},{80,16},{96,32},{112,48},{1... | collective-permute-start | bytes 196616 | tf_op jit(solution)/shard_map/ppermute | solution.py:388
  86.5 1.6 %collective-permute-start.16 = (f32[32,512]{1,0:T(8,128)S(1)}, f32[32,512]{1,0:T(8,128)S(1)}, u32[]{:S(2)}, u32[]{:S(2)}) collective-permute-start(f32[32,512]{1,0:T(8,128)S(1)} %collective-permute-done.15.refs_2_), channel_id=1, source_target_pairs={{0,16},{16,0},{32,48},{48,32},{64,80},{80,64},{96,112},{112,96},{1... | collective-permute-start | bytes 196616 | tf_op jit(solution)/shard_map/ppermute | solution.py:388
  89.8 8.7 %collective-permute-start.17 = (f32[64,256]{1,0:T(8,128)S(1)}, f32[64,256]{1,0:T(8,128)S(1)}, u32[]{:S(2)}, u32[]{:S(2)}) collective-permute-start(f32[64,256]{1,0:T(8,128)S(1)} %get-tuple-element.78.refs_1_), channel_id=1, source_target_pairs={{0,192},{16,208},{32,224},{48,240},{64,128},{80,144},{96,160},{112... | collective-permute-start | bytes 196616 | tf_op jit(solution)/shard_map/ppermute | solution.py:388

commit v13 on v12

--- a/solution.py
+++ b/solution.py
@@ -107,9 +107,10 @@
     return 128 * (R * j // 128)
 
 
-def panel_out(rows, j, y_ref, z_ref, m_ref):
+def panel_out(rows, j, y_ref, z_ref, m_ref, minv=None):
     split = M - lanes_from(j)
-    minv = chol_inverse(rows[:, :128], R * j - lanes_from(j))
+    if minv is None:
+        minv = chol_inverse(rows[:, :128], R * j - lanes_from(j))
     m_ref[...] = minv
     panel = mm(minv, jnp.concatenate([rows, rows], axis=0))
     z_ref[...] = panel[:, :split]
@@ -127,9 +128,11 @@
             )
     for copy in copies:
         copy.start()
-    for copy in copies[:3]:
-        copy.wait()
-    panel_out(head[...], 0, y_ref, z_ref, m_ref)
+    copies[0].wait()
+    minv = chol_inverse(head[:, :128], 0)
+    copies[1].wait()
+    copies[2].wait()
+    panel_out(head[...], 0, y_ref, z_ref, m_ref, minv)
     for copy in copies[3:]:
         copy.wait()
 

time: 101 us -> 101 us (level)
  no operation moved by 1% of the time
where the time goes in v13:
time: 101 us
  waiting for transfers between devices  34.5 us (34%)
  Pallas kernels  34.4 us (34%)
  starting transfers between devices  31.8 us (31%)
    ppermute x18, waiting for transfers between devices, exchange(): lax.ppermute(value, axis, [(s, s ^ mask) for s in range(lax.axis_size(axi...  34.5 us
    pallas_call x27, Pallas kernels, call(): pl.pallas_call(kernel, out_shape=shapes, in_specs=[hb if i in hbm else vm...  34.4 us
    ppermute x18, starting transfers between devices, exchange(): lax.ppermute(value, axis, [(s, s ^ mask) for s in range(lax.axis_size(axi...  31.8 us
  transfers between devices with their start and end apart: 18, of which 10 were waited for; matrix products, arithmetic and copies ran while one was open for 0% of the time, Pallas kernels for 21%

profile of v13, /device:TPU:39, one launch (start us, length us, event | category | flops | bytes accessed | tf_op | source)
XLA Modules:
  0.0 100.9 jit_solution(5812925930833234086)
XLA Ops:
  0.0 2.3 %shard_map.46 = (f32[64,640]{1,0:T(8,128)S(1)}, f32[64,256]{1,0:T(8,128)S(1)}, f32[64,128]{1,0:T(8,128)S(1)}, f32[192,896]{1,0:T(8,128)S(1)}) custom-call(f32[256,256]{1,0:T(8,128)} %d_any.1, f32[256,512]{1,0:T(8,128)} %b_any.1, f32[256,128]{1,0:T(8,128)} %t_any.1), custom_call_target="tpu_custom_call" | custom-call | flops 10000000 | bytes 1000000 | tf_op jit(solution)/shard_map/pallas_call | solution.py:377
  2.3 0.6 collective-permute-start
  2.9 1.8 %shard_map.47 = (f32[64,640]{1,0:T(8,128)S(1)}, f32[64,256]{1,0:T(8,128)S(1)}, f32[64,128]{1,0:T(8,128)S(1)}) custom-call(f32[192,896]{1,0:T(8,128)S(1)} %get-tuple-element.44.refs_0_, f32[64,640]{1,0:T(8,128)S(1)} %get-tuple-element.43.refs_1_.refs_0_, f32[64,256]{1,0:T(8,128)S(1)} %get-tuple-element.45.refs_2_.refs_3_.refs_4_), custom_call_target="tpu_custom_call" | custom-call | flops 10000000 | bytes 1000000 | tf_op jit(solution)/shard_map/pallas_call | solution.py:377
  4.7 1.0 collective-permute-start.1
  5.7 1.8 %shard_map.48 = (f32[64,640]{1,0:T(8,128)S(1)}, f32[64,128]{1,0:T(8,128)S(1)}, f32[64,128]{1,0:T(8,128)S(1)}) custom-call(f32[192,896]{1,0:T(8,128)S(1)} %get-tuple-element.44.refs_0_, f32[64,640]{1,0:T(8,128)S(1)} %get-tuple-element.43.refs_1_.refs_0_, f32[64,640]{1,0:T(8,128)S(1)} %get-tuple-element.46.refs_2_.refs_1_, ...), custom_call_target="tpu_custom_call" | custom-call | flops 10000000 | bytes 1000000 | tf_op jit(solution)/shard_map/pallas_call | solution.py:377
  7.5 1.8 %shard_map.49 = (f32[64,640]{1,0:T(8,128)S(1)}, f32[64,128]{1,0:T(8,128)S(1)}, f32[64,128]{1,0:T(8,128)S(1)}) custom-call(f32[192,896]{1,0:T(8,128)S(1)} %get-tuple-element.44.refs_0_, f32[64,640]{1,0:T(8,128)S(1)} %get-tuple-element.43.refs_1_.refs_0_, f32[64,640]{1,0:T(8,128)S(1)} %get-tuple-element.46.refs_2_.refs_1_, ...), custom_call_target="tpu_custom_call" | custom-call | flops 10000000 | bytes 1000000 | tf_op jit(solution)/shard_map/pallas_call | solution.py:377
  9.3 0.6 collective-permute-start.3
  10.0 0.9 collective-permute-start.2
  10.9 2.3 %shard_map.51.refs_2_.refs_3_.w_ref = f32[256,640]{1,0:T(8,128)S(1)} custom-call(f32[64,640]{1,0:T(8,128)S(1)} %get-tuple-element.43.refs_1_.refs_0_, f32[64,640]{1,0:T(8,128)S(1)} %get-tuple-element.46.refs_2_.refs_1_, f32[64,640]{1,0:T(8,128)S(1)} %get-tuple-element.48.refs_3_.refs_2_, f32[64,640]{1,0:T(8,128)S(1)} %get-tuple-element.50.refs_3_, ...), custom_call_target="tpu_custom_call" | custom-call | flops 10000000 | bytes 1000000 | tf_op jit(solution)/shard_map/pallas_call | solution.py:377
  13.2 0.0 collective-permute-done.1.refs_5_
  13.2 0.0 collective-permute-done.refs_4_
  13.2 0.0 copy-start
  13.2 1.9 %shard_map.50 = (f32[64,2304]{1,0:T(8,128)S(1)}, f32[64,1152]{1,0:T(8,128)S(1)}) custom-call(f32[64,640]{1,0:T(8,128)S(1)} %get-tuple-element.43.refs_1_.refs_0_, f32[64,640]{1,0:T(8,128)S(1)} %get-tuple-element.46.refs_2_.refs_1_, f32[64,640]{1,0:T(8,128)S(1)} %get-tuple-element.48.refs_3_.refs_2_, f32[64,640]{1,0:T(8,128)S(1)} %get-tuple-element.50.refs_3_, ...), custom_call_target="tpu_custom_call" | custom-call | flops 10000000 | bytes 1000000 | tf_op jit(solution)/shard_map/pallas_call | solution.py:377
  15.1 0.0 collective-permute-done.3.refs_1_
  15.1 2.4 %collective-permute-done.2.refs_0_ = f32[64,640]{1,0:T(8,128)S(1)} collective-permute-done((f32[64,640]{1,0:T(8,128)S(1)}, f32[64,640]{1,0:T(8,128)S(1)}, u32[]{:S(2)}, u32[]{:S(2)}) %collective-permute-start.2) | collective-permute-done | bytes 163872 | tf_op jit(solution)/shard_map/ppermute | solution.py:391
  17.4 0.0 copy-done
  17.5 2.3 %shard_map.52 = (f32[64,640]{1,0:T(8,128)S(1)}, f32[64,128]{1,0:T(8,128)S(1)}, f32[64,640]{1,0:T(8,128)S(1)}, f32[64,896]{1,0:T(8,128)S(1)}) custom-call(f32[8,64]{1,0:T(8,128)S(1)} %copy-done, f32[64,2304]{1,0:T(8,128)S(1)} %get-tuple-element.52.own_ref, f32[64,640]{1,0:T(8,128)S(1)} %collective-permute-done.2.refs_0_, ...), custom_call_target="tpu_custom_call" | custom-call | flops 10000000 | bytes 1000000 | tf_op jit(solution)/shard_map/pallas_call | solution.py:377
  19.8 0.8 shard_map.53.refs_4_.refs_0_
  20.6 0.3 collective-permute-start.5
  20.9 2.5 %collective-permute-start.4 = (f32[64,640]{1,0:T(8,128)S(1)}, f32[64,640]{1,0:T(8,128)S(1)}, u32[]{:S(2)}, u32[]{:S(2)}) collective-permute-start(f32[64,640]{1,0:T(8,128)S(1)} %get-tuple-element.59.refs_1_.refs_0_), channel_id=1, source_target_pairs={{0,3},{1,2},{2,1},{3,0},{4,7},{5,6},{6,5},{7,4},{8,11},{9,10},{10,... | collective-permute-start | bytes 491528 | tf_op jit(solution)/shard_map/ppermute | solution.py:391
  23.4 0.2 collective-permute-start.6
  23.5 8.3 %collective-permute-done.4.refs_2_ = f32[64,640]{1,0:T(8,128)S(1)} collective-permute-done((f32[64,640]{1,0:T(8,128)S(1)}, f32[64,640]{1,0:T(8,128)S(1)}, u32[]{:S(2)}, u32[]{:S(2)}) %collective-permute-start.4) | collective-permute-done | bytes 163872 | tf_op jit(solution)/shard_map/ppermute | solution.py:391
  31.9 1.5 %shard_map.54 = (f32[64,640]{1,0:T(8,128)S(1)}, f32[64,128]{1,0:T(8,128)S(1)}) custom-call(f32[8,64]{1,0:T(8,128)S(1)} %copy-done, f32[64,640]{1,0:T(8,128)S(1)} %get-tuple-element.59.refs_1_.refs_0_, f32[64,640]{1,0:T(8,128)S(1)} %collective-permute-done.4.refs_2_, f32[256,640]{1,0:T(8,128)S(1)} %shard_map.51.refs_2_.refs_3_.w_ref, ...), custom_call_target="tpu_custom_call" | custom-call | flops 10000000 | bytes 1000000 | tf_op jit(solution)/shard_map/pallas_call | solution.py:377
  33.4 0.5 shard_map.55.own_ref
  33.9 0.0 collective-permute-done.5.got_ref
  34.0 1.4 %collective-permute-start.8 = (f32[64,1152]{1,0:T(8,128)S(1)}, f32[64,1152]{1,0:T(8,128)S(1)}, u32[]{:S(2)}, u32[]{:S(2)}) collective-permute-start(f32[64,1152]{1,0:T(8,128)S(1)} %shard_map.56.refs_4_.refs_0_), channel_id=1, source_target_pairs={{0,4},{1,5},{2,6},{3,7},{4,0},{5,1},{6,2},{7,3},{8,12},{9,13},{10,... | collective-permute-start | bytes 884744 | tf_op jit(solution)/shard_map/ppermute | solution.py:391
  35.3 1.5 %collective-permute-done.6.refs_3_ = f32[64,896]{1,0:T(8,128)S(1)} collective-permute-done((f32[64,896]{1,0:T(8,128)S(1)}, f32[64,896]{1,0:T(8,128)S(1)}, u32[]{:S(2)}, u32[]{:S(2)}) %collective-permute-start.6) | collective-permute-done | bytes 229408 | tf_op jit(solution)/shard_map/ppermute | solution.py:391
  36.8 0.4 shard_map.57
  37.2 1.6 %collective-permute-start.7 = (f32[64,512]{1,0:T(8,128)S(1)}, f32[64,512]{1,0:T(8,128)S(1)}, u32[]{:S(2)}, u32[]{:S(2)}) collective-permute-start(f32[64,512]{1,0:T(8,128)S(1)} %get-tuple-element.62.refs_1_.refs_0_), channel_id=1, source_target_pairs={{0,4},{1,5},{2,6},{3,7},{4,0},{5,1},{6,2},{7,3},{8,12},{9,13},{10,... | collective-permute-start | bytes 393224 | tf_op jit(solution)/shard_map/ppermute | solution.py:391
  38.8 2.5 %collective-permute-done.7.refs_2_ = f32[64,512]{1,0:T(8,128)S(1)} collective-permute-done((f32[64,512]{1,0:T(8,128)S(1)}, f32[64,512]{1,0:T(8,128)S(1)}, u32[]{:S(2)}, u32[]{:S(2)}) %collective-permute-start.7) | collective-permute-done | bytes 131104 | tf_op jit(solution)/shard_map/ppermute | solution.py:391
  41.3 1.4 %shard_map.58 = (f32[64,512]{1,0:T(8,128)S(1)}, f32[64,128]{1,0:T(8,128)S(1)}) custom-call(f32[8,64]{1,0:T(8,128)S(1)} %copy-done, f32[64,512]{1,0:T(8,128)S(1)} %get-tuple-element.62.refs_1_.refs_0_, f32[64,512]{1,0:T(8,128)S(1)} %collective-permute-done.7.refs_2_, f32[256,640]{1,0:T(8,128)S(1)} %shard_map.51.refs_2_.refs_3_.w_ref, ...), custom_call_target="tpu_custom_call" | custom-call | flops 10000000 | bytes 1000000 | tf_op jit(solution)/shard_map/pallas_call | solution.py:377
  42.8 0.5 shard_map.59.own_ref
  43.3 0.0 collective-permute-done.8.got_ref
  43.4 2.8 %collective-permute-start.11 = (f32[64,1152]{1,0:T(8,128)S(1)}, f32[64,1152]{1,0:T(8,128)S(1)}, u32[]{:S(2)}, u32[]{:S(2)}) collective-permute-start(f32[64,1152]{1,0:T(8,128)S(1)} %shard_map.60.refs_4_.refs_0_), channel_id=1, source_target_pairs={{0,12},{1,13},{2,14},{3,15},{4,8},{5,9},{6,10},{7,11},{8,4},{9,5},... | collective-permute-start | bytes 884744 | tf_op jit(solution)/shard_map/ppermute | solution.py:391
  46.2 0.0 collective-permute-start.9
  46.2 3.8 %collective-permute-done.9.refs_3_ = f32[64,512]{1,0:T(8,128)S(1)} collective-permute-done((f32[64,512]{1,0:T(8,128)S(1)}, f32[64,512]{1,0:T(8,128)S(1)}, u32[]{:S(2)}, u32[]{:S(2)}) %collective-permute-start.9) | collective-permute-done | bytes 131104 | tf_op jit(solution)/shard_map/ppermute | solution.py:391
  50.0 0.4 shard_map.61.refs_1_
  50.5 1.1 %collective-permute-start.10 = (f32[64,512]{1,0:T(8,128)S(1)}, f32[64,512]{1,0:T(8,128)S(1)}, u32[]{:S(2)}, u32[]{:S(2)}) collective-permute-start(f32[64,512]{1,0:T(8,128)S(1)} %shard_map.61.refs_1_), channel_id=1, source_target_pairs={{0,12},{1,13},{2,14},{3,15},{4,8},{5,9},{6,10},{7,11},{8,4},{9,5},... | collective-permute-start | bytes 393224 | tf_op jit(solution)/shard_map/ppermute | solution.py:391
  51.5 5.5 %collective-permute-done.10.refs_2_ = f32[64,512]{1,0:T(8,128)S(1)} collective-permute-done((f32[64,512]{1,0:T(8,128)S(1)}, f32[64,512]{1,0:T(8,128)S(1)}, u32[]{:S(2)}, u32[]{:S(2)}) %collective-permute-start.10) | collective-permute-done | bytes 131104 | tf_op jit(solution)/shard_map/ppermute | solution.py:391
  57.0 1.4 %shard_map.62 = (f32[64,512]{1,0:T(8,128)S(1)}, f32[64,128]{1,0:T(8,128)S(1)}) custom-call(f32[8,64]{1,0:T(8,128)S(1)} %copy-done, f32[64,512]{1,0:T(8,128)S(1)} %shard_map.61.refs_1_, f32[64,512]{1,0:T(8,128)S(1)} %collective-permute-done.10.refs_2_, f32[256,640]{1,0:T(8,128)S(1)} %shard_map.51.refs_2_.refs_3_.w_ref, f32[64,1152]{1,0:T(8,128)S(1)} %shard_map.60.refs_4_.refs_0_), custom_call_target="tpu_custom_call" | custom-call | flops 10000000 | bytes 1000000 | tf_op jit(solution)/shard_map/pallas_call | solution.py:377
  58.5 0.5 shard_map.63.own_ref
  59.0 0.0 collective-permute-done.11.got_ref
  59.1 8.3 %collective-permute-start.12 = (f32[64,1152]{1,0:T(8,128)S(1)}, f32[64,1152]{1,0:T(8,128)S(1)}, u32[]{:S(2)}, u32[]{:S(2)}) collective-permute-start(f32[64,1152]{1,0:T(8,128)S(1)} %shard_map.64.refs_1_.refs_4_), channel_id=1, source_target_pairs={{0,16},{16,0},{32,48},{48,32},{64,80},{80,64},{96,112},{112,96},{1... | collective-permute-start | bytes 884744 | tf_op jit(solution)/shard_map/ppermute | solution.py:391
  67.4 1.2 %collective-permute-done.12.refs_2_ = f32[64,1152]{1,0:T(8,128)S(1)} collective-permute-done((f32[64,1152]{1,0:T(8,128)S(1)}, f32[64,1152]{1,0:T(8,128)S(1)}, u32[]{:S(2)}, u32[]{:S(2)}) %collective-permute-start.12) | collective-permute-done | bytes 294944 | tf_op jit(solution)/shard_map/ppermute | solution.py:391
  68.6 1.9 %shard_map.65 = (f32[64,384]{1,0:T(8,128)S(1)}, f32[64,128]{1,0:T(8,128)S(1)}, f32[64,768]{1,0:T(8,128)S(1)}, f32[32,768]{1,0:T(8,128)S(1)}) custom-call(f32[8,64]{1,0:T(8,128)S(1)} %copy-done, f32[64,1152]{1,0:T(8,128)S(1)} %shard_map.64.refs_1_.refs_4_, f32[64,1152]{1,0:T(8,128)S(1)} %collective-permute-done.12.refs_2_, ...), custom_call_target="tpu_custom_call" | custom-call | flops 10000000 | bytes 1000000 | tf_op jit(solution)/shard_map/pallas_call | solution.py:377
  70.5 0.1 collective-permute-start.13
  70.6 4.0 %collective-permute-done.13.refs_2_ = f32[32,768]{1,0:T(8,128)S(1)} collective-permute-done((f32[32,768]{1,0:T(8,128)S(1)}, f32[32,768]{1,0:T(8,128)S(1)}, u32[]{:S(2)}, u32[]{:S(2)}) %collective-permute-start.13) | collective-permute-done | bytes 98336 | tf_op jit(solution)/shard_map/ppermute | solution.py:391
  74.6 1.2 %collective-permute-start.14 = (f32[32,768]{1,0:T(8,128)S(1)}, f32[32,768]{1,0:T(8,128)S(1)}, u32[]{:S(2)}, u32[]{:S(2)}) collective-permute-start(f32[32,768]{1,0:T(8,128)S(1)} %collective-permute-done.13.refs_2_), channel_id=1, source_target_pairs={{0,16},{16,0},{32,48},{48,32},{64,80},{80,64},{96,112},{112,96},{1... | collective-permute-start | bytes 294920 | tf_op jit(solution)/shard_map/ppermute | solution.py:391
  75.8 1.4 %shard_map.66.w_ref = f32[256,512]{1,0:T(8,128)S(1)} custom-call(f32[256,640]{1,0:T(8,128)S(1)} %shard_map.51.refs_2_.refs_3_.w_ref, f32[64,640]{1,0:T(8,128)S(1)} %get-tuple-element.58.refs_2_.p_ref, f32[64,128]{1,0:T(8,128)S(1)} %get-tuple-element.68.m_ref, f32[64,640]{1,0:T(8,128)S(1)} %get-tuple-element.60.refs_1_.refs_4_.p2_ref, ...), custom_call_target="tpu_custom_call" | custom-call | flops 10000000 | bytes 1000000 | tf_op jit(solution)/shard_map/pallas_call | solution.py:377
  77.2 1.3 %shard_map.67.refs_4_.w_ref = f32[256,384]{1,0:T(8,128)S(1)} custom-call(f32[256,512]{1,0:T(8,128)S(1)} %shard_map.66.w_ref, f32[64,512]{1,0:T(8,128)S(1)} %get-tuple-element.63.refs_1_.refs_4_.p_ref, f32[64,128]{1,0:T(8,128)S(1)} %get-tuple-element.70.m_ref, f32[64,512]{1,0:T(8,128)S(1)} %get-tuple-element.65.refs_1_.p2_ref, ...), custom_call_target="tpu_custom_call" | custom-call | flops 10000000 | bytes 1000000 | tf_op jit(solution)/shard_map/pallas_call | solution.py:377
  78.6 0.0 collective-permute-done.14.refs_3_
  78.6 1.7 %shard_map.68 = (f32[64,384]{1,0:T(8,128)S(1)}, f32[64,128]{1,0:T(8,128)S(1)}, f32[64,512]{1,0:T(8,128)S(1)}, f32[32,512]{1,0:T(8,128)S(1)}) custom-call(f32[8,64]{1,0:T(8,128)S(1)} %copy-done, f32[64,768]{1,0:T(8,128)S(1)} %get-tuple-element.66.refs_1_, f32[32,768]{1,0:T(8,128)S(1)} %collective-permute-done.13.refs_2_, ...), custom_call_target="tpu_custom_call" | custom-call | flops 10000000 | bytes 1000000 | tf_op jit(solution)/shard_map/pallas_call | solution.py:377
  80.3 3.1 %collective-permute-start.15 = (f32[32,512]{1,0:T(8,128)S(1)}, f32[32,512]{1,0:T(8,128)S(1)}, u32[]{:S(2)}, u32[]{:S(2)}) collective-permute-start(f32[32,512]{1,0:T(8,128)S(1)} %get-tuple-element.73), channel_id=1, source_target_pairs={{0,64},{16,80},{32,96},{48,112},{64,0},{80,16},{96,32},{112,48},{1... | collective-permute-start | bytes 196616 | tf_op jit(solution)/shard_map/ppermute | solution.py:391
  83.4 3.0 %collective-permute-done.15.refs_2_ = f32[32,512]{1,0:T(8,128)S(1)} collective-permute-done((f32[32,512]{1,0:T(8,128)S(1)}, f32[32,512]{1,0:T(8,128)S(1)}, u32[]{:S(2)}, u32[]{:S(2)}) %collective-permute-start.15) | collective-permute-done | bytes 65568 | tf_op jit(solution)/shard_map/ppermute | solution.py:391
  86.4 0.5 collective-permute-start.16
  86.9 1.1 %shard_map.69.refs_4_.refs_0_ = f32[256,256]{1,0:T(8,128)S(1)} custom-call(f32[256,384]{1,0:T(8,128)S(1)} %shard_map.67.refs_4_.w_ref, f32[64,384]{1,0:T(8,128)S(1)} %get-tuple-element.74.p_ref, f32[64,128]{1,0:T(8,128)S(1)} %get-tuple-element.75.m_ref, f32[64,384]{1,0:T(8,128)S(1)} %get-tuple-element.76.p2_ref, f32[64,128]{1,0:T(8,128)S(1)} %get-tuple-element.77.m2_ref), custom_call_target="tpu_custom_call" | custom-call | flops 10000000 | bytes 1000000 | tf_op jit(solution)/shard_map/pallas_call | solution.py:377
  87.9 0.0 collective-permute-done.16.refs_3_
  88.0 1.8 %shard_map.70 = (f32[64,256]{1,0:T(8,128)S(1)}, f32[64,128]{1,0:T(8,128)S(1)}, f32[64,256]{1,0:T(8,128)S(1)}) custom-call(f32[8,64]{1,0:T(8,128)S(1)} %copy-done, f32[64,512]{1,0:T(8,128)S(1)} %get-tuple-element.72.refs_1_, f32[32,512]{1,0:T(8,128)S(1)} %collective-permute-done.15.refs_2_, f32[32,512]{1,0:T(8,128)S(1)} %collective-permute-done.16.refs_3_, ...), custom_call_target="tpu_custom_call" | custom-call | flops 10000000 | bytes 1000000 | tf_op jit(solution)/shard_map/pallas_call | solution.py:377
  89.7 5.6 %collective-permute-start.17 = (f32[64,256]{1,0:T(8,128)S(1)}, f32[64,256]{1,0:T(8,128)S(1)}, u32[]{:S(2)}, u32[]{:S(2)}) collective-permute-start(f32[64,256]{1,0:T(8,128)S(1)} %get-tuple-element.78.refs_1_), channel_id=1, source_target_pairs={{0,192},{16,208},{32,224},{48,240},{64,128},{80,144},{96,160},{112... | collective-permute-start | bytes 196616 | tf_op jit(solution)/shard_map/ppermute | solution.py:391
  95.3 0.8 shard_map.71.refs_3_
  96.1 2.3 %collective-permute-done.17.refs_2_ = f32[64,256]{1,0:T(8,128)S(1)} collective-permute-done((f32[64,256]{1,0:T(8,128)S(1)}, f32[64,256]{1,0:T(8,128)S(1)}, u32[]{:S(2)}, u32[]{:S(2)}) %collective-permute-start.17) | collective-permute-done | bytes 65568 | tf_op jit(solution)/shard_map/ppermute | solution.py:391
  98.4 2.5 %shard_map.72 = f32[256,128]{1,0:T(8,128)} custom-call(f32[8,64]{1,0:T(8,128)S(1)} %copy-done, f32[64,256]{1,0:T(8,128)S(1)} %get-tuple-element.78.refs_1_, f32[64,256]{1,0:T(8,128)S(1)} %collective-permute-done.17.refs_2_, f32[256,256]{1,0:T(8,128)S(1)} %shard_map.71.refs_3_), custom_call_target="tpu_custom_call" | custom-call | flops 10000000 | bytes 1000000 | tf_op jit(solution)/shard_map/pallas_call | solution.py:377
  (3 shorter events, 0.1 us)
Async XLA Ops:
  2.3 10.9 %collective-permute-start = (f32[64,640]{1,0:T(8,128)S(1)}, f32[64,640]{1,0:T(8,128)S(1)}, u32[]{:S(2)}, u32[]{:S(2)}) collective-permute-start(f32[64,640]{1,0:T(8,128)S(1)} %get-tuple-element.43.refs_1_.refs_0_), channel_id=1, source_target_pairs={{0,1},{1,0},{2,3},{3,2},{4,5},{5,4},{6,7},{7,6},{8,9},{9,8},{10,11... | collective-permute-start | bytes 491528 | tf_op jit(solution)/shard_map/ppermute | solution.py:391
  4.7 8.4 %collective-permute-start.1 = (f32[64,640]{1,0:T(8,128)S(1)}, f32[64,640]{1,0:T(8,128)S(1)}, u32[]{:S(2)}, u32[]{:S(2)}) collective-permute-start(f32[64,640]{1,0:T(8,128)S(1)} %get-tuple-element.46.refs_2_.refs_1_), channel_id=1, source_target_pairs={{0,1},{1,0},{2,3},{3,2},{4,5},{5,4},{6,7},{7,6},{8,9},{9,8},{10,11... | collective-permute-start | bytes 491528 | tf_op jit(solution)/shard_map/ppermute | solution.py:391
  9.3 5.7 %collective-permute-start.3 = (f32[64,640]{1,0:T(8,128)S(1)}, f32[64,640]{1,0:T(8,128)S(1)}, u32[]{:S(2)}, u32[]{:S(2)}) collective-permute-start(f32[64,640]{1,0:T(8,128)S(1)} %get-tuple-element.50.refs_3_), channel_id=1, source_target_pairs={{0,1},{1,0},{2,3},{3,2},{4,5},{5,4},{6,7},{7,6},{8,9},{9,8},{10,11... | collective-permute-start | bytes 491528 | tf_op jit(solution)/shard_map/ppermute | solution.py:391
  10.0 7.5 %collective-permute-start.2 = (f32[64,640]{1,0:T(8,128)S(1)}, f32[64,640]{1,0:T(8,128)S(1)}, u32[]{:S(2)}, u32[]{:S(2)}) collective-permute-start(f32[64,640]{1,0:T(8,128)S(1)} %get-tuple-element.48.refs_3_.refs_2_), channel_id=1, source_target_pairs={{0,1},{1,0},{2,3},{3,2},{4,5},{5,4},{6,7},{7,6},{8,9},{9,8},{10,11... | collective-permute-start | bytes 491528 | tf_op jit(solution)/shard_map/ppermute | solution.py:391
  13.2 4.3 %copy-start = (f32[8,64]{1,0:T(8,128)S(1)}, f32[8,64]{1,0:T(8,128)}, u32[]{:S(2)}) copy-start(f32[8,64]{1,0:T(8,128)} %refs_0_.13) | copy-start | bytes 6148
  20.6 13.3 %collective-permute-start.5 = (f32[64,1152]{1,0:T(8,128)S(1)}, f32[64,1152]{1,0:T(8,128)S(1)}, u32[]{:S(2)}, u32[]{:S(2)}) collective-permute-start(f32[64,1152]{1,0:T(8,128)S(1)} %shard_map.53.refs_4_.refs_0_), channel_id=1, source_target_pairs={{0,3},{1,2},{2,1},{3,0},{4,7},{5,6},{6,5},{7,4},{8,11},{9,10},{10,... | collective-permute-start | bytes 884744 | tf_op jit(solution)/shard_map/ppermute | solution.py:391
  20.9 11.0 %collective-permute-start.4 = (f32[64,640]{1,0:T(8,128)S(1)}, f32[64,640]{1,0:T(8,128)S(1)}, u32[]{:S(2)}, u32[]{:S(2)}) collective-permute-start(f32[64,640]{1,0:T(8,128)S(1)} %get-tuple-element.59.refs_1_.refs_0_), channel_id=1, source_target_pairs={{0,3},{1,2},{2,1},{3,0},{4,7},{5,6},{6,5},{7,4},{8,11},{9,10},{10,... | collective-permute-start | bytes 491528 | tf_op jit(solution)/shard_map/ppermute | solution.py:391
  23.4 13.4 %collective-permute-start.6 = (f32[64,896]{1,0:T(8,128)S(1)}, f32[64,896]{1,0:T(8,128)S(1)}, u32[]{:S(2)}, u32[]{:S(2)}) collective-permute-start(f32[64,896]{1,0:T(8,128)S(1)} %get-tuple-element.61.refs_1_), channel_id=1, source_target_pairs={{0,3},{1,2},{2,1},{3,0},{4,7},{5,6},{6,5},{7,4},{8,11},{9,10},{10,... | collective-permute-start | bytes 688136 | tf_op jit(solution)/shard_map/ppermute | solution.py:391
  34.0 9.4 %collective-permute-start.8 = (f32[64,1152]{1,0:T(8,128)S(1)}, f32[64,1152]{1,0:T(8,128)S(1)}, u32[]{:S(2)}, u32[]{:S(2)}) collective-permute-start(f32[64,1152]{1,0:T(8,128)S(1)} %shard_map.56.refs_4_.refs_0_), channel_id=1, source_target_pairs={{0,4},{1,5},{2,6},{3,7},{4,0},{5,1},{6,2},{7,3},{8,12},{9,13},{10,... | collective-permute-start | bytes 884744 | tf_op jit(solution)/shard_map/ppermute | solution.py:391
  37.2 4.1 %collective-permute-start.7 = (f32[64,512]{1,0:T(8,128)S(1)}, f32[64,512]{1,0:T(8,128)S(1)}, u32[]{:S(2)}, u32[]{:S(2)}) collective-permute-start(f32[64,512]{1,0:T(8,128)S(1)} %get-tuple-element.62.refs_1_.refs_0_), channel_id=1, source_target_pairs={{0,4},{1,5},{2,6},{3,7},{4,0},{5,1},{6,2},{7,3},{8,12},{9,13},{10,... | collective-permute-start | bytes 393224 | tf_op jit(solution)/shard_map/ppermute | solution.py:391
  43.4 15.6 %collective-permute-start.11 = (f32[64,1152]{1,0:T(8,128)S(1)}, f32[64,1152]{1,0:T(8,128)S(1)}, u32[]{:S(2)}, u32[]{:S(2)}) collective-permute-start(f32[64,1152]{1,0:T(8,128)S(1)} %shard_map.60.refs_4_.refs_0_), channel_id=1, source_target_pairs={{0,12},{1,13},{2,14},{3,15},{4,8},{5,9},{6,10},{7,11},{8,4},{9,5},... | collective-permute-start | bytes 884744 | tf_op jit(solution)/shard_map/ppermute | solution.py:391
  46.2 3.8 %collective-permute-start.9 = (f32[64,512]{1,0:T(8,128)S(1)}, f32[64,512]{1,0:T(8,128)S(1)}, u32[]{:S(2)}, u32[]{:S(2)}) collective-permute-start(f32[64,512]{1,0:T(8,128)S(1)} %get-tuple-element.64.refs_1_), channel_id=1, source_target_pairs={{0,4},{1,5},{2,6},{3,7},{4,0},{5,1},{6,2},{7,3},{8,12},{9,13},{10,... | collective-permute-start | bytes 393224 | tf_op jit(solution)/shard_map/ppermute | solution.py:391
  50.5 6.5 %collective-permute-start.10 = (f32[64,512]{1,0:T(8,128)S(1)}, f32[64,512]{1,0:T(8,128)S(1)}, u32[]{:S(2)}, u32[]{:S(2)}) collective-permute-start(f32[64,512]{1,0:T(8,128)S(1)} %shard_map.61.refs_1_), channel_id=1, source_target_pairs={{0,12},{1,13},{2,14},{3,15},{4,8},{5,9},{6,10},{7,11},{8,4},{9,5},... | collective-permute-start | bytes 393224 | tf_op jit(solution)/shard_map/ppermute | solution.py:391
  59.1 9.5 %collective-permute-start.12 = (f32[64,1152]{1,0:T(8,128)S(1)}, f32[64,1152]{1,0:T(8,128)S(1)}, u32[]{:S(2)}, u32[]{:S(2)}) collective-permute-start(f32[64,1152]{1,0:T(8,128)S(1)} %shard_map.64.refs_1_.refs_4_), channel_id=1, source_target_pairs={{0,16},{16,0},{32,48},{48,32},{64,80},{80,64},{96,112},{112,96},{1... | collective-permute-start | bytes 884744 | tf_op jit(solution)/shard_map/ppermute | solution.py:391
  70.5 4.1 %collective-permute-start.13 = (f32[32,768]{1,0:T(8,128)S(1)}, f32[32,768]{1,0:T(8,128)S(1)}, u32[]{:S(2)}, u32[]{:S(2)}) collective-permute-start(f32[32,768]{1,0:T(8,128)S(1)} %get-tuple-element.67), channel_id=1, source_target_pairs={{0,32},{16,48},{32,0},{48,16},{64,96},{80,112},{96,64},{112,80},{1... | collective-permute-start | bytes 294920 | tf_op jit(solution)/shard_map/ppermute | solution.py:391
  74.6 4.0 %collective-permute-start.14 = (f32[32,768]{1,0:T(8,128)S(1)}, f32[32,768]{1,0:T(8,128)S(1)}, u32[]{:S(2)}, u32[]{:S(2)}) collective-permute-start(f32[32,768]{1,0:T(8,128)S(1)} %collective-permute-done.13.refs_2_), channel_id=1, source_target_pairs={{0,16},{16,0},{32,48},{48,32},{64,80},{80,64},{96,112},{112,96},{1... | collective-permute-start | bytes 294920 | tf_op jit(solution)/shard_map/ppermute | solution.py:391
  80.3 6.1 %collective-permute-start.15 = (f32[32,512]{1,0:T(8,128)S(1)}, f32[32,512]{1,0:T(8,128)S(1)}, u32[]{:S(2)}, u32[]{:S(2)}) collective-permute-start(f32[32,512]{1,0:T(8,128)S(1)} %get-tuple-element.73), channel_id=1, source_target_pairs={{0,64},{16,80},{32,96},{48,112},{64,0},{80,16},{96,32},{112,48},{1... | collective-permute-start | bytes 196616 | tf_op jit(solution)/shard_map/ppermute | solution.py:391
  86.4 1.6 %collective-permute-start.16 = (f32[32,512]{1,0:T(8,128)S(1)}, f32[32,512]{1,0:T(8,128)S(1)}, u32[]{:S(2)}, u32[]{:S(2)}) collective-permute-start(f32[32,512]{1,0:T(8,128)S(1)} %collective-permute-done.15.refs_2_), channel_id=1, source_target_pairs={{0,16},{16,0},{32,48},{48,32},{64,80},{80,64},{96,112},{112,96},{1... | collective-permute-start | bytes 196616 | tf_op jit(solution)/shard_map/ppermute | solution.py:391
  89.7 8.7 %collective-permute-start.17 = (f32[64,256]{1,0:T(8,128)S(1)}, f32[64,256]{1,0:T(8,128)S(1)}, u32[]{:S(2)}, u32[]{:S(2)}) collective-permute-start(f32[64,256]{1,0:T(8,128)S(1)} %get-tuple-element.78.refs_1_), channel_id=1, source_target_pairs={{0,192},{16,208},{32,224},{48,240},{64,128},{80,144},{96,160},{112... | collective-permute-start | bytes 196616 | tf_op jit(solution)/shard_map/ppermute | solution.py:391
